TPU v7x, 32 devices: a whole 2x2x4 slice. The times are simulated.
32 devices in a mesh: shots: 2 (over x), gx: 8 (over z, y), gy: 2 (over core).
Axes of the slice: x: 2, y: 2, z: 4, core: 2. Of those that a mesh axis runs over, the one named last changes fastest.
Arguments:
- field_now: float32 [512, 96, 128], P(('shots', 'gx'), 'gy'), parts along dimension 0, may hold values from -6 to 6
- field_prev: float32 [512, 96, 128], P(('shots', 'gx'), 'gy'), parts along dimension 0, may hold values from -6 to 6
- courant_squared: float32 [256, 96, 128], P('gx', 'gy'), may hold values from 0.05 to 0.18, as said below
- source_cells: int32 [3, 16], P(None, 'shots'), parts along dimension 1, may hold values from 0 to 127, as said below
- source_wave: float32 [4, 16], P(None, 'shots'), parts along dimension 1, may hold values from -8 to 8
- receiver_cells: int32 [3, 512], P(None, 'shots'), parts along dimension 1, may hold values from 0 to 127, as said below
- receiver_wave: float32 [4, 512], P(None, 'shots'), parts along dimension 1, may hold values from -8 to 8
- snapshot_steps: int32 [4, 2], P('shots'), parts along dimension 0, may hold values from 1 to 4, as said below
- lag_offsets: int32 [17], replicated, may hold values from -8 to 8
Outputs:
- final_field: float32 [512, 96, 128], P(('shots', 'gx'), 'gy'), parts along dimension 0
- extended_image: float32 [256, 17, 1536], P(('shots', 'gx'), None, 'gy'), parts along dimension 0
There are 2 independent parts, one for each index of `shots`. A program takes and returns all parts, laid end to end along the dimension named above; an argument that names none is the same for every part. Nothing has to cross between parts.
Inputs may be any that keep to these rules, and one draw needn't show every extreme that they name: `courant_squared`: both fields' rows of the same model cell hold the same value. `source_cells`: row 0 is an x cell below 128, row 1 a y cell below 96, row 2 a z cell below 128. `receiver_cells`: row 0 is an x cell below 128, row 1 a y cell below 96, row 2 a z cell below 128. `snapshot_steps`: column 0 lies in 1 to 2, column 1 in 3 to 4.
All inputs are finite; a program needn't handle non-finite values.
Results may differ from a plain program's by a relative error of at most 0.0003.
Values sent between devices are 32-bit elements; how exact they have to be, the bound alone decides.
No kernel may reach another device: no remote copies, remote signals or barrier semaphores. Data moves between devices by JAX's collectives and lax.ppermute only.
A program may use at most 64 MiB of HBM per device.

v0:
```python
import jax
import jax.numpy as jnp
from jax import lax
from jax.experimental import pallas as pl
from jax.experimental.pallas import tpu as pltpu
from jax.sharding import PartitionSpec as P

STEPS = 4
WIDTH = 4
LAGMAX = 8
REACH = LAGMAX // 2
GROUP = 4
SIDE = 8

SCALE = 5040.0
BAND = (8064.0, -1008.0, 128.0, -9.0)
CENTRE = 3.0 * (-205.0 / 72.0)
WEIGHTS = (1.6, -0.2, 8.0 / 315.0, -1.0 / 560.0)

F32 = jnp.float32
BF16 = jnp.bfloat16


def shape(*dims, dtype=F32):
    return jax.ShapeDtypeStruct(dims, dtype)


def params(megabytes):
    return pltpu.CompilerParams(vmem_limit_bytes=megabytes << 20)


def spec(space):
    return pl.BlockSpec(memory_space=space)


def cost(count, flops_each, arrays):
    return pl.CostEstimate(
        flops=int(count * flops_each), bytes_accessed=int(4 * count * arrays), transcendentals=0
    )


def split3(values):
    high = values.astype(BF16)
    rest = values - high.astype(F32)
    middle = rest.astype(BF16)
    low = (rest - middle.astype(F32)).astype(BF16)
    return high, middle, low


def exact_dot(values, matrix):
    parts = [jnp.dot(part, matrix, preferred_element_type=F32) for part in split3(values)]
    return (parts[2] + parts[1]) + parts[0]


class Place:
    def __init__(self):
        loop_size = lax.axis_size("gx")
        self.half = loop_size // 2
        relative = lax.rem(lax.axis_index("gx") + loop_size - loop_size // 4, loop_size)
        self.field = relative // self.half
        self.slab = lax.rem(relative, self.half)
        self.even = lax.rem(self.slab, 2) == 0
        self.y = lax.axis_index("gy")

    def block(self, count_y):
        return pl.multiple_of((1 - self.y) * (count_y - SIDE), SIDE)


def first_faces(field):
    count_x, count_y, count_z = field.shape

    def kernel(field_ref, near_ref, far_ref, side_ref, sems):
        place = Place()
        top = count_x - WIDTH
        near_start = jnp.where(place.even, top, 0)
        copies = [
            pltpu.make_async_copy(field_ref.at[pl.ds(top - near_start, WIDTH)], far_ref, sems.at[0]),
            pltpu.make_async_copy(field_ref.at[pl.ds(near_start, WIDTH)], near_ref, sems.at[1]),
            pltpu.make_async_copy(
                field_ref.at[:, pl.ds(place.block(count_y), SIDE)], side_ref, sems.at[2]
            ),
        ]
        for copy in copies:
            copy.start()
        for copy in copies:
            copy.wait()

    return pl.pallas_call(
        kernel,
        out_shape=face_shapes(count_x, count_y, count_z),
        in_specs=[spec(pltpu.HBM)],
        out_specs=(spec(pltpu.VMEM),) * 3,
        scratch_shapes=[pltpu.SemaphoreType.DMA((3,))],
        compiler_params=params(8),
        name="first_faces",
    )(field)


def face_shapes(count_x, count_y, count_z):
    slab = shape(WIDTH, count_y, count_z)
    return slab, slab, shape(count_x, SIDE, count_z)


def even_rows(level_ref, offset_x, offset_y, count_a, b):
    rows, stride, lanes = level_ref.shape
    flat = level_ref.reshape(rows * stride, lanes)
    start = offset_x * stride + offset_y + 2 * b
    return flat[pl.ds(start, count_a, stride=2 * stride), :]


def inner_step(number, points, waves, current, faces, previous, courant, snapshots=None):
    count_x, count_y, count_z = current.shape
    count_a, count_b = count_x // 2, count_y // 2
    first = faces is None
    last = number == STEPS - 1
    snapshot = number == STEPS // 2
    count_j = points.shape[1]

    def kernel(*refs):
        refs = list(refs)
        take = lambda count: [refs.pop(0) for _ in range(count)]
        points_ref, waves_ref, current_ref = take(3)
        if not first:
            near_ref, far_ref, side_ref = take(3)
        previous_ref, courant_ref = take(2)
        if snapshot:
            (steps_ref,) = take(1)
        next_ref, qx_ref, qy_ref = take(3)
        if first:
            kept_ref, cx_ref, cy_ref = take(3)
        elif not last:
            (whole_ref,) = take(1)
        if snapshot or last:
            (even_ref,) = take(1)
        padded, zpart = take(2)
        if first:
            before_ref, sems = take(2)
        if snapshot:
            wanted, sems = take(2)

        place = Place()
        block = place.block(count_y)
        rows, columns = pl.ds(WIDTH, count_x), pl.ds(SIDE, count_y)
        if first:
            copies = [
                pltpu.make_async_copy(current_ref, padded.at[rows, columns], sems.at[0]),
                pltpu.make_async_copy(previous_ref, before_ref, sems.at[1]),
                pltpu.make_async_copy(courant_ref, kept_ref, sems.at[2]),
            ]
            for copy in copies:
                copy.start()
        else:
            before_ref, kept_ref = previous_ref, courant_ref
        if snapshot:
            copies = [pltpu.make_async_copy(steps_ref, wanted, sems.at[0])]
            copies[0].start()

        zero_x = jnp.zeros((WIDTH, count_y + 2 * SIDE, count_z), F32)
        padded[pl.ds(0, WIDTH)] = zero_x
        padded[pl.ds(count_x + WIDTH, WIDTH)] = zero_x
        zero_y = jnp.zeros((count_x, SIDE, count_z), F32)
        padded[rows, pl.ds(0, SIDE)] = zero_y
        padded[rows, pl.ds(count_y + SIDE, SIDE)] = zero_y

        px = points_ref[0:1, :] - place.slab * count_x
        py = points_ref[1:2, :] - place.y * count_y
        inside = (px >= 0) & (px < count_x) & (py >= 0) & (py < count_y)
        home = jnp.where(inside, px * count_y + py, -1)
        amounts = waves_ref[number : number + 1, :]
        spread = jnp.where(
            lax.broadcasted_iota(jnp.int32, (count_z, count_j), 0) == points_ref[2:3, :],
            amounts,
            0.0,
        )
        spread = split3(spread)

        gap = jnp.abs(
            lax.broadcasted_iota(jnp.int32, (count_z, count_z), 0)
            - lax.broadcasted_iota(jnp.int32, (count_z, count_z), 1)
        )
        band = jnp.zeros((count_z, count_z), F32)
        for offset, weight in enumerate(BAND, 1):
            band = jnp.where(gap == offset, weight, band)
        band = band.astype(BF16)

        if first:
            copies[0].wait()
        else:
            padded[rows, columns] = current_ref[...]
            low, high = pl.ds(WIDTH, WIDTH), pl.ds(count_x, WIDTH)

            @pl.when(place.even)
            def _():
                padded[high, columns] = near_ref[...]
                padded[low, columns] = far_ref[...]

            @pl.when(jnp.logical_not(place.even))
            def _():
                padded[low, columns] = near_ref[...]
                padded[high, columns] = far_ref[...]

            padded[rows, pl.ds(pl.multiple_of(block + SIDE, SIDE), SIDE)] = side_ref[...]

        chunk = 8

        def multiply(index, _):
            start = pl.multiple_of(index * chunk, chunk)
            values = padded[pl.ds(start + WIDTH, chunk), columns]
            zpart[pl.ds(start, chunk)] = exact_dot(
                values.reshape(chunk * count_y, count_z), band
            ).reshape(chunk, count_y, count_z)
            return 0

        lax.fori_loop(0, count_x // chunk, multiply, 0)
        if first:
            copies[1].wait()
            copies[2].wait()

        def row(x, _):
            middle = padded[x + WIDTH, columns]
            total = CENTRE * middle + (1.0 / SCALE) * zpart[x]
            for offset, weight in enumerate(WEIGHTS, 1):
                paired = padded[x + WIDTH + offset, columns] + padded[x + WIDTH - offset, columns]
                paired = paired + (
                    padded[x + WIDTH, pl.ds(SIDE + offset, count_y)]
                    + padded[x + WIDTH, pl.ds(SIDE - offset, count_y)]
                )
                total = total + weight * paired
            here = x * count_y + lax.broadcasted_iota(jnp.int32, (count_y, count_j), 0)
            hit = jnp.where(here == home, 1.0, 0.0).astype(BF16)
            added = [
                lax.dot_general(
                    hit, part, (((1,), (1,)), ((), ())), preferred_element_type=F32
                )
                for part in spread
            ]
            added = (added[2] + added[1]) + added[0]
            if not first and not last:
                whole_ref[x] = middle
            next_ref[x] = (2.0 * middle - before_ref[x] + kept_ref[x] * total) + added
            return 0

        lax.fori_loop(0, count_x, row, 0)

        qx_ref[pl.ds(0, WIDTH)] = next_ref[pl.ds(0, WIDTH)]
        qx_ref[pl.ds(WIDTH, WIDTH)] = next_ref[pl.ds(count_x - WIDTH, WIDTH)]
        qy_ref[...] = next_ref[:, pl.ds(block, SIDE)]
        if first:
            cx_ref[pl.ds(0, WIDTH)] = kept_ref[pl.ds(0, WIDTH)]
            cx_ref[pl.ds(WIDTH, WIDTH)] = kept_ref[pl.ds(count_x - WIDTH, WIDTH)]
            cy_ref[...] = kept_ref[:, pl.ds(block, SIDE)]
        if last:
            for b in range(count_b):
                even_ref[b] = even_rows(padded, WIDTH, SIDE, count_a, b)
        if snapshot:
            copies[0].wait()
            earlier = wanted[place.field, 0] == number - 1

            @pl.when(earlier)
            def _():
                for b in range(count_b):
                    even_ref[b] = even_rows(previous_ref, 0, 0, count_a, b)

            @pl.when(jnp.logical_not(earlier))
            def _():
                for b in range(count_b):
                    even_ref[b] = even_rows(padded, WIDTH, SIDE, count_a, b)

    full = shape(count_x, count_y, count_z)
    slab, side = shape(2 * WIDTH, count_y, count_z), shape(count_x, SIDE, count_z)
    even = shape(count_b, count_a, count_z)
    outs = [full, slab, side]
    if first:
        outs += [full, slab, side]
    elif not last:
        outs.append(full)
    if snapshot or last:
        outs.append(even)
    place_of = spec(pltpu.HBM) if first else spec(pltpu.VMEM)
    operands, specs = [points, waves, current], [spec(pltpu.VMEM)] * 2 + [place_of]
    if not first:
        operands += list(faces)
        specs += [spec(pltpu.VMEM)] * 3
    operands += [previous, courant]
    specs += [place_of] * 2
    scratch = [
        pltpu.VMEM((count_x + 2 * WIDTH, count_y + 2 * SIDE, count_z), F32),
        pltpu.VMEM(full.shape, F32),
    ]
    if first:
        scratch += [pltpu.VMEM(full.shape, F32), pltpu.SemaphoreType.DMA((3,))]
    if snapshot:
        operands.append(snapshots)
        specs.append(spec(pltpu.HBM))
        scratch += [
            pltpu.SMEM(snapshots.shape, jnp.int32),
            pltpu.SemaphoreType.DMA((1,)),
        ]
    return pl.pallas_call(
        kernel,
        out_shape=tuple(outs),
        in_specs=specs,
        out_specs=(spec(pltpu.VMEM),) * len(outs),
        scratch_shapes=scratch,
        compiler_params=params(20),
        cost_estimate=cost(count_x * count_y * count_z, 60, 6),
        name=f"inner_step_{number}",
    )(*operands)


def low_terms(halo_ref, r):
    total = None
    for k in range(r + 1, WIDTH + 1):
        term = WEIGHTS[k - 1] * halo_ref[WIDTH + r - k]
        total = term if total is None else total + term
    return total


def high_terms(halo_ref, r):
    total = None
    for k in range(WIDTH - r, WIDTH + 1):
        term = WEIGHTS[k - 1] * halo_ref[r + k - WIDTH]
        total = term if total is None else total + term
    return total


def add_halo(place, parts, halos, outs):
    qx_ref, qy_ref, cx_ref, cy_ref = parts
    near_in, far_in, side_in = halos
    near_out, far_out, side_out = outs
    count_y, count_x = qx_ref.shape[1], qy_ref.shape[0]
    block = place.block(count_y)

    def along_x(low_in, high_in, low_out, high_out):
        for r in range(WIDTH):
            low_out[r] = qx_ref[r] + cx_ref[r] * low_terms(low_in, r)
            high_out[r] = qx_ref[WIDTH + r] + cx_ref[WIDTH + r] * high_terms(high_in, r)
        side_out[pl.ds(0, WIDTH)] = low_out[:, pl.ds(block, SIDE)]
        side_out[pl.ds(count_x - WIDTH, WIDTH)] = high_out[:, pl.ds(block, SIDE)]

    inner = pl.ds(WIDTH, count_x - 2 * WIDTH)
    side_out[inner] = qy_ref[inner]

    @pl.when(place.even)
    def _():
        along_x(far_in, near_in, far_out, near_out)

    @pl.when(jnp.logical_not(place.even))
    def _():
        along_x(near_in, far_in, near_out, far_out)

    def along_y(shifts, masks):
        halo = side_in[...]
        depth, lanes = halo.shape[0], halo.shape[2]
        line = lax.broadcasted_iota(jnp.int32, (1, SIDE, lanes), 1)
        total = None
        for k in range(1, WIDTH + 1):
            weight = jnp.where(masks(line, k), WEIGHTS[k - 1], 0.0)
            term = weight * pltpu.roll(halo, shifts(k), 1)
            total = term if total is None else total + term
        side_out[...] = side_out[...] + cy_ref[...] * total

    @pl.when(place.y == 0)
    def _():
        along_y(lambda k: SIDE - k, lambda line, k: line >= SIDE - k)

    @pl.when(place.y != 0)
    def _():
        along_y(lambda k: k, lambda line, k: line < k)

    def corners(low_out, high_out):
        low_out[:, pl.ds(block, SIDE)] = side_out[pl.ds(0, WIDTH)]
        high_out[:, pl.ds(block, SIDE)] = side_out[pl.ds(count_x - WIDTH, WIDTH)]

    @pl.when(place.even)
    def _():
        corners(far_out, near_out)

    @pl.when(jnp.logical_not(place.even))
    def _():
        corners(near_out, far_out)


def halo_step(parts, halos):
    count_y, (count_x, _, count_z) = parts[0].shape[1], parts[1].shape

    def kernel(*refs):
        add_halo(Place(), refs[:4], refs[4:7], refs[7:])

    return pl.pallas_call(
        kernel,
        out_shape=face_shapes(count_x, count_y, count_z),
        in_specs=[spec(pltpu.VMEM)] * 7,
        out_specs=(spec(pltpu.VMEM),) * 3,
        compiler_params=params(8),
        cost_estimate=cost(16 * count_y * count_z, 10, 6),
        name="halo_step",
    )(*parts, *halos)


def pack_matrix(window, count_z):
    half = count_z // GROUP
    size = GROUP * count_z
    row = lax.broadcasted_iota(jnp.int32, (size, size), 0)
    column = lax.broadcasted_iota(jnp.int32, (size, size), 1)
    row_b, row_z = row // count_z, row % count_z
    kind = column // count_z
    parity = kind % 2
    lane_b, lane_i = (column % count_z) // half, column % half
    main = (row_b == lane_b) & (row_z == 2 * (half * window + lane_i) + parity)
    is_low = window == 0
    wanted_b = jnp.where(is_low, lane_b + GROUP - 1, lane_b + 1) % GROUP
    wanted_z = 2 * (half * (1 - window) + lane_i) + parity
    useful = jnp.where(is_low, lane_i < REACH, lane_i >= half - REACH)
    edge = (row_b == wanted_b) & (row_z == wanted_z) & useful
    return jnp.where(kind < 2, main, edge).astype(BF16)


def packed(even_ref, matrix_ref):
    count_b, _, count_z = even_ref.shape
    rows = [
        jnp.concatenate([even_ref[b + i] for i in range(GROUP)], axis=1)
        for b in range(0, count_b, GROUP)
    ]
    result = exact_dot(jnp.concatenate(rows, axis=0), matrix_ref[...])
    return [result[:, kind * count_z : (kind + 1) * count_z] for kind in range(4)]


def pack_own(even, matrix):
    count_b, count_a, count_z = even.shape
    total_rows = count_b // GROUP * count_a

    def kernel(even_ref, matrix_ref, out_ref):
        for kind, part in enumerate(packed(even_ref, matrix_ref)):
            out_ref[kind] = part

    return pl.pallas_call(
        kernel,
        out_shape=shape(4, total_rows, count_z),
        in_specs=[spec(pltpu.VMEM)] * 2,
        out_specs=spec(pltpu.VMEM),
        compiler_params=params(8),
        cost_estimate=cost(count_b * count_a * count_z, 1024, 4),
        name="pack_own",
    )(even, matrix)


def edge_slots(count_a, groups, count_z):
    fits = count_z // GROUP // REACH
    slots = []
    for index in range(2 * groups):
        slots.append((index // groups, index % groups, index // fits * count_a, index % fits * REACH))
    return slots, -(-2 * groups // fits) * count_a


def send_into(even_ref, matrix_ref, out_ref):
    count_b, count_a, count_z = even_ref.shape
    groups = count_b // GROUP
    total_rows = groups * count_a
    parts = packed(even_ref, matrix_ref)
    out_ref[pl.ds(0, total_rows), :] = parts[0]
    out_ref[pl.ds(total_rows, total_rows), :] = parts[1]
    slots, _ = edge_slots(count_a, groups, count_z)
    sums = {}
    for parity, g, row, shift in slots:
        part = parts[2 + parity][g * count_a : (g + 1) * count_a]
        part = pltpu.roll(part, shift, 1) if shift else part
        sums[row] = sums[row] + part if row in sums else part
    for row, part in sums.items():
        out_ref[pl.ds(2 * total_rows + row, count_a), :] = part


def sent_shape(count_a, count_b, count_z):
    groups = count_b // GROUP
    _, extra = edge_slots(count_a, groups, count_z)
    return shape(2 * groups * count_a + extra, count_z)


def pack_sent(even, matrix):
    count_b, count_a, count_z = even.shape

    def kernel(even_ref, matrix_ref, out_ref):
        send_into(even_ref, matrix_ref, out_ref)

    return pl.pallas_call(
        kernel,
        out_shape=sent_shape(count_a, count_b, count_z),
        in_specs=[spec(pltpu.VMEM)] * 2,
        out_specs=spec(pltpu.VMEM),
        compiler_params=params(8),
        cost_estimate=cost(count_b * count_a * count_z, 1024, 4),
        name="pack_sent",
    )(even, matrix)


def last_step(snapshots, even_before, current, parts, halos, matrix):
    count_x, count_y, count_z = current.shape
    count_a, count_b = count_x // 2, count_y // 2

    def kernel(
        steps_ref, even_ref, current_ref, qx_ref, qy_ref, cx_ref, cy_ref, near_ref, far_ref,
        side_ref, matrix_ref, final_ref, late_ref, sent_ref, near_out, far_out, side_out,
        wanted, sems,
    ):
        place = Place()
        copy = pltpu.make_async_copy(steps_ref, wanted, sems.at[0])
        copy.start()
        add_halo(
            place, (qx_ref, qy_ref, cx_ref, cy_ref), (near_ref, far_ref, side_ref),
            (near_out, far_out, side_out),
        )
        low, high = pl.ds(0, WIDTH), pl.ds(count_x - WIDTH, WIDTH)

        @pl.when(place.even)
        def _():
            final_ref[high] = near_out[...]
            final_ref[low] = far_out[...]

        @pl.when(jnp.logical_not(place.even))
        def _():
            final_ref[low] = near_out[...]
            final_ref[high] = far_out[...]

        final_ref[:, pl.ds(place.block(count_y), SIDE)] = side_out[...]
        copy.wait()
        wants_last = wanted[place.field, 1] == STEPS

        @pl.when(wants_last)
        def _():
            for b in range(count_b):
                late_ref[b] = even_rows(final_ref, 0, 0, count_a, b)

        @pl.when(jnp.logical_not(wants_last))
        def _():
            late_ref[...] = even_ref[...]

        send_into(late_ref, matrix_ref, sent_ref)

    slab, _, side = face_shapes(count_x, count_y, count_z)
    return pl.pallas_call(
        kernel,
        out_shape=(
            shape(*current.shape),
            shape(count_b, count_a, count_z),
            sent_shape(count_a, count_b, count_z),
        ),
        in_specs=[spec(pltpu.HBM)] + [spec(pltpu.VMEM)] * 10,
        out_specs=(spec(pltpu.VMEM),) * 3,
        scratch_shapes=[
            pltpu.VMEM(slab.shape, F32),
            pltpu.VMEM(slab.shape, F32),
            pltpu.VMEM(side.shape, F32),
            pltpu.SMEM(snapshots.shape, jnp.int32),
            pltpu.SemaphoreType.DMA((1,)),
        ],
        input_output_aliases={2: 0},
        compiler_params=params(12),
        cost_estimate=cost(count_x * count_y * count_z, 10, 3),
        name="last_step",
    )(snapshots, even_before, current, *parts, *halos, matrix)


def write_out(level):
    def kernel(level_ref, out_ref, sem):
        copy = pltpu.make_async_copy(level_ref, out_ref, sem)
        copy.start()
        copy.wait()

    return pl.pallas_call(
        kernel,
        out_shape=shape(*level.shape),
        in_specs=[spec(pltpu.VMEM)],
        out_specs=spec(pltpu.HBM),
        scratch_shapes=[pltpu.SemaphoreType.DMA],
        compiler_params=params(4),
        cost_estimate=cost(level.size, 0, 2),
        name="write_out",
    )(level)


def lag_image(lags, own, other, before, count_a):
    _, total_rows, count_z = own.shape
    groups = total_rows // count_a
    count_h = lags.shape[0]
    half = count_z // GROUP
    last = before is not None

    def kernel(*refs):
        refs = list(refs)
        take = lambda count: [refs.pop(0) for _ in range(count)]
        lags_ref, own_ref, other_ref = take(3)
        if last:
            (before_ref,) = take(1)
        (out_ref,) = take(1)
        edges, lag_of, sems = take(3)
        if last:
            (store,) = take(1)
        else:
            store = out_ref
        place = Place()
        copy = pltpu.make_async_copy(lags_ref, lag_of, sems.at[0])
        copy.start()
        is_source = place.field == 0
        lane = lax.broadcasted_iota(jnp.int32, (count_a, count_z), 1) % half
        useful = jnp.where(is_source, lane, half - 1 - lane) < REACH
        slots, _ = edge_slots(count_a, groups, count_z)
        for parity, g, row, shift in slots:
            part = other_ref[pl.ds(2 * total_rows + row, count_a), :]
            part = pltpu.roll(part, count_z - shift, 1) if shift else part
            edges[parity, pl.ds(g * count_a, count_a), :] = jnp.where(useful, part, 0.0)
        copy.wait()
        lane = lax.broadcasted_iota(jnp.int32, (1, count_z), 1) % half

        def moved(main, edge, shift):
            mask = (lane < shift) | (lane >= half + shift)
            return pltpu.roll(jnp.where(mask, edge, main), (count_z - shift) & (count_z - 1), 1)

        def one(h, _):
            lag = lag_of[h]
            parity = lag & 1
            source_shift = -((lag + parity) >> 1)
            receiver_shift = (lag - parity) >> 1
            own_shift = jnp.where(is_source, source_shift, receiver_shift)
            other_shift = jnp.where(is_source, receiver_shift, source_shift)
            other_rows = pl.ds(pl.multiple_of(parity * total_rows, 8), total_rows)
            product = moved(own_ref[parity], own_ref[2 + parity], own_shift)
            product = product * moved(other_ref[other_rows, :], edges[parity], other_shift)
            for g in range(groups):
                part = product[g * count_a : (g + 1) * count_a]
                lanes = pl.ds(g * count_z, count_z)
                if last:
                    part = part + before_ref[h, :, lanes]
                store[h, :, lanes] = part
            if last:
                pltpu.make_async_copy(store.at[h], out_ref.at[h], sems.at[1]).start()
            return 0

        lax.fori_loop(0, count_h, one, 0)
        if last:
            pltpu.make_async_copy(store, out_ref, sems.at[1]).wait()

    out = (count_h, count_a, groups * count_z)
    operands = [lags, own, other] + ([before] if last else [])
    return pl.pallas_call(
        kernel,
        out_shape=shape(*out),
        in_specs=[spec(pltpu.HBM)] + [spec(pltpu.VMEM)] * (len(operands) - 1),
        out_specs=spec(pltpu.HBM if last else pltpu.VMEM),
        scratch_shapes=[
            pltpu.VMEM((2, total_rows, count_z), F32),
            pltpu.SMEM((count_h,), jnp.int32),
            pltpu.SemaphoreType.DMA((2,)),
        ]
        + ([pltpu.VMEM(out, F32)] if last else []),
        compiler_params=params(12),
        cost_estimate=cost(count_h * total_rows * count_z, 10, 2),
        name="lag_image",
    )(*operands)


def body(
    field_now,
    field_prev,
    courant_squared,
    source_cells,
    source_wave,
    receiver_cells,
    receiver_wave,
    snapshot_steps,
    lag_offsets,
):
    count_x, count_y, count_z = field_now.shape
    loop_size = lax.axis_size("gx")
    half_size = loop_size // 2
    turn = loop_size // 4
    assert lax.axis_size("gy") == 2 and half_size % 2 == 0

    field = ((lax.axis_index("gx") - turn + loop_size) % loop_size) // half_size
    slabs = [(i - turn) % loop_size % half_size for i in range(loop_size)]

    def pairs(odd):
        found = []
        for i, slab in enumerate(slabs):
            if slab % 2 == odd and slab != half_size - 1:
                j = (i + 1) % loop_size
                found += [(i, j), (j, i)]
        return found

    near_pairs, far_pairs = pairs(0), pairs(1)
    across = [(i, (i + half_size) % loop_size) for i in range(loop_size)]

    def exchange(faces):
        near, far, side = faces
        far_in = lax.ppermute(far, "gx", far_pairs)
        near_in = lax.ppermute(near, "gx", near_pairs)
        return near_in, far_in, lax.ppermute(side, "gy", [(0, 1), (1, 0)])

    most = -(-max(source_cells.shape[1], receiver_cells.shape[1]) // 128) * 128

    def chosen(source, receiver, empty):
        source, receiver = (
            jnp.pad(array, ((0, 0), (0, most - array.shape[1])), constant_values=empty)
            for array in (source, receiver)
        )
        return jnp.where(field == 0, source, receiver)

    points = chosen(source_cells, receiver_cells, -1)
    waves = chosen(source_wave, receiver_wave, 0.0)
    own_matrix = pack_matrix(field, count_z)
    sent_matrix = pack_matrix(1 - field, count_z)

    halos = exchange(first_faces(field_now))
    next1, qx, qy, courant, cx, cy = inner_step(
        0, points, waves, field_now, None, field_prev, courant_squared
    )
    faces = halo_step((qx, qy, cx, cy), halos)
    halos = exchange(faces)
    next2, qx, qy, whole1 = inner_step(1, points, waves, next1, faces, field_now, courant)
    faces = halo_step((qx, qy, cx, cy), halos)
    halos = exchange(faces)
    next3, qx, qy, whole2, early = inner_step(
        2, points, waves, next2, faces, whole1, courant, snapshot_steps
    )
    faces = halo_step((qx, qy, cx, cy), halos)
    halos = exchange(faces)
    other_early = lax.ppermute(pack_sent(early, sent_matrix), "gx", across)
    own_early = pack_own(early, own_matrix)
    next4, qx, qy, even3 = inner_step(3, points, waves, next3, faces, whole2, courant)
    final, late, sent_late = last_step(
        snapshot_steps, even3, next4, (qx, qy, cx, cy), halos, sent_matrix
    )
    other_late = lax.ppermute(sent_late, "gx", across)
    partial = lag_image(lag_offsets, own_early, other_early, None, count_x // 2)
    own_late = pack_own(late, own_matrix)
    image = lag_image(lag_offsets, own_late, other_late, partial, count_x // 2)
    return write_out(final), jnp.transpose(image, (1, 0, 2))


def solution(mesh):
    placed = (
        P(("shots", "gx"), "gy", None),
        P(("shots", "gx"), "gy", None),
        P("gx", "gy", None),
        P(None, "shots"),
        P(None, "shots"),
        P(None, "shots"),
        P(None, "shots"),
        P("shots", None),
        P(),
    )
    return jax.shard_map(
        body,
        mesh=mesh,
        in_specs=placed,
        out_specs=(P(("shots", "gx"), "gy", None), P(("shots", "gx"), None, "gy")),
        check_vma=False,
    )
```

profile of v0, /device:TPU:0, one launch (start us, length us, event | category | flops | bytes accessed | tf_op | source)
XLA Modules:
  0.0 72.6 jit_solution(16580835382240239965)
XLA Ops:
  0.6 1.1 %copy-done = f32[32,48,128]{2,1,0:T(8,128)S(1)} copy-done((f32[32,48,128]{2,1,0:T(8,128)S(1)}, f32[32,48,128]{2,1,0:T(8,128)}, u32[]{:S(2)}) %copy-start) | copy-done | bytes 786456
  1.8 0.3 first_faces.1
  2.0 3.1 %collective-permute-start = (f32[4,48,128]{2,1,0:T(8,128)S(1)}, f32[4,48,128]{2,1,0:T(8,128)S(1)}, u32[]{:S(2)}, u32[]{:S(2)}) collective-permute-start(f32[4,48,128]{2,1,0:T(8,128)S(1)} %get-tuple-element.41), channel_id=1, source_target_pairs={{0,2},{2,0},{4,6},{6,4},{8,10},{10,8},{12,14},{14,12},{1,3},{3,1},... | collective-permute-start | bytes 294920 | tf_op jit(solution)/shard_map/ppermute | solution.py:695
  5.1 5.4 %collective-permute-start.1 = (f32[4,48,128]{2,1,0:T(8,128)S(1)}, f32[4,48,128]{2,1,0:T(8,128)S(1)}, u32[]{:S(2)}, u32[]{:S(2)}) collective-permute-start(f32[4,48,128]{2,1,0:T(8,128)S(1)} %get-tuple-element.42), channel_id=1, source_target_pairs={{6,8},{8,6},{14,0},{0,14},{7,9},{9,7},{15,1},{1,15},{22,24},{24,22... | collective-permute-start | bytes 294920 | tf_op jit(solution)/shard_map/ppermute | solution.py:694
  10.6 0.1 collective-permute-start.2
  10.7 0.7 copy-done.6
  11.4 0.7 copy-done.7
  12.1 1.1 %copy-done.2 = f32[32,48,128]{2,1,0:T(8,128)S(1)} copy-done((f32[32,48,128]{2,1,0:T(8,128)S(1)}, f32[32,48,128]{2,1,0:T(8,128)}, u32[]{:S(2)}) %copy-start.2) | copy-done | bytes 786456
  13.2 1.1 %copy-done.3 = f32[32,48,128]{2,1,0:T(8,128)S(1)} copy-done((f32[32,48,128]{2,1,0:T(8,128)S(1)}, f32[32,48,128]{2,1,0:T(8,128)}, u32[]{:S(2)}) %copy-start.3) | copy-done | bytes 786456
  14.3 7.8 %inner_step_0.1 = (f32[32,48,128]{2,1,0:T(8,128)S(1)}, f32[8,48,128]{2,1,0:T(8,128)S(1)}, f32[32,8,128]{2,1,0:T(8,128)S(1)}, f32[32,48,128]{2,1,0:T(8,128)S(1)},...) custom-call(s32[3,256]{1,0:T(4,128)S(1)} %pad_select_fusion.1.refs_0_, f32[4,256]{1,0:T(4,128)S(1)} %pad_select_fusion.refs_1_, ...), custom_call_target="tpu_custom_call" | custom-call | flops 11796480 | bytes 4718592 | tf_op jit(solution)/shard_map/inner_step_0/pallas_call | solution.py:299
  22.1 0.2 halo_step.3
  22.3 0.5 collective-permute-start.5
  22.8 3.1 %collective-permute-start.4 = (f32[4,48,128]{2,1,0:T(8,128)S(1)}, f32[4,48,128]{2,1,0:T(8,128)S(1)}, u32[]{:S(2)}, u32[]{:S(2)}) collective-permute-start(f32[4,48,128]{2,1,0:T(8,128)S(1)} %get-tuple-element.45.refs_4_), channel_id=1, source_target_pairs={{6,8},{8,6},{14,0},{0,14},{7,9},{9,7},{15,1},{1,15},{22,24},{24,22... | collective-permute-start | bytes 294920 | tf_op jit(solution)/shard_map/ppermute | solution.py:694
  25.9 7.6 %inner_step_1.1 = (f32[32,48,128]{2,1,0:T(8,128)S(1)}, f32[8,48,128]{2,1,0:T(8,128)S(1)}, f32[32,8,128]{2,1,0:T(8,128)S(1)}, f32[32,48,128]{2,1,0:T(8,128)S(1)}) custom-call(s32[3,256]{1,0:T(4,128)S(1)} %pad_select_fusion.1.refs_0_, f32[4,256]{1,0:T(4,128)S(1)} %pad_select_fusion.refs_1_, f32[32,48,128]{2,1,0:T(8,128)S(1)} %get-tuple-element.36.refs_2_, ...), custom_call_target="tpu_custom_call" | custom-call | flops 11796480 | bytes 4718592 | tf_op jit(solution)/shard_map/inner_step_1/pallas_call | solution.py:299
  33.5 0.2 halo_step.4
  33.9 5.5 %collective-permute-start.7 = (f32[4,48,128]{2,1,0:T(8,128)S(1)}, f32[4,48,128]{2,1,0:T(8,128)S(1)}, u32[]{:S(2)}, u32[]{:S(2)}) collective-permute-start(f32[4,48,128]{2,1,0:T(8,128)S(1)} %get-tuple-element.52.refs_4_), channel_id=1, source_target_pairs={{6,8},{8,6},{14,0},{0,14},{7,9},{9,7},{15,1},{1,15},{22,24},{24,22... | collective-permute-start | bytes 294920 | tf_op jit(solution)/shard_map/ppermute | solution.py:694
  39.4 0.7 copy-done.4
  40.0 7.7 %inner_step_2.1 = (f32[32,48,128]{2,1,0:T(8,128)S(1)}, f32[8,48,128]{2,1,0:T(8,128)S(1)}, f32[32,8,128]{2,1,0:T(8,128)S(1)}, f32[32,48,128]{2,1,0:T(8,128)S(1)}, f32[24,16,128]{2,1,0:T(8,128)S(1)}) custom-call(s32[3,256]{1,0:T(4,128)S(1)} %pad_select_fusion.1.refs_0_, f32[4,256]{1,0:T(4,128)S(1)} %pad_select_fusion.refs_1_, ...), custom_call_target="tpu_custom_call" | custom-call | flops 11796480 | bytes 4718592 | tf_op jit(solution)/shard_map/inner_step_2/pallas_call | solution.py:299
  47.8 0.2 halo_step.5
  48.0 3.1 %collective-permute-start.10 = (f32[4,48,128]{2,1,0:T(8,128)S(1)}, f32[4,48,128]{2,1,0:T(8,128)S(1)}, u32[]{:S(2)}, u32[]{:S(2)}) collective-permute-start(f32[4,48,128]{2,1,0:T(8,128)S(1)} %get-tuple-element.59.refs_4_), channel_id=1, source_target_pairs={{6,8},{8,6},{14,0},{0,14},{7,9},{9,7},{15,1},{1,15},{22,24},{24,22... | collective-permute-start | bytes 294920 | tf_op jit(solution)/shard_map/ppermute | solution.py:694
  51.2 1.2 %fusion.19 = (bf16[512,512]{1,0:T(8,128)(2,1)S(1)}, bf16[512,512]{1,0:T(8,128)(2,1)S(1)}) fusion(s32[512]{0:T(512)S(1)} %get-tuple-element.75, s32[512]{0:T(512)S(1)} %get-tuple-element.76, s32[512]{0:T(512)S(1)} %get-tuple-element.72, s32[512]{0:T(512)S(1)} %get-tuple-element.77, pred[512]{0:T(512)(128)(4,1)S(1)} %get-tuple-element.79, pred[]{:T(512)S(6)} %eq.41, ...), kind=kLoop, calls=%fused_computation.47 | loop fusion | flops 21757952 | bytes 1062410 | tf_op jit(solution)/shard_map/convert_element_type | solution.py:416
  52.4 0.5 pack_sent.1
  53.0 7.7 %inner_step_3.1 = (f32[32,48,128]{2,1,0:T(8,128)S(1)}, f32[8,48,128]{2,1,0:T(8,128)S(1)}, f32[32,8,128]{2,1,0:T(8,128)S(1)}, f32[24,16,128]{2,1,0:T(8,128)S(1)}) custom-call(s32[3,256]{1,0:T(4,128)S(1)} %pad_select_fusion.1.refs_0_, f32[4,256]{1,0:T(4,128)S(1)} %pad_select_fusion.refs_1_, f32[32,48,128]{2,1,0:T(8,128)S(1)} %get-tuple-element.55.refs_2_, ...), custom_call_target="tpu_custom_call" | custom-call | flops 11796480 | bytes 4718592 | tf_op jit(solution)/shard_map/inner_step_3/pallas_call | solution.py:299
  60.7 1.2 %last_step.1 = (f32[32,48,128]{2,1,0:T(8,128)S(1)}, f32[24,16,128]{2,1,0:T(8,128)S(1)}, f32[224,128]{1,0:T(8,128)S(1)}) custom-call(s32[2,2]{1,0:T(2,128)S(1)} %copy-done.4, f32[24,16,128]{2,1,0:T(8,128)S(1)} %get-tuple-element.62.even_ref, f32[32,48,128]{2,1,0:T(8,128)S(1)} %get-tuple-element.63.current_ref, ...), custom_call_target="tpu_custom_call", output_to_operand_aliasing={{0}: (2, {})} | custom-call | flops 1966080 | bytes 2359296 | tf_op jit(solution)/shard_map/last_step/pallas_call | solution.py:540
  61.9 2.9 %collective-permute-start.12 = (f32[224,128]{1,0:T(8,128)S(1)}, f32[224,128]{1,0:T(8,128)S(1)}, u32[]{:S(2)}, u32[]{:S(2)}) collective-permute-start(f32[224,128]{1,0:T(8,128)S(1)} %get-tuple-element.68), channel_id=1, source_target_pairs={{0,8},{2,10},{4,12},{6,14},{8,0},{10,2},{12,4},{14,6},{1,9},{3,11}... | collective-permute-start | bytes 344072 | tf_op jit(solution)/shard_map/ppermute | solution.py:732
  64.7 0.4 pack_own.3.refs_1_
  65.1 0.3 copy-done.5
  65.4 2.2 %lag_image.2.refs_3_ = f32[17,16,768]{2,1,0:T(8,128)S(1)} custom-call(s32[17]{0:T(128)S(1)} %copy-done.5, f32[4,96,128]{2,1,0:T(8,128)S(1)} %pack_own.3.refs_1_, f32[224,128]{1,0:T(8,128)S(1)} %collective-permute-done.13.refs_2_), custom_call_target="tpu_custom_call" | custom-call | flops 2088960 | bytes 1671168 | tf_op jit(solution)/shard_map/lag_image/pallas_call | solution.py:644
  67.6 0.9 %write_out.1 = f32[32,48,128]{2,1,0:T(8,128)} custom-call(f32[32,48,128]{2,1,0:T(8,128)S(1)} %get-tuple-element.66.level_ref), custom_call_target="tpu_custom_call" | custom-call | bytes 1572864 | tf_op jit(solution)/shard_map/write_out/pallas_call | solution.py:569
  68.5 0.4 pack_own.2.refs_1_
  68.9 0.8 %collective-permute-done.12.refs_2_ = f32[224,128]{1,0:T(8,128)S(1)} collective-permute-done((f32[224,128]{1,0:T(8,128)S(1)}, f32[224,128]{1,0:T(8,128)S(1)}, u32[]{:S(2)}, u32[]{:S(2)}) %collective-permute-start.12) | collective-permute-done | bytes 114720 | tf_op jit(solution)/shard_map/ppermute | solution.py:732
  69.7 2.9 %lag_image.3 = f32[17,16,768]{2,1,0:T(8,128)} custom-call(s32[17]{0:T(128)S(1)} %copy-done.5, f32[4,96,128]{2,1,0:T(8,128)S(1)} %pack_own.2.refs_1_, f32[224,128]{1,0:T(8,128)S(1)} %collective-permute-done.12.refs_2_, f32[17,16,768]{2,1,0:T(8,128)S(1)} %lag_image.2.refs_3_), custom_call_target="tpu_custom_call" | custom-call | flops 2088960 | bytes 1671168 | tf_op jit(solution)/shard_map/lag_image/pallas_call | solution.py:644
  (39 shorter events, 0.5 us)
Async XLA Ops:
  0.6 1.1 %copy-start = (f32[32,48,128]{2,1,0:T(8,128)S(1)}, f32[32,48,128]{2,1,0:T(8,128)}, u32[]{:S(2)}) copy-start(f32[32,48,128]{2,1,0:T(8,128)} %refs_6_.1) | copy-start | bytes 2359300
  1.8 10.3 %copy-start.1 = (f32[32,48,128]{2,1,0:T(8,128)S(1)}, f32[32,48,128]{2,1,0:T(8,128)}, u32[]{:S(2)}) copy-start(f32[32,48,128]{2,1,0:T(8,128)} %refs_6_.1) | copy-start | bytes 2359300
  2.0 20.1 %collective-permute-start = (f32[4,48,128]{2,1,0:T(8,128)S(1)}, f32[4,48,128]{2,1,0:T(8,128)S(1)}, u32[]{:S(2)}, u32[]{:S(2)}) collective-permute-start(f32[4,48,128]{2,1,0:T(8,128)S(1)} %get-tuple-element.41), channel_id=1, source_target_pairs={{0,2},{2,0},{4,6},{6,4},{8,10},{10,8},{12,14},{14,12},{1,3},{3,1},... | collective-permute-start | bytes 294920 | tf_op jit(solution)/shard_map/ppermute | solution.py:695
  5.1 17.0 %collective-permute-start.1 = (f32[4,48,128]{2,1,0:T(8,128)S(1)}, f32[4,48,128]{2,1,0:T(8,128)S(1)}, u32[]{:S(2)}, u32[]{:S(2)}) collective-permute-start(f32[4,48,128]{2,1,0:T(8,128)S(1)} %get-tuple-element.42), channel_id=1, source_target_pairs={{6,8},{8,6},{14,0},{0,14},{7,9},{9,7},{15,1},{1,15},{22,24},{24,22... | collective-permute-start | bytes 294920 | tf_op jit(solution)/shard_map/ppermute | solution.py:694
  10.6 11.6 %collective-permute-start.2 = (f32[32,8,128]{2,1,0:T(8,128)S(1)}, f32[32,8,128]{2,1,0:T(8,128)S(1)}, u32[]{:S(2)}, u32[]{:S(2)}) collective-permute-start(f32[32,8,128]{2,1,0:T(8,128)S(1)} %get-tuple-element.43), channel_id=1, source_target_pairs={{0,1},{1,0},{2,3},{3,2},{4,5},{5,4},{6,7},{7,6},{8,9},{9,8},{10,11... | collective-permute-start | bytes 393224 | tf_op jit(solution)/shard_map/ppermute | solution.py:696
  10.7 0.7 copy-start.6
  10.7 0.7 copy-start.8
  11.4 0.7 copy-start.7
  11.4 0.7 copy-start.9
  12.1 1.1 %copy-start.2 = (f32[32,48,128]{2,1,0:T(8,128)S(1)}, f32[32,48,128]{2,1,0:T(8,128)}, u32[]{:S(2)}) copy-start(f32[32,48,128]{2,1,0:T(8,128)} %refs_3_.1) | copy-start | bytes 2359300
  13.2 1.1 %copy-start.3 = (f32[32,48,128]{2,1,0:T(8,128)S(1)}, f32[32,48,128]{2,1,0:T(8,128)}, u32[]{:S(2)}) copy-start(f32[32,48,128]{2,1,0:T(8,128)} %refs_4_.1) | copy-start | bytes 2359300
  22.3 11.2 %collective-permute-start.5 = (f32[32,8,128]{2,1,0:T(8,128)S(1)}, f32[32,8,128]{2,1,0:T(8,128)S(1)}, u32[]{:S(2)}, u32[]{:S(2)}) collective-permute-start(f32[32,8,128]{2,1,0:T(8,128)S(1)} %get-tuple-element.46.refs_5_), channel_id=1, source_target_pairs={{0,1},{1,0},{2,3},{3,2},{4,5},{5,4},{6,7},{7,6},{8,9},{9,8},{10,11... | collective-permute-start | bytes 393224 | tf_op jit(solution)/shard_map/ppermute | solution.py:696
  22.8 10.7 %collective-permute-start.3 = (f32[4,48,128]{2,1,0:T(8,128)S(1)}, f32[4,48,128]{2,1,0:T(8,128)S(1)}, u32[]{:S(2)}, u32[]{:S(2)}) collective-permute-start(f32[4,48,128]{2,1,0:T(8,128)S(1)} %get-tuple-element.44.refs_3_), channel_id=1, source_target_pairs={{0,2},{2,0},{4,6},{6,4},{8,10},{10,8},{12,14},{14,12},{1,3},{3,1},... | collective-permute-start | bytes 294920 | tf_op jit(solution)/shard_map/ppermute | solution.py:695
  22.8 10.7 %collective-permute-start.4 = (f32[4,48,128]{2,1,0:T(8,128)S(1)}, f32[4,48,128]{2,1,0:T(8,128)S(1)}, u32[]{:S(2)}, u32[]{:S(2)}) collective-permute-start(f32[4,48,128]{2,1,0:T(8,128)S(1)} %get-tuple-element.45.refs_4_), channel_id=1, source_target_pairs={{6,8},{8,6},{14,0},{0,14},{7,9},{9,7},{15,1},{1,15},{22,24},{24,22... | collective-permute-start | bytes 294920 | tf_op jit(solution)/shard_map/ppermute | solution.py:694
  33.7 14.1 %collective-permute-start.8 = (f32[32,8,128]{2,1,0:T(8,128)S(1)}, f32[32,8,128]{2,1,0:T(8,128)S(1)}, u32[]{:S(2)}, u32[]{:S(2)}) collective-permute-start(f32[32,8,128]{2,1,0:T(8,128)S(1)} %get-tuple-element.53.refs_5_), channel_id=1, source_target_pairs={{0,1},{1,0},{2,3},{3,2},{4,5},{5,4},{6,7},{7,6},{8,9},{9,8},{10,11... | collective-permute-start | bytes 393224 | tf_op jit(solution)/shard_map/ppermute | solution.py:696
  33.8 14.0 %collective-permute-start.6 = (f32[4,48,128]{2,1,0:T(8,128)S(1)}, f32[4,48,128]{2,1,0:T(8,128)S(1)}, u32[]{:S(2)}, u32[]{:S(2)}) collective-permute-start(f32[4,48,128]{2,1,0:T(8,128)S(1)} %get-tuple-element.51.refs_3_), channel_id=1, source_target_pairs={{0,2},{2,0},{4,6},{6,4},{8,10},{10,8},{12,14},{14,12},{1,3},{3,1},... | collective-permute-start | bytes 294920 | tf_op jit(solution)/shard_map/ppermute | solution.py:695
  33.9 13.9 %collective-permute-start.7 = (f32[4,48,128]{2,1,0:T(8,128)S(1)}, f32[4,48,128]{2,1,0:T(8,128)S(1)}, u32[]{:S(2)}, u32[]{:S(2)}) collective-permute-start(f32[4,48,128]{2,1,0:T(8,128)S(1)} %get-tuple-element.52.refs_4_), channel_id=1, source_target_pairs={{6,8},{8,6},{14,0},{0,14},{7,9},{9,7},{15,1},{1,15},{22,24},{24,22... | collective-permute-start | bytes 294920 | tf_op jit(solution)/shard_map/ppermute | solution.py:694
  39.4 0.7 copy-start.4
  48.0 12.7 %collective-permute-start.9 = (f32[4,48,128]{2,1,0:T(8,128)S(1)}, f32[4,48,128]{2,1,0:T(8,128)S(1)}, u32[]{:S(2)}, u32[]{:S(2)}) collective-permute-start(f32[4,48,128]{2,1,0:T(8,128)S(1)} %get-tuple-element.58.refs_3_), channel_id=1, source_target_pairs={{0,2},{2,0},{4,6},{6,4},{8,10},{10,8},{12,14},{14,12},{1,3},{3,1},... | collective-permute-start | bytes 294920 | tf_op jit(solution)/shard_map/ppermute | solution.py:695
  48.0 12.7 %collective-permute-start.10 = (f32[4,48,128]{2,1,0:T(8,128)S(1)}, f32[4,48,128]{2,1,0:T(8,128)S(1)}, u32[]{:S(2)}, u32[]{:S(2)}) collective-permute-start(f32[4,48,128]{2,1,0:T(8,128)S(1)} %get-tuple-element.59.refs_4_), channel_id=1, source_target_pairs={{6,8},{8,6},{14,0},{0,14},{7,9},{9,7},{15,1},{1,15},{22,24},{24,22... | collective-permute-start | bytes 294920 | tf_op jit(solution)/shard_map/ppermute | solution.py:694
  51.1 9.6 %collective-permute-start.11 = (f32[32,8,128]{2,1,0:T(8,128)S(1)}, f32[32,8,128]{2,1,0:T(8,128)S(1)}, u32[]{:S(2)}, u32[]{:S(2)}) collective-permute-start(f32[32,8,128]{2,1,0:T(8,128)S(1)} %get-tuple-element.60.refs_5_), channel_id=1, source_target_pairs={{0,1},{1,0},{2,3},{3,2},{4,5},{5,4},{6,7},{7,6},{8,9},{9,8},{10,11... | collective-permute-start | bytes 393224 | tf_op jit(solution)/shard_map/ppermute | solution.py:696
  52.9 12.2 %collective-permute-start.13 = (f32[224,128]{1,0:T(8,128)S(1)}, f32[224,128]{1,0:T(8,128)S(1)}, u32[]{:S(2)}, u32[]{:S(2)}) collective-permute-start(f32[224,128]{1,0:T(8,128)S(1)} %pack_sent.1), channel_id=1, source_target_pairs={{0,8},{2,10},{4,12},{6,14},{8,0},{10,2},{12,4},{14,6},{1,9},{3,11}... | collective-permute-start | bytes 344072 | tf_op jit(solution)/shard_map/ppermute | solution.py:726
  61.9 7.8 %collective-permute-start.12 = (f32[224,128]{1,0:T(8,128)S(1)}, f32[224,128]{1,0:T(8,128)S(1)}, u32[]{:S(2)}, u32[]{:S(2)}) collective-permute-start(f32[224,128]{1,0:T(8,128)S(1)} %get-tuple-element.68), channel_id=1, source_target_pairs={{0,8},{2,10},{4,12},{6,14},{8,0},{10,2},{12,4},{14,6},{1,9},{3,11}... | collective-permute-start | bytes 344072 | tf_op jit(solution)/shard_map/ppermute | solution.py:732
  64.7 0.7 copy-start.5
where the time goes:
time: 73.1 us; the launch traced here: 72.6 us
  Pallas kernels  39.8 us (54%)
  starting transfers between devices  23.9 us (33%)
  local copies, waits for them, and re-layouts  5.69 us (8%)
  other arithmetic  1.27 us (2%)
  between operations  1.04 us (1%)
  waiting for transfers between devices  0.86 us (1%)
    pallas_call x4, Pallas kernels, inner_step(): pl.pallas_call(kernel, out_shape=tuple(outs), in_specs=specs, out_specs=(...  30.7 us
    ppermute x4, starting transfers between devices, exchange(): far_in = lax.ppermute(far, 'gx', far_pairs)  17.1 us
    unnamed x20, local copies, waits for them, and re-layouts  5.69 us
    pallas_call x2, Pallas kernels, lag_image(): pl.pallas_call(kernel, out_shape=shape(*out), in_specs=[spec(pltpu.HBM)]...  5.06 us
    ppermute x4, starting transfers between devices, exchange(): near_in = lax.ppermute(near, 'gx', near_pairs)  3.21 us
    ppermute x1, starting transfers between devices, body(): other_late = lax.ppermute(sent_late, 'gx', across)  2.87 us
  transfers between devices with their start and end apart: 14, of which 1 were waited for; matrix products, arithmetic and copies ran while one was open for 2% of the time, Pallas kernels for 50%

commit v1 on v0

--- a/solution.py
+++ b/solution.py
@@ -132,7 +132,7 @@
             (whole_ref,) = take(1)
         if snapshot or last:
             (even_ref,) = take(1)
-        padded, zpart = take(2)
+        padded, zpart, addpart = take(3)
         if first:
             before_ref, sems = take(2)
         if snapshot:
@@ -209,6 +209,16 @@
             zpart[pl.ds(start, chunk)] = exact_dot(
                 values.reshape(chunk * count_y, count_z), band
             ).reshape(chunk, count_y, count_z)
+            here = start * count_y + lax.broadcasted_iota(
+                jnp.int32, (chunk * count_y, count_j), 0
+            )
+            hit = jnp.where(here == home, 1.0, 0.0).astype(BF16)
+            added = [
+                lax.dot_general(hit, part, (((1,), (1,)), ((), ())), preferred_element_type=F32)
+                for part in spread
+            ]
+            added = (added[2] + added[1]) + added[0]
+            addpart[pl.ds(start, chunk)] = added.reshape(chunk, count_y, count_z)
             return 0
 
         lax.fori_loop(0, count_x // chunk, multiply, 0)
@@ -226,21 +236,12 @@
                     + padded[x + WIDTH, pl.ds(SIDE - offset, count_y)]
                 )
                 total = total + weight * paired
-            here = x * count_y + lax.broadcasted_iota(jnp.int32, (count_y, count_j), 0)
-            hit = jnp.where(here == home, 1.0, 0.0).astype(BF16)
-            added = [
-                lax.dot_general(
-                    hit, part, (((1,), (1,)), ((), ())), preferred_element_type=F32
-                )
-                for part in spread
-            ]
-            added = (added[2] + added[1]) + added[0]
             if not first and not last:
                 whole_ref[x] = middle
-            next_ref[x] = (2.0 * middle - before_ref[x] + kept_ref[x] * total) + added
+            next_ref[x] = (2.0 * middle - before_ref[x] + kept_ref[x] * total) + addpart[x]
             return 0
 
-        lax.fori_loop(0, count_x, row, 0)
+        lax.fori_loop(0, count_x, row, 0, unroll=4)
 
         qx_ref[pl.ds(0, WIDTH)] = next_ref[pl.ds(0, WIDTH)]
         qx_ref[pl.ds(WIDTH, WIDTH)] = next_ref[pl.ds(count_x - WIDTH, WIDTH)]
@@ -285,6 +286,7 @@
     specs += [place_of] * 2
     scratch = [
         pltpu.VMEM((count_x + 2 * WIDTH, count_y + 2 * SIDE, count_z), F32),
+        pltpu.VMEM(full.shape, F32),
         pltpu.VMEM(full.shape, F32),
     ]
     if first:
@@ -635,7 +637,7 @@
                 pltpu.make_async_copy(store.at[h], out_ref.at[h], sems.at[1]).start()
             return 0
 
-        lax.fori_loop(0, count_h, one, 0)
+        lax.fori_loop(0, count_h, one, 0, unroll=True)
         if last:
             pltpu.make_async_copy(store, out_ref, sems.at[1]).wait()
 
@@ -709,6 +711,10 @@
     own_matrix = pack_matrix(field, count_z)
     sent_matrix = pack_matrix(1 - field, count_z)
 
+    field_now, field_prev, courant_squared = (
+        pltpu.with_memory_space_constraint(array, pltpu.HBM)
+        for array in (field_now, field_prev, courant_squared)
+    )
     halos = exchange(first_faces(field_now))
     next1, qx, qy, courant, cx, cy = inner_step(
         0, points, waves, field_now, None, field_prev, courant_squared

time: 73.1 us -> 55.6 us (0.76)
  Pallas kernels: 39.8 us -> 20.3 us
  waiting for transfers between devices: 0.86 us -> 7.09 us
  local copies, waits for them, and re-layouts: 5.69 us -> 2.3 us
    pallas_call x4, Pallas kernels: 30.7 us -> 12.7 us  [inner_step(): pl.pallas_call(kernel, out_shape=tuple(outs), in_specs=specs, out_specs=(...]
    ppermute x4, waiting for transfers between devices: 0.01 us -> 5.14 us  [exchange(): far_in = lax.ppermute(far, 'gx', far_pairs)]
    unnamed x20 -> x12, local copies, waits for them, and re-layouts: 5.69 us -> 2.3 us
    pallas_call x2, Pallas kernels: 5.06 us -> 2.83 us  [lag_image(): pl.pallas_call(kernel, out_shape=shape(*out), in_specs=[spec(pltpu.HBM)]...]
    ppermute x1, waiting for transfers between devices: 0.82 us -> 1.92 us  [body(): other_late = lax.ppermute(sent_late, 'gx', across)]
    pallas_call x1, Pallas kernels: 0.27 us -> 1.05 us  [first_faces(): pl.pallas_call(kernel, out_shape=face_shapes(count_x, count_y, count_z),...]
  transfers between devices with their start and end apart: 14 -> 14, of which waited for: 1 -> 4; matrix products, arithmetic and copies ran while one was open for 2% -> 2% of each run, Pallas kernels for 50% -> 31%
where the time goes in v1:
time: 55.6 us; the launch traced here: 55.2 us
  starting transfers between devices  23.3 us (42%)
  Pallas kernels  20.3 us (37%)
  waiting for transfers between devices  7.09 us (13%)
  local copies, waits for them, and re-layouts  2.3 us (4%)
  other arithmetic  1.27 us (2%)
  between operations  0.97 us (2%)
    ppermute x4, starting transfers between devices, exchange(): far_in = lax.ppermute(far, 'gx', far_pairs)  17 us
    pallas_call x4, Pallas kernels, inner_step(): pl.pallas_call(kernel, out_shape=tuple(outs), in_specs=specs, out_specs=(...  12.7 us
    ppermute x4, waiting for transfers between devices, exchange(): far_in = lax.ppermute(far, 'gx', far_pairs)  5.14 us
    ppermute x4, starting transfers between devices, exchange(): near_in = lax.ppermute(near, 'gx', near_pairs)  3.21 us
    pallas_call x2, Pallas kernels, lag_image(): pl.pallas_call(kernel, out_shape=shape(*out), in_specs=[spec(pltpu.HBM)]...  2.83 us
    unnamed x12, local copies, waits for them, and re-layouts  2.3 us
    ppermute x1, starting transfers between devices, body(): other_late = lax.ppermute(sent_late, 'gx', across)  2.28 us
    ppermute x1, waiting for transfers between devices, body(): other_late = lax.ppermute(sent_late, 'gx', across)  1.92 us
  transfers between devices with their start and end apart: 14, of which 4 were waited for; matrix products, arithmetic and copies ran while one was open for 2% of the time, Pallas kernels for 31%

profile of v1, /device:TPU:0, one launch (start us, length us, event | category | flops | bytes accessed | tf_op | source)
XLA Modules:
  0.0 55.2 jit_solution(5724588284531124679)
XLA Ops:
  0.6 1.0 %first_faces.1 = (f32[4,48,128]{2,1,0:T(8,128)S(1)}, f32[4,48,128]{2,1,0:T(8,128)S(1)}, f32[32,8,128]{2,1,0:T(8,128)S(1)}) custom-call(f32[32,48,128]{2,1,0:T(8,128)} %refs_6_.1), custom_call_target="tpu_custom_call" | custom-call | tf_op jit(solution)/shard_map/first_faces/pallas_call | solution.py:88
  1.7 3.1 %collective-permute-start = (f32[4,48,128]{2,1,0:T(8,128)S(1)}, f32[4,48,128]{2,1,0:T(8,128)S(1)}, u32[]{:S(2)}, u32[]{:S(2)}) collective-permute-start(f32[4,48,128]{2,1,0:T(8,128)S(1)} %get-tuple-element.41), channel_id=1, source_target_pairs={{0,2},{2,0},{4,6},{6,4},{8,10},{10,8},{12,14},{14,12},{1,3},{3,1},... | collective-permute-start | bytes 294920 | tf_op jit(solution)/shard_map/ppermute | solution.py:697
  4.7 5.4 %collective-permute-start.1 = (f32[4,48,128]{2,1,0:T(8,128)S(1)}, f32[4,48,128]{2,1,0:T(8,128)S(1)}, u32[]{:S(2)}, u32[]{:S(2)}) collective-permute-start(f32[4,48,128]{2,1,0:T(8,128)S(1)} %get-tuple-element.42), channel_id=1, source_target_pairs={{6,8},{8,6},{14,0},{0,14},{7,9},{9,7},{15,1},{1,15},{22,24},{24,22... | collective-permute-start | bytes 294920 | tf_op jit(solution)/shard_map/ppermute | solution.py:696
  10.2 0.1 collective-permute-start.2
  10.3 0.7 %copy-done.2 = s32[3,256]{1,0:T(4,128)S(1)} copy-done((s32[3,256]{1,0:T(4,128)S(1)}, s32[3,256]{1,0:T(4,128)}, u32[]{:S(2)}) %copy-start.2) | copy-done | bytes 3096
  11.0 0.7 %copy-done.3 = f32[4,256]{1,0:T(4,128)S(1)} copy-done((f32[4,256]{1,0:T(4,128)S(1)}, f32[4,256]{1,0:T(4,128)}, u32[]{:S(2)}) %copy-start.3) | copy-done | bytes 4120
  11.7 3.6 %inner_step_0.1 = (f32[32,48,128]{2,1,0:T(8,128)S(1)}, f32[8,48,128]{2,1,0:T(8,128)S(1)}, f32[32,8,128]{2,1,0:T(8,128)S(1)}, f32[32,48,128]{2,1,0:T(8,128)S(1)},...) custom-call(s32[3,256]{1,0:T(4,128)S(1)} %pad_select_fusion.1.refs_0_, f32[4,256]{1,0:T(4,128)S(1)} %pad_select_fusion.refs_1_, ...), custom_call_target="tpu_custom_call" | custom-call | flops 11796480 | bytes 4718592 | tf_op jit(solution)/shard_map/inner_step_0/pallas_call | solution.py:301
  15.4 0.2 halo_step.3
  15.5 0.5 collective-permute-start.5
  16.1 3.6 %collective-permute-start.4 = (f32[4,48,128]{2,1,0:T(8,128)S(1)}, f32[4,48,128]{2,1,0:T(8,128)S(1)}, u32[]{:S(2)}, u32[]{:S(2)}) collective-permute-start(f32[4,48,128]{2,1,0:T(8,128)S(1)} %get-tuple-element.45.refs_4_), channel_id=1, source_target_pairs={{6,8},{8,6},{14,0},{0,14},{7,9},{9,7},{15,1},{1,15},{22,24},{24,22... | collective-permute-start | bytes 294920 | tf_op jit(solution)/shard_map/ppermute | solution.py:696
  19.7 3.7 %inner_step_1.1 = (f32[32,48,128]{2,1,0:T(8,128)S(1)}, f32[8,48,128]{2,1,0:T(8,128)S(1)}, f32[32,8,128]{2,1,0:T(8,128)S(1)}, f32[32,48,128]{2,1,0:T(8,128)S(1)}) custom-call(s32[3,256]{1,0:T(4,128)S(1)} %pad_select_fusion.1.refs_0_, f32[4,256]{1,0:T(4,128)S(1)} %pad_select_fusion.refs_1_, f32[32,48,128]{2,1,0:T(8,128)S(1)} %get-tuple-element.36.refs_2_, ...), custom_call_target="tpu_custom_call" | custom-call | flops 11796480 | bytes 4718592 | tf_op jit(solution)/shard_map/inner_step_1/pallas_call | solution.py:301
  23.4 2.0 %collective-permute-done.4.refs_5_ = f32[4,48,128]{2,1,0:T(8,128)S(1)} collective-permute-done((f32[4,48,128]{2,1,0:T(8,128)S(1)}, f32[4,48,128]{2,1,0:T(8,128)S(1)}, u32[]{:S(2)}, u32[]{:S(2)}) %collective-permute-start.4) | collective-permute-done | bytes 98336 | tf_op jit(solution)/shard_map/ppermute | solution.py:696
  25.5 0.2 halo_step.4
  25.8 4.0 %collective-permute-start.7 = (f32[4,48,128]{2,1,0:T(8,128)S(1)}, f32[4,48,128]{2,1,0:T(8,128)S(1)}, u32[]{:S(2)}, u32[]{:S(2)}) collective-permute-start(f32[4,48,128]{2,1,0:T(8,128)S(1)} %get-tuple-element.52.refs_4_), channel_id=1, source_target_pairs={{6,8},{8,6},{14,0},{0,14},{7,9},{9,7},{15,1},{1,15},{22,24},{24,22... | collective-permute-start | bytes 294920 | tf_op jit(solution)/shard_map/ppermute | solution.py:696
  29.8 0.7 %copy-done = s32[2,2]{1,0:T(2,128)S(1)} copy-done((s32[2,2]{1,0:T(2,128)S(1)}, s32[2,2]{1,0:T(2,128)}, u32[]{:S(2)}) %copy-start) | copy-done | bytes 40
  30.5 2.7 %inner_step_2.1 = (f32[32,48,128]{2,1,0:T(8,128)S(1)}, f32[8,48,128]{2,1,0:T(8,128)S(1)}, f32[32,8,128]{2,1,0:T(8,128)S(1)}, f32[32,48,128]{2,1,0:T(8,128)S(1)}, f32[24,16,128]{2,1,0:T(8,128)S(1)}) custom-call(s32[3,256]{1,0:T(4,128)S(1)} %pad_select_fusion.1.refs_0_, f32[4,256]{1,0:T(4,128)S(1)} %pad_select_fusion.refs_1_, ...), custom_call_target="tpu_custom_call" | custom-call | flops 11796480 | bytes 4718592 | tf_op jit(solution)/shard_map/inner_step_2/pallas_call | solution.py:301
  33.1 2.4 %collective-permute-done.7.refs_5_ = f32[4,48,128]{2,1,0:T(8,128)S(1)} collective-permute-done((f32[4,48,128]{2,1,0:T(8,128)S(1)}, f32[4,48,128]{2,1,0:T(8,128)S(1)}, u32[]{:S(2)}, u32[]{:S(2)}) %collective-permute-start.7) | collective-permute-done | bytes 98336 | tf_op jit(solution)/shard_map/ppermute | solution.py:696
  35.5 0.1 halo_step.5
  35.7 4.0 %collective-permute-start.10 = (f32[4,48,128]{2,1,0:T(8,128)S(1)}, f32[4,48,128]{2,1,0:T(8,128)S(1)}, u32[]{:S(2)}, u32[]{:S(2)}) collective-permute-start(f32[4,48,128]{2,1,0:T(8,128)S(1)} %get-tuple-element.59.refs_4_), channel_id=1, source_target_pairs={{6,8},{8,6},{14,0},{0,14},{7,9},{9,7},{15,1},{1,15},{22,24},{24,22... | collective-permute-start | bytes 294920 | tf_op jit(solution)/shard_map/ppermute | solution.py:696
  39.8 1.2 %fusion.19 = (bf16[512,512]{1,0:T(8,128)(2,1)S(1)}, bf16[512,512]{1,0:T(8,128)(2,1)S(1)}) fusion(s32[512]{0:T(512)S(1)} %get-tuple-element.75, s32[512]{0:T(512)S(1)} %get-tuple-element.76, s32[512]{0:T(512)S(1)} %get-tuple-element.72, s32[512]{0:T(512)S(1)} %get-tuple-element.77, pred[512]{0:T(512)(128)(4,1)S(1)} %get-tuple-element.79, pred[]{:T(512)S(6)} %eq.41, ...), kind=kLoop, calls=%fused_computation.47 | loop fusion | flops 21757952 | bytes 1062410 | tf_op jit(solution)/shard_map/convert_element_type | solution.py:418
  41.0 0.5 pack_sent.1
  41.6 2.7 %inner_step_3.1 = (f32[32,48,128]{2,1,0:T(8,128)S(1)}, f32[8,48,128]{2,1,0:T(8,128)S(1)}, f32[32,8,128]{2,1,0:T(8,128)S(1)}, f32[24,16,128]{2,1,0:T(8,128)S(1)}) custom-call(s32[3,256]{1,0:T(4,128)S(1)} %pad_select_fusion.1.refs_0_, f32[4,256]{1,0:T(4,128)S(1)} %pad_select_fusion.refs_1_, f32[32,48,128]{2,1,0:T(8,128)S(1)} %get-tuple-element.55.refs_2_, ...), custom_call_target="tpu_custom_call" | custom-call | flops 11796480 | bytes 4718592 | tf_op jit(solution)/shard_map/inner_step_3/pallas_call | solution.py:301
  44.3 0.7 %collective-permute-done.10.far_ref = f32[4,48,128]{2,1,0:T(8,128)S(1)} collective-permute-done((f32[4,48,128]{2,1,0:T(8,128)S(1)}, f32[4,48,128]{2,1,0:T(8,128)S(1)}, u32[]{:S(2)}, u32[]{:S(2)}) %collective-permute-start.10) | collective-permute-done | bytes 98336 | tf_op jit(solution)/shard_map/ppermute | solution.py:696
  45.1 1.1 %last_step.1 = (f32[32,48,128]{2,1,0:T(8,128)S(1)}, f32[24,16,128]{2,1,0:T(8,128)S(1)}, f32[224,128]{1,0:T(8,128)S(1)}) custom-call(s32[2,2]{1,0:T(2,128)S(1)} %copy-done, f32[24,16,128]{2,1,0:T(8,128)S(1)} %get-tuple-element.62.even_ref, f32[32,48,128]{2,1,0:T(8,128)S(1)} %get-tuple-element.63.current_ref, ...), custom_call_target="tpu_custom_call", output_to_operand_aliasing={{0}: (2, {})} | custom-call | flops 1966080 | bytes 2359296 | tf_op jit(solution)/shard_map/last_step/pallas_call | solution.py:542
  46.2 2.3 %collective-permute-start.12 = (f32[224,128]{1,0:T(8,128)S(1)}, f32[224,128]{1,0:T(8,128)S(1)}, u32[]{:S(2)}, u32[]{:S(2)}) collective-permute-start(f32[224,128]{1,0:T(8,128)S(1)} %get-tuple-element.68), channel_id=1, source_target_pairs={{0,8},{2,10},{4,12},{6,14},{8,0},{10,2},{12,4},{14,6},{1,9},{3,11}... | collective-permute-start | bytes 344072 | tf_op jit(solution)/shard_map/ppermute | solution.py:738
  48.5 0.4 pack_own.3.refs_1_
  48.9 0.3 copy-done.1
  49.1 1.1 %lag_image.2.refs_3_ = f32[17,16,768]{2,1,0:T(8,128)S(1)} custom-call(s32[17]{0:T(128)S(1)} %copy-done.1, f32[4,96,128]{2,1,0:T(8,128)S(1)} %pack_own.3.refs_1_, f32[224,128]{1,0:T(8,128)S(1)} %collective-permute-done.13.refs_2_), custom_call_target="tpu_custom_call" | custom-call | flops 2088960 | bytes 1671168 | tf_op jit(solution)/shard_map/lag_image/pallas_call | solution.py:646
  50.2 0.9 %write_out.1 = f32[32,48,128]{2,1,0:T(8,128)} custom-call(f32[32,48,128]{2,1,0:T(8,128)S(1)} %get-tuple-element.66.level_ref), custom_call_target="tpu_custom_call" | custom-call | bytes 1572864 | tf_op jit(solution)/shard_map/write_out/pallas_call | solution.py:571
  51.1 0.4 pack_own.2.refs_1_
  51.5 1.9 %collective-permute-done.12.refs_2_ = f32[224,128]{1,0:T(8,128)S(1)} collective-permute-done((f32[224,128]{1,0:T(8,128)S(1)}, f32[224,128]{1,0:T(8,128)S(1)}, u32[]{:S(2)}, u32[]{:S(2)}) %collective-permute-start.12) | collective-permute-done | bytes 114720 | tf_op jit(solution)/shard_map/ppermute | solution.py:738
  53.5 1.7 %lag_image.3 = f32[17,16,768]{2,1,0:T(8,128)} custom-call(s32[17]{0:T(128)S(1)} %copy-done.1, f32[4,96,128]{2,1,0:T(8,128)S(1)} %pack_own.2.refs_1_, f32[224,128]{1,0:T(8,128)S(1)} %collective-permute-done.12.refs_2_, f32[17,16,768]{2,1,0:T(8,128)S(1)} %lag_image.2.refs_3_), custom_call_target="tpu_custom_call" | custom-call | flops 2088960 | bytes 1671168 | tf_op jit(solution)/shard_map/lag_image/pallas_call | solution.py:646
  (31 shorter events, 0.5 us)
Async XLA Ops:
  1.7 13.7 %collective-permute-start = (f32[4,48,128]{2,1,0:T(8,128)S(1)}, f32[4,48,128]{2,1,0:T(8,128)S(1)}, u32[]{:S(2)}, u32[]{:S(2)}) collective-permute-start(f32[4,48,128]{2,1,0:T(8,128)S(1)} %get-tuple-element.41), channel_id=1, source_target_pairs={{0,2},{2,0},{4,6},{6,4},{8,10},{10,8},{12,14},{14,12},{1,3},{3,1},... | collective-permute-start | bytes 294920 | tf_op jit(solution)/shard_map/ppermute | solution.py:697
  4.7 10.6 %collective-permute-start.1 = (f32[4,48,128]{2,1,0:T(8,128)S(1)}, f32[4,48,128]{2,1,0:T(8,128)S(1)}, u32[]{:S(2)}, u32[]{:S(2)}) collective-permute-start(f32[4,48,128]{2,1,0:T(8,128)S(1)} %get-tuple-element.42), channel_id=1, source_target_pairs={{6,8},{8,6},{14,0},{0,14},{7,9},{9,7},{15,1},{1,15},{22,24},{24,22... | collective-permute-start | bytes 294920 | tf_op jit(solution)/shard_map/ppermute | solution.py:696
  10.2 5.2 %collective-permute-start.2 = (f32[32,8,128]{2,1,0:T(8,128)S(1)}, f32[32,8,128]{2,1,0:T(8,128)S(1)}, u32[]{:S(2)}, u32[]{:S(2)}) collective-permute-start(f32[32,8,128]{2,1,0:T(8,128)S(1)} %get-tuple-element.43), channel_id=1, source_target_pairs={{0,1},{1,0},{2,3},{3,2},{4,5},{5,4},{6,7},{7,6},{8,9},{9,8},{10,11... | collective-permute-start | bytes 393224 | tf_op jit(solution)/shard_map/ppermute | solution.py:698
  10.3 0.7 %copy-start.2 = (s32[3,256]{1,0:T(4,128)S(1)}, s32[3,256]{1,0:T(4,128)}, u32[]{:S(2)}) copy-start(s32[3,256]{1,0:T(4,128)} %param.14) | copy-start | bytes 9220
  10.3 0.7 %copy-start.4 = (s32[3,8]{1,0:T(4,128)S(1)}, s32[3,8]{1,0:T(4,128)}, u32[]{:S(2)}) copy-start(s32[3,8]{1,0:T(4,128)} %param.12) | copy-start | bytes 292
  11.0 0.7 %copy-start.3 = (f32[4,256]{1,0:T(4,128)S(1)}, f32[4,256]{1,0:T(4,128)}, u32[]{:S(2)}) copy-start(f32[4,256]{1,0:T(4,128)} %param.15) | copy-start | bytes 12292
  11.0 0.7 %copy-start.5 = (f32[4,8]{1,0:T(4,128)S(1)}, f32[4,8]{1,0:T(4,128)}, u32[]{:S(2)}) copy-start(f32[4,8]{1,0:T(4,128)} %param.13) | copy-start | bytes 388
  15.5 9.9 %collective-permute-start.5 = (f32[32,8,128]{2,1,0:T(8,128)S(1)}, f32[32,8,128]{2,1,0:T(8,128)S(1)}, u32[]{:S(2)}, u32[]{:S(2)}) collective-permute-start(f32[32,8,128]{2,1,0:T(8,128)S(1)} %get-tuple-element.46.refs_5_), channel_id=1, source_target_pairs={{0,1},{1,0},{2,3},{3,2},{4,5},{5,4},{6,7},{7,6},{8,9},{9,8},{10,11... | collective-permute-start | bytes 393224 | tf_op jit(solution)/shard_map/ppermute | solution.py:698
  16.1 7.3 %collective-permute-start.3 = (f32[4,48,128]{2,1,0:T(8,128)S(1)}, f32[4,48,128]{2,1,0:T(8,128)S(1)}, u32[]{:S(2)}, u32[]{:S(2)}) collective-permute-start(f32[4,48,128]{2,1,0:T(8,128)S(1)} %get-tuple-element.44.refs_3_), channel_id=1, source_target_pairs={{0,2},{2,0},{4,6},{6,4},{8,10},{10,8},{12,14},{14,12},{1,3},{3,1},... | collective-permute-start | bytes 294920 | tf_op jit(solution)/shard_map/ppermute | solution.py:697
  16.1 9.4 %collective-permute-start.4 = (f32[4,48,128]{2,1,0:T(8,128)S(1)}, f32[4,48,128]{2,1,0:T(8,128)S(1)}, u32[]{:S(2)}, u32[]{:S(2)}) collective-permute-start(f32[4,48,128]{2,1,0:T(8,128)S(1)} %get-tuple-element.45.refs_4_), channel_id=1, source_target_pairs={{6,8},{8,6},{14,0},{0,14},{7,9},{9,7},{15,1},{1,15},{22,24},{24,22... | collective-permute-start | bytes 294920 | tf_op jit(solution)/shard_map/ppermute | solution.py:696
  25.6 9.9 %collective-permute-start.8 = (f32[32,8,128]{2,1,0:T(8,128)S(1)}, f32[32,8,128]{2,1,0:T(8,128)S(1)}, u32[]{:S(2)}, u32[]{:S(2)}) collective-permute-start(f32[32,8,128]{2,1,0:T(8,128)S(1)} %get-tuple-element.53.refs_5_), channel_id=1, source_target_pairs={{0,1},{1,0},{2,3},{3,2},{4,5},{5,4},{6,7},{7,6},{8,9},{9,8},{10,11... | collective-permute-start | bytes 393224 | tf_op jit(solution)/shard_map/ppermute | solution.py:698
  25.7 7.4 %collective-permute-start.6 = (f32[4,48,128]{2,1,0:T(8,128)S(1)}, f32[4,48,128]{2,1,0:T(8,128)S(1)}, u32[]{:S(2)}, u32[]{:S(2)}) collective-permute-start(f32[4,48,128]{2,1,0:T(8,128)S(1)} %get-tuple-element.51.refs_3_), channel_id=1, source_target_pairs={{0,2},{2,0},{4,6},{6,4},{8,10},{10,8},{12,14},{14,12},{1,3},{3,1},... | collective-permute-start | bytes 294920 | tf_op jit(solution)/shard_map/ppermute | solution.py:697
  25.8 9.7 %collective-permute-start.7 = (f32[4,48,128]{2,1,0:T(8,128)S(1)}, f32[4,48,128]{2,1,0:T(8,128)S(1)}, u32[]{:S(2)}, u32[]{:S(2)}) collective-permute-start(f32[4,48,128]{2,1,0:T(8,128)S(1)} %get-tuple-element.52.refs_4_), channel_id=1, source_target_pairs={{6,8},{8,6},{14,0},{0,14},{7,9},{9,7},{15,1},{1,15},{22,24},{24,22... | collective-permute-start | bytes 294920 | tf_op jit(solution)/shard_map/ppermute | solution.py:696
  29.8 0.7 %copy-start = (s32[2,2]{1,0:T(2,128)S(1)}, s32[2,2]{1,0:T(2,128)}, u32[]{:S(2)}) copy-start(s32[2,2]{1,0:T(2,128)} %steps_ref.1) | copy-start | bytes 52
  35.7 8.7 %collective-permute-start.9 = (f32[4,48,128]{2,1,0:T(8,128)S(1)}, f32[4,48,128]{2,1,0:T(8,128)S(1)}, u32[]{:S(2)}, u32[]{:S(2)}) collective-permute-start(f32[4,48,128]{2,1,0:T(8,128)S(1)} %get-tuple-element.58.refs_3_), channel_id=1, source_target_pairs={{0,2},{2,0},{4,6},{6,4},{8,10},{10,8},{12,14},{14,12},{1,3},{3,1},... | collective-permute-start | bytes 294920 | tf_op jit(solution)/shard_map/ppermute | solution.py:697
  35.7 9.3 %collective-permute-start.10 = (f32[4,48,128]{2,1,0:T(8,128)S(1)}, f32[4,48,128]{2,1,0:T(8,128)S(1)}, u32[]{:S(2)}, u32[]{:S(2)}) collective-permute-start(f32[4,48,128]{2,1,0:T(8,128)S(1)} %get-tuple-element.59.refs_4_), channel_id=1, source_target_pairs={{6,8},{8,6},{14,0},{0,14},{7,9},{9,7},{15,1},{1,15},{22,24},{24,22... | collective-permute-start | bytes 294920 | tf_op jit(solution)/shard_map/ppermute | solution.py:696
  39.7 5.3 %collective-permute-start.11 = (f32[32,8,128]{2,1,0:T(8,128)S(1)}, f32[32,8,128]{2,1,0:T(8,128)S(1)}, u32[]{:S(2)}, u32[]{:S(2)}) collective-permute-start(f32[32,8,128]{2,1,0:T(8,128)S(1)} %get-tuple-element.60.refs_5_), channel_id=1, source_target_pairs={{0,1},{1,0},{2,3},{3,2},{4,5},{5,4},{6,7},{7,6},{8,9},{9,8},{10,11... | collective-permute-start | bytes 393224 | tf_op jit(solution)/shard_map/ppermute | solution.py:698
  41.5 7.4 %collective-permute-start.13 = (f32[224,128]{1,0:T(8,128)S(1)}, f32[224,128]{1,0:T(8,128)S(1)}, u32[]{:S(2)}, u32[]{:S(2)}) collective-permute-start(f32[224,128]{1,0:T(8,128)S(1)} %pack_sent.1), channel_id=1, source_target_pairs={{0,8},{2,10},{4,12},{6,14},{8,0},{10,2},{12,4},{14,6},{1,9},{3,11}... | collective-permute-start | bytes 344072 | tf_op jit(solution)/shard_map/ppermute | solution.py:732
  46.2 7.2 %collective-permute-start.12 = (f32[224,128]{1,0:T(8,128)S(1)}, f32[224,128]{1,0:T(8,128)S(1)}, u32[]{:S(2)}, u32[]{:S(2)}) collective-permute-start(f32[224,128]{1,0:T(8,128)S(1)} %get-tuple-element.68), channel_id=1, source_target_pairs={{0,8},{2,10},{4,12},{6,14},{8,0},{10,2},{12,4},{14,6},{1,9},{3,11}... | collective-permute-start | bytes 344072 | tf_op jit(solution)/shard_map/ppermute | solution.py:738
  48.5 0.7 %copy-start.1 = (s32[17]{0:T(128)S(1)}, s32[17]{0:T(128)}, u32[]{:S(2)}) copy-start(s32[17]{0:T(128)} %refs_0_.3) | copy-start | bytes 208

commit v2 on v1

--- a/solution.py
+++ b/solution.py
@@ -1,5 +1,6 @@
 import jax
 import jax.numpy as jnp
+import numpy as np
 from jax import lax
 from jax.experimental import pallas as pl
 from jax.experimental.pallas import tpu as pltpu
@@ -66,18 +67,36 @@
         return pl.multiple_of((1 - self.y) * (count_y - SIDE), SIDE)
 
 
-def first_faces(field):
+def first_far(field):
     count_x, count_y, count_z = field.shape
 
-    def kernel(field_ref, near_ref, far_ref, side_ref, sems):
+    def kernel(field_ref, far_ref, sem):
+        start = jnp.where(Place().even, 0, count_x - WIDTH)
+        copy = pltpu.make_async_copy(field_ref.at[pl.ds(start, WIDTH)], far_ref, sem)
+        copy.start()
+        copy.wait()
+
+    return pl.pallas_call(
+        kernel,
+        out_shape=shape(WIDTH, count_y, count_z),
+        in_specs=[spec(pltpu.HBM)],
+        out_specs=spec(pltpu.VMEM),
+        scratch_shapes=[pltpu.SemaphoreType.DMA],
+        compiler_params=params(8),
+        name="first_far",
+    )(field)
+
+
+def first_near(field):
+    count_x, count_y, count_z = field.shape
+
+    def kernel(field_ref, near_ref, side_ref, sems):
         place = Place()
-        top = count_x - WIDTH
-        near_start = jnp.where(place.even, top, 0)
+        start = jnp.where(place.even, count_x - WIDTH, 0)
         copies = [
-            pltpu.make_async_copy(field_ref.at[pl.ds(top - near_start, WIDTH)], far_ref, sems.at[0]),
-            pltpu.make_async_copy(field_ref.at[pl.ds(near_start, WIDTH)], near_ref, sems.at[1]),
+            pltpu.make_async_copy(field_ref.at[pl.ds(start, WIDTH)], near_ref, sems.at[0]),
             pltpu.make_async_copy(
-                field_ref.at[:, pl.ds(place.block(count_y), SIDE)], side_ref, sems.at[2]
+                field_ref.at[:, pl.ds(place.block(count_y), SIDE)], side_ref, sems.at[1]
             ),
         ]
         for copy in copies:
@@ -87,12 +106,12 @@
 
     return pl.pallas_call(
         kernel,
-        out_shape=face_shapes(count_x, count_y, count_z),
+        out_shape=face_shapes(count_x, count_y, count_z)[1:],
         in_specs=[spec(pltpu.HBM)],
-        out_specs=(spec(pltpu.VMEM),) * 3,
-        scratch_shapes=[pltpu.SemaphoreType.DMA((3,))],
+        out_specs=(spec(pltpu.VMEM),) * 2,
+        scratch_shapes=[pltpu.SemaphoreType.DMA((2,))],
         compiler_params=params(8),
-        name="first_faces",
+        name="first_near",
     )(field)
 
 
@@ -108,7 +127,7 @@
     return flat[pl.ds(start, count_a, stride=2 * stride), :]
 
 
-def inner_step(number, points, waves, current, faces, previous, courant, snapshots=None):
+def inner_step(number, points, waves, current, faces, previous, courant, snapshots=None, matrices=None):
     count_x, count_y, count_z = current.shape
     count_a, count_b = count_x // 2, count_y // 2
     first = faces is None
@@ -121,22 +140,24 @@
         take = lambda count: [refs.pop(0) for _ in range(count)]
         points_ref, waves_ref, current_ref = take(3)
         if not first:
-            near_ref, far_ref, side_ref = take(3)
+            far_ref, near_ref, side_ref = take(3)
         previous_ref, courant_ref = take(2)
         if snapshot:
-            (steps_ref,) = take(1)
+            steps_ref, matrices_ref = take(2)
         next_ref, qx_ref, qy_ref = take(3)
         if first:
             kept_ref, cx_ref, cy_ref = take(3)
-        elif not last:
+        if not last:
             (whole_ref,) = take(1)
-        if snapshot or last:
+        if snapshot:
+            own_out, sent_out, own_matrix, sent_matrix, flag_ref = take(5)
+        if last:
             (even_ref,) = take(1)
         padded, zpart, addpart = take(3)
         if first:
             before_ref, sems = take(2)
         if snapshot:
-            wanted, sems = take(2)
+            even_ref, wanted, sems = take(3)
 
         place = Place()
         block = place.block(count_y)
@@ -152,8 +173,13 @@
         else:
             before_ref, kept_ref = previous_ref, courant_ref
         if snapshot:
-            copies = [pltpu.make_async_copy(steps_ref, wanted, sems.at[0])]
-            copies[0].start()
+            copies = [
+                pltpu.make_async_copy(steps_ref, wanted, sems.at[0]),
+                pltpu.make_async_copy(matrices_ref.at[place.field], own_matrix, sems.at[1]),
+                pltpu.make_async_copy(matrices_ref.at[1 - place.field], sent_matrix, sems.at[2]),
+            ]
+            for copy in copies:
+                copy.start()
 
         zero_x = jnp.zeros((WIDTH, count_y + 2 * SIDE, count_z), F32)
         padded[pl.ds(0, WIDTH)] = zero_x
@@ -236,7 +262,7 @@
                     + padded[x + WIDTH, pl.ds(SIDE - offset, count_y)]
                 )
                 total = total + weight * paired
-            if not first and not last:
+            if not last:
                 whole_ref[x] = middle
             next_ref[x] = (2.0 * middle - before_ref[x] + kept_ref[x] * total) + addpart[x]
             return 0
@@ -254,7 +280,11 @@
             for b in range(count_b):
                 even_ref[b] = even_rows(padded, WIDTH, SIDE, count_a, b)
         if snapshot:
-            copies[0].wait()
+            for copy in copies:
+                copy.wait()
+            flag_ref[...] = jnp.where(
+                wanted[place.field, 1] == STEPS, jnp.ones(flag_ref.shape, F32), 0.0
+            )
             earlier = wanted[place.field, 0] == number - 1
 
             @pl.when(earlier)
@@ -266,6 +296,10 @@
             def _():
                 for b in range(count_b):
                     even_ref[b] = even_rows(padded, WIDTH, SIDE, count_a, b)
+
+            for kind, part in enumerate(packed(even_ref, own_matrix)):
+                own_out[kind] = part
+            send_into(even_ref, sent_matrix, sent_out)
 
     full = shape(count_x, count_y, count_z)
     slab, side = shape(2 * WIDTH, count_y, count_z), shape(count_x, SIDE, count_z)
@@ -273,9 +307,18 @@
     outs = [full, slab, side]
     if first:
         outs += [full, slab, side]
-    elif not last:
+    if not last:
         outs.append(full)
-    if snapshot or last:
+    if snapshot:
+        size = GROUP * count_z
+        outs += [
+            shape(4, count_b // GROUP * count_a, count_z),
+            sent_shape(count_a, count_b, count_z),
+            shape(size, size, dtype=BF16),
+            shape(size, size, dtype=BF16),
+            shape(8, count_z),
+        ]
+    if last:
         outs.append(even)
     place_of = spec(pltpu.HBM) if first else spec(pltpu.VMEM)
     operands, specs = [points, waves, current], [spec(pltpu.VMEM)] * 2 + [place_of]
@@ -292,11 +335,12 @@
     if first:
         scratch += [pltpu.VMEM(full.shape, F32), pltpu.SemaphoreType.DMA((3,))]
     if snapshot:
-        operands.append(snapshots)
-        specs.append(spec(pltpu.HBM))
+        operands += [snapshots, matrices]
+        specs += [spec(pltpu.HBM)] * 2
         scratch += [
+            pltpu.VMEM(even.shape, F32),
             pltpu.SMEM(snapshots.shape, jnp.int32),
-            pltpu.SemaphoreType.DMA((1,)),
+            pltpu.SemaphoreType.DMA((3,)),
         ]
     return pl.pallas_call(
         kernel,
@@ -306,7 +350,6 @@
         scratch_shapes=scratch,
         compiler_params=params(20),
         cost_estimate=cost(count_x * count_y * count_z, 60, 6),
-        name=f"inner_step_{number}",
     )(*operands)
 
 
@@ -328,8 +371,8 @@
 
 def add_halo(place, parts, halos, outs):
     qx_ref, qy_ref, cx_ref, cy_ref = parts
-    near_in, far_in, side_in = halos
-    near_out, far_out, side_out = outs
+    far_in, near_in, side_in = halos
+    far_out, near_out, side_out = outs
     count_y, count_x = qx_ref.shape[1], qy_ref.shape[0]
     block = place.block(count_y)
 
@@ -353,7 +396,7 @@
 
     def along_y(shifts, masks):
         halo = side_in[...]
-        depth, lanes = halo.shape[0], halo.shape[2]
+        lanes = halo.shape[2]
         line = lax.broadcasted_iota(jnp.int32, (1, SIDE, lanes), 1)
         total = None
         for k in range(1, WIDTH + 1):
@@ -403,19 +446,17 @@
 def pack_matrix(window, count_z):
     half = count_z // GROUP
     size = GROUP * count_z
-    row = lax.broadcasted_iota(jnp.int32, (size, size), 0)
-    column = lax.broadcasted_iota(jnp.int32, (size, size), 1)
+    row, column = np.arange(size)[:, None], np.arange(size)[None, :]
     row_b, row_z = row // count_z, row % count_z
     kind = column // count_z
     parity = kind % 2
     lane_b, lane_i = (column % count_z) // half, column % half
     main = (row_b == lane_b) & (row_z == 2 * (half * window + lane_i) + parity)
-    is_low = window == 0
-    wanted_b = jnp.where(is_low, lane_b + GROUP - 1, lane_b + 1) % GROUP
+    wanted_b = (lane_b + (GROUP - 1 if window == 0 else 1)) % GROUP
     wanted_z = 2 * (half * (1 - window) + lane_i) + parity
-    useful = jnp.where(is_low, lane_i < REACH, lane_i >= half - REACH)
+    useful = lane_i < REACH if window == 0 else lane_i >= half - REACH
     edge = (row_b == wanted_b) & (row_z == wanted_z) & useful
-    return jnp.where(kind < 2, main, edge).astype(BF16)
+    return np.where(kind < 2, main, edge).astype(np.float32)
 
 
 def packed(even_ref, matrix_ref):
@@ -478,38 +519,18 @@
     return shape(2 * groups * count_a + extra, count_z)
 
 
-def pack_sent(even, matrix):
-    count_b, count_a, count_z = even.shape
-
-    def kernel(even_ref, matrix_ref, out_ref):
-        send_into(even_ref, matrix_ref, out_ref)
-
-    return pl.pallas_call(
-        kernel,
-        out_shape=sent_shape(count_a, count_b, count_z),
-        in_specs=[spec(pltpu.VMEM)] * 2,
-        out_specs=spec(pltpu.VMEM),
-        compiler_params=params(8),
-        cost_estimate=cost(count_b * count_a * count_z, 1024, 4),
-        name="pack_sent",
-    )(even, matrix)
-
-
-def last_step(snapshots, even_before, current, parts, halos, matrix):
+def last_step(flag, even_before, current, parts, halos, matrix):
     count_x, count_y, count_z = current.shape
     count_a, count_b = count_x // 2, count_y // 2
 
     def kernel(
-        steps_ref, even_ref, current_ref, qx_ref, qy_ref, cx_ref, cy_ref, near_ref, far_ref,
-        side_ref, matrix_ref, final_ref, late_ref, sent_ref, near_out, far_out, side_out,
-        wanted, sems,
+        flag_ref, even_ref, current_ref, qx_ref, qy_ref, cx_ref, cy_ref, far_ref, near_ref,
+        side_ref, matrix_ref, final_ref, late_ref, sent_ref, far_out, near_out, side_out,
     ):
         place = Place()
-        copy = pltpu.make_async_copy(steps_ref, wanted, sems.at[0])
-        copy.start()
         add_halo(
-            place, (qx_ref, qy_ref, cx_ref, cy_ref), (near_ref, far_ref, side_ref),
-            (near_out, far_out, side_out),
+            place, (qx_ref, qy_ref, cx_ref, cy_ref), (far_ref, near_ref, side_ref),
+            (far_out, near_out, side_out),
         )
         low, high = pl.ds(0, WIDTH), pl.ds(count_x - WIDTH, WIDTH)
 
@@ -524,18 +545,11 @@
             final_ref[high] = far_out[...]
 
         final_ref[:, pl.ds(place.block(count_y), SIDE)] = side_out[...]
-        copy.wait()
-        wants_last = wanted[place.field, 1] == STEPS
-
-        @pl.when(wants_last)
-        def _():
-            for b in range(count_b):
-                late_ref[b] = even_rows(final_ref, 0, 0, count_a, b)
-
-        @pl.when(jnp.logical_not(wants_last))
-        def _():
-            late_ref[...] = even_ref[...]
-
+        wants_last = jnp.broadcast_to(flag_ref[0:1, :], (count_a, count_z)) > 0.5
+        for b in range(count_b):
+            late_ref[b] = jnp.where(
+                wants_last, even_rows(final_ref, 0, 0, count_a, b), even_ref[b]
+            )
         send_into(late_ref, matrix_ref, sent_ref)
 
     slab, _, side = face_shapes(count_x, count_y, count_z)
@@ -546,20 +560,18 @@
             shape(count_b, count_a, count_z),
             sent_shape(count_a, count_b, count_z),
         ),
-        in_specs=[spec(pltpu.HBM)] + [spec(pltpu.VMEM)] * 10,
+        in_specs=[spec(pltpu.VMEM)] * 11,
         out_specs=(spec(pltpu.VMEM),) * 3,
         scratch_shapes=[
             pltpu.VMEM(slab.shape, F32),
             pltpu.VMEM(slab.shape, F32),
             pltpu.VMEM(side.shape, F32),
-            pltpu.SMEM(snapshots.shape, jnp.int32),
-            pltpu.SemaphoreType.DMA((1,)),
         ],
         input_output_aliases={2: 0},
         compiler_params=params(12),
         cost_estimate=cost(count_x * count_y * count_z, 10, 3),
         name="last_step",
-    )(snapshots, even_before, current, *parts, *halos, matrix)
+    )(flag, even_before, current, *parts, *halos, matrix)
 
 
 def write_out(level):
@@ -671,7 +683,7 @@
     snapshot_steps,
     lag_offsets,
 ):
-    count_x, count_y, count_z = field_now.shape
+    count_x, _, count_z = field_now.shape
     loop_size = lax.axis_size("gx")
     half_size = loop_size // 2
     turn = loop_size // 4
@@ -691,11 +703,16 @@
     near_pairs, far_pairs = pairs(0), pairs(1)
     across = [(i, (i + half_size) % loop_size) for i in range(loop_size)]
 
+    def send_far(far):
+        return lax.ppermute(far, "gx", far_pairs)
+
+    def send_near(near, side):
+        near = lax.ppermute(near, "gx", near_pairs)
+        return near, lax.ppermute(side, "gy", [(0, 1), (1, 0)])
+
     def exchange(faces):
-        near, far, side = faces
-        far_in = lax.ppermute(far, "gx", far_pairs)
-        near_in = lax.ppermute(near, "gx", near_pairs)
-        return near_in, far_in, lax.ppermute(side, "gy", [(0, 1), (1, 0)])
+        far, near, side = faces
+        return (send_far(far), *send_near(near, side))
 
     most = -(-max(source_cells.shape[1], receiver_cells.shape[1]) // 128) * 128
 
@@ -708,32 +725,33 @@
 
     points = chosen(source_cells, receiver_cells, -1)
     waves = chosen(source_wave, receiver_wave, 0.0)
-    own_matrix = pack_matrix(field, count_z)
-    sent_matrix = pack_matrix(1 - field, count_z)
-
-    field_now, field_prev, courant_squared = (
+    matrices = jnp.asarray(
+        np.stack([pack_matrix(window, count_z) for window in (0, 1)]), dtype=BF16
+    )
+    field_now, field_prev, courant_squared, matrices = (
         pltpu.with_memory_space_constraint(array, pltpu.HBM)
-        for array in (field_now, field_prev, courant_squared)
+        for array in (field_now, field_prev, courant_squared, matrices)
     )
-    halos = exchange(first_faces(field_now))
-    next1, qx, qy, courant, cx, cy = inner_step(
+    far = send_far(first_far(field_now))
+    faces = first_near(field_now)
+    halos = (far, *send_near(*faces))
+    next1, qx, qy, courant, cx, cy, whole0 = inner_step(
         0, points, waves, field_now, None, field_prev, courant_squared
     )
     faces = halo_step((qx, qy, cx, cy), halos)
     halos = exchange(faces)
-    next2, qx, qy, whole1 = inner_step(1, points, waves, next1, faces, field_now, courant)
+    next2, qx, qy, whole1 = inner_step(1, points, waves, next1, faces, whole0, courant)
     faces = halo_step((qx, qy, cx, cy), halos)
     halos = exchange(faces)
-    next3, qx, qy, whole2, early = inner_step(
-        2, points, waves, next2, faces, whole1, courant, snapshot_steps
+    next3, qx, qy, whole2, own_early, sent_early, own_matrix, sent_matrix, flag = inner_step(
+        2, points, waves, next2, faces, whole1, courant, snapshot_steps, matrices
     )
     faces = halo_step((qx, qy, cx, cy), halos)
     halos = exchange(faces)
-    other_early = lax.ppermute(pack_sent(early, sent_matrix), "gx", across)
-    own_early = pack_own(early, own_matrix)
+    other_early = lax.ppermute(sent_early, "gx", across)
     next4, qx, qy, even3 = inner_step(3, points, waves, next3, faces, whole2, courant)
     final, late, sent_late = last_step(
-        snapshot_steps, even3, next4, (qx, qy, cx, cy), halos, sent_matrix
+        flag, even3, next4, (qx, qy, cx, cy), halos, sent_matrix
     )
     other_late = lax.ppermute(sent_late, "gx", across)
     partial = lag_image(lag_offsets, own_early, other_early, None, count_x // 2)

time: 55.6 us -> 58.7 us (1.056)
  waiting for transfers between devices: 7.09 us -> 13.1 us
  other arithmetic: 1.27 us -> 0.01 us
  starting transfers between devices: 23.3 us -> 22.1 us
  Pallas kernels: 20.3 us -> 19.5 us
    ppermute x13, waiting for transfers between devices: 5.16 us -> 10.4 us  [the longest x4 7.43 us: send_far(): return lax.ppermute(far, 'gx', far_pairs)]
    ppermute x1, starting transfers between devices: 2.28 us -> 0.07 us  [body(): other_late = lax.ppermute(sent_late, 'gx', across)]
    convert_element_type x1 -> x0, other arithmetic: 1.23 us -> none  [pack_matrix(): return jnp.where(kind < 2, main, edge).astype(BF16)]
    ppermute x13, starting transfers between devices: 21 us -> 22.1 us  [the longest x4 18.4 us: send_far(): return lax.ppermute(far, 'gx', far_pairs)]
    ppermute x1, waiting for transfers between devices: 1.92 us -> 2.71 us  [body(): other_late = lax.ppermute(sent_late, 'gx', across)]
  transfers between devices with their start and end apart: 14 -> 14, of which waited for: 4 -> 6; matrix products, arithmetic and copies ran while one was open for 2% -> 0% of each run, Pallas kernels for 31% -> 28%
where the time goes in v2:
time: 58.7 us; the launch traced here: 58.3 us
  starting transfers between devices  22.1 us (38%)
  Pallas kernels  19.5 us (33%)
  waiting for transfers between devices  13.1 us (22%)
  local copies, waits for them, and re-layouts  2.6 us (4%)
  between operations  0.93 us (2%)
    ppermute x4, starting transfers between devices, send_far(): return lax.ppermute(far, 'gx', far_pairs)  18.4 us
    pallas_call x4, Pallas kernels, inner_step(): pl.pallas_call(kernel, out_shape=tuple(outs), in_specs=specs, out_specs=(...  12.3 us
    ppermute x4, waiting for transfers between devices, send_far(): return lax.ppermute(far, 'gx', far_pairs)  7.43 us
    ppermute x4, waiting for transfers between devices, send_near(): near = lax.ppermute(near, 'gx', near_pairs)  2.97 us
    pallas_call x2, Pallas kernels, lag_image(): pl.pallas_call(kernel, out_shape=shape(*out), in_specs=[spec(pltpu.HBM)]...  2.85 us
    ppermute x4, starting transfers between devices, send_near(): near = lax.ppermute(near, 'gx', near_pairs)  2.79 us
    ppermute x1, waiting for transfers between devices, body(): other_late = lax.ppermute(sent_late, 'gx', across)  2.71 us
    unnamed x12, local copies, waits for them, and re-layouts  2.6 us
  transfers between devices with their start and end apart: 14, of which 6 were waited for; matrix products, arithmetic and copies ran while one was open for 0% of the time, Pallas kernels for 28%

profile of v2, /device:TPU:0, one launch (start us, length us, event | category | flops | bytes accessed | tf_op | source)
XLA Modules:
  0.0 58.3 jit_solution(4592432665709431727)
XLA Ops:
  0.6 1.0 %first_near.1 = (f32[4,48,128]{2,1,0:T(8,128)S(1)}, f32[32,8,128]{2,1,0:T(8,128)S(1)}) custom-call(f32[32,48,128]{2,1,0:T(8,128)} %field_ref.3), custom_call_target="tpu_custom_call" | custom-call | tf_op jit(solution)/shard_map/first_near/pallas_call | solution.py:107
  1.7 0.6 collective-permute-start.2
  2.2 2.6 %collective-permute-start.1 = (f32[4,48,128]{2,1,0:T(8,128)S(1)}, f32[4,48,128]{2,1,0:T(8,128)S(1)}, u32[]{:S(2)}, u32[]{:S(2)}) collective-permute-start(f32[4,48,128]{2,1,0:T(8,128)S(1)} %get-tuple-element.45), channel_id=1, source_target_pairs={{0,2},{2,0},{4,6},{6,4},{8,10},{10,8},{12,14},{14,12},{1,3},{3,1},... | collective-permute-start | bytes 294920 | tf_op jit(solution)/shard_map/ppermute | solution.py:710
  4.8 0.9 %first_far.1 = f32[4,48,128]{2,1,0:T(8,128)S(1)} custom-call(f32[32,48,128]{2,1,0:T(8,128)} %field_ref.3), custom_call_target="tpu_custom_call" | custom-call | tf_op jit(solution)/shard_map/first_far/pallas_call | solution.py:79
  5.7 5.5 %collective-permute-start = (f32[4,48,128]{2,1,0:T(8,128)S(1)}, f32[4,48,128]{2,1,0:T(8,128)S(1)}, u32[]{:S(2)}, u32[]{:S(2)}) collective-permute-start(f32[4,48,128]{2,1,0:T(8,128)S(1)} %first_far.1), channel_id=1, source_target_pairs={{6,8},{8,6},{14,0},{0,14},{7,9},{9,7},{15,1},{1,15},{22,24},{24,22... | collective-permute-start | bytes 294920 | tf_op jit(solution)/shard_map/ppermute | solution.py:707
  11.2 0.7 %copy-done.2 = f32[4,256]{1,0:T(4,128)S(1)} copy-done((f32[4,256]{1,0:T(4,128)S(1)}, f32[4,256]{1,0:T(4,128)}, u32[]{:S(2)}) %copy-start.2) | copy-done | bytes 4120
  11.9 0.7 %copy-done.3 = s32[3,256]{1,0:T(4,128)S(1)} copy-done((s32[3,256]{1,0:T(4,128)S(1)}, s32[3,256]{1,0:T(4,128)}, u32[]{:S(2)}) %copy-start.3) | copy-done | bytes 3096
  12.6 3.5 %shard_map.113 = (f32[32,48,128]{2,1,0:T(8,128)S(1)}, f32[8,48,128]{2,1,0:T(8,128)S(1)}, f32[32,8,128]{2,1,0:T(8,128)S(1)}, f32[32,48,128]{2,1,0:T(8,128)S(1)}, ...) custom-call(s32[3,256]{1,0:T(4,128)S(1)} %pad_select_fusion.1.refs_0_, ...), custom_call_target="tpu_custom_call" | custom-call | flops 11796480 | bytes 4718592 | tf_op jit(solution)/shard_map/pallas_call | solution.py:345
  16.2 0.2 halo_step.3
  16.4 4.4 %collective-permute-start.3 = (f32[4,48,128]{2,1,0:T(8,128)S(1)}, f32[4,48,128]{2,1,0:T(8,128)S(1)}, u32[]{:S(2)}, u32[]{:S(2)}) collective-permute-start(f32[4,48,128]{2,1,0:T(8,128)S(1)} %get-tuple-element.47.refs_3_), channel_id=1, source_target_pairs={{6,8},{8,6},{14,0},{0,14},{7,9},{9,7},{15,1},{1,15},{22,24},{24,22... | collective-permute-start | bytes 294920 | tf_op jit(solution)/shard_map/ppermute | solution.py:707
  20.8 0.1 collective-permute-start.4
  20.9 2.6 %shard_map.114 = (f32[32,48,128]{2,1,0:T(8,128)S(1)}, f32[8,48,128]{2,1,0:T(8,128)S(1)}, f32[32,8,128]{2,1,0:T(8,128)S(1)}, f32[32,48,128]{2,1,0:T(8,128)S(1)}) custom-call(s32[3,256]{1,0:T(4,128)S(1)} %pad_select_fusion.1.refs_0_, f32[4,256]{1,0:T(4,128)S(1)} %pad_select_fusion.refs_1_, f32[32,48,128]{2,1,0:T(8,128)S(1)} %get-tuple-element.40.refs_2_, ...), custom_call_target="tpu_custom_call" | custom-call | flops 11796480 | bytes 4718592 | tf_op jit(solution)/shard_map/pallas_call | solution.py:345
  23.5 2.8 %collective-permute-done.3.refs_4_ = f32[4,48,128]{2,1,0:T(8,128)S(1)} collective-permute-done((f32[4,48,128]{2,1,0:T(8,128)S(1)}, f32[4,48,128]{2,1,0:T(8,128)S(1)}, u32[]{:S(2)}, u32[]{:S(2)}) %collective-permute-start.3) | collective-permute-done | bytes 98336 | tf_op jit(solution)/shard_map/ppermute | solution.py:707
  26.3 1.6 %collective-permute-done.4.refs_5_ = f32[4,48,128]{2,1,0:T(8,128)S(1)} collective-permute-done((f32[4,48,128]{2,1,0:T(8,128)S(1)}, f32[4,48,128]{2,1,0:T(8,128)S(1)}, u32[]{:S(2)}, u32[]{:S(2)}) %collective-permute-start.4) | collective-permute-done | bytes 98336 | tf_op jit(solution)/shard_map/ppermute | solution.py:710
  27.9 0.1 halo_step.4
  28.1 0.1 collective-permute-start.8
  28.2 4.1 %collective-permute-start.6 = (f32[4,48,128]{2,1,0:T(8,128)S(1)}, f32[4,48,128]{2,1,0:T(8,128)S(1)}, u32[]{:S(2)}, u32[]{:S(2)}) collective-permute-start(f32[4,48,128]{2,1,0:T(8,128)S(1)} %get-tuple-element.55.refs_3_), channel_id=1, source_target_pairs={{6,8},{8,6},{14,0},{0,14},{7,9},{9,7},{15,1},{1,15},{22,24},{24,22... | collective-permute-start | bytes 294920 | tf_op jit(solution)/shard_map/ppermute | solution.py:707
  32.4 0.7 %copy-done.1 = s32[2,2]{1,0:T(2,128)S(1)} copy-done((s32[2,2]{1,0:T(2,128)S(1)}, s32[2,2]{1,0:T(2,128)}, u32[]{:S(2)}) %copy-start.1) | copy-done | bytes 40
  33.1 3.4 %shard_map.115 = (f32[32,48,128]{2,1,0:T(8,128)S(1)}, f32[8,48,128]{2,1,0:T(8,128)S(1)}, f32[32,8,128]{2,1,0:T(8,128)S(1)}, f32[32,48,128]{2,1,0:T(8,128)S(1)}, ...) custom-call(s32[3,256]{1,0:T(4,128)S(1)} %pad_select_fusion.1.refs_0, ...), custom_call_target="tpu_custom_call" | custom-call | flops 11796480 | bytes 4718592 | tf_op jit(solution)/shard_map/pallas_call | solution.py:345
  36.5 1.5 %collective-permute-done.6.refs_4_ = f32[4,48,128]{2,1,0:T(8,128)S(1)} collective-permute-done((f32[4,48,128]{2,1,0:T(8,128)S(1)}, f32[4,48,128]{2,1,0:T(8,128)S(1)}, u32[]{:S(2)}, u32[]{:S(2)}) %collective-permute-start.6) | collective-permute-done | bytes 98336 | tf_op jit(solution)/shard_map/ppermute | solution.py:707
  38.0 1.3 %collective-permute-done.7.refs_5_ = f32[4,48,128]{2,1,0:T(8,128)S(1)} collective-permute-done((f32[4,48,128]{2,1,0:T(8,128)S(1)}, f32[4,48,128]{2,1,0:T(8,128)S(1)}, u32[]{:S(2)}, u32[]{:S(2)}) %collective-permute-start.7) | collective-permute-done | bytes 98336 | tf_op jit(solution)/shard_map/ppermute | solution.py:710
  39.4 0.2 halo_step.5
  39.7 4.4 %collective-permute-start.9 = (f32[4,48,128]{2,1,0:T(8,128)S(1)}, f32[4,48,128]{2,1,0:T(8,128)S(1)}, u32[]{:S(2)}, u32[]{:S(2)}) collective-permute-start(f32[4,48,128]{2,1,0:T(8,128)S(1)} %get-tuple-element.63.refs_3_), channel_id=1, source_target_pairs={{6,8},{8,6},{14,0},{0,14},{7,9},{9,7},{15,1},{1,15},{22,24},{24,22... | collective-permute-start | bytes 294920 | tf_op jit(solution)/shard_map/ppermute | solution.py:707
  44.2 2.7 %shard_map.116 = (f32[32,48,128]{2,1,0:T(8,128)S(1)}, f32[8,48,128]{2,1,0:T(8,128)S(1)}, f32[32,8,128]{2,1,0:T(8,128)S(1)}, f32[24,16,128]{2,1,0:T(8,128)S(1)}) custom-call(s32[3,256]{1,0:T(4,128)S(1)} %pad_select_fusion.1.refs_0_, f32[4,256]{1,0:T(4,128)S(1)} %pad_select_fusion.refs_1_, f32[32,48,128]{2,1,0:T(8,128)S(1)} %get-tuple-element.60.refs_2_, ...), custom_call_target="tpu_custom_call" | custom-call | flops 11796480 | bytes 4718592 | tf_op jit(solution)/shard_map/pallas_call | solution.py:345
  46.9 3.1 %collective-permute-done.9.far_ref = f32[4,48,128]{2,1,0:T(8,128)S(1)} collective-permute-done((f32[4,48,128]{2,1,0:T(8,128)S(1)}, f32[4,48,128]{2,1,0:T(8,128)S(1)}, u32[]{:S(2)}, u32[]{:S(2)}) %collective-permute-start.9) | collective-permute-done | bytes 98336 | tf_op jit(solution)/shard_map/ppermute | solution.py:707
  50.1 0.7 %last_step.1 = (f32[32,48,128]{2,1,0:T(8,128)S(1)}, f32[24,16,128]{2,1,0:T(8,128)S(1)}, f32[224,128]{1,0:T(8,128)S(1)}) custom-call(f32[8,128]{1,0:T(8,128)S(1)} %get-tuple-element.59.flag_ref, f32[24,16,128]{2,1,0:T(8,128)S(1)} %get-tuple-element.67.even_ref, f32[32,48,128]{2,1,0:T(8,128)S(1)} %get-tuple-element.68.current_ref, ...), custom_call_target="tpu_custom_call", output_to_operand_aliasing={{0}: (2, {})} | custom-call | flops 1966080 | bytes 2359296 | tf_op jit(solution)/shard_map/last_step/pallas_call | solution.py:556
  50.9 0.6 copy-done
  51.4 1.1 %lag_image.2.refs_3_ = f32[17,16,768]{2,1,0:T(8,128)S(1)} custom-call(s32[17]{0:T(128)S(1)} %copy-done, f32[4,96,128]{2,1,0:T(8,128)S(1)} %get-tuple-element.76.refs_1_, f32[224,128]{1,0:T(8,128)S(1)} %collective-permute-done.13.refs_2_), custom_call_target="tpu_custom_call" | custom-call | flops 2088960 | bytes 1671168 | tf_op jit(solution)/shard_map/lag_image/pallas_call | solution.py:658
  52.6 0.9 %write_out.1 = f32[32,48,128]{2,1,0:T(8,128)} custom-call(f32[32,48,128]{2,1,0:T(8,128)S(1)} %get-tuple-element.72.level_ref), custom_call_target="tpu_custom_call" | custom-call | bytes 1572864 | tf_op jit(solution)/shard_map/write_out/pallas_call | solution.py:583
  53.5 0.4 pack_own.1.refs_1_
  53.8 2.7 %collective-permute-done.12.refs_2_ = f32[224,128]{1,0:T(8,128)S(1)} collective-permute-done((f32[224,128]{1,0:T(8,128)S(1)}, f32[224,128]{1,0:T(8,128)S(1)}, u32[]{:S(2)}, u32[]{:S(2)}) %collective-permute-start.12) | collective-permute-done | bytes 114720 | tf_op jit(solution)/shard_map/ppermute | solution.py:756
  56.6 1.7 %lag_image.3 = f32[17,16,768]{2,1,0:T(8,128)} custom-call(s32[17]{0:T(128)S(1)} %copy-done, f32[4,96,128]{2,1,0:T(8,128)S(1)} %pack_own.1.refs_1_, f32[224,128]{1,0:T(8,128)S(1)} %collective-permute-done.12.refs_2_, f32[17,16,768]{2,1,0:T(8,128)S(1)} %lag_image.2.refs_3_), custom_call_target="tpu_custom_call" | custom-call | flops 2088960 | bytes 1671168 | tf_op jit(solution)/shard_map/lag_image/pallas_call | solution.py:658
  (24 shorter events, 0.5 us)
Async XLA Ops:
  1.7 14.5 %collective-permute-start.2 = (f32[32,8,128]{2,1,0:T(8,128)S(1)}, f32[32,8,128]{2,1,0:T(8,128)S(1)}, u32[]{:S(2)}, u32[]{:S(2)}) collective-permute-start(f32[32,8,128]{2,1,0:T(8,128)S(1)} %get-tuple-element.46), channel_id=1, source_target_pairs={{0,1},{1,0},{2,3},{3,2},{4,5},{5,4},{6,7},{7,6},{8,9},{9,8},{10,11... | collective-permute-start | bytes 393224 | tf_op jit(solution)/shard_map/ppermute | solution.py:711
  2.2 13.9 %collective-permute-start.1 = (f32[4,48,128]{2,1,0:T(8,128)S(1)}, f32[4,48,128]{2,1,0:T(8,128)S(1)}, u32[]{:S(2)}, u32[]{:S(2)}) collective-permute-start(f32[4,48,128]{2,1,0:T(8,128)S(1)} %get-tuple-element.45), channel_id=1, source_target_pairs={{0,2},{2,0},{4,6},{6,4},{8,10},{10,8},{12,14},{14,12},{1,3},{3,1},... | collective-permute-start | bytes 294920 | tf_op jit(solution)/shard_map/ppermute | solution.py:710
  5.7 10.5 %collective-permute-start = (f32[4,48,128]{2,1,0:T(8,128)S(1)}, f32[4,48,128]{2,1,0:T(8,128)S(1)}, u32[]{:S(2)}, u32[]{:S(2)}) collective-permute-start(f32[4,48,128]{2,1,0:T(8,128)S(1)} %first_far.1), channel_id=1, source_target_pairs={{6,8},{8,6},{14,0},{0,14},{7,9},{9,7},{15,1},{1,15},{22,24},{24,22... | collective-permute-start | bytes 294920 | tf_op jit(solution)/shard_map/ppermute | solution.py:707
  11.2 0.7 %copy-start.2 = (f32[4,256]{1,0:T(4,128)S(1)}, f32[4,256]{1,0:T(4,128)}, u32[]{:S(2)}) copy-start(f32[4,256]{1,0:T(4,128)} %param.16) | copy-start | bytes 12292
  11.2 0.7 %copy-start.4 = (f32[4,8]{1,0:T(4,128)S(1)}, f32[4,8]{1,0:T(4,128)}, u32[]{:S(2)}) copy-start(f32[4,8]{1,0:T(4,128)} %param.14) | copy-start | bytes 388
  11.9 0.7 %copy-start.3 = (s32[3,256]{1,0:T(4,128)S(1)}, s32[3,256]{1,0:T(4,128)}, u32[]{:S(2)}) copy-start(s32[3,256]{1,0:T(4,128)} %param.15) | copy-start | bytes 9220
  11.9 0.7 %copy-start.5 = (s32[3,8]{1,0:T(4,128)S(1)}, s32[3,8]{1,0:T(4,128)}, u32[]{:S(2)}) copy-start(s32[3,8]{1,0:T(4,128)} %param.13) | copy-start | bytes 292
  16.3 11.6 %collective-permute-start.5 = (f32[32,8,128]{2,1,0:T(8,128)S(1)}, f32[32,8,128]{2,1,0:T(8,128)S(1)}, u32[]{:S(2)}, u32[]{:S(2)}) collective-permute-start(f32[32,8,128]{2,1,0:T(8,128)S(1)} %get-tuple-element.49.refs_5_), channel_id=1, source_target_pairs={{0,1},{1,0},{2,3},{3,2},{4,5},{5,4},{6,7},{7,6},{8,9},{9,8},{10,11... | collective-permute-start | bytes 393224 | tf_op jit(solution)/shard_map/ppermute | solution.py:711
  16.4 9.9 %collective-permute-start.3 = (f32[4,48,128]{2,1,0:T(8,128)S(1)}, f32[4,48,128]{2,1,0:T(8,128)S(1)}, u32[]{:S(2)}, u32[]{:S(2)}) collective-permute-start(f32[4,48,128]{2,1,0:T(8,128)S(1)} %get-tuple-element.47.refs_3_), channel_id=1, source_target_pairs={{6,8},{8,6},{14,0},{0,14},{7,9},{9,7},{15,1},{1,15},{22,24},{24,22... | collective-permute-start | bytes 294920 | tf_op jit(solution)/shard_map/ppermute | solution.py:707
  20.8 7.1 %collective-permute-start.4 = (f32[4,48,128]{2,1,0:T(8,128)S(1)}, f32[4,48,128]{2,1,0:T(8,128)S(1)}, u32[]{:S(2)}, u32[]{:S(2)}) collective-permute-start(f32[4,48,128]{2,1,0:T(8,128)S(1)} %get-tuple-element.48.refs_4_), channel_id=1, source_target_pairs={{0,2},{2,0},{4,6},{6,4},{8,10},{10,8},{12,14},{14,12},{1,3},{3,1},... | collective-permute-start | bytes 294920 | tf_op jit(solution)/shard_map/ppermute | solution.py:710
  28.1 11.3 %collective-permute-start.8 = (f32[32,8,128]{2,1,0:T(8,128)S(1)}, f32[32,8,128]{2,1,0:T(8,128)S(1)}, u32[]{:S(2)}, u32[]{:S(2)}) collective-permute-start(f32[32,8,128]{2,1,0:T(8,128)S(1)} %get-tuple-element.57.refs_5_), channel_id=1, source_target_pairs={{0,1},{1,0},{2,3},{3,2},{4,5},{5,4},{6,7},{7,6},{8,9},{9,8},{10,11... | collective-permute-start | bytes 393224 | tf_op jit(solution)/shard_map/ppermute | solution.py:711
  28.2 9.9 %collective-permute-start.6 = (f32[4,48,128]{2,1,0:T(8,128)S(1)}, f32[4,48,128]{2,1,0:T(8,128)S(1)}, u32[]{:S(2)}, u32[]{:S(2)}) collective-permute-start(f32[4,48,128]{2,1,0:T(8,128)S(1)} %get-tuple-element.55.refs_3_), channel_id=1, source_target_pairs={{6,8},{8,6},{14,0},{0,14},{7,9},{9,7},{15,1},{1,15},{22,24},{24,22... | collective-permute-start | bytes 294920 | tf_op jit(solution)/shard_map/ppermute | solution.py:707
  32.3 7.1 %collective-permute-start.7 = (f32[4,48,128]{2,1,0:T(8,128)S(1)}, f32[4,48,128]{2,1,0:T(8,128)S(1)}, u32[]{:S(2)}, u32[]{:S(2)}) collective-permute-start(f32[4,48,128]{2,1,0:T(8,128)S(1)} %get-tuple-element.56.refs_4_), channel_id=1, source_target_pairs={{0,2},{2,0},{4,6},{6,4},{8,10},{10,8},{12,14},{14,12},{1,3},{3,1},... | collective-permute-start | bytes 294920 | tf_op jit(solution)/shard_map/ppermute | solution.py:710
  32.4 0.7 %copy-start.1 = (s32[2,2]{1,0:T(2,128)S(1)}, s32[2,2]{1,0:T(2,128)}, u32[]{:S(2)}) copy-start(s32[2,2]{1,0:T(2,128)} %refs_8_.1) | copy-start | bytes 52
  39.5 10.5 %collective-permute-start.11 = (f32[32,8,128]{2,1,0:T(8,128)S(1)}, f32[32,8,128]{2,1,0:T(8,128)S(1)}, u32[]{:S(2)}, u32[]{:S(2)}) collective-permute-start(f32[32,8,128]{2,1,0:T(8,128)S(1)} %get-tuple-element.65.refs_5_), channel_id=1, source_target_pairs={{0,1},{1,0},{2,3},{3,2},{4,5},{5,4},{6,7},{7,6},{8,9},{9,8},{10,11... | collective-permute-start | bytes 393224 | tf_op jit(solution)/shard_map/ppermute | solution.py:711
  39.6 7.3 %collective-permute-start.10 = (f32[4,48,128]{2,1,0:T(8,128)S(1)}, f32[4,48,128]{2,1,0:T(8,128)S(1)}, u32[]{:S(2)}, u32[]{:S(2)}) collective-permute-start(f32[4,48,128]{2,1,0:T(8,128)S(1)} %get-tuple-element.64.refs_4_), channel_id=1, source_target_pairs={{0,2},{2,0},{4,6},{6,4},{8,10},{10,8},{12,14},{14,12},{1,3},{3,1},... | collective-permute-start | bytes 294920 | tf_op jit(solution)/shard_map/ppermute | solution.py:710
  39.7 10.4 %collective-permute-start.9 = (f32[4,48,128]{2,1,0:T(8,128)S(1)}, f32[4,48,128]{2,1,0:T(8,128)S(1)}, u32[]{:S(2)}, u32[]{:S(2)}) collective-permute-start(f32[4,48,128]{2,1,0:T(8,128)S(1)} %get-tuple-element.63.refs_3_), channel_id=1, source_target_pairs={{6,8},{8,6},{14,0},{0,14},{7,9},{9,7},{15,1},{1,15},{22,24},{24,22... | collective-permute-start | bytes 294920 | tf_op jit(solution)/shard_map/ppermute | solution.py:707
  44.1 6.8 %collective-permute-start.13 = (f32[224,128]{1,0:T(8,128)S(1)}, f32[224,128]{1,0:T(8,128)S(1)}, u32[]{:S(2)}, u32[]{:S(2)}) collective-permute-start(f32[224,128]{1,0:T(8,128)S(1)} %get-tuple-element.77), channel_id=1, source_target_pairs={{0,8},{2,10},{4,12},{6,14},{8,0},{10,2},{12,4},{14,6},{1,9},{3,11}... | collective-permute-start | bytes 344072 | tf_op jit(solution)/shard_map/ppermute | solution.py:751
  50.8 0.7 %copy-start = (s32[17]{0:T(128)S(1)}, s32[17]{0:T(128)}, u32[]{:S(2)}) copy-start(s32[17]{0:T(128)} %refs_0_.3) | copy-start | bytes 208
  50.8 5.8 %collective-permute-start.12 = (f32[224,128]{1,0:T(8,128)S(1)}, f32[224,128]{1,0:T(8,128)S(1)}, u32[]{:S(2)}, u32[]{:S(2)}) collective-permute-start(f32[224,128]{1,0:T(8,128)S(1)} %get-tuple-element.75), channel_id=1, source_target_pairs={{0,8},{2,10},{4,12},{6,14},{8,0},{10,2},{12,4},{14,6},{1,9},{3,11}... | collective-permute-start | bytes 344072 | tf_op jit(solution)/shard_map/ppermute | solution.py:756

commit v3 on v2

--- a/solution.py
+++ b/solution.py
@@ -67,37 +67,24 @@
         return pl.multiple_of((1 - self.y) * (count_y - SIDE), SIDE)
 
 
-def first_far(field):
+def first_faces(field):
     count_x, count_y, count_z = field.shape
-
-    def kernel(field_ref, far_ref, sem):
-        start = jnp.where(Place().even, 0, count_x - WIDTH)
-        copy = pltpu.make_async_copy(field_ref.at[pl.ds(start, WIDTH)], far_ref, sem)
-        copy.start()
-        copy.wait()
-
-    return pl.pallas_call(
-        kernel,
-        out_shape=shape(WIDTH, count_y, count_z),
-        in_specs=[spec(pltpu.HBM)],
-        out_specs=spec(pltpu.VMEM),
-        scratch_shapes=[pltpu.SemaphoreType.DMA],
-        compiler_params=params(8),
-        name="first_far",
-    )(field)
-
-
-def first_near(field):
-    count_x, count_y, count_z = field.shape
-
-    def kernel(field_ref, near_ref, side_ref, sems):
+    top = count_x - WIDTH
+
+    def kernel(field_ref, far_ref, near_ref, side_ref, whole_ref, sems):
         place = Place()
-        start = jnp.where(place.even, count_x - WIDTH, 0)
+        far = jnp.where(place.even, 0, top)
+        sources = [
+            field_ref.at[pl.ds(far, WIDTH)],
+            field_ref.at[pl.ds(top - far, WIDTH)],
+            field_ref.at[:, pl.ds(place.block(count_y), SIDE)],
+            field_ref,
+        ]
         copies = [
-            pltpu.make_async_copy(field_ref.at[pl.ds(start, WIDTH)], near_ref, sems.at[0]),
-            pltpu.make_async_copy(
-                field_ref.at[:, pl.ds(place.block(count_y), SIDE)], side_ref, sems.at[1]
-            ),
+            pltpu.make_async_copy(source, target, sems.at[index])
+            for index, (source, target) in enumerate(
+                zip(sources, (far_ref, near_ref, side_ref, whole_ref))
+            )
         ]
         for copy in copies:
             copy.start()
@@ -106,12 +93,12 @@
 
     return pl.pallas_call(
         kernel,
-        out_shape=face_shapes(count_x, count_y, count_z)[1:],
+        out_shape=(*face_shapes(count_x, count_y, count_z), shape(*field.shape)),
         in_specs=[spec(pltpu.HBM)],
-        out_specs=(spec(pltpu.VMEM),) * 2,
-        scratch_shapes=[pltpu.SemaphoreType.DMA((2,))],
+        out_specs=(spec(pltpu.VMEM),) * 4,
+        scratch_shapes=[pltpu.SemaphoreType.DMA((4,))],
         compiler_params=params(8),
-        name="first_near",
+        name="first_faces",
     )(field)
 
 
@@ -133,12 +120,19 @@
     first = faces is None
     last = number == STEPS - 1
     snapshot = number == STEPS // 2
-    count_j = points.shape[1]
+    if first:
+        count_j = -(-max(array.shape[1] for array in points) // 128) * 128
+    else:
+        count_j = points.shape[1]
 
     def kernel(*refs):
         refs = list(refs)
         take = lambda count: [refs.pop(0) for _ in range(count)]
-        points_ref, waves_ref, current_ref = take(3)
+        if first:
+            raw_refs = take(4)
+        else:
+            points_ref, waves_ref = take(2)
+        (current_ref,) = take(1)
         if not first:
             far_ref, near_ref, side_ref = take(3)
         previous_ref, courant_ref = take(2)
@@ -146,8 +140,8 @@
             steps_ref, matrices_ref = take(2)
         next_ref, qx_ref, qy_ref = take(3)
         if first:
-            kept_ref, cx_ref, cy_ref = take(3)
-        if not last:
+            kept_ref, cx_ref, cy_ref, points_ref, waves_ref = take(5)
+        elif not last:
             (whole_ref,) = take(1)
         if snapshot:
             own_out, sent_out, own_matrix, sent_matrix, flag_ref = take(5)
@@ -155,7 +149,9 @@
             (even_ref,) = take(1)
         padded, zpart, addpart = take(3)
         if first:
-            before_ref, sems = take(2)
+            before_ref = take(1)[0]
+            raw_refs_in, raw_refs = raw_refs, take(4)
+            (sems,) = take(1)
         if snapshot:
             even_ref, wanted, sems = take(3)
 
@@ -164,9 +160,13 @@
         rows, columns = pl.ds(WIDTH, count_x), pl.ds(SIDE, count_y)
         if first:
             copies = [
-                pltpu.make_async_copy(current_ref, padded.at[rows, columns], sems.at[0]),
-                pltpu.make_async_copy(previous_ref, before_ref, sems.at[1]),
-                pltpu.make_async_copy(courant_ref, kept_ref, sems.at[2]),
+                pltpu.make_async_copy(source, target, sems.at[index])
+                for index, (source, target) in enumerate(
+                    zip(
+                        (*raw_refs_in, previous_ref, courant_ref),
+                        (*raw_refs, before_ref, kept_ref),
+                    )
+                )
             ]
             for copy in copies:
                 copy.start()
@@ -188,6 +188,41 @@
         padded[rows, pl.ds(0, SIDE)] = zero_y
         padded[rows, pl.ds(count_y + SIDE, SIDE)] = zero_y
 
+        padded[rows, columns] = current_ref[...]
+        if not first:
+            low, high = pl.ds(WIDTH, WIDTH), pl.ds(count_x, WIDTH)
+
+            @pl.when(place.even)
+            def _():
+                padded[high, columns] = near_ref[...]
+                padded[low, columns] = far_ref[...]
+
+            @pl.when(jnp.logical_not(place.even))
+            def _():
+                padded[low, columns] = near_ref[...]
+                padded[high, columns] = far_ref[...]
+
+            padded[rows, pl.ds(pl.multiple_of(block + SIDE, SIDE), SIDE)] = side_ref[...]
+
+        if first:
+            for copy in copies[:4]:
+                copy.wait()
+            points_ref[...] = jnp.full(points_ref.shape, -1, jnp.int32)
+            waves_ref[...] = jnp.zeros(waves_ref.shape, F32)
+
+            def choose(cells_ref, wave_ref):
+                count = cells_ref.shape[1]
+                points_ref[pl.ds(0, 3), pl.ds(0, count)] = cells_ref[...]
+                waves_ref[pl.ds(0, STEPS), pl.ds(0, count)] = wave_ref[...]
+
+            @pl.when(place.field == 0)
+            def _():
+                choose(raw_refs[0], raw_refs[1])
+
+            @pl.when(place.field != 0)
+            def _():
+                choose(raw_refs[2], raw_refs[3])
+
         px = points_ref[0:1, :] - place.slab * count_x
         py = points_ref[1:2, :] - place.y * count_y
         inside = (px >= 0) & (px < count_x) & (py >= 0) & (py < count_y)
@@ -208,24 +243,6 @@
         for offset, weight in enumerate(BAND, 1):
             band = jnp.where(gap == offset, weight, band)
         band = band.astype(BF16)
-
-        if first:
-            copies[0].wait()
-        else:
-            padded[rows, columns] = current_ref[...]
-            low, high = pl.ds(WIDTH, WIDTH), pl.ds(count_x, WIDTH)
-
-            @pl.when(place.even)
-            def _():
-                padded[high, columns] = near_ref[...]
-                padded[low, columns] = far_ref[...]
-
-            @pl.when(jnp.logical_not(place.even))
-            def _():
-                padded[low, columns] = near_ref[...]
-                padded[high, columns] = far_ref[...]
-
-            padded[rows, pl.ds(pl.multiple_of(block + SIDE, SIDE), SIDE)] = side_ref[...]
 
         chunk = 8
 
@@ -249,8 +266,8 @@
 
         lax.fori_loop(0, count_x // chunk, multiply, 0)
         if first:
-            copies[1].wait()
-            copies[2].wait()
+            for copy in copies[4:]:
+                copy.wait()
 
         def row(x, _):
             middle = padded[x + WIDTH, columns]
@@ -262,7 +279,7 @@
                     + padded[x + WIDTH, pl.ds(SIDE - offset, count_y)]
                 )
                 total = total + weight * paired
-            if not last:
+            if not first and not last:
                 whole_ref[x] = middle
             next_ref[x] = (2.0 * middle - before_ref[x] + kept_ref[x] * total) + addpart[x]
             return 0
@@ -306,8 +323,8 @@
     even = shape(count_b, count_a, count_z)
     outs = [full, slab, side]
     if first:
-        outs += [full, slab, side]
-    if not last:
+        outs += [full, slab, side, shape(8, count_j, dtype=jnp.int32), shape(8, count_j)]
+    elif not last:
         outs.append(full)
     if snapshot:
         size = GROUP * count_z
@@ -321,7 +338,8 @@
     if last:
         outs.append(even)
     place_of = spec(pltpu.HBM) if first else spec(pltpu.VMEM)
-    operands, specs = [points, waves, current], [spec(pltpu.VMEM)] * 2 + [place_of]
+    operands = [*points, current] if first else [points, waves, current]
+    specs = [place_of] * (len(operands) - 1) + [spec(pltpu.VMEM)]
     if not first:
         operands += list(faces)
         specs += [spec(pltpu.VMEM)] * 3
@@ -333,7 +351,9 @@
         pltpu.VMEM(full.shape, F32),
     ]
     if first:
-        scratch += [pltpu.VMEM(full.shape, F32), pltpu.SemaphoreType.DMA((3,))]
+        scratch.append(pltpu.VMEM(full.shape, F32))
+        scratch += [pltpu.VMEM(array.shape, array.dtype) for array in points]
+        scratch.append(pltpu.SemaphoreType.DMA((6,)))
     if snapshot:
         operands += [snapshots, matrices]
         specs += [spec(pltpu.HBM)] * 2
@@ -689,7 +709,6 @@
     turn = loop_size // 4
     assert lax.axis_size("gy") == 2 and half_size % 2 == 0
 
-    field = ((lax.axis_index("gx") - turn + loop_size) % loop_size) // half_size
     slabs = [(i - turn) % loop_size % half_size for i in range(loop_size)]
 
     def pairs(odd):
@@ -714,29 +733,20 @@
         far, near, side = faces
         return (send_far(far), *send_near(near, side))
 
-    most = -(-max(source_cells.shape[1], receiver_cells.shape[1]) // 128) * 128
-
-    def chosen(source, receiver, empty):
-        source, receiver = (
-            jnp.pad(array, ((0, 0), (0, most - array.shape[1])), constant_values=empty)
-            for array in (source, receiver)
-        )
-        return jnp.where(field == 0, source, receiver)
-
-    points = chosen(source_cells, receiver_cells, -1)
-    waves = chosen(source_wave, receiver_wave, 0.0)
     matrices = jnp.asarray(
         np.stack([pack_matrix(window, count_z) for window in (0, 1)]), dtype=BF16
     )
-    field_now, field_prev, courant_squared, matrices = (
+    raw = (source_cells, source_wave, receiver_cells, receiver_wave)
+    field_now, field_prev, courant_squared, matrices, snapshot_steps, lag_offsets, *raw = (
         pltpu.with_memory_space_constraint(array, pltpu.HBM)
-        for array in (field_now, field_prev, courant_squared, matrices)
+        for array in (
+            field_now, field_prev, courant_squared, matrices, snapshot_steps, lag_offsets, *raw
+        )
     )
-    far = send_far(first_far(field_now))
-    faces = first_near(field_now)
-    halos = (far, *send_near(*faces))
-    next1, qx, qy, courant, cx, cy, whole0 = inner_step(
-        0, points, waves, field_now, None, field_prev, courant_squared
+    *faces, whole0 = first_faces(field_now)
+    halos = exchange(faces)
+    next1, qx, qy, courant, cx, cy, points, waves = inner_step(
+        0, raw, None, whole0, None, field_prev, courant_squared
     )
     faces = halo_step((qx, qy, cx, cy), halos)
     halos = exchange(faces)
@@ -746,9 +756,9 @@
     next3, qx, qy, whole2, own_early, sent_early, own_matrix, sent_matrix, flag = inner_step(
         2, points, waves, next2, faces, whole1, courant, snapshot_steps, matrices
     )
+    other_early = lax.ppermute(sent_early, "gx", across)
     faces = halo_step((qx, qy, cx, cy), halos)
     halos = exchange(faces)
-    other_early = lax.ppermute(sent_early, "gx", across)
     next4, qx, qy, even3 = inner_step(3, points, waves, next3, faces, whole2, courant)
     final, late, sent_late = last_step(
         flag, even3, next4, (qx, qy, cx, cy), halos, sent_matrix

time: 58.7 us -> 58 us (0.988)
  waiting for transfers between devices: 13.1 us -> 16.2 us
  local copies, waits for them, and re-layouts: 2.6 us -> 0 us
  starting transfers between devices: 22.1 us -> 21.4 us
    unnamed x12 -> x0, local copies, waits for them, and re-layouts: 2.6 us -> none
    ppermute x4, starting transfers between devices: 2.79 us -> 0.28 us  [send_near(): near = lax.ppermute(near, 'gx', near_pairs)]
    ppermute x4, waiting for transfers between devices: 2.97 us -> 5 us  [send_near(): near = lax.ppermute(near, 'gx', near_pairs)]
    ppermute x4, starting transfers between devices: 18.4 us -> 20.2 us  [send_far(): return lax.ppermute(far, 'gx', far_pairs)]
    ppermute x4, waiting for transfers between devices: 7.43 us -> 8.04 us  [send_far(): return lax.ppermute(far, 'gx', far_pairs)]
    pallas_call x2 -> x1, Pallas kernels: 1.92 us -> 1.36 us  [first_faces(): pl.pallas_call(kernel, out_shape=(*face_shapes(count_x, count_y, count_z)...]
  transfers between devices with their start and end apart: 14 -> 14, of which waited for: 6 -> 7; matrix products, arithmetic and copies ran while one was open for 0% -> 0% of each run, Pallas kernels for 28% -> 27%
where the time goes in v3:
time: 58 us; the launch traced here: 57.7 us
  starting transfers between devices  21.4 us (37%)
  Pallas kernels  19.2 us (33%)
  waiting for transfers between devices  16.2 us (28%)
  between operations  0.84 us (1%)
    ppermute x4, starting transfers between devices, send_far(): return lax.ppermute(far, 'gx', far_pairs)  20.2 us
    pallas_call x4, Pallas kernels, inner_step(): pl.pallas_call(kernel, out_shape=tuple(outs), in_specs=specs, out_specs=(...  12.4 us
    ppermute x4, waiting for transfers between devices, send_far(): return lax.ppermute(far, 'gx', far_pairs)  8.04 us
    ppermute x4, waiting for transfers between devices, send_near(): near = lax.ppermute(near, 'gx', near_pairs)  5 us
    ppermute x1, waiting for transfers between devices, body(): other_late = lax.ppermute(sent_late, 'gx', across)  3.17 us
    pallas_call x2, Pallas kernels, lag_image(): pl.pallas_call(kernel, out_shape=shape(*out), in_specs=[spec(pltpu.HBM)]...  3.03 us
    pallas_call x1, Pallas kernels, first_faces(): pl.pallas_call(kernel, out_shape=(*face_shapes(count_x, count_y, count_z)...  1.36 us
  transfers between devices with their start and end apart: 14, of which 7 were waited for; matrix products, arithmetic and copies ran while one was open for 0% of the time, Pallas kernels for 27%

profile of v3, /device:TPU:0, one launch (start us, length us, event | category | flops | bytes accessed | tf_op | source)
XLA Modules:
  0.0 57.7 jit_solution(3857797501489330021)
XLA Ops:
  0.6 1.4 %first_faces.1 = (f32[4,48,128]{2,1,0:T(8,128)S(1)}, f32[4,48,128]{2,1,0:T(8,128)S(1)}, f32[32,8,128]{2,1,0:T(8,128)S(1)}, f32[32,48,128]{2,1,0:T(8,128)S(1)}) custom-call(f32[32,48,128]{2,1,0:T(8,128)} %field_ref.1), custom_call_target="tpu_custom_call" | custom-call | tf_op jit(solution)/shard_map/first_faces/pallas_call | solution.py:94
  2.0 0.6 collective-permute-start.2
  2.6 7.5 %collective-permute-start = (f32[4,48,128]{2,1,0:T(8,128)S(1)}, f32[4,48,128]{2,1,0:T(8,128)S(1)}, u32[]{:S(2)}, u32[]{:S(2)}) collective-permute-start(f32[4,48,128]{2,1,0:T(8,128)S(1)} %get-tuple-element.51), channel_id=1, source_target_pairs={{6,8},{8,6},{14,0},{0,14},{7,9},{9,7},{15,1},{1,15},{22,24},{24,22... | collective-permute-start | bytes 294920 | tf_op jit(solution)/shard_map/ppermute | solution.py:726
  10.0 0.1 collective-permute-start.1
  10.1 3.4 %shard_map.113 = (f32[32,48,128]{2,1,0:T(8,128)S(1)}, f32[8,48,128]{2,1,0:T(8,128)S(1)}, f32[32,8,128]{2,1,0:T(8,128)S(1)}, f32[32,48,128]{2,1,0:T(8,128)S(1)}, ...) custom-call(s32[3,8]{1,0:T(4,128)} %refs_0_.3, ...), custom_call_target="tpu_custom_call" | custom-call | flops 11796480 | bytes 4718592 | tf_op jit(solution)/shard_map/pallas_call | solution.py:365
  13.5 2.0 %collective-permute-done.1.refs_5_ = f32[4,48,128]{2,1,0:T(8,128)S(1)} collective-permute-done((f32[4,48,128]{2,1,0:T(8,128)S(1)}, f32[4,48,128]{2,1,0:T(8,128)S(1)}, u32[]{:S(2)}, u32[]{:S(2)}) %collective-permute-start.1) | collective-permute-done | bytes 98336 | tf_op jit(solution)/shard_map/ppermute | solution.py:729
  15.6 0.1 halo_step.3
  15.7 0.1 collective-permute-start.5
  15.8 4.2 %collective-permute-start.3 = (f32[4,48,128]{2,1,0:T(8,128)S(1)}, f32[4,48,128]{2,1,0:T(8,128)S(1)}, u32[]{:S(2)}, u32[]{:S(2)}) collective-permute-start(f32[4,48,128]{2,1,0:T(8,128)S(1)} %get-tuple-element.54.refs_3_), channel_id=1, source_target_pairs={{6,8},{8,6},{14,0},{0,14},{7,9},{9,7},{15,1},{1,15},{22,24},{24,22... | collective-permute-start | bytes 294920 | tf_op jit(solution)/shard_map/ppermute | solution.py:726
  20.0 0.1 collective-permute-start.4
  20.1 2.6 %shard_map.114 = (f32[32,48,128]{2,1,0:T(8,128)S(1)}, f32[8,48,128]{2,1,0:T(8,128)S(1)}, f32[32,8,128]{2,1,0:T(8,128)S(1)}, f32[32,48,128]{2,1,0:T(8,128)S(1)}) custom-call(s32[8,256]{1,0:T(8,128)S(1)} %get-tuple-element.44.refs_0_, f32[8,256]{1,0:T(8,128)S(1)} %get-tuple-element.45.refs_1_, f32[32,48,128]{2,1,0:T(8,128)S(1)} %get-tuple-element.46.refs_2_, ...), custom_call_target="tpu_custom_call" | custom-call | flops 11796480 | bytes 4718592 | tf_op jit(solution)/shard_map/pallas_call | solution.py:365
  22.7 2.9 %collective-permute-done.3.refs_4_ = f32[4,48,128]{2,1,0:T(8,128)S(1)} collective-permute-done((f32[4,48,128]{2,1,0:T(8,128)S(1)}, f32[4,48,128]{2,1,0:T(8,128)S(1)}, u32[]{:S(2)}, u32[]{:S(2)}) %collective-permute-start.3) | collective-permute-done | bytes 98336 | tf_op jit(solution)/shard_map/ppermute | solution.py:726
  25.7 1.4 %collective-permute-done.4.refs_5_ = f32[4,48,128]{2,1,0:T(8,128)S(1)} collective-permute-done((f32[4,48,128]{2,1,0:T(8,128)S(1)}, f32[4,48,128]{2,1,0:T(8,128)S(1)}, u32[]{:S(2)}, u32[]{:S(2)}) %collective-permute-start.4) | collective-permute-done | bytes 98336 | tf_op jit(solution)/shard_map/ppermute | solution.py:729
  27.1 0.1 halo_step.4
  27.3 0.1 collective-permute-start.8
  27.4 4.3 %collective-permute-start.6 = (f32[4,48,128]{2,1,0:T(8,128)S(1)}, f32[4,48,128]{2,1,0:T(8,128)S(1)}, u32[]{:S(2)}, u32[]{:S(2)}) collective-permute-start(f32[4,48,128]{2,1,0:T(8,128)S(1)} %get-tuple-element.61.refs_3_), channel_id=1, source_target_pairs={{6,8},{8,6},{14,0},{0,14},{7,9},{9,7},{15,1},{1,15},{22,24},{24,22... | collective-permute-start | bytes 294920 | tf_op jit(solution)/shard_map/ppermute | solution.py:726
  31.7 0.1 collective-permute-start.7
  31.8 3.5 %shard_map.115 = (f32[32,48,128]{2,1,0:T(8,128)S(1)}, f32[8,48,128]{2,1,0:T(8,128)S(1)}, f32[32,8,128]{2,1,0:T(8,128)S(1)}, f32[32,48,128]{2,1,0:T(8,128)S(1)}, ...) custom-call(s32[8,256]{1,0:T(8,128)S(1)} %get-tuple-element.44.refs_, ...), custom_call_target="tpu_custom_call" | custom-call | flops 11796480 | bytes 4718592 | tf_op jit(solution)/shard_map/pallas_call | solution.py:365
  35.3 2.0 %collective-permute-done.6.refs_4_ = f32[4,48,128]{2,1,0:T(8,128)S(1)} collective-permute-done((f32[4,48,128]{2,1,0:T(8,128)S(1)}, f32[4,48,128]{2,1,0:T(8,128)S(1)}, u32[]{:S(2)}, u32[]{:S(2)}) %collective-permute-start.6) | collective-permute-done | bytes 98336 | tf_op jit(solution)/shard_map/ppermute | solution.py:726
  37.2 1.5 %collective-permute-done.7.refs_5_ = f32[4,48,128]{2,1,0:T(8,128)S(1)} collective-permute-done((f32[4,48,128]{2,1,0:T(8,128)S(1)}, f32[4,48,128]{2,1,0:T(8,128)S(1)}, u32[]{:S(2)}, u32[]{:S(2)}) %collective-permute-start.7) | collective-permute-done | bytes 98336 | tf_op jit(solution)/shard_map/ppermute | solution.py:729
  38.8 0.1 halo_step.5
  38.9 0.1 collective-permute-start.11
  39.1 4.2 %collective-permute-start.9 = (f32[4,48,128]{2,1,0:T(8,128)S(1)}, f32[4,48,128]{2,1,0:T(8,128)S(1)}, u32[]{:S(2)}, u32[]{:S(2)}) collective-permute-start(f32[4,48,128]{2,1,0:T(8,128)S(1)} %get-tuple-element.69.refs_3_), channel_id=1, source_target_pairs={{6,8},{8,6},{14,0},{0,14},{7,9},{9,7},{15,1},{1,15},{22,24},{24,22... | collective-permute-start | bytes 294920 | tf_op jit(solution)/shard_map/ppermute | solution.py:726
  43.3 0.1 collective-permute-start.13
  43.4 2.9 %shard_map.116 = (f32[32,48,128]{2,1,0:T(8,128)S(1)}, f32[8,48,128]{2,1,0:T(8,128)S(1)}, f32[32,8,128]{2,1,0:T(8,128)S(1)}, f32[24,16,128]{2,1,0:T(8,128)S(1)}) custom-call(s32[8,256]{1,0:T(8,128)S(1)} %get-tuple-element.44.refs_0_, f32[8,256]{1,0:T(8,128)S(1)} %get-tuple-element.45.refs_1_, f32[32,48,128]{2,1,0:T(8,128)S(1)} %get-tuple-element.66.refs_2_, ...), custom_call_target="tpu_custom_call" | custom-call | flops 11796480 | bytes 4718592 | tf_op jit(solution)/shard_map/pallas_call | solution.py:365
  46.3 3.1 %collective-permute-done.9.far_ref = f32[4,48,128]{2,1,0:T(8,128)S(1)} collective-permute-done((f32[4,48,128]{2,1,0:T(8,128)S(1)}, f32[4,48,128]{2,1,0:T(8,128)S(1)}, u32[]{:S(2)}, u32[]{:S(2)}) %collective-permute-start.9) | collective-permute-done | bytes 98336 | tf_op jit(solution)/shard_map/ppermute | solution.py:726
  49.4 0.7 %last_step.1 = (f32[32,48,128]{2,1,0:T(8,128)S(1)}, f32[24,16,128]{2,1,0:T(8,128)S(1)}, f32[224,128]{1,0:T(8,128)S(1)}) custom-call(f32[8,128]{1,0:T(8,128)S(1)} %get-tuple-element.65.flag_ref, f32[24,16,128]{2,1,0:T(8,128)S(1)} %get-tuple-element.73.even_ref, f32[32,48,128]{2,1,0:T(8,128)S(1)} %get-tuple-element.74.current_ref, ...), custom_call_target="tpu_custom_call", output_to_operand_aliasing={{0}: (2, {})} | custom-call | flops 1966080 | bytes 2359296 | tf_op jit(solution)/shard_map/last_step/pallas_call | solution.py:576
  50.2 1.2 %lag_image.2.refs_3_ = f32[17,16,768]{2,1,0:T(8,128)S(1)} custom-call(s32[17]{0:T(128)} %refs_0_.5, f32[4,96,128]{2,1,0:T(8,128)S(1)} %get-tuple-element.82.refs_1_, f32[224,128]{1,0:T(8,128)S(1)} %collective-permute-done.13.refs_2_), custom_call_target="tpu_custom_call" | custom-call | flops 2088960 | bytes 1671168 | tf_op jit(solution)/shard_map/lag_image/pallas_call | solution.py:678
  51.4 0.9 %write_out.1 = f32[32,48,128]{2,1,0:T(8,128)} custom-call(f32[32,48,128]{2,1,0:T(8,128)S(1)} %get-tuple-element.78.level_ref), custom_call_target="tpu_custom_call" | custom-call | bytes 1572864 | tf_op jit(solution)/shard_map/write_out/pallas_call | solution.py:603
  52.3 0.4 pack_own.1.refs_1_
  52.7 3.2 %collective-permute-done.12.refs_2_ = f32[224,128]{1,0:T(8,128)S(1)} collective-permute-done((f32[224,128]{1,0:T(8,128)S(1)}, f32[224,128]{1,0:T(8,128)S(1)}, u32[]{:S(2)}, u32[]{:S(2)}) %collective-permute-start.12) | collective-permute-done | bytes 114720 | tf_op jit(solution)/shard_map/ppermute | solution.py:766
  55.9 1.8 %lag_image.3 = f32[17,16,768]{2,1,0:T(8,128)} custom-call(s32[17]{0:T(128)} %refs_0_.5, f32[4,96,128]{2,1,0:T(8,128)S(1)} %pack_own.1.refs_1_, f32[224,128]{1,0:T(8,128)S(1)} %collective-permute-done.12.refs_2_, f32[17,16,768]{2,1,0:T(8,128)S(1)} %lag_image.2.refs_3_), custom_call_target="tpu_custom_call" | custom-call | flops 2088960 | bytes 1671168 | tf_op jit(solution)/shard_map/lag_image/pallas_call | solution.py:678
  (9 shorter events, 0.2 us)
Async XLA Ops:
  2.0 13.6 %collective-permute-start.2 = (f32[32,8,128]{2,1,0:T(8,128)S(1)}, f32[32,8,128]{2,1,0:T(8,128)S(1)}, u32[]{:S(2)}, u32[]{:S(2)}) collective-permute-start(f32[32,8,128]{2,1,0:T(8,128)S(1)} %get-tuple-element.53), channel_id=1, source_target_pairs={{0,1},{1,0},{2,3},{3,2},{4,5},{5,4},{6,7},{7,6},{8,9},{9,8},{10,11... | collective-permute-start | bytes 393224 | tf_op jit(solution)/shard_map/ppermute | solution.py:730
  2.6 11.0 %collective-permute-start = (f32[4,48,128]{2,1,0:T(8,128)S(1)}, f32[4,48,128]{2,1,0:T(8,128)S(1)}, u32[]{:S(2)}, u32[]{:S(2)}) collective-permute-start(f32[4,48,128]{2,1,0:T(8,128)S(1)} %get-tuple-element.51), channel_id=1, source_target_pairs={{6,8},{8,6},{14,0},{0,14},{7,9},{9,7},{15,1},{1,15},{22,24},{24,22... | collective-permute-start | bytes 294920 | tf_op jit(solution)/shard_map/ppermute | solution.py:726
  10.0 5.5 %collective-permute-start.1 = (f32[4,48,128]{2,1,0:T(8,128)S(1)}, f32[4,48,128]{2,1,0:T(8,128)S(1)}, u32[]{:S(2)}, u32[]{:S(2)}) collective-permute-start(f32[4,48,128]{2,1,0:T(8,128)S(1)} %get-tuple-element.52), channel_id=1, source_target_pairs={{0,2},{2,0},{4,6},{6,4},{8,10},{10,8},{12,14},{14,12},{1,3},{3,1},... | collective-permute-start | bytes 294920 | tf_op jit(solution)/shard_map/ppermute | solution.py:729
  15.7 11.4 %collective-permute-start.5 = (f32[32,8,128]{2,1,0:T(8,128)S(1)}, f32[32,8,128]{2,1,0:T(8,128)S(1)}, u32[]{:S(2)}, u32[]{:S(2)}) collective-permute-start(f32[32,8,128]{2,1,0:T(8,128)S(1)} %get-tuple-element.56.refs_5_), channel_id=1, source_target_pairs={{0,1},{1,0},{2,3},{3,2},{4,5},{5,4},{6,7},{7,6},{8,9},{9,8},{10,11... | collective-permute-start | bytes 393224 | tf_op jit(solution)/shard_map/ppermute | solution.py:730
  15.8 9.9 %collective-permute-start.3 = (f32[4,48,128]{2,1,0:T(8,128)S(1)}, f32[4,48,128]{2,1,0:T(8,128)S(1)}, u32[]{:S(2)}, u32[]{:S(2)}) collective-permute-start(f32[4,48,128]{2,1,0:T(8,128)S(1)} %get-tuple-element.54.refs_3_), channel_id=1, source_target_pairs={{6,8},{8,6},{14,0},{0,14},{7,9},{9,7},{15,1},{1,15},{22,24},{24,22... | collective-permute-start | bytes 294920 | tf_op jit(solution)/shard_map/ppermute | solution.py:726
  20.0 7.1 %collective-permute-start.4 = (f32[4,48,128]{2,1,0:T(8,128)S(1)}, f32[4,48,128]{2,1,0:T(8,128)S(1)}, u32[]{:S(2)}, u32[]{:S(2)}) collective-permute-start(f32[4,48,128]{2,1,0:T(8,128)S(1)} %get-tuple-element.55.refs_4_), channel_id=1, source_target_pairs={{0,2},{2,0},{4,6},{6,4},{8,10},{10,8},{12,14},{14,12},{1,3},{3,1},... | collective-permute-start | bytes 294920 | tf_op jit(solution)/shard_map/ppermute | solution.py:729
  27.3 11.5 %collective-permute-start.8 = (f32[32,8,128]{2,1,0:T(8,128)S(1)}, f32[32,8,128]{2,1,0:T(8,128)S(1)}, u32[]{:S(2)}, u32[]{:S(2)}) collective-permute-start(f32[32,8,128]{2,1,0:T(8,128)S(1)} %get-tuple-element.63.refs_5_), channel_id=1, source_target_pairs={{0,1},{1,0},{2,3},{3,2},{4,5},{5,4},{6,7},{7,6},{8,9},{9,8},{10,11... | collective-permute-start | bytes 393224 | tf_op jit(solution)/shard_map/ppermute | solution.py:730
  27.4 9.9 %collective-permute-start.6 = (f32[4,48,128]{2,1,0:T(8,128)S(1)}, f32[4,48,128]{2,1,0:T(8,128)S(1)}, u32[]{:S(2)}, u32[]{:S(2)}) collective-permute-start(f32[4,48,128]{2,1,0:T(8,128)S(1)} %get-tuple-element.61.refs_3_), channel_id=1, source_target_pairs={{6,8},{8,6},{14,0},{0,14},{7,9},{9,7},{15,1},{1,15},{22,24},{24,22... | collective-permute-start | bytes 294920 | tf_op jit(solution)/shard_map/ppermute | solution.py:726
  31.7 7.1 %collective-permute-start.7 = (f32[4,48,128]{2,1,0:T(8,128)S(1)}, f32[4,48,128]{2,1,0:T(8,128)S(1)}, u32[]{:S(2)}, u32[]{:S(2)}) collective-permute-start(f32[4,48,128]{2,1,0:T(8,128)S(1)} %get-tuple-element.62.refs_4_), channel_id=1, source_target_pairs={{0,2},{2,0},{4,6},{6,4},{8,10},{10,8},{12,14},{14,12},{1,3},{3,1},... | collective-permute-start | bytes 294920 | tf_op jit(solution)/shard_map/ppermute | solution.py:729
  38.9 10.5 %collective-permute-start.11 = (f32[32,8,128]{2,1,0:T(8,128)S(1)}, f32[32,8,128]{2,1,0:T(8,128)S(1)}, u32[]{:S(2)}, u32[]{:S(2)}) collective-permute-start(f32[32,8,128]{2,1,0:T(8,128)S(1)} %get-tuple-element.71.refs_5_), channel_id=1, source_target_pairs={{0,1},{1,0},{2,3},{3,2},{4,5},{5,4},{6,7},{7,6},{8,9},{9,8},{10,11... | collective-permute-start | bytes 393224 | tf_op jit(solution)/shard_map/ppermute | solution.py:730
  39.0 7.3 %collective-permute-start.10 = (f32[4,48,128]{2,1,0:T(8,128)S(1)}, f32[4,48,128]{2,1,0:T(8,128)S(1)}, u32[]{:S(2)}, u32[]{:S(2)}) collective-permute-start(f32[4,48,128]{2,1,0:T(8,128)S(1)} %get-tuple-element.70.refs_4_), channel_id=1, source_target_pairs={{0,2},{2,0},{4,6},{6,4},{8,10},{10,8},{12,14},{14,12},{1,3},{3,1},... | collective-permute-start | bytes 294920 | tf_op jit(solution)/shard_map/ppermute | solution.py:729
  39.1 10.4 %collective-permute-start.9 = (f32[4,48,128]{2,1,0:T(8,128)S(1)}, f32[4,48,128]{2,1,0:T(8,128)S(1)}, u32[]{:S(2)}, u32[]{:S(2)}) collective-permute-start(f32[4,48,128]{2,1,0:T(8,128)S(1)} %get-tuple-element.69.refs_3_), channel_id=1, source_target_pairs={{6,8},{8,6},{14,0},{0,14},{7,9},{9,7},{15,1},{1,15},{22,24},{24,22... | collective-permute-start | bytes 294920 | tf_op jit(solution)/shard_map/ppermute | solution.py:726
  43.3 6.9 %collective-permute-start.13 = (f32[224,128]{1,0:T(8,128)S(1)}, f32[224,128]{1,0:T(8,128)S(1)}, u32[]{:S(2)}, u32[]{:S(2)}) collective-permute-start(f32[224,128]{1,0:T(8,128)S(1)} %get-tuple-element.83), channel_id=1, source_target_pairs={{0,8},{2,10},{4,12},{6,14},{8,0},{10,2},{12,4},{14,6},{1,9},{3,11}... | collective-permute-start | bytes 344072 | tf_op jit(solution)/shard_map/ppermute | solution.py:759
  50.1 5.8 %collective-permute-start.12 = (f32[224,128]{1,0:T(8,128)S(1)}, f32[224,128]{1,0:T(8,128)S(1)}, u32[]{:S(2)}, u32[]{:S(2)}) collective-permute-start(f32[224,128]{1,0:T(8,128)S(1)} %get-tuple-element.81), channel_id=1, source_target_pairs={{0,8},{2,10},{4,12},{6,14},{8,0},{10,2},{12,4},{14,6},{1,9},{3,11}... | collective-permute-start | bytes 344072 | tf_op jit(solution)/shard_map/ppermute | solution.py:766

commit v4 on v3

--- a/solution.py
+++ b/solution.py
@@ -71,20 +71,17 @@
     count_x, count_y, count_z = field.shape
     top = count_x - WIDTH
 
-    def kernel(field_ref, far_ref, near_ref, side_ref, whole_ref, sems):
+    def kernel(field_ref, far_ref, near_ref, side_ref, sems):
         place = Place()
         far = jnp.where(place.even, 0, top)
         sources = [
             field_ref.at[pl.ds(far, WIDTH)],
             field_ref.at[pl.ds(top - far, WIDTH)],
             field_ref.at[:, pl.ds(place.block(count_y), SIDE)],
-            field_ref,
         ]
         copies = [
             pltpu.make_async_copy(source, target, sems.at[index])
-            for index, (source, target) in enumerate(
-                zip(sources, (far_ref, near_ref, side_ref, whole_ref))
-            )
+            for index, (source, target) in enumerate(zip(sources, (far_ref, near_ref, side_ref)))
         ]
         for copy in copies:
             copy.start()
@@ -93,10 +90,10 @@
 
     return pl.pallas_call(
         kernel,
-        out_shape=(*face_shapes(count_x, count_y, count_z), shape(*field.shape)),
+        out_shape=face_shapes(count_x, count_y, count_z),
         in_specs=[spec(pltpu.HBM)],
-        out_specs=(spec(pltpu.VMEM),) * 4,
-        scratch_shapes=[pltpu.SemaphoreType.DMA((4,))],
+        out_specs=(spec(pltpu.VMEM),) * 3,
+        scratch_shapes=[pltpu.SemaphoreType.DMA((3,))],
         compiler_params=params(8),
         name="first_faces",
     )(field)
@@ -141,7 +138,7 @@
         next_ref, qx_ref, qy_ref = take(3)
         if first:
             kept_ref, cx_ref, cy_ref, points_ref, waves_ref = take(5)
-        elif not last:
+        if not last:
             (whole_ref,) = take(1)
         if snapshot:
             own_out, sent_out, own_matrix, sent_matrix, flag_ref = take(5)
@@ -163,8 +160,8 @@
                 pltpu.make_async_copy(source, target, sems.at[index])
                 for index, (source, target) in enumerate(
                     zip(
-                        (*raw_refs_in, previous_ref, courant_ref),
-                        (*raw_refs, before_ref, kept_ref),
+                        (*raw_refs_in, current_ref, previous_ref, courant_ref),
+                        (*raw_refs, padded.at[rows, columns], before_ref, kept_ref),
                     )
                 )
             ]
@@ -188,8 +185,8 @@
         padded[rows, pl.ds(0, SIDE)] = zero_y
         padded[rows, pl.ds(count_y + SIDE, SIDE)] = zero_y
 
-        padded[rows, columns] = current_ref[...]
         if not first:
+            padded[rows, columns] = current_ref[...]
             low, high = pl.ds(WIDTH, WIDTH), pl.ds(count_x, WIDTH)
 
             @pl.when(place.even)
@@ -244,6 +241,8 @@
             band = jnp.where(gap == offset, weight, band)
         band = band.astype(BF16)
 
+        if first:
+            copies[4].wait()
         chunk = 8
 
         def multiply(index, _):
@@ -266,7 +265,7 @@
 
         lax.fori_loop(0, count_x // chunk, multiply, 0)
         if first:
-            for copy in copies[4:]:
+            for copy in copies[5:]:
                 copy.wait()
 
         def row(x, _):
@@ -279,7 +278,7 @@
                     + padded[x + WIDTH, pl.ds(SIDE - offset, count_y)]
                 )
                 total = total + weight * paired
-            if not first and not last:
+            if not last:
                 whole_ref[x] = middle
             next_ref[x] = (2.0 * middle - before_ref[x] + kept_ref[x] * total) + addpart[x]
             return 0
@@ -324,7 +323,7 @@
     outs = [full, slab, side]
     if first:
         outs += [full, slab, side, shape(8, count_j, dtype=jnp.int32), shape(8, count_j)]
-    elif not last:
+    if not last:
         outs.append(full)
     if snapshot:
         size = GROUP * count_z
@@ -339,7 +338,7 @@
         outs.append(even)
     place_of = spec(pltpu.HBM) if first else spec(pltpu.VMEM)
     operands = [*points, current] if first else [points, waves, current]
-    specs = [place_of] * (len(operands) - 1) + [spec(pltpu.VMEM)]
+    specs = [place_of] * len(operands)
     if not first:
         operands += list(faces)
         specs += [spec(pltpu.VMEM)] * 3
@@ -353,7 +352,7 @@
     if first:
         scratch.append(pltpu.VMEM(full.shape, F32))
         scratch += [pltpu.VMEM(array.shape, array.dtype) for array in points]
-        scratch.append(pltpu.SemaphoreType.DMA((6,)))
+        scratch.append(pltpu.SemaphoreType.DMA((7,)))
     if snapshot:
         operands += [snapshots, matrices]
         specs += [spec(pltpu.HBM)] * 2
@@ -539,40 +538,48 @@
     return shape(2 * groups * count_a + extra, count_z)
 
 
-def last_step(flag, even_before, current, parts, halos, matrix):
+def last_step(which, flag, even_before, current, late, parts, halos, matrix):
     count_x, count_y, count_z = current.shape
     count_a, count_b = count_x // 2, count_y // 2
-
-    def kernel(
-        flag_ref, even_ref, current_ref, qx_ref, qy_ref, cx_ref, cy_ref, far_ref, near_ref,
-        side_ref, matrix_ref, final_ref, late_ref, sent_ref, far_out, near_out, side_out,
-    ):
+    keep = late is not None
+
+    def kernel(*refs):
+        refs = list(refs)
+        take = lambda count: [refs.pop(0) for _ in range(count)]
+        flag_ref, even_ref, _ = take(3)
+        if keep:
+            take(1)
+        parts_in, halos_in = take(4), take(3)
+        matrix_ref, final_ref, late_ref, sent_ref = take(4)
+        faces = take(3)
         place = Place()
-        add_halo(
-            place, (qx_ref, qy_ref, cx_ref, cy_ref), (far_ref, near_ref, side_ref),
-            (far_out, near_out, side_out),
-        )
-        low, high = pl.ds(0, WIDTH), pl.ds(count_x - WIDTH, WIDTH)
-
-        @pl.when(place.even)
+
+        @pl.when(place.field == which)
         def _():
-            final_ref[high] = near_out[...]
-            final_ref[low] = far_out[...]
-
-        @pl.when(jnp.logical_not(place.even))
-        def _():
-            final_ref[low] = near_out[...]
-            final_ref[high] = far_out[...]
-
-        final_ref[:, pl.ds(place.block(count_y), SIDE)] = side_out[...]
-        wants_last = jnp.broadcast_to(flag_ref[0:1, :], (count_a, count_z)) > 0.5
-        for b in range(count_b):
-            late_ref[b] = jnp.where(
-                wants_last, even_rows(final_ref, 0, 0, count_a, b), even_ref[b]
-            )
-        send_into(late_ref, matrix_ref, sent_ref)
+            add_halo(place, parts_in, halos_in, faces)
+            far_out, near_out, side_out = faces
+            low, high = pl.ds(0, WIDTH), pl.ds(count_x - WIDTH, WIDTH)
+
+            @pl.when(place.even)
+            def _():
+                final_ref[high] = near_out[...]
+                final_ref[low] = far_out[...]
+
+            @pl.when(jnp.logical_not(place.even))
+            def _():
+                final_ref[low] = near_out[...]
+                final_ref[high] = far_out[...]
+
+            final_ref[:, pl.ds(place.block(count_y), SIDE)] = side_out[...]
+            wants_last = jnp.broadcast_to(flag_ref[0:1, :], (count_a, count_z)) > 0.5
+            for b in range(count_b):
+                late_ref[b] = jnp.where(
+                    wants_last, even_rows(final_ref, 0, 0, count_a, b), even_ref[b]
+                )
+            send_into(late_ref, matrix_ref, sent_ref)
 
     slab, _, side = face_shapes(count_x, count_y, count_z)
+    operands = [flag, even_before, current, *([late] if keep else []), *parts, *halos, matrix]
     return pl.pallas_call(
         kernel,
         out_shape=(
@@ -580,85 +587,81 @@
             shape(count_b, count_a, count_z),
             sent_shape(count_a, count_b, count_z),
         ),
-        in_specs=[spec(pltpu.VMEM)] * 11,
+        in_specs=[spec(pltpu.VMEM)] * len(operands),
         out_specs=(spec(pltpu.VMEM),) * 3,
         scratch_shapes=[
             pltpu.VMEM(slab.shape, F32),
             pltpu.VMEM(slab.shape, F32),
             pltpu.VMEM(side.shape, F32),
         ],
-        input_output_aliases={2: 0},
+        input_output_aliases={2: 0, 3: 1} if keep else {2: 0},
         compiler_params=params(12),
         cost_estimate=cost(count_x * count_y * count_z, 10, 3),
-        name="last_step",
-    )(flag, even_before, current, *parts, *halos, matrix)
-
-
-def write_out(level):
-    def kernel(level_ref, out_ref, sem):
-        copy = pltpu.make_async_copy(level_ref, out_ref, sem)
-        copy.start()
-        copy.wait()
-
-    return pl.pallas_call(
-        kernel,
-        out_shape=shape(*level.shape),
-        in_specs=[spec(pltpu.VMEM)],
-        out_specs=spec(pltpu.HBM),
-        scratch_shapes=[pltpu.SemaphoreType.DMA],
-        compiler_params=params(4),
-        cost_estimate=cost(level.size, 0, 2),
-        name="write_out",
-    )(level)
-
-
-def lag_image(lags, own, other, before, count_a):
+    )(*operands)
+
+
+def lag_image(count_a, lags, own, others, before=None, level=None):
     _, total_rows, count_z = own.shape
-    groups = total_rows // count_a
-    count_h = lags.shape[0]
+    count_h = lags.shape[1]
     half = count_z // GROUP
     last = before is not None
+    width = total_rows // count_a * count_z
+    groups = total_rows // count_a
 
     def kernel(*refs):
         refs = list(refs)
         take = lambda count: [refs.pop(0) for _ in range(count)]
-        lags_ref, own_ref, other_ref = take(3)
+        lags_ref, own_ref = take(2)
+        other_refs = take(len(others))
         if last:
-            (before_ref,) = take(1)
+            before_ref, level_ref = take(2)
         (out_ref,) = take(1)
-        edges, lag_of, sems = take(3)
         if last:
-            (store,) = take(1)
+            (final_ref,) = take(1)
+        mains, edges = take(2)
+        if last:
+            store, sems = take(2)
         else:
             store = out_ref
         place = Place()
-        copy = pltpu.make_async_copy(lags_ref, lag_of, sems.at[0])
-        copy.start()
+        if last:
+            final = pltpu.make_async_copy(level_ref, final_ref, sems.at[0])
+            final.start()
         is_source = place.field == 0
         lane = lax.broadcasted_iota(jnp.int32, (count_a, count_z), 1) % half
         useful = jnp.where(is_source, lane, half - 1 - lane) < REACH
         slots, _ = edge_slots(count_a, groups, count_z)
-        for parity, g, row, shift in slots:
-            part = other_ref[pl.ds(2 * total_rows + row, count_a), :]
-            part = pltpu.roll(part, count_z - shift, 1) if shift else part
-            edges[parity, pl.ds(g * count_a, count_a), :] = jnp.where(useful, part, 0.0)
-        copy.wait()
+
+        def unpack(other_ref):
+            for parity in range(2):
+                mains[parity] = other_ref[pl.ds(parity * total_rows, total_rows), :]
+            for parity, g, row, shift in slots:
+                part = other_ref[pl.ds(2 * total_rows + row, count_a), :]
+                part = pltpu.roll(part, count_z - shift, 1) if shift else part
+                edges[parity, pl.ds(g * count_a, count_a), :] = jnp.where(useful, part, 0.0)
+
+        if len(other_refs) == 1:
+            unpack(other_refs[0])
+        else:
+            for which, other_ref in enumerate(other_refs):
+                pl.when(place.field == which)(lambda other_ref=other_ref: unpack(other_ref))
+
         lane = lax.broadcasted_iota(jnp.int32, (1, count_z), 1) % half
+        all_lags = lags_ref[...]
 
         def moved(main, edge, shift):
             mask = (lane < shift) | (lane >= half + shift)
             return pltpu.roll(jnp.where(mask, edge, main), (count_z - shift) & (count_z - 1), 1)
 
-        def one(h, _):
-            lag = lag_of[h]
+        for h in range(count_h):
+            lag = all_lags[0, h]
             parity = lag & 1
             source_shift = -((lag + parity) >> 1)
             receiver_shift = (lag - parity) >> 1
             own_shift = jnp.where(is_source, source_shift, receiver_shift)
             other_shift = jnp.where(is_source, receiver_shift, source_shift)
-            other_rows = pl.ds(pl.multiple_of(parity * total_rows, 8), total_rows)
             product = moved(own_ref[parity], own_ref[2 + parity], own_shift)
-            product = product * moved(other_ref[other_rows, :], edges[parity], other_shift)
+            product = product * moved(mains[parity], edges[parity], other_shift)
             for g in range(groups):
                 part = product[g * count_a : (g + 1) * count_a]
                 lanes = pl.ds(g * count_z, count_z)
@@ -667,28 +670,24 @@
                 store[h, :, lanes] = part
             if last:
                 pltpu.make_async_copy(store.at[h], out_ref.at[h], sems.at[1]).start()
-            return 0
-
-        lax.fori_loop(0, count_h, one, 0, unroll=True)
         if last:
             pltpu.make_async_copy(store, out_ref, sems.at[1]).wait()
-
-    out = (count_h, count_a, groups * count_z)
-    operands = [lags, own, other] + ([before] if last else [])
+            final.wait()
+
+    image = shape(count_h, count_a, width)
+    operands = [lags, own, *others] + ([before, level] if last else [])
+    scratch = [pltpu.VMEM((2, total_rows, count_z), F32)] * 2
+    if last:
+        scratch += [pltpu.VMEM(image.shape, F32), pltpu.SemaphoreType.DMA((2,))]
     return pl.pallas_call(
         kernel,
-        out_shape=shape(*out),
-        in_specs=[spec(pltpu.HBM)] + [spec(pltpu.VMEM)] * (len(operands) - 1),
-        out_specs=spec(pltpu.HBM if last else pltpu.VMEM),
-        scratch_shapes=[
-            pltpu.VMEM((2, total_rows, count_z), F32),
-            pltpu.SMEM((count_h,), jnp.int32),
-            pltpu.SemaphoreType.DMA((2,)),
-        ]
-        + ([pltpu.VMEM(out, F32)] if last else []),
+        out_shape=(image, shape(*level.shape)) if last else image,
+        in_specs=[spec(pltpu.VMEM)] * len(operands),
+        out_specs=(spec(pltpu.HBM),) * 2 if last else spec(pltpu.VMEM),
+        scratch_shapes=scratch,
         compiler_params=params(12),
         cost_estimate=cost(count_h * total_rows * count_z, 10, 2),
-        name="lag_image",
+        name="last_image" if last else "early_image",
     )(*operands)
 
 
@@ -721,9 +720,15 @@
 
     near_pairs, far_pairs = pairs(0), pairs(1)
     across = [(i, (i + half_size) % loop_size) for i in range(loop_size)]
-
-    def send_far(far):
-        return lax.ppermute(far, "gx", far_pairs)
+    fields = [(i - turn) % loop_size // half_size for i in range(loop_size)]
+
+    def of(which, found):
+        return [(i, j) for i, j in found if fields[i] == which]
+
+    def send_far(far, which=None):
+        if which is None:
+            return lax.ppermute(far, "gx", far_pairs)
+        return lax.ppermute(far, "gx", of(which, far_pairs))
 
     def send_near(near, side):
         near = lax.ppermute(near, "gx", near_pairs)
@@ -737,16 +742,14 @@
         np.stack([pack_matrix(window, count_z) for window in (0, 1)]), dtype=BF16
     )
     raw = (source_cells, source_wave, receiver_cells, receiver_wave)
-    field_now, field_prev, courant_squared, matrices, snapshot_steps, lag_offsets, *raw = (
+    lags = lag_offsets.reshape(1, -1)
+    field_now, field_prev, courant_squared, matrices, snapshot_steps, *raw = (
         pltpu.with_memory_space_constraint(array, pltpu.HBM)
-        for array in (
-            field_now, field_prev, courant_squared, matrices, snapshot_steps, lag_offsets, *raw
-        )
-    )
-    *faces, whole0 = first_faces(field_now)
-    halos = exchange(faces)
-    next1, qx, qy, courant, cx, cy, points, waves = inner_step(
-        0, raw, None, whole0, None, field_prev, courant_squared
+        for array in (field_now, field_prev, courant_squared, matrices, snapshot_steps, *raw)
+    )
+    halos = exchange(first_faces(field_now))
+    next1, qx, qy, courant, cx, cy, points, waves, whole0 = inner_step(
+        0, raw, None, field_now, None, field_prev, courant_squared
     )
     faces = halo_step((qx, qy, cx, cy), halos)
     halos = exchange(faces)
@@ -758,16 +761,25 @@
     )
     other_early = lax.ppermute(sent_early, "gx", across)
     faces = halo_step((qx, qy, cx, cy), halos)
-    halos = exchange(faces)
+    far, near, side = faces
+    near, side = send_near(near, side)
+    fars = send_far(far, 0), send_far(far, 1)
     next4, qx, qy, even3 = inner_step(3, points, waves, next3, faces, whole2, courant)
-    final, late, sent_late = last_step(
-        flag, even3, next4, (qx, qy, cx, cy), halos, sent_matrix
-    )
-    other_late = lax.ppermute(sent_late, "gx", across)
-    partial = lag_image(lag_offsets, own_early, other_early, None, count_x // 2)
+    parts = (qx, qy, cx, cy)
+    final, late, sent = last_step(
+        0, flag, even3, next4, None, parts, (fars[0], near, side), sent_matrix
+    )
+    from_source = lax.ppermute(sent, "gx", of(0, across))
+    partial = lag_image(count_x // 2, lags, own_early, [other_early])
+    final, late, sent = last_step(
+        1, flag, even3, final, late, parts, (fars[1], near, side), sent_matrix
+    )
+    from_receiver = lax.ppermute(sent, "gx", of(1, across))
     own_late = pack_own(late, own_matrix)
-    image = lag_image(lag_offsets, own_late, other_late, partial, count_x // 2)
-    return write_out(final), jnp.transpose(image, (1, 0, 2))
+    image, final = lag_image(
+        count_x // 2, lags, own_late, [from_receiver, from_source], partial, final
+    )
+    return final, jnp.transpose(image, (1, 0, 2))
 
 
 def solution(mesh):

time: 58 us -> 62.5 us (1.078)
  starting transfers between devices: 21.4 us -> 25.1 us
  local copies, waits for them, and re-layouts: 0 us -> 0.65 us
    ppermute x1 -> x4, starting transfers between devices: 0.07 us -> 7.97 us  [the longest x2 4.91 us: send_far(): return lax.ppermute(far, 'gx', of(which, far_pairs))]
    ppermute x4 -> x3, starting transfers between devices: 20.2 us -> 16 us  [send_far(): return lax.ppermute(far, 'gx', far_pairs)]
    ppermute x1 -> x4, waiting for transfers between devices: 3.17 us -> 6.52 us  [the longest x1 3.44 us: body(): from_source = lax.ppermute(sent, 'gx', of(0, across))]
    ppermute x4 -> x3, waiting for transfers between devices: 8.04 us -> 4.9 us  [send_far(): return lax.ppermute(far, 'gx', far_pairs)]
    unnamed x0 -> x2, local copies, waits for them, and re-layouts: none -> 0.65 us
    pallas_call x4 -> x3, Pallas kernels: 5.28 us -> 5.2 us  [the longest x2 4.15 us: lag_image(): pl.pallas_call(kernel, out_shape=(image, shape(*level.shape)) if last els...]
  transfers between devices with their start and end apart: 14 -> 16, of which waited for: 7 -> 7; matrix products, arithmetic and copies ran while one was open for 0% -> 0% of each run, Pallas kernels for 27% -> 25%
where the time goes in v4:
time: 62.5 us; the launch traced here: 62.2 us
  starting transfers between devices  25.1 us (40%)
  Pallas kernels  19.4 us (31%)
  waiting for transfers between devices  16.1 us (26%)
  between operations  0.89 us (1%)
  local copies, waits for them, and re-layouts  0.65 us (1%)
    ppermute x3, starting transfers between devices, send_far(): return lax.ppermute(far, 'gx', far_pairs)  16 us
    pallas_call x4, Pallas kernels, inner_step(): pl.pallas_call(kernel, out_shape=tuple(outs), in_specs=specs, out_specs=(...  12.7 us
    ppermute x2, starting transfers between devices, send_far(): return lax.ppermute(far, 'gx', of(which, far_pairs))  4.91 us
    ppermute x3, waiting for transfers between devices, send_far(): return lax.ppermute(far, 'gx', far_pairs)  4.9 us
    ppermute x4, waiting for transfers between devices, send_near(): near = lax.ppermute(near, 'gx', near_pairs)  4.69 us
    pallas_call x2, Pallas kernels, lag_image(): pl.pallas_call(kernel, out_shape=(image, shape(*level.shape)) if last els...  4.15 us
    ppermute x1, waiting for transfers between devices, body(): from_source = lax.ppermute(sent, 'gx', of(0, across))  3.44 us
    ppermute x2, waiting for transfers between devices, send_far(): return lax.ppermute(far, 'gx', of(which, far_pairs))  3.08 us
  transfers between devices with their start and end apart: 16, of which 7 were waited for; matrix products, arithmetic and copies ran while one was open for 0% of the time, Pallas kernels for 25%

profile of v4, /device:TPU:0, one launch (start us, length us, event | category | flops | bytes accessed | tf_op | source)
XLA Modules:
  0.0 62.2 jit_solution(8805440416804620049)
XLA Ops:
  0.6 1.0 %first_faces.1 = (f32[4,48,128]{2,1,0:T(8,128)S(1)}, f32[4,48,128]{2,1,0:T(8,128)S(1)}, f32[32,8,128]{2,1,0:T(8,128)S(1)}) custom-call(f32[32,48,128]{2,1,0:T(8,128)} %field_ref.1), custom_call_target="tpu_custom_call" | custom-call | tf_op jit(solution)/shard_map/first_faces/pallas_call | solution.py:91
  1.7 0.6 collective-permute-start.2
  2.2 7.5 %collective-permute-start = (f32[4,48,128]{2,1,0:T(8,128)S(1)}, f32[4,48,128]{2,1,0:T(8,128)S(1)}, u32[]{:S(2)}, u32[]{:S(2)}) collective-permute-start(f32[4,48,128]{2,1,0:T(8,128)S(1)} %get-tuple-element.55), channel_id=1, source_target_pairs={{6,8},{8,6},{14,0},{0,14},{7,9},{9,7},{15,1},{1,15},{22,24},{24,22... | collective-permute-start | bytes 294920 | tf_op jit(solution)/shard_map/ppermute | solution.py:730
  9.7 0.1 collective-permute-start.1
  9.8 3.7 %shard_map.113 = (f32[32,48,128]{2,1,0:T(8,128)S(1)}, f32[8,48,128]{2,1,0:T(8,128)S(1)}, f32[32,8,128]{2,1,0:T(8,128)S(1)}, f32[32,48,128]{2,1,0:T(8,128)S(1)}, ...) custom-call(s32[3,8]{1,0:T(4,128)} %refs_0_.1, ...), custom_call_target="tpu_custom_call" | custom-call | flops 11796480 | bytes 4718592 | tf_op jit(solution)/shard_map/pallas_call | solution.py:364
  13.5 1.7 %collective-permute-done.1.refs_5_ = f32[4,48,128]{2,1,0:T(8,128)S(1)} collective-permute-done((f32[4,48,128]{2,1,0:T(8,128)S(1)}, f32[4,48,128]{2,1,0:T(8,128)S(1)}, u32[]{:S(2)}, u32[]{:S(2)}) %collective-permute-start.1) | collective-permute-done | bytes 98336 | tf_op jit(solution)/shard_map/ppermute | solution.py:734
  15.2 0.1 halo_step.3
  15.4 0.1 collective-permute-start.5
  15.5 4.2 %collective-permute-start.3 = (f32[4,48,128]{2,1,0:T(8,128)S(1)}, f32[4,48,128]{2,1,0:T(8,128)S(1)}, u32[]{:S(2)}, u32[]{:S(2)}) collective-permute-start(f32[4,48,128]{2,1,0:T(8,128)S(1)} %get-tuple-element.58.refs_3_), channel_id=1, source_target_pairs={{6,8},{8,6},{14,0},{0,14},{7,9},{9,7},{15,1},{1,15},{22,24},{24,22... | collective-permute-start | bytes 294920 | tf_op jit(solution)/shard_map/ppermute | solution.py:730
  19.7 0.1 collective-permute-start.4
  19.8 2.6 %shard_map.114 = (f32[32,48,128]{2,1,0:T(8,128)S(1)}, f32[8,48,128]{2,1,0:T(8,128)S(1)}, f32[32,8,128]{2,1,0:T(8,128)S(1)}, f32[32,48,128]{2,1,0:T(8,128)S(1)}) custom-call(s32[8,256]{1,0:T(8,128)S(1)} %get-tuple-element.48.refs_0_, f32[8,256]{1,0:T(8,128)S(1)} %get-tuple-element.49.refs_1_, f32[32,48,128]{2,1,0:T(8,128)S(1)} %get-tuple-element.50.refs_2_, ...), custom_call_target="tpu_custom_call" | custom-call | flops 11796480 | bytes 4718592 | tf_op jit(solution)/shard_map/pallas_call | solution.py:364
  22.4 2.9 %collective-permute-done.3.refs_4_ = f32[4,48,128]{2,1,0:T(8,128)S(1)} collective-permute-done((f32[4,48,128]{2,1,0:T(8,128)S(1)}, f32[4,48,128]{2,1,0:T(8,128)S(1)}, u32[]{:S(2)}, u32[]{:S(2)}) %collective-permute-start.3) | collective-permute-done | bytes 98336 | tf_op jit(solution)/shard_map/ppermute | solution.py:730
  25.4 1.4 %collective-permute-done.4.refs_5_ = f32[4,48,128]{2,1,0:T(8,128)S(1)} collective-permute-done((f32[4,48,128]{2,1,0:T(8,128)S(1)}, f32[4,48,128]{2,1,0:T(8,128)S(1)}, u32[]{:S(2)}, u32[]{:S(2)}) %collective-permute-start.4) | collective-permute-done | bytes 98336 | tf_op jit(solution)/shard_map/ppermute | solution.py:734
  26.8 0.1 halo_step.4
  27.0 0.1 collective-permute-start.8
  27.0 4.3 %collective-permute-start.6 = (f32[4,48,128]{2,1,0:T(8,128)S(1)}, f32[4,48,128]{2,1,0:T(8,128)S(1)}, u32[]{:S(2)}, u32[]{:S(2)}) collective-permute-start(f32[4,48,128]{2,1,0:T(8,128)S(1)} %get-tuple-element.66.refs_3_), channel_id=1, source_target_pairs={{6,8},{8,6},{14,0},{0,14},{7,9},{9,7},{15,1},{1,15},{22,24},{24,22... | collective-permute-start | bytes 294920 | tf_op jit(solution)/shard_map/ppermute | solution.py:730
  31.4 3.5 %shard_map.115 = (f32[32,48,128]{2,1,0:T(8,128)S(1)}, f32[8,48,128]{2,1,0:T(8,128)S(1)}, f32[32,8,128]{2,1,0:T(8,128)S(1)}, f32[32,48,128]{2,1,0:T(8,128)S(1)}, ...) custom-call(s32[8,256]{1,0:T(8,128)S(1)} %get-tuple-element.48.refs_, ...), custom_call_target="tpu_custom_call" | custom-call | flops 11796480 | bytes 4718592 | tf_op jit(solution)/shard_map/pallas_call | solution.py:364
  35.0 2.0 %collective-permute-done.6.refs_4_ = f32[4,48,128]{2,1,0:T(8,128)S(1)} collective-permute-done((f32[4,48,128]{2,1,0:T(8,128)S(1)}, f32[4,48,128]{2,1,0:T(8,128)S(1)}, u32[]{:S(2)}, u32[]{:S(2)}) %collective-permute-start.6) | collective-permute-done | bytes 98336 | tf_op jit(solution)/shard_map/ppermute | solution.py:730
  36.9 1.5 %collective-permute-done.7.refs_5_ = f32[4,48,128]{2,1,0:T(8,128)S(1)} collective-permute-done((f32[4,48,128]{2,1,0:T(8,128)S(1)}, f32[4,48,128]{2,1,0:T(8,128)S(1)}, u32[]{:S(2)}, u32[]{:S(2)}) %collective-permute-start.7) | collective-permute-done | bytes 98336 | tf_op jit(solution)/shard_map/ppermute | solution.py:734
  38.4 0.1 halo_step.5
  38.7 0.7 %collective-permute-start.9 = (f32[4,48,128]{2,1,0:T(8,128)S(1)}, f32[4,48,128]{2,1,0:T(8,128)S(1)}, u32[]{:S(2)}, u32[]{:S(2)}) collective-permute-start(f32[4,48,128]{2,1,0:T(8,128)S(1)} %get-tuple-element.74.refs_3_), channel_id=1, source_target_pairs={{6,8},{8,6},{7,9},{9,7},{22,24},{24,22},{23,25},{25,23}} | collective-permute-start | bytes 294920 | tf_op jit(solution)/shard_map/ppermute | solution.py:731
  39.4 4.2 %collective-permute-start.12 = (f32[4,48,128]{2,1,0:T(8,128)S(1)}, f32[4,48,128]{2,1,0:T(8,128)S(1)}, u32[]{:S(2)}, u32[]{:S(2)}) collective-permute-start(f32[4,48,128]{2,1,0:T(8,128)S(1)} %get-tuple-element.74.refs_3_), channel_id=1, source_target_pairs={{14,0},{0,14},{15,1},{1,15},{30,16},{16,30},{31,17},{17,31}} | collective-permute-start | bytes 294920 | tf_op jit(solution)/shard_map/ppermute | solution.py:731
  43.8 2.9 %shard_map.116 = (f32[32,48,128]{2,1,0:T(8,128)S(1)}, f32[8,48,128]{2,1,0:T(8,128)S(1)}, f32[32,8,128]{2,1,0:T(8,128)S(1)}, f32[24,16,128]{2,1,0:T(8,128)S(1)}) custom-call(s32[8,256]{1,0:T(8,128)S(1)} %get-tuple-element.48.refs_0_, f32[8,256]{1,0:T(8,128)S(1)} %get-tuple-element.49.refs_1_, f32[32,48,128]{2,1,0:T(8,128)S(1)} %get-tuple-element.71.refs_2_, ...), custom_call_target="tpu_custom_call" | custom-call | flops 11796480 | bytes 4718592 | tf_op jit(solution)/shard_map/pallas_call | solution.py:364
  46.7 3.1 %collective-permute-done.12.refs_8_ = f32[4,48,128]{2,1,0:T(8,128)S(1)} collective-permute-done((f32[4,48,128]{2,1,0:T(8,128)S(1)}, f32[4,48,128]{2,1,0:T(8,128)S(1)}, u32[]{:S(2)}, u32[]{:S(2)}) %collective-permute-start.12) | collective-permute-done | bytes 98336 | tf_op jit(solution)/shard_map/ppermute | solution.py:731
  49.8 0.7 %shard_map.118 = (f32[32,48,128]{2,1,0:T(8,128)S(1)}, f32[24,16,128]{2,1,0:T(8,128)S(1)}, f32[224,128]{1,0:T(8,128)S(1)}) custom-call(f32[8,128]{1,0:T(8,128)S(1)} %get-tuple-element.70.refs_0_, f32[24,16,128]{2,1,0:T(8,128)S(1)} %get-tuple-element.78.refs_1_, ...), custom_call_target="tpu_custom_call", output_to_operand_aliasing={{0}: (2, {}), {1}: (3, {})} | custom-call | flops 1966080 | bytes 2359296 | tf_op jit(solution)/shard_map/pallas_call | solution.py:583
  50.5 1.8 %collective-permute-start.13 = (f32[224,128]{1,0:T(8,128)S(1)}, f32[224,128]{1,0:T(8,128)S(1)}, u32[]{:S(2)}, u32[]{:S(2)}) collective-permute-start(f32[224,128]{1,0:T(8,128)S(1)} %get-tuple-element.87), channel_id=1, source_target_pairs={{0,8},{2,10},{12,4},{14,6},{1,9},{3,11},{13,5},{15,7},{16,24},{18,... | collective-permute-start | bytes 344072 | tf_op jit(solution)/shard_map/ppermute | solution.py:777
  52.2 1.3 %collective-permute-start.14 = (f32[224,128]{1,0:T(8,128)S(1)}, f32[224,128]{1,0:T(8,128)S(1)}, u32[]{:S(2)}, u32[]{:S(2)}) collective-permute-start(f32[224,128]{1,0:T(8,128)S(1)} %get-tuple-element.88), channel_id=1, source_target_pairs={{4,12},{6,14},{8,0},{10,2},{5,13},{7,15},{9,1},{11,3},{20,28},{22,... | collective-permute-start | bytes 344072 | tf_op jit(solution)/shard_map/ppermute | solution.py:772
  53.6 0.6 %copy-done = s32[17]{0:T(128)S(1)} copy-done((s32[17]{0:T(128)S(1)}, s32[17]{0:T(128)}, u32[]{:S(2)}) %copy-start) | copy-done | bytes 92
  54.2 1.8 %early_image.1.refs_4_ = f32[17,16,768]{2,1,0:T(8,128)S(1)} custom-call(s32[1,17]{1,0:T(1,128)S(1)} %bitcast.2, f32[4,96,128]{2,1,0:T(8,128)S(1)} %get-tuple-element.89.refs_1_, f32[224,128]{1,0:T(8,128)S(1)} %collective-permute-done.15.refs_2_), custom_call_target="tpu_custom_call" | custom-call | flops 2088960 | bytes 1671168 | tf_op jit(solution)/shard_map/early_image/pallas_call | solution.py:682
  56.0 0.4 pack_own.1.refs_1_
  56.4 3.4 %collective-permute-done.14.refs_3_ = f32[224,128]{1,0:T(8,128)S(1)} collective-permute-done((f32[224,128]{1,0:T(8,128)S(1)}, f32[224,128]{1,0:T(8,128)S(1)}, u32[]{:S(2)}, u32[]{:S(2)}) %collective-permute-start.14) | collective-permute-done | bytes 114720 | tf_op jit(solution)/shard_map/ppermute | solution.py:772
  59.8 2.4 %last_image.1 = (f32[17,16,768]{2,1,0:T(8,128)}, f32[32,48,128]{2,1,0:T(8,128)}) custom-call(s32[1,17]{1,0:T(1,128)S(1)} %bitcast.3, f32[4,96,128]{2,1,0:T(8,128)S(1)} %pack_own.1.refs_1_, f32[224,128]{1,0:T(8,128)S(1)} %collective-permute-done.13.refs_2_, f32[224,128]{1,0:T(8,128)S(1)} %collective-permute-done.14.refs_3_, ...), custom_call_target="tpu_custom_call" | custom-call | flops 2088960 | bytes 1671168 | tf_op jit(solution)/shard_map/last_image/pallas_call | solution.py:682
  (15 shorter events, 0.3 us)
Async XLA Ops:
  1.7 13.6 %collective-permute-start.2 = (f32[32,8,128]{2,1,0:T(8,128)S(1)}, f32[32,8,128]{2,1,0:T(8,128)S(1)}, u32[]{:S(2)}, u32[]{:S(2)}) collective-permute-start(f32[32,8,128]{2,1,0:T(8,128)S(1)} %get-tuple-element.57), channel_id=1, source_target_pairs={{0,1},{1,0},{2,3},{3,2},{4,5},{5,4},{6,7},{7,6},{8,9},{9,8},{10,11... | collective-permute-start | bytes 393224 | tf_op jit(solution)/shard_map/ppermute | solution.py:735
  2.2 11.3 %collective-permute-start = (f32[4,48,128]{2,1,0:T(8,128)S(1)}, f32[4,48,128]{2,1,0:T(8,128)S(1)}, u32[]{:S(2)}, u32[]{:S(2)}) collective-permute-start(f32[4,48,128]{2,1,0:T(8,128)S(1)} %get-tuple-element.55), channel_id=1, source_target_pairs={{6,8},{8,6},{14,0},{0,14},{7,9},{9,7},{15,1},{1,15},{22,24},{24,22... | collective-permute-start | bytes 294920 | tf_op jit(solution)/shard_map/ppermute | solution.py:730
  9.7 5.5 %collective-permute-start.1 = (f32[4,48,128]{2,1,0:T(8,128)S(1)}, f32[4,48,128]{2,1,0:T(8,128)S(1)}, u32[]{:S(2)}, u32[]{:S(2)}) collective-permute-start(f32[4,48,128]{2,1,0:T(8,128)S(1)} %get-tuple-element.56), channel_id=1, source_target_pairs={{0,2},{2,0},{4,6},{6,4},{8,10},{10,8},{12,14},{14,12},{1,3},{3,1},... | collective-permute-start | bytes 294920 | tf_op jit(solution)/shard_map/ppermute | solution.py:734
  15.4 11.4 %collective-permute-start.5 = (f32[32,8,128]{2,1,0:T(8,128)S(1)}, f32[32,8,128]{2,1,0:T(8,128)S(1)}, u32[]{:S(2)}, u32[]{:S(2)}) collective-permute-start(f32[32,8,128]{2,1,0:T(8,128)S(1)} %get-tuple-element.60.refs_5_), channel_id=1, source_target_pairs={{0,1},{1,0},{2,3},{3,2},{4,5},{5,4},{6,7},{7,6},{8,9},{9,8},{10,11... | collective-permute-start | bytes 393224 | tf_op jit(solution)/shard_map/ppermute | solution.py:735
  15.5 9.9 %collective-permute-start.3 = (f32[4,48,128]{2,1,0:T(8,128)S(1)}, f32[4,48,128]{2,1,0:T(8,128)S(1)}, u32[]{:S(2)}, u32[]{:S(2)}) collective-permute-start(f32[4,48,128]{2,1,0:T(8,128)S(1)} %get-tuple-element.58.refs_3_), channel_id=1, source_target_pairs={{6,8},{8,6},{14,0},{0,14},{7,9},{9,7},{15,1},{1,15},{22,24},{24,22... | collective-permute-start | bytes 294920 | tf_op jit(solution)/shard_map/ppermute | solution.py:730
  19.7 7.1 %collective-permute-start.4 = (f32[4,48,128]{2,1,0:T(8,128)S(1)}, f32[4,48,128]{2,1,0:T(8,128)S(1)}, u32[]{:S(2)}, u32[]{:S(2)}) collective-permute-start(f32[4,48,128]{2,1,0:T(8,128)S(1)} %get-tuple-element.59.refs_4_), channel_id=1, source_target_pairs={{0,2},{2,0},{4,6},{6,4},{8,10},{10,8},{12,14},{14,12},{1,3},{3,1},... | collective-permute-start | bytes 294920 | tf_op jit(solution)/shard_map/ppermute | solution.py:734
  27.0 11.5 %collective-permute-start.8 = (f32[32,8,128]{2,1,0:T(8,128)S(1)}, f32[32,8,128]{2,1,0:T(8,128)S(1)}, u32[]{:S(2)}, u32[]{:S(2)}) collective-permute-start(f32[32,8,128]{2,1,0:T(8,128)S(1)} %get-tuple-element.68.refs_5_), channel_id=1, source_target_pairs={{0,1},{1,0},{2,3},{3,2},{4,5},{5,4},{6,7},{7,6},{8,9},{9,8},{10,11... | collective-permute-start | bytes 393224 | tf_op jit(solution)/shard_map/ppermute | solution.py:735
  27.0 9.9 %collective-permute-start.6 = (f32[4,48,128]{2,1,0:T(8,128)S(1)}, f32[4,48,128]{2,1,0:T(8,128)S(1)}, u32[]{:S(2)}, u32[]{:S(2)}) collective-permute-start(f32[4,48,128]{2,1,0:T(8,128)S(1)} %get-tuple-element.66.refs_3_), channel_id=1, source_target_pairs={{6,8},{8,6},{14,0},{0,14},{7,9},{9,7},{15,1},{1,15},{22,24},{24,22... | collective-permute-start | bytes 294920 | tf_op jit(solution)/shard_map/ppermute | solution.py:730
  31.4 7.1 %collective-permute-start.7 = (f32[4,48,128]{2,1,0:T(8,128)S(1)}, f32[4,48,128]{2,1,0:T(8,128)S(1)}, u32[]{:S(2)}, u32[]{:S(2)}) collective-permute-start(f32[4,48,128]{2,1,0:T(8,128)S(1)} %get-tuple-element.67.refs_4_), channel_id=1, source_target_pairs={{0,2},{2,0},{4,6},{6,4},{8,10},{10,8},{12,14},{14,12},{1,3},{3,1},... | collective-permute-start | bytes 294920 | tf_op jit(solution)/shard_map/ppermute | solution.py:734
  38.6 8.1 %collective-permute-start.11 = (f32[32,8,128]{2,1,0:T(8,128)S(1)}, f32[32,8,128]{2,1,0:T(8,128)S(1)}, u32[]{:S(2)}, u32[]{:S(2)}) collective-permute-start(f32[32,8,128]{2,1,0:T(8,128)S(1)} %get-tuple-element.76.refs_5_), channel_id=1, source_target_pairs={{0,1},{1,0},{2,3},{3,2},{4,5},{5,4},{6,7},{7,6},{8,9},{9,8},{10,11... | collective-permute-start | bytes 393224 | tf_op jit(solution)/shard_map/ppermute | solution.py:735
  38.7 8.0 %collective-permute-start.10 = (f32[4,48,128]{2,1,0:T(8,128)S(1)}, f32[4,48,128]{2,1,0:T(8,128)S(1)}, u32[]{:S(2)}, u32[]{:S(2)}) collective-permute-start(f32[4,48,128]{2,1,0:T(8,128)S(1)} %get-tuple-element.75.refs_4_), channel_id=1, source_target_pairs={{0,2},{2,0},{4,6},{6,4},{8,10},{10,8},{12,14},{14,12},{1,3},{3,1},... | collective-permute-start | bytes 294920 | tf_op jit(solution)/shard_map/ppermute | solution.py:734
  38.7 7.9 %collective-permute-start.9 = (f32[4,48,128]{2,1,0:T(8,128)S(1)}, f32[4,48,128]{2,1,0:T(8,128)S(1)}, u32[]{:S(2)}, u32[]{:S(2)}) collective-permute-start(f32[4,48,128]{2,1,0:T(8,128)S(1)} %get-tuple-element.74.refs_3_), channel_id=1, source_target_pairs={{6,8},{8,6},{7,9},{9,7},{22,24},{24,22},{23,25},{25,23}} | collective-permute-start | bytes 294920 | tf_op jit(solution)/shard_map/ppermute | solution.py:731
  39.4 10.4 %collective-permute-start.12 = (f32[4,48,128]{2,1,0:T(8,128)S(1)}, f32[4,48,128]{2,1,0:T(8,128)S(1)}, u32[]{:S(2)}, u32[]{:S(2)}) collective-permute-start(f32[4,48,128]{2,1,0:T(8,128)S(1)} %get-tuple-element.74.refs_3_), channel_id=1, source_target_pairs={{14,0},{0,14},{15,1},{1,15},{30,16},{16,30},{31,17},{17,31}} | collective-permute-start | bytes 294920 | tf_op jit(solution)/shard_map/ppermute | solution.py:731
  43.7 9.9 %collective-permute-start.15 = (f32[224,128]{1,0:T(8,128)S(1)}, f32[224,128]{1,0:T(8,128)S(1)}, u32[]{:S(2)}, u32[]{:S(2)}) collective-permute-start(f32[224,128]{1,0:T(8,128)S(1)} %get-tuple-element.90), channel_id=1, source_target_pairs={{0,8},{2,10},{4,12},{6,14},{8,0},{10,2},{12,4},{14,6},{1,9},{3,11}... | collective-permute-start | bytes 344072 | tf_op jit(solution)/shard_map/ppermute | solution.py:762
  50.5 5.9 %collective-permute-start.13 = (f32[224,128]{1,0:T(8,128)S(1)}, f32[224,128]{1,0:T(8,128)S(1)}, u32[]{:S(2)}, u32[]{:S(2)}) collective-permute-start(f32[224,128]{1,0:T(8,128)S(1)} %get-tuple-element.87), channel_id=1, source_target_pairs={{0,8},{2,10},{12,4},{14,6},{1,9},{3,11},{13,5},{15,7},{16,24},{18,... | collective-permute-start | bytes 344072 | tf_op jit(solution)/shard_map/ppermute | solution.py:777
  52.2 7.6 %collective-permute-start.14 = (f32[224,128]{1,0:T(8,128)S(1)}, f32[224,128]{1,0:T(8,128)S(1)}, u32[]{:S(2)}, u32[]{:S(2)}) collective-permute-start(f32[224,128]{1,0:T(8,128)S(1)} %get-tuple-element.88), channel_id=1, source_target_pairs={{4,12},{6,14},{8,0},{10,2},{5,13},{7,15},{9,1},{11,3},{20,28},{22,... | collective-permute-start | bytes 344072 | tf_op jit(solution)/shard_map/ppermute | solution.py:772
  53.6 0.7 %copy-start = (s32[17]{0:T(128)S(1)}, s32[17]{0:T(128)}, u32[]{:S(2)}) copy-start(s32[17]{0:T(128)} %param.18) | copy-start | bytes 208

commit v5 on v3

--- a/solution.py
+++ b/solution.py
@@ -49,8 +49,10 @@
 
 
 def exact_dot(values, matrix):
-    parts = [jnp.dot(part, matrix, preferred_element_type=F32) for part in split3(values)]
-    return (parts[2] + parts[1]) + parts[0]
+    rows = values.shape[0]
+    stacked = jnp.concatenate(split3(values), axis=0)
+    result = jnp.dot(stacked, matrix, preferred_element_type=F32)
+    return (result[2 * rows :] + result[rows : 2 * rows]) + result[:rows]
 
 
 class Place:
@@ -398,8 +400,12 @@
 
     def along_x(low_in, high_in, low_out, high_out):
         for r in range(WIDTH):
-            low_out[r] = qx_ref[r] + cx_ref[r] * low_terms(low_in, r)
-            high_out[r] = qx_ref[WIDTH + r] + cx_ref[WIDTH + r] * high_terms(high_in, r)
+            low, high = qx_ref[r], qx_ref[WIDTH + r]
+            if low_in is not None:
+                low = low + cx_ref[r] * low_terms(low_in, r)
+            if high_in is not None:
+                high = high + cx_ref[WIDTH + r] * high_terms(high_in, r)
+            low_out[r], high_out[r] = low, high
         side_out[pl.ds(0, WIDTH)] = low_out[:, pl.ds(block, SIDE)]
         side_out[pl.ds(count_x - WIDTH, WIDTH)] = high_out[:, pl.ds(block, SIDE)]
 
@@ -539,17 +545,17 @@
     return shape(2 * groups * count_a + extra, count_z)
 
 
-def last_step(flag, even_before, current, parts, halos, matrix):
+def last_step(flag, even_before, current, parts, near, side, matrix):
     count_x, count_y, count_z = current.shape
     count_a, count_b = count_x // 2, count_y // 2
 
     def kernel(
-        flag_ref, even_ref, current_ref, qx_ref, qy_ref, cx_ref, cy_ref, far_ref, near_ref,
-        side_ref, matrix_ref, final_ref, late_ref, sent_ref, far_out, near_out, side_out,
+        flag_ref, even_ref, current_ref, qx_ref, qy_ref, cx_ref, cy_ref, near_ref, side_ref,
+        matrix_ref, final_ref, late_ref, sent_ref, far_out, near_out, side_out,
     ):
         place = Place()
         add_halo(
-            place, (qx_ref, qy_ref, cx_ref, cy_ref), (far_ref, near_ref, side_ref),
+            place, (qx_ref, qy_ref, cx_ref, cy_ref), (None, near_ref, side_ref),
             (far_out, near_out, side_out),
         )
         low, high = pl.ds(0, WIDTH), pl.ds(count_x - WIDTH, WIDTH)
@@ -572,7 +578,7 @@
             )
         send_into(late_ref, matrix_ref, sent_ref)
 
-    slab, _, side = face_shapes(count_x, count_y, count_z)
+    slab, _, side_shape = face_shapes(count_x, count_y, count_z)
     return pl.pallas_call(
         kernel,
         out_shape=(
@@ -580,18 +586,77 @@
             shape(count_b, count_a, count_z),
             sent_shape(count_a, count_b, count_z),
         ),
-        in_specs=[spec(pltpu.VMEM)] * 11,
+        in_specs=[spec(pltpu.VMEM)] * 10,
         out_specs=(spec(pltpu.VMEM),) * 3,
         scratch_shapes=[
             pltpu.VMEM(slab.shape, F32),
             pltpu.VMEM(slab.shape, F32),
-            pltpu.VMEM(side.shape, F32),
+            pltpu.VMEM(side_shape.shape, F32),
         ],
         input_output_aliases={2: 0},
         compiler_params=params(12),
         cost_estimate=cost(count_x * count_y * count_z, 10, 3),
         name="last_step",
-    )(flag, even_before, current, *parts, *halos, matrix)
+    )(flag, even_before, current, *parts, near, side, matrix)
+
+
+def far_rows(count_b):
+    return -(-2 * (count_b // GROUP) // 16) * 16
+
+
+def last_far(flag, final, late, cx, far, matrix):
+    count_x, count_y, count_z = final.shape
+    count_b, count_a, _ = late.shape
+    rows, pair = far_rows(count_b), WIDTH // 2
+
+    def kernel(
+        flag_ref, final_in, late_in, cx_ref, far_ref, matrix_ref, final_ref, late_ref, sent_ref, lhs,
+    ):
+        place = Place()
+        wants_last = jnp.broadcast_to(flag_ref[0:1, :], (1, count_z)) > 0.5
+        lhs[...] = jnp.zeros_like(lhs)
+
+        def correct(first_x, first_c, first_a, terms):
+            for r in range(WIDTH):
+                final_ref[first_x + r] = final_ref[first_x + r] + cx_ref[first_c + r] * terms(
+                    far_ref, r
+                )
+            for b in range(count_b):
+                for i in range(pair):
+                    value = jnp.where(
+                        wants_last,
+                        final_ref[first_x + 2 * i, pl.ds(2 * b, 1), :],
+                        late_ref[b, pl.ds(first_a + i, 1), :],
+                    )
+                    late_ref[b, pl.ds(first_a + i, 1), :] = value
+                    lanes = pl.ds(b % GROUP * count_z, count_z)
+                    lhs[pl.ds(b // GROUP * pair + i, 1), lanes] = value
+
+        @pl.when(place.even)
+        def _():
+            correct(0, 0, 0, low_terms)
+
+        @pl.when(jnp.logical_not(place.even))
+        def _():
+            correct(count_x - WIDTH, WIDTH, count_a - pair, high_terms)
+
+        result = exact_dot(lhs[...], matrix_ref[...])
+        parts = [result[:, kind * count_z : (kind + 1) * count_z] for kind in range(4)]
+        sent_ref[pl.ds(0, rows), :] = parts[0]
+        sent_ref[pl.ds(rows, rows), :] = parts[1]
+        sent_ref[pl.ds(2 * rows, rows), :] = parts[2] + pltpu.roll(parts[3], REACH, 1)
+
+    return pl.pallas_call(
+        kernel,
+        out_shape=(shape(*final.shape), shape(*late.shape), shape(3 * rows, count_z)),
+        in_specs=[spec(pltpu.VMEM)] * 6,
+        out_specs=(spec(pltpu.VMEM),) * 3,
+        scratch_shapes=[pltpu.VMEM((rows, GROUP * count_z), F32)],
+        input_output_aliases={1: 0, 2: 1},
+        compiler_params=params(12),
+        cost_estimate=cost(WIDTH * count_y * count_z, 20, 3),
+        name="last_far",
+    )(flag, final, late, cx, far, matrix)
 
 
 def write_out(level):
@@ -612,53 +677,99 @@
     )(level)
 
 
-def lag_image(lags, own, other, before, count_a):
+CODE_BITS = 5
+PER_CODE = 6
+
+
+def lag_image(count_a, lags, own, other, extra=None, before=None):
     _, total_rows, count_z = own.shape
     groups = total_rows // count_a
-    count_h = lags.shape[0]
     half = count_z // GROUP
     last = before is not None
+    count_h = before.shape[0] if last else lags.shape[0]
+    codes = -(-count_h // PER_CODE)
+    pair = WIDTH // 2
 
     def kernel(*refs):
         refs = list(refs)
         take = lambda count: [refs.pop(0) for _ in range(count)]
         lags_ref, own_ref, other_ref = take(3)
         if last:
-            (before_ref,) = take(1)
+            extra_ref, before_ref = take(2)
         (out_ref,) = take(1)
-        edges, lag_of, sems = take(3)
+        if not last:
+            (codes_ref,) = take(1)
+        mains, edges = take(2)
         if last:
-            (store,) = take(1)
+            store, sem = take(2)
         else:
             store = out_ref
+            lag_of, sem = take(2)
         place = Place()
-        copy = pltpu.make_async_copy(lags_ref, lag_of, sems.at[0])
-        copy.start()
+        if last:
+            packed_lags = [lags_ref[k : k + 1, :][0, 0] for k in range(codes)]
+            mask = (1 << CODE_BITS) - 1
+            lag_list = [
+                ((packed_lags[h // PER_CODE] >> (h % PER_CODE * CODE_BITS)) & mask) - LAGMAX
+                for h in range(count_h)
+            ]
+        else:
+            copy = pltpu.make_async_copy(lags_ref, lag_of, sem)
+            copy.start()
         is_source = place.field == 0
-        lane = lax.broadcasted_iota(jnp.int32, (count_a, count_z), 1) % half
-        useful = jnp.where(is_source, lane, half - 1 - lane) < REACH
+
+        def useful(rows):
+            lane = lax.broadcasted_iota(jnp.int32, (rows, count_z), 1) % half
+            return jnp.where(is_source, lane, half - 1 - lane) < REACH
+
         slots, _ = edge_slots(count_a, groups, count_z)
+        for parity in range(2):
+            mains[parity] = other_ref[pl.ds(parity * total_rows, total_rows), :]
         for parity, g, row, shift in slots:
             part = other_ref[pl.ds(2 * total_rows + row, count_a), :]
             part = pltpu.roll(part, count_z - shift, 1) if shift else part
-            edges[parity, pl.ds(g * count_a, count_a), :] = jnp.where(useful, part, 0.0)
-        copy.wait()
+            edges[parity, pl.ds(g * count_a, count_a), :] = jnp.where(useful(count_a), part, 0.0)
+        if last:
+            rows = extra_ref.shape[0] // 3
+            border = extra_ref[pl.ds(2 * rows, rows), :]
+            borders = [
+                jnp.where(useful(rows), part, 0.0)
+                for part in (border, pltpu.roll(border, count_z - REACH, 1))
+            ]
+
+            def overwrite(first_a):
+                for g in range(groups):
+                    target = pl.ds(g * count_a + first_a, pair)
+                    for parity in range(2):
+                        mains[parity, target, :] = extra_ref[
+                            pl.ds(parity * rows + g * pair, pair), :
+                        ]
+                        edges[parity, target, :] = borders[parity][g * pair : (g + 1) * pair]
+
+            pl.when(place.even)(lambda: overwrite(0))
+            pl.when(jnp.logical_not(place.even))(lambda: overwrite(count_a - pair))
+        else:
+            copy.wait()
+            lag_list = [lag_of[h] for h in range(count_h)]
+            for k in range(codes):
+                code = jnp.int32(0)
+                for h in range(k * PER_CODE, min((k + 1) * PER_CODE, count_h)):
+                    code = code | ((lag_list[h] + LAGMAX) << (h % PER_CODE * CODE_BITS))
+                codes_ref[k : k + 1, :] = jnp.full((1, count_z), code, jnp.int32)
         lane = lax.broadcasted_iota(jnp.int32, (1, count_z), 1) % half
 
         def moved(main, edge, shift):
             mask = (lane < shift) | (lane >= half + shift)
             return pltpu.roll(jnp.where(mask, edge, main), (count_z - shift) & (count_z - 1), 1)
 
-        def one(h, _):
-            lag = lag_of[h]
+        for h, lag in enumerate(lag_list):
             parity = lag & 1
             source_shift = -((lag + parity) >> 1)
             receiver_shift = (lag - parity) >> 1
             own_shift = jnp.where(is_source, source_shift, receiver_shift)
             other_shift = jnp.where(is_source, receiver_shift, source_shift)
-            other_rows = pl.ds(pl.multiple_of(parity * total_rows, 8), total_rows)
             product = moved(own_ref[parity], own_ref[2 + parity], own_shift)
-            product = product * moved(other_ref[other_rows, :], edges[parity], other_shift)
+            product = product * moved(mains[parity], edges[parity], other_shift)
             for g in range(groups):
                 part = product[g * count_a : (g + 1) * count_a]
                 lanes = pl.ds(g * count_z, count_z)
@@ -666,29 +777,25 @@
                     part = part + before_ref[h, :, lanes]
                 store[h, :, lanes] = part
             if last:
-                pltpu.make_async_copy(store.at[h], out_ref.at[h], sems.at[1]).start()
-            return 0
-
-        lax.fori_loop(0, count_h, one, 0, unroll=True)
+                pltpu.make_async_copy(store.at[h], out_ref.at[h], sem).start()
         if last:
-            pltpu.make_async_copy(store, out_ref, sems.at[1]).wait()
-
-    out = (count_h, count_a, groups * count_z)
-    operands = [lags, own, other] + ([before] if last else [])
+            pltpu.make_async_copy(store, out_ref, sem).wait()
+
+    image = shape(count_h, count_a, groups * count_z)
+    operands = [lags, own, other] + ([extra, before] if last else [])
+    scratch = [pltpu.VMEM((2, total_rows, count_z), F32)] * 2
+    scratch.append(pltpu.VMEM(image.shape, F32) if last else pltpu.SMEM((count_h,), jnp.int32))
+    scratch.append(pltpu.SemaphoreType.DMA)
     return pl.pallas_call(
         kernel,
-        out_shape=shape(*out),
-        in_specs=[spec(pltpu.HBM)] + [spec(pltpu.VMEM)] * (len(operands) - 1),
-        out_specs=spec(pltpu.HBM if last else pltpu.VMEM),
-        scratch_shapes=[
-            pltpu.VMEM((2, total_rows, count_z), F32),
-            pltpu.SMEM((count_h,), jnp.int32),
-            pltpu.SemaphoreType.DMA((2,)),
-        ]
-        + ([pltpu.VMEM(out, F32)] if last else []),
+        out_shape=image if last else (image, shape(8, count_z, dtype=jnp.int32)),
+        in_specs=[spec(pltpu.VMEM if last else pltpu.HBM)]
+        + [spec(pltpu.VMEM)] * (len(operands) - 1),
+        out_specs=spec(pltpu.HBM) if last else (spec(pltpu.VMEM),) * 2,
+        scratch_shapes=scratch,
         compiler_params=params(12),
         cost_estimate=cost(count_h * total_rows * count_z, 10, 2),
-        name="lag_image",
+        name="last_image" if last else "early_image",
     )(*operands)
 
 
@@ -758,15 +865,17 @@
     )
     other_early = lax.ppermute(sent_early, "gx", across)
     faces = halo_step((qx, qy, cx, cy), halos)
-    halos = exchange(faces)
+    far, near, side = exchange(faces)
     next4, qx, qy, even3 = inner_step(3, points, waves, next3, faces, whole2, courant)
     final, late, sent_late = last_step(
-        flag, even3, next4, (qx, qy, cx, cy), halos, sent_matrix
+        flag, even3, next4, (qx, qy, cx, cy), near, side, sent_matrix
     )
     other_late = lax.ppermute(sent_late, "gx", across)
-    partial = lag_image(lag_offsets, own_early, other_early, None, count_x // 2)
+    partial, codes = lag_image(count_x // 2, lag_offsets, own_early, other_early)
+    final, late, sent_far = last_far(flag, final, late, cx, far, sent_matrix)
+    extra = lax.ppermute(sent_far, "gx", across)
     own_late = pack_own(late, own_matrix)
-    image = lag_image(lag_offsets, own_late, other_late, partial, count_x // 2)
+    image = lag_image(count_x // 2, codes, own_late, other_late, extra, partial)
     return write_out(final), jnp.transpose(image, (1, 0, 2))
 
 

time: 58 us -> 57.1 us (0.984)
  waiting for transfers between devices: 16.2 us -> 13 us
  starting transfers between devices: 21.4 us -> 24.5 us
  Pallas kernels: 19.2 us -> 18.6 us
    ppermute x1, waiting for transfers between devices: 3.17 us -> 0.01 us  [body(): other_late = lax.ppermute(sent_late, 'gx', across)]
    ppermute x4, waiting for transfers between devices: 8.04 us -> 5.06 us  [send_far(): return lax.ppermute(far, 'gx', far_pairs)]
    ppermute x0 -> x1, waiting for transfers between devices: none -> 2.89 us  [body(): extra = lax.ppermute(sent_far, 'gx', across)]
    ppermute x1, starting transfers between devices: 0.07 us -> 2.96 us  [body(): other_late = lax.ppermute(sent_late, 'gx', across)]
    pallas_call x2 -> x3, Pallas kernels: 3.03 us -> 2.71 us  [the longest x2 2.45 us: lag_image(): pl.pallas_call(kernel, out_shape=image if last else (image, shape(8, coun...]
  transfers between devices with their start and end apart: 14 -> 15, of which waited for: 7 -> 6; matrix products, arithmetic and copies ran while one was open for 0% -> 0% of each run, Pallas kernels for 27% -> 27%
where the time goes in v5:
time: 57.1 us; the launch traced here: 56.8 us
  starting transfers between devices  24.5 us (43%)
  Pallas kernels  18.6 us (33%)
  waiting for transfers between devices  13 us (23%)
  between operations  0.85 us (1%)
    ppermute x4, starting transfers between devices, send_far(): return lax.ppermute(far, 'gx', far_pairs)  20.2 us
    pallas_call x4, Pallas kernels, inner_step(): pl.pallas_call(kernel, out_shape=tuple(outs), in_specs=specs, out_specs=(...  12.3 us
    ppermute x4, waiting for transfers between devices, send_far(): return lax.ppermute(far, 'gx', far_pairs)  5.06 us
    ppermute x4, waiting for transfers between devices, send_near(): near = lax.ppermute(near, 'gx', near_pairs)  5 us
    ppermute x1, starting transfers between devices, body(): other_late = lax.ppermute(sent_late, 'gx', across)  2.96 us
    ppermute x1, waiting for transfers between devices, body(): extra = lax.ppermute(sent_far, 'gx', across)  2.89 us
    pallas_call x2, Pallas kernels, lag_image(): pl.pallas_call(kernel, out_shape=image if last else (image, shape(8, coun...  2.45 us
    pallas_call x1, Pallas kernels, first_faces(): pl.pallas_call(kernel, out_shape=(*face_shapes(count_x, count_y, count_z)...  1.36 us
  transfers between devices with their start and end apart: 15, of which 6 were waited for; matrix products, arithmetic and copies ran while one was open for 0% of the time, Pallas kernels for 27%

profile of v5, /device:TPU:0, one launch (start us, length us, event | category | flops | bytes accessed | tf_op | source)
XLA Modules:
  0.0 56.8 jit_solution(2401094105583226523)
XLA Ops:
  0.6 1.4 %first_faces.1 = (f32[4,48,128]{2,1,0:T(8,128)S(1)}, f32[4,48,128]{2,1,0:T(8,128)S(1)}, f32[32,8,128]{2,1,0:T(8,128)S(1)}, f32[32,48,128]{2,1,0:T(8,128)S(1)}) custom-call(f32[32,48,128]{2,1,0:T(8,128)} %field_ref.1), custom_call_target="tpu_custom_call" | custom-call | tf_op jit(solution)/shard_map/first_faces/pallas_call | solution.py:96
  2.0 0.6 collective-permute-start.2
  2.6 7.5 %collective-permute-start = (f32[4,48,128]{2,1,0:T(8,128)S(1)}, f32[4,48,128]{2,1,0:T(8,128)S(1)}, u32[]{:S(2)}, u32[]{:S(2)}) collective-permute-start(f32[4,48,128]{2,1,0:T(8,128)S(1)} %get-tuple-element.56), channel_id=1, source_target_pairs={{6,8},{8,6},{14,0},{0,14},{7,9},{9,7},{15,1},{1,15},{22,24},{24,22... | collective-permute-start | bytes 294920 | tf_op jit(solution)/shard_map/ppermute | solution.py:833
  10.0 0.1 collective-permute-start.1
  10.1 3.4 %shard_map.113 = (f32[32,48,128]{2,1,0:T(8,128)S(1)}, f32[8,48,128]{2,1,0:T(8,128)S(1)}, f32[32,8,128]{2,1,0:T(8,128)S(1)}, f32[32,48,128]{2,1,0:T(8,128)S(1)}, ...) custom-call(s32[3,8]{1,0:T(4,128)} %refs_0_.2, ...), custom_call_target="tpu_custom_call" | custom-call | flops 11796480 | bytes 4718592 | tf_op jit(solution)/shard_map/pallas_call | solution.py:367
  13.5 2.0 %collective-permute-done.1.refs_5_ = f32[4,48,128]{2,1,0:T(8,128)S(1)} collective-permute-done((f32[4,48,128]{2,1,0:T(8,128)S(1)}, f32[4,48,128]{2,1,0:T(8,128)S(1)}, u32[]{:S(2)}, u32[]{:S(2)}) %collective-permute-start.1) | collective-permute-done | bytes 98336 | tf_op jit(solution)/shard_map/ppermute | solution.py:836
  15.6 0.1 halo_step.3
  15.7 0.1 collective-permute-start.5
  15.8 4.2 %collective-permute-start.3 = (f32[4,48,128]{2,1,0:T(8,128)S(1)}, f32[4,48,128]{2,1,0:T(8,128)S(1)}, u32[]{:S(2)}, u32[]{:S(2)}) collective-permute-start(f32[4,48,128]{2,1,0:T(8,128)S(1)} %get-tuple-element.59.refs_3_), channel_id=1, source_target_pairs={{6,8},{8,6},{14,0},{0,14},{7,9},{9,7},{15,1},{1,15},{22,24},{24,22... | collective-permute-start | bytes 294920 | tf_op jit(solution)/shard_map/ppermute | solution.py:833
  20.0 0.1 collective-permute-start.4
  20.1 2.6 %shard_map.114 = (f32[32,48,128]{2,1,0:T(8,128)S(1)}, f32[8,48,128]{2,1,0:T(8,128)S(1)}, f32[32,8,128]{2,1,0:T(8,128)S(1)}, f32[32,48,128]{2,1,0:T(8,128)S(1)}) custom-call(s32[8,256]{1,0:T(8,128)S(1)} %get-tuple-element.49.refs_0_, f32[8,256]{1,0:T(8,128)S(1)} %get-tuple-element.50.refs_1_, f32[32,48,128]{2,1,0:T(8,128)S(1)} %get-tuple-element.51.refs_2_, ...), custom_call_target="tpu_custom_call" | custom-call | flops 11796480 | bytes 4718592 | tf_op jit(solution)/shard_map/pallas_call | solution.py:367
  22.7 2.9 %collective-permute-done.3.refs_4_ = f32[4,48,128]{2,1,0:T(8,128)S(1)} collective-permute-done((f32[4,48,128]{2,1,0:T(8,128)S(1)}, f32[4,48,128]{2,1,0:T(8,128)S(1)}, u32[]{:S(2)}, u32[]{:S(2)}) %collective-permute-start.3) | collective-permute-done | bytes 98336 | tf_op jit(solution)/shard_map/ppermute | solution.py:833
  25.7 1.4 %collective-permute-done.4.refs_5_ = f32[4,48,128]{2,1,0:T(8,128)S(1)} collective-permute-done((f32[4,48,128]{2,1,0:T(8,128)S(1)}, f32[4,48,128]{2,1,0:T(8,128)S(1)}, u32[]{:S(2)}, u32[]{:S(2)}) %collective-permute-start.4) | collective-permute-done | bytes 98336 | tf_op jit(solution)/shard_map/ppermute | solution.py:836
  27.1 0.1 halo_step.4
  27.3 0.1 collective-permute-start.8
  27.4 4.3 %collective-permute-start.6 = (f32[4,48,128]{2,1,0:T(8,128)S(1)}, f32[4,48,128]{2,1,0:T(8,128)S(1)}, u32[]{:S(2)}, u32[]{:S(2)}) collective-permute-start(f32[4,48,128]{2,1,0:T(8,128)S(1)} %get-tuple-element.66.refs_3_), channel_id=1, source_target_pairs={{6,8},{8,6},{14,0},{0,14},{7,9},{9,7},{15,1},{1,15},{22,24},{24,22... | collective-permute-start | bytes 294920 | tf_op jit(solution)/shard_map/ppermute | solution.py:833
  31.7 0.1 collective-permute-start.7
  31.7 3.4 %shard_map.115 = (f32[32,48,128]{2,1,0:T(8,128)S(1)}, f32[8,48,128]{2,1,0:T(8,128)S(1)}, f32[32,8,128]{2,1,0:T(8,128)S(1)}, f32[32,48,128]{2,1,0:T(8,128)S(1)}, ...) custom-call(s32[8,256]{1,0:T(8,128)S(1)} %get-tuple-element.49.refs_, ...), custom_call_target="tpu_custom_call" | custom-call | flops 11796480 | bytes 4718592 | tf_op jit(solution)/shard_map/pallas_call | solution.py:367
  35.1 2.1 %collective-permute-done.6.refs_4_ = f32[4,48,128]{2,1,0:T(8,128)S(1)} collective-permute-done((f32[4,48,128]{2,1,0:T(8,128)S(1)}, f32[4,48,128]{2,1,0:T(8,128)S(1)}, u32[]{:S(2)}, u32[]{:S(2)}) %collective-permute-start.6) | collective-permute-done | bytes 98336 | tf_op jit(solution)/shard_map/ppermute | solution.py:833
  37.2 1.5 %collective-permute-done.7.refs_5_ = f32[4,48,128]{2,1,0:T(8,128)S(1)} collective-permute-done((f32[4,48,128]{2,1,0:T(8,128)S(1)}, f32[4,48,128]{2,1,0:T(8,128)S(1)}, u32[]{:S(2)}, u32[]{:S(2)}) %collective-permute-start.7) | collective-permute-done | bytes 98336 | tf_op jit(solution)/shard_map/ppermute | solution.py:836
  38.8 0.1 halo_step.5
  39.1 4.2 %collective-permute-start.11 = (f32[4,48,128]{2,1,0:T(8,128)S(1)}, f32[4,48,128]{2,1,0:T(8,128)S(1)}, u32[]{:S(2)}, u32[]{:S(2)}) collective-permute-start(f32[4,48,128]{2,1,0:T(8,128)S(1)} %get-tuple-element.74.refs_3_), channel_id=1, source_target_pairs={{6,8},{8,6},{14,0},{0,14},{7,9},{9,7},{15,1},{1,15},{22,24},{24,22... | collective-permute-start | bytes 294920 | tf_op jit(solution)/shard_map/ppermute | solution.py:833
  43.4 2.9 %shard_map.116 = (f32[32,48,128]{2,1,0:T(8,128)S(1)}, f32[8,48,128]{2,1,0:T(8,128)S(1)}, f32[32,8,128]{2,1,0:T(8,128)S(1)}, f32[24,16,128]{2,1,0:T(8,128)S(1)}) custom-call(s32[8,256]{1,0:T(8,128)S(1)} %get-tuple-element.49.refs_0_, f32[8,256]{1,0:T(8,128)S(1)} %get-tuple-element.50.refs_1_, f32[32,48,128]{2,1,0:T(8,128)S(1)} %get-tuple-element.71.refs_2_, ...), custom_call_target="tpu_custom_call" | custom-call | flops 11796480 | bytes 4718592 | tf_op jit(solution)/shard_map/pallas_call | solution.py:367
  46.3 0.6 %last_step.1 = (f32[32,48,128]{2,1,0:T(8,128)S(1)}, f32[24,16,128]{2,1,0:T(8,128)S(1)}, f32[224,128]{1,0:T(8,128)S(1)}) custom-call(f32[8,128]{1,0:T(8,128)S(1)} %get-tuple-element.70.flag_ref, f32[24,16,128]{2,1,0:T(8,128)S(1)} %get-tuple-element.78.even_ref, f32[32,48,128]{2,1,0:T(8,128)S(1)} %get-tuple-element.79.current_ref, ...), custom_call_target="tpu_custom_call", output_to_operand_aliasing={{0}: (2, {})} | custom-call | flops 1966080 | bytes 2359296 | tf_op jit(solution)/shard_map/last_step/pallas_call | solution.py:582
  46.9 3.0 %collective-permute-start.13 = (f32[224,128]{1,0:T(8,128)S(1)}, f32[224,128]{1,0:T(8,128)S(1)}, u32[]{:S(2)}, u32[]{:S(2)}) collective-permute-start(f32[224,128]{1,0:T(8,128)S(1)} %get-tuple-element.91), channel_id=1, source_target_pairs={{0,8},{2,10},{4,12},{6,14},{8,0},{10,2},{12,4},{14,6},{1,9},{3,11}... | collective-permute-start | bytes 344072 | tf_op jit(solution)/shard_map/ppermute | solution.py:873
  49.9 0.3 last_far.1
  50.2 0.1 collective-permute-start.14
  50.3 1.2 %early_image.1 = (f32[17,16,768]{2,1,0:T(8,128)S(1)}, s32[8,128]{1,0:T(8,128)S(1)}) custom-call(s32[17]{0:T(128)} %refs_0_.3, f32[4,96,128]{2,1,0:T(8,128)S(1)} %get-tuple-element.86.refs_1_, f32[224,128]{1,0:T(8,128)S(1)} %collective-permute-done.12.refs_2_), custom_call_target="tpu_custom_call" | custom-call | flops 2088960 | bytes 1671168 | tf_op jit(solution)/shard_map/early_image/pallas_call | solution.py:789
  51.5 0.9 %write_out.1 = f32[32,48,128]{2,1,0:T(8,128)} custom-call(f32[32,48,128]{2,1,0:T(8,128)S(1)} %get-tuple-element.85.level_ref), custom_call_target="tpu_custom_call" | custom-call | bytes 1572864 | tf_op jit(solution)/shard_map/write_out/pallas_call | solution.py:668
  52.4 0.3 pack_own.1.refs_1_
  52.7 2.9 %collective-permute-done.14.refs_3_ = f32[48,128]{1,0:T(8,128)S(1)} collective-permute-done((f32[48,128]{1,0:T(8,128)S(1)}, f32[48,128]{1,0:T(8,128)S(1)}, u32[]{:S(2)}, u32[]{:S(2)}) %collective-permute-start.14) | collective-permute-done | bytes 24608 | tf_op jit(solution)/shard_map/ppermute | solution.py:876
  55.6 1.3 %last_image.1 = f32[17,16,768]{2,1,0:T(8,128)} custom-call(s32[8,128]{1,0:T(8,128)S(1)} %get-tuple-element.88.refs_0_, f32[4,96,128]{2,1,0:T(8,128)S(1)} %pack_own.1.refs_1_, f32[224,128]{1,0:T(8,128)S(1)} %collective-permute-done.13.refs_2_, f32[48,128]{1,0:T(8,128)S(1)} %collective-permute-done.14.refs_3_, f32[17,16,768]{2,1,0:T(8,128)S(1)} %get-tuple-element.93.refs_4_), custom_call_target="tpu_custom_call" | custom-call | flops 2088960 | bytes 1671168 | tf_op jit(solution)/shard_map/last_image/pallas_call | solution.py:789
  (12 shorter events, 0.2 us)
Async XLA Ops:
  2.0 13.6 %collective-permute-start.2 = (f32[32,8,128]{2,1,0:T(8,128)S(1)}, f32[32,8,128]{2,1,0:T(8,128)S(1)}, u32[]{:S(2)}, u32[]{:S(2)}) collective-permute-start(f32[32,8,128]{2,1,0:T(8,128)S(1)} %get-tuple-element.58), channel_id=1, source_target_pairs={{0,1},{1,0},{2,3},{3,2},{4,5},{5,4},{6,7},{7,6},{8,9},{9,8},{10,11... | collective-permute-start | bytes 393224 | tf_op jit(solution)/shard_map/ppermute | solution.py:837
  2.6 11.0 %collective-permute-start = (f32[4,48,128]{2,1,0:T(8,128)S(1)}, f32[4,48,128]{2,1,0:T(8,128)S(1)}, u32[]{:S(2)}, u32[]{:S(2)}) collective-permute-start(f32[4,48,128]{2,1,0:T(8,128)S(1)} %get-tuple-element.56), channel_id=1, source_target_pairs={{6,8},{8,6},{14,0},{0,14},{7,9},{9,7},{15,1},{1,15},{22,24},{24,22... | collective-permute-start | bytes 294920 | tf_op jit(solution)/shard_map/ppermute | solution.py:833
  10.0 5.5 %collective-permute-start.1 = (f32[4,48,128]{2,1,0:T(8,128)S(1)}, f32[4,48,128]{2,1,0:T(8,128)S(1)}, u32[]{:S(2)}, u32[]{:S(2)}) collective-permute-start(f32[4,48,128]{2,1,0:T(8,128)S(1)} %get-tuple-element.57), channel_id=1, source_target_pairs={{0,2},{2,0},{4,6},{6,4},{8,10},{10,8},{12,14},{14,12},{1,3},{3,1},... | collective-permute-start | bytes 294920 | tf_op jit(solution)/shard_map/ppermute | solution.py:836
  15.7 11.4 %collective-permute-start.5 = (f32[32,8,128]{2,1,0:T(8,128)S(1)}, f32[32,8,128]{2,1,0:T(8,128)S(1)}, u32[]{:S(2)}, u32[]{:S(2)}) collective-permute-start(f32[32,8,128]{2,1,0:T(8,128)S(1)} %get-tuple-element.61.refs_5_), channel_id=1, source_target_pairs={{0,1},{1,0},{2,3},{3,2},{4,5},{5,4},{6,7},{7,6},{8,9},{9,8},{10,11... | collective-permute-start | bytes 393224 | tf_op jit(solution)/shard_map/ppermute | solution.py:837
  15.8 9.9 %collective-permute-start.3 = (f32[4,48,128]{2,1,0:T(8,128)S(1)}, f32[4,48,128]{2,1,0:T(8,128)S(1)}, u32[]{:S(2)}, u32[]{:S(2)}) collective-permute-start(f32[4,48,128]{2,1,0:T(8,128)S(1)} %get-tuple-element.59.refs_3_), channel_id=1, source_target_pairs={{6,8},{8,6},{14,0},{0,14},{7,9},{9,7},{15,1},{1,15},{22,24},{24,22... | collective-permute-start | bytes 294920 | tf_op jit(solution)/shard_map/ppermute | solution.py:833
  20.0 7.1 %collective-permute-start.4 = (f32[4,48,128]{2,1,0:T(8,128)S(1)}, f32[4,48,128]{2,1,0:T(8,128)S(1)}, u32[]{:S(2)}, u32[]{:S(2)}) collective-permute-start(f32[4,48,128]{2,1,0:T(8,128)S(1)} %get-tuple-element.60.refs_4_), channel_id=1, source_target_pairs={{0,2},{2,0},{4,6},{6,4},{8,10},{10,8},{12,14},{14,12},{1,3},{3,1},... | collective-permute-start | bytes 294920 | tf_op jit(solution)/shard_map/ppermute | solution.py:836
  27.3 11.5 %collective-permute-start.8 = (f32[32,8,128]{2,1,0:T(8,128)S(1)}, f32[32,8,128]{2,1,0:T(8,128)S(1)}, u32[]{:S(2)}, u32[]{:S(2)}) collective-permute-start(f32[32,8,128]{2,1,0:T(8,128)S(1)} %get-tuple-element.68.refs_5_), channel_id=1, source_target_pairs={{0,1},{1,0},{2,3},{3,2},{4,5},{5,4},{6,7},{7,6},{8,9},{9,8},{10,11... | collective-permute-start | bytes 393224 | tf_op jit(solution)/shard_map/ppermute | solution.py:837
  27.4 9.9 %collective-permute-start.6 = (f32[4,48,128]{2,1,0:T(8,128)S(1)}, f32[4,48,128]{2,1,0:T(8,128)S(1)}, u32[]{:S(2)}, u32[]{:S(2)}) collective-permute-start(f32[4,48,128]{2,1,0:T(8,128)S(1)} %get-tuple-element.66.refs_3_), channel_id=1, source_target_pairs={{6,8},{8,6},{14,0},{0,14},{7,9},{9,7},{15,1},{1,15},{22,24},{24,22... | collective-permute-start | bytes 294920 | tf_op jit(solution)/shard_map/ppermute | solution.py:833
  31.7 7.1 %collective-permute-start.7 = (f32[4,48,128]{2,1,0:T(8,128)S(1)}, f32[4,48,128]{2,1,0:T(8,128)S(1)}, u32[]{:S(2)}, u32[]{:S(2)}) collective-permute-start(f32[4,48,128]{2,1,0:T(8,128)S(1)} %get-tuple-element.67.refs_4_), channel_id=1, source_target_pairs={{0,2},{2,0},{4,6},{6,4},{8,10},{10,8},{12,14},{14,12},{1,3},{3,1},... | collective-permute-start | bytes 294920 | tf_op jit(solution)/shard_map/ppermute | solution.py:836
  38.9 7.4 %collective-permute-start.10 = (f32[32,8,128]{2,1,0:T(8,128)S(1)}, f32[32,8,128]{2,1,0:T(8,128)S(1)}, u32[]{:S(2)}, u32[]{:S(2)}) collective-permute-start(f32[32,8,128]{2,1,0:T(8,128)S(1)} %get-tuple-element.76.refs_5_), channel_id=1, source_target_pairs={{0,1},{1,0},{2,3},{3,2},{4,5},{5,4},{6,7},{7,6},{8,9},{9,8},{10,11... | collective-permute-start | bytes 393224 | tf_op jit(solution)/shard_map/ppermute | solution.py:837
  39.0 7.3 %collective-permute-start.9 = (f32[4,48,128]{2,1,0:T(8,128)S(1)}, f32[4,48,128]{2,1,0:T(8,128)S(1)}, u32[]{:S(2)}, u32[]{:S(2)}) collective-permute-start(f32[4,48,128]{2,1,0:T(8,128)S(1)} %get-tuple-element.75.refs_4_), channel_id=1, source_target_pairs={{0,2},{2,0},{4,6},{6,4},{8,10},{10,8},{12,14},{14,12},{1,3},{3,1},... | collective-permute-start | bytes 294920 | tf_op jit(solution)/shard_map/ppermute | solution.py:836
  39.1 10.8 %collective-permute-start.11 = (f32[4,48,128]{2,1,0:T(8,128)S(1)}, f32[4,48,128]{2,1,0:T(8,128)S(1)}, u32[]{:S(2)}, u32[]{:S(2)}) collective-permute-start(f32[4,48,128]{2,1,0:T(8,128)S(1)} %get-tuple-element.74.refs_3_), channel_id=1, source_target_pairs={{6,8},{8,6},{14,0},{0,14},{7,9},{9,7},{15,1},{1,15},{22,24},{24,22... | collective-permute-start | bytes 294920 | tf_op jit(solution)/shard_map/ppermute | solution.py:833
  43.3 7.0 %collective-permute-start.12 = (f32[224,128]{1,0:T(8,128)S(1)}, f32[224,128]{1,0:T(8,128)S(1)}, u32[]{:S(2)}, u32[]{:S(2)}) collective-permute-start(f32[224,128]{1,0:T(8,128)S(1)} %get-tuple-element.87), channel_id=1, source_target_pairs={{0,8},{2,10},{4,12},{6,14},{8,0},{10,2},{12,4},{14,6},{1,9},{3,11}... | collective-permute-start | bytes 344072 | tf_op jit(solution)/shard_map/ppermute | solution.py:866
  46.9 8.7 %collective-permute-start.13 = (f32[224,128]{1,0:T(8,128)S(1)}, f32[224,128]{1,0:T(8,128)S(1)}, u32[]{:S(2)}, u32[]{:S(2)}) collective-permute-start(f32[224,128]{1,0:T(8,128)S(1)} %get-tuple-element.91), channel_id=1, source_target_pairs={{0,8},{2,10},{4,12},{6,14},{8,0},{10,2},{12,4},{14,6},{1,9},{3,11}... | collective-permute-start | bytes 344072 | tf_op jit(solution)/shard_map/ppermute | solution.py:873
  50.2 5.4 %collective-permute-start.14 = (f32[48,128]{1,0:T(8,128)S(1)}, f32[48,128]{1,0:T(8,128)S(1)}, u32[]{:S(2)}, u32[]{:S(2)}) collective-permute-start(f32[48,128]{1,0:T(8,128)S(1)} %get-tuple-element.92), channel_id=1, source_target_pairs={{0,8},{2,10},{4,12},{6,14},{8,0},{10,2},{12,4},{14,6},{1,9},{3,11}... | collective-permute-start | bytes 73736 | tf_op jit(solution)/shard_map/ppermute | solution.py:876

commit v6 on v5

--- a/solution.py
+++ b/solution.py
@@ -122,7 +122,10 @@
     first = faces is None
     last = number == STEPS - 1
     snapshot = number == STEPS // 2
-    if first:
+    ahead = number == 1
+    if last:
+        count_j = 0
+    elif first:
         count_j = -(-max(array.shape[1] for array in points) // 128) * 128
     else:
         count_j = points.shape[1]
@@ -132,6 +135,8 @@
         take = lambda count: [refs.pop(0) for _ in range(count)]
         if first:
             raw_refs = take(4)
+        elif last:
+            (added_ref,) = take(1)
         else:
             points_ref, waves_ref = take(2)
         (current_ref,) = take(1)
@@ -147,9 +152,13 @@
             (whole_ref,) = take(1)
         if snapshot:
             own_out, sent_out, own_matrix, sent_matrix, flag_ref = take(5)
+        if ahead:
+            (ahead_ref,) = take(1)
         if last:
             (even_ref,) = take(1)
         padded, zpart, addpart = take(3)
+        if last:
+            addpart = added_ref
         if first:
             before_ref = take(1)[0]
             raw_refs_in, raw_refs = raw_refs, take(4)
@@ -225,17 +234,21 @@
             def _():
                 choose(raw_refs[2], raw_refs[3])
 
-        px = points_ref[0:1, :] - place.slab * count_x
-        py = points_ref[1:2, :] - place.y * count_y
-        inside = (px >= 0) & (px < count_x) & (py >= 0) & (py < count_y)
-        home = jnp.where(inside, px * count_y + py, -1)
-        amounts = waves_ref[number : number + 1, :]
-        spread = jnp.where(
-            lax.broadcasted_iota(jnp.int32, (count_z, count_j), 0) == points_ref[2:3, :],
-            amounts,
-            0.0,
-        )
-        spread = split3(spread)
+        if not last:
+            px = points_ref[0:1, :] - place.slab * count_x
+            py = points_ref[1:2, :] - place.y * count_y
+            inside = (px >= 0) & (px < count_x) & (py >= 0) & (py < count_y)
+            home = jnp.where(inside, px * count_y + py, -1)
+            at_z = (
+                lax.broadcasted_iota(jnp.int32, (count_z, count_j), 0) == points_ref[2:3, :]
+            )
+
+            def spread_of(step):
+                return split3(jnp.where(at_z, waves_ref[step : step + 1, :], 0.0))
+
+            spreads = [(addpart, spread_of(number))]
+            if ahead:
+                spreads.append((ahead_ref, spread_of(STEPS - 1)))
 
         gap = jnp.abs(
             lax.broadcasted_iota(jnp.int32, (count_z, count_z), 0)
@@ -254,16 +267,21 @@
             zpart[pl.ds(start, chunk)] = exact_dot(
                 values.reshape(chunk * count_y, count_z), band
             ).reshape(chunk, count_y, count_z)
+            if last:
+                return 0
             here = start * count_y + lax.broadcasted_iota(
                 jnp.int32, (chunk * count_y, count_j), 0
             )
             hit = jnp.where(here == home, 1.0, 0.0).astype(BF16)
-            added = [
-                lax.dot_general(hit, part, (((1,), (1,)), ((), ())), preferred_element_type=F32)
-                for part in spread
-            ]
-            added = (added[2] + added[1]) + added[0]
-            addpart[pl.ds(start, chunk)] = added.reshape(chunk, count_y, count_z)
+            for target, spread in spreads:
+                added = [
+                    lax.dot_general(
+                        hit, part, (((1,), (1,)), ((), ())), preferred_element_type=F32
+                    )
+                    for part in spread
+                ]
+                added = (added[2] + added[1]) + added[0]
+                target[pl.ds(start, chunk)] = added.reshape(chunk, count_y, count_z)
             return 0
 
         lax.fori_loop(0, count_x // chunk, multiply, 0)
@@ -337,10 +355,17 @@
             shape(size, size, dtype=BF16),
             shape(8, count_z),
         ]
+    if ahead:
+        outs.append(full)
     if last:
         outs.append(even)
     place_of = spec(pltpu.HBM) if first else spec(pltpu.VMEM)
-    operands = [*points, current] if first else [points, waves, current]
+    if first:
+        operands = [*points, current]
+    elif last:
+        operands = [points, current]
+    else:
+        operands = [points, waves, current]
     specs = [place_of] * (len(operands) - 1) + [spec(pltpu.VMEM)]
     if not first:
         operands += list(faces)
@@ -857,7 +882,7 @@
     )
     faces = halo_step((qx, qy, cx, cy), halos)
     halos = exchange(faces)
-    next2, qx, qy, whole1 = inner_step(1, points, waves, next1, faces, whole0, courant)
+    next2, qx, qy, whole1, added = inner_step(1, points, waves, next1, faces, whole0, courant)
     faces = halo_step((qx, qy, cx, cy), halos)
     halos = exchange(faces)
     next3, qx, qy, whole2, own_early, sent_early, own_matrix, sent_matrix, flag = inner_step(
@@ -866,7 +891,7 @@
     other_early = lax.ppermute(sent_early, "gx", across)
     faces = halo_step((qx, qy, cx, cy), halos)
     far, near, side = exchange(faces)
-    next4, qx, qy, even3 = inner_step(3, points, waves, next3, faces, whole2, courant)
+    next4, qx, qy, even3 = inner_step(3, added, None, next3, faces, whole2, courant)
     final, late, sent_late = last_step(
         flag, even3, next4, (qx, qy, cx, cy), near, side, sent_matrix
     )

time: 57.1 us -> 57 us (level)
    ppermute x1, waiting for transfers between devices: 0.01 us -> 3.1 us  [body(): other_early = lax.ppermute(sent_early, 'gx', across)]
    ppermute x1, waiting for transfers between devices: 2.89 us -> 0.2 us  [body(): extra = lax.ppermute(sent_far, 'gx', across)]
    ppermute x4, waiting for transfers between devices: 5.06 us -> 4.47 us  [send_far(): return lax.ppermute(far, 'gx', far_pairs)]
  transfers between devices with their start and end apart: 15 -> 15, of which waited for: 6 -> 8; matrix products, arithmetic and copies ran while one was open for 0% -> 0% of each run, Pallas kernels for 27% -> 28%
where the time goes in v6:
time: 57 us; the launch traced here: 56.7 us
  starting transfers between devices  24.4 us (43%)
  Pallas kernels  18.7 us (33%)
  waiting for transfers between devices  12.8 us (22%)
  between operations  0.85 us (1%)
    ppermute x4, starting transfers between devices, send_far(): return lax.ppermute(far, 'gx', far_pairs)  20.2 us
    pallas_call x4, Pallas kernels, inner_step(): pl.pallas_call(kernel, out_shape=tuple(outs), in_specs=specs, out_specs=(...  12.4 us
    ppermute x4, waiting for transfers between devices, send_near(): near = lax.ppermute(near, 'gx', near_pairs)  5 us
    ppermute x4, waiting for transfers between devices, send_far(): return lax.ppermute(far, 'gx', far_pairs)  4.47 us
    ppermute x1, waiting for transfers between devices, body(): other_early = lax.ppermute(sent_early, 'gx', across)  3.1 us
    ppermute x1, starting transfers between devices, body(): other_late = lax.ppermute(sent_late, 'gx', across)  2.98 us
    pallas_call x2, Pallas kernels, lag_image(): pl.pallas_call(kernel, out_shape=image if last else (image, shape(8, coun...  2.45 us
    pallas_call x1, Pallas kernels, first_faces(): pl.pallas_call(kernel, out_shape=(*face_shapes(count_x, count_y, count_z)...  1.36 us
  transfers between devices with their start and end apart: 15, of which 8 were waited for; matrix products, arithmetic and copies ran while one was open for 0% of the time, Pallas kernels for 28%

profile of v6, /device:TPU:0, one launch (start us, length us, event | category | flops | bytes accessed | tf_op | source)
XLA Modules:
  0.0 56.7 jit_solution(13425235866147893444)
XLA Ops:
  0.6 1.4 %first_faces.1 = (f32[4,48,128]{2,1,0:T(8,128)S(1)}, f32[4,48,128]{2,1,0:T(8,128)S(1)}, f32[32,8,128]{2,1,0:T(8,128)S(1)}, f32[32,48,128]{2,1,0:T(8,128)S(1)}) custom-call(f32[32,48,128]{2,1,0:T(8,128)} %field_ref.1), custom_call_target="tpu_custom_call" | custom-call | tf_op jit(solution)/shard_map/first_faces/pallas_call | solution.py:96
  2.0 0.6 collective-permute-start.2
  2.6 7.5 %collective-permute-start = (f32[4,48,128]{2,1,0:T(8,128)S(1)}, f32[4,48,128]{2,1,0:T(8,128)S(1)}, u32[]{:S(2)}, u32[]{:S(2)}) collective-permute-start(f32[4,48,128]{2,1,0:T(8,128)S(1)} %get-tuple-element.57), channel_id=1, source_target_pairs={{6,8},{8,6},{14,0},{0,14},{7,9},{9,7},{15,1},{1,15},{22,24},{24,22... | collective-permute-start | bytes 294920 | tf_op jit(solution)/shard_map/ppermute | solution.py:858
  10.0 0.1 collective-permute-start.1
  10.1 3.4 %shard_map.113 = (f32[32,48,128]{2,1,0:T(8,128)S(1)}, f32[8,48,128]{2,1,0:T(8,128)S(1)}, f32[32,8,128]{2,1,0:T(8,128)S(1)}, f32[32,48,128]{2,1,0:T(8,128)S(1)}, ...) custom-call(s32[3,8]{1,0:T(4,128)} %refs_0_.2, ...), custom_call_target="tpu_custom_call" | custom-call | flops 11796480 | bytes 4718592 | tf_op jit(solution)/shard_map/pallas_call | solution.py:392
  13.5 2.0 %collective-permute-done.1.refs_5_ = f32[4,48,128]{2,1,0:T(8,128)S(1)} collective-permute-done((f32[4,48,128]{2,1,0:T(8,128)S(1)}, f32[4,48,128]{2,1,0:T(8,128)S(1)}, u32[]{:S(2)}, u32[]{:S(2)}) %collective-permute-start.1) | collective-permute-done | bytes 98336 | tf_op jit(solution)/shard_map/ppermute | solution.py:861
  15.6 0.1 halo_step.3
  15.7 0.1 collective-permute-start.5
  15.8 4.2 %collective-permute-start.3 = (f32[4,48,128]{2,1,0:T(8,128)S(1)}, f32[4,48,128]{2,1,0:T(8,128)S(1)}, u32[]{:S(2)}, u32[]{:S(2)}) collective-permute-start(f32[4,48,128]{2,1,0:T(8,128)S(1)} %get-tuple-element.60.refs_3_), channel_id=1, source_target_pairs={{6,8},{8,6},{14,0},{0,14},{7,9},{9,7},{15,1},{1,15},{22,24},{24,22... | collective-permute-start | bytes 294920 | tf_op jit(solution)/shard_map/ppermute | solution.py:858
  20.0 0.1 collective-permute-start.4
  20.1 3.3 %shard_map.114 = (f32[32,48,128]{2,1,0:T(8,128)S(1)}, f32[8,48,128]{2,1,0:T(8,128)S(1)}, f32[32,8,128]{2,1,0:T(8,128)S(1)}, f32[32,48,128]{2,1,0:T(8,128)S(1)}, f32[32,48,128]{2,1,0:T(8,128)S(1)}) custom-call(s32[8,256]{1,0:T(8,128)S(1)} %get-tuple-element.50.refs_0_, f32[8,256]{1,0:T(8,128)S(1)} %get-tuple-element.51.refs_1_, ...), custom_call_target="tpu_custom_call" | custom-call | flops 11796480 | bytes 4718592 | tf_op jit(solution)/shard_map/pallas_call | solution.py:392
  23.5 2.2 %collective-permute-done.3.refs_4_ = f32[4,48,128]{2,1,0:T(8,128)S(1)} collective-permute-done((f32[4,48,128]{2,1,0:T(8,128)S(1)}, f32[4,48,128]{2,1,0:T(8,128)S(1)}, u32[]{:S(2)}, u32[]{:S(2)}) %collective-permute-start.3) | collective-permute-done | bytes 98336 | tf_op jit(solution)/shard_map/ppermute | solution.py:858
  25.7 1.4 %collective-permute-done.4.refs_5_ = f32[4,48,128]{2,1,0:T(8,128)S(1)} collective-permute-done((f32[4,48,128]{2,1,0:T(8,128)S(1)}, f32[4,48,128]{2,1,0:T(8,128)S(1)}, u32[]{:S(2)}, u32[]{:S(2)}) %collective-permute-start.4) | collective-permute-done | bytes 98336 | tf_op jit(solution)/shard_map/ppermute | solution.py:861
  27.1 0.1 halo_step.4
  27.3 0.1 collective-permute-start.8
  27.4 4.3 %collective-permute-start.6 = (f32[4,48,128]{2,1,0:T(8,128)S(1)}, f32[4,48,128]{2,1,0:T(8,128)S(1)}, u32[]{:S(2)}, u32[]{:S(2)}) collective-permute-start(f32[4,48,128]{2,1,0:T(8,128)S(1)} %get-tuple-element.67.refs_3_), channel_id=1, source_target_pairs={{6,8},{8,6},{14,0},{0,14},{7,9},{9,7},{15,1},{1,15},{22,24},{24,22... | collective-permute-start | bytes 294920 | tf_op jit(solution)/shard_map/ppermute | solution.py:858
  31.7 3.4 %shard_map.115 = (f32[32,48,128]{2,1,0:T(8,128)S(1)}, f32[8,48,128]{2,1,0:T(8,128)S(1)}, f32[32,8,128]{2,1,0:T(8,128)S(1)}, f32[32,48,128]{2,1,0:T(8,128)S(1)}, ...) custom-call(s32[8,256]{1,0:T(8,128)S(1)} %get-tuple-element.50.refs_, ...), custom_call_target="tpu_custom_call" | custom-call | flops 11796480 | bytes 4718592 | tf_op jit(solution)/shard_map/pallas_call | solution.py:392
  35.1 2.1 %collective-permute-done.6.refs_4_ = f32[4,48,128]{2,1,0:T(8,128)S(1)} collective-permute-done((f32[4,48,128]{2,1,0:T(8,128)S(1)}, f32[4,48,128]{2,1,0:T(8,128)S(1)}, u32[]{:S(2)}, u32[]{:S(2)}) %collective-permute-start.6) | collective-permute-done | bytes 98336 | tf_op jit(solution)/shard_map/ppermute | solution.py:858
  37.2 1.5 %collective-permute-done.7.refs_5_ = f32[4,48,128]{2,1,0:T(8,128)S(1)} collective-permute-done((f32[4,48,128]{2,1,0:T(8,128)S(1)}, f32[4,48,128]{2,1,0:T(8,128)S(1)}, u32[]{:S(2)}, u32[]{:S(2)}) %collective-permute-start.7) | collective-permute-done | bytes 98336 | tf_op jit(solution)/shard_map/ppermute | solution.py:861
  38.8 0.1 halo_step.5
  39.1 4.2 %collective-permute-start.11 = (f32[4,48,128]{2,1,0:T(8,128)S(1)}, f32[4,48,128]{2,1,0:T(8,128)S(1)}, u32[]{:S(2)}, u32[]{:S(2)}) collective-permute-start(f32[4,48,128]{2,1,0:T(8,128)S(1)} %get-tuple-element.76.refs_2_), channel_id=1, source_target_pairs={{6,8},{8,6},{14,0},{0,14},{7,9},{9,7},{15,1},{1,15},{22,24},{24,22... | collective-permute-start | bytes 294920 | tf_op jit(solution)/shard_map/ppermute | solution.py:858
  43.4 2.3 %shard_map.116 = (f32[32,48,128]{2,1,0:T(8,128)S(1)}, f32[8,48,128]{2,1,0:T(8,128)S(1)}, f32[32,8,128]{2,1,0:T(8,128)S(1)}, f32[24,16,128]{2,1,0:T(8,128)S(1)}) custom-call(f32[32,48,128]{2,1,0:T(8,128)S(1)} %get-tuple-element.72.refs_0_, f32[32,48,128]{2,1,0:T(8,128)S(1)} %get-tuple-element.73.refs_1_, f32[4,48,128]{2,1,0:T(8,128)S(1)} %get-tuple-element.76.refs_2_, ...), custom_call_target="tpu_custom_call" | custom-call | flops 11796480 | bytes 4718592 | tf_op jit(solution)/shard_map/pallas_call | solution.py:392
  45.7 0.6 %last_step.1 = (f32[32,48,128]{2,1,0:T(8,128)S(1)}, f32[24,16,128]{2,1,0:T(8,128)S(1)}, f32[224,128]{1,0:T(8,128)S(1)}) custom-call(f32[8,128]{1,0:T(8,128)S(1)} %get-tuple-element.71.flag_ref, f32[24,16,128]{2,1,0:T(8,128)S(1)} %get-tuple-element.80.even_ref, f32[32,48,128]{2,1,0:T(8,128)S(1)} %get-tuple-element.81.current_ref, ...), custom_call_target="tpu_custom_call", output_to_operand_aliasing={{0}: (2, {})} | custom-call | flops 1966080 | bytes 2359296 | tf_op jit(solution)/shard_map/last_step/pallas_call | solution.py:607
  46.3 3.0 %collective-permute-start.13 = (f32[224,128]{1,0:T(8,128)S(1)}, f32[224,128]{1,0:T(8,128)S(1)}, u32[]{:S(2)}, u32[]{:S(2)}) collective-permute-start(f32[224,128]{1,0:T(8,128)S(1)} %get-tuple-element.93), channel_id=1, source_target_pairs={{0,8},{2,10},{4,12},{6,14},{8,0},{10,2},{12,4},{14,6},{1,9},{3,11}... | collective-permute-start | bytes 344072 | tf_op jit(solution)/shard_map/ppermute | solution.py:898
  49.3 0.2 collective-permute-done.11.far_ref
  49.4 0.2 last_far.1
  49.7 3.1 %collective-permute-done.12.refs_2_ = f32[224,128]{1,0:T(8,128)S(1)} collective-permute-done((f32[224,128]{1,0:T(8,128)S(1)}, f32[224,128]{1,0:T(8,128)S(1)}, u32[]{:S(2)}, u32[]{:S(2)}) %collective-permute-start.12) | collective-permute-done | bytes 114720 | tf_op jit(solution)/shard_map/ppermute | solution.py:891
  52.8 1.2 %early_image.1 = (f32[17,16,768]{2,1,0:T(8,128)S(1)}, s32[8,128]{1,0:T(8,128)S(1)}) custom-call(s32[17]{0:T(128)} %refs_0_.3, f32[4,96,128]{2,1,0:T(8,128)S(1)} %get-tuple-element.88.refs_1_, f32[224,128]{1,0:T(8,128)S(1)} %collective-permute-done.12.refs_2_), custom_call_target="tpu_custom_call" | custom-call | flops 2088960 | bytes 1671168 | tf_op jit(solution)/shard_map/early_image/pallas_call | solution.py:814
  54.0 0.9 %write_out.1 = f32[32,48,128]{2,1,0:T(8,128)} custom-call(f32[32,48,128]{2,1,0:T(8,128)S(1)} %get-tuple-element.87.level_ref), custom_call_target="tpu_custom_call" | custom-call | bytes 1572864 | tf_op jit(solution)/shard_map/write_out/pallas_call | solution.py:693
  54.9 0.3 pack_own.1.refs_1_
  55.2 0.2 collective-permute-done.14.refs_3_
  55.4 1.3 %last_image.1 = f32[17,16,768]{2,1,0:T(8,128)} custom-call(s32[8,128]{1,0:T(8,128)S(1)} %get-tuple-element.90.refs_0_, f32[4,96,128]{2,1,0:T(8,128)S(1)} %pack_own.1.refs_1_, f32[224,128]{1,0:T(8,128)S(1)} %collective-permute-done.13.refs_2_, f32[48,128]{1,0:T(8,128)S(1)} %collective-permute-done.14.refs_3_, f32[17,16,768]{2,1,0:T(8,128)S(1)} %get-tuple-element.95.refs_4_), custom_call_target="tpu_custom_call" | custom-call | flops 2088960 | bytes 1671168 | tf_op jit(solution)/shard_map/last_image/pallas_call | solution.py:814
  (12 shorter events, 0.3 us)
Async XLA Ops:
  2.0 13.6 %collective-permute-start.2 = (f32[32,8,128]{2,1,0:T(8,128)S(1)}, f32[32,8,128]{2,1,0:T(8,128)S(1)}, u32[]{:S(2)}, u32[]{:S(2)}) collective-permute-start(f32[32,8,128]{2,1,0:T(8,128)S(1)} %get-tuple-element.59), channel_id=1, source_target_pairs={{0,1},{1,0},{2,3},{3,2},{4,5},{5,4},{6,7},{7,6},{8,9},{9,8},{10,11... | collective-permute-start | bytes 393224 | tf_op jit(solution)/shard_map/ppermute | solution.py:862
  2.6 11.0 %collective-permute-start = (f32[4,48,128]{2,1,0:T(8,128)S(1)}, f32[4,48,128]{2,1,0:T(8,128)S(1)}, u32[]{:S(2)}, u32[]{:S(2)}) collective-permute-start(f32[4,48,128]{2,1,0:T(8,128)S(1)} %get-tuple-element.57), channel_id=1, source_target_pairs={{6,8},{8,6},{14,0},{0,14},{7,9},{9,7},{15,1},{1,15},{22,24},{24,22... | collective-permute-start | bytes 294920 | tf_op jit(solution)/shard_map/ppermute | solution.py:858
  10.0 5.5 %collective-permute-start.1 = (f32[4,48,128]{2,1,0:T(8,128)S(1)}, f32[4,48,128]{2,1,0:T(8,128)S(1)}, u32[]{:S(2)}, u32[]{:S(2)}) collective-permute-start(f32[4,48,128]{2,1,0:T(8,128)S(1)} %get-tuple-element.58), channel_id=1, source_target_pairs={{0,2},{2,0},{4,6},{6,4},{8,10},{10,8},{12,14},{14,12},{1,3},{3,1},... | collective-permute-start | bytes 294920 | tf_op jit(solution)/shard_map/ppermute | solution.py:861
  15.7 11.4 %collective-permute-start.5 = (f32[32,8,128]{2,1,0:T(8,128)S(1)}, f32[32,8,128]{2,1,0:T(8,128)S(1)}, u32[]{:S(2)}, u32[]{:S(2)}) collective-permute-start(f32[32,8,128]{2,1,0:T(8,128)S(1)} %get-tuple-element.62.refs_5_), channel_id=1, source_target_pairs={{0,1},{1,0},{2,3},{3,2},{4,5},{5,4},{6,7},{7,6},{8,9},{9,8},{10,11... | collective-permute-start | bytes 393224 | tf_op jit(solution)/shard_map/ppermute | solution.py:862
  15.8 9.9 %collective-permute-start.3 = (f32[4,48,128]{2,1,0:T(8,128)S(1)}, f32[4,48,128]{2,1,0:T(8,128)S(1)}, u32[]{:S(2)}, u32[]{:S(2)}) collective-permute-start(f32[4,48,128]{2,1,0:T(8,128)S(1)} %get-tuple-element.60.refs_3_), channel_id=1, source_target_pairs={{6,8},{8,6},{14,0},{0,14},{7,9},{9,7},{15,1},{1,15},{22,24},{24,22... | collective-permute-start | bytes 294920 | tf_op jit(solution)/shard_map/ppermute | solution.py:858
  20.0 7.1 %collective-permute-start.4 = (f32[4,48,128]{2,1,0:T(8,128)S(1)}, f32[4,48,128]{2,1,0:T(8,128)S(1)}, u32[]{:S(2)}, u32[]{:S(2)}) collective-permute-start(f32[4,48,128]{2,1,0:T(8,128)S(1)} %get-tuple-element.61.refs_4_), channel_id=1, source_target_pairs={{0,2},{2,0},{4,6},{6,4},{8,10},{10,8},{12,14},{14,12},{1,3},{3,1},... | collective-permute-start | bytes 294920 | tf_op jit(solution)/shard_map/ppermute | solution.py:861
  27.3 11.5 %collective-permute-start.8 = (f32[32,8,128]{2,1,0:T(8,128)S(1)}, f32[32,8,128]{2,1,0:T(8,128)S(1)}, u32[]{:S(2)}, u32[]{:S(2)}) collective-permute-start(f32[32,8,128]{2,1,0:T(8,128)S(1)} %get-tuple-element.69.refs_5_), channel_id=1, source_target_pairs={{0,1},{1,0},{2,3},{3,2},{4,5},{5,4},{6,7},{7,6},{8,9},{9,8},{10,11... | collective-permute-start | bytes 393224 | tf_op jit(solution)/shard_map/ppermute | solution.py:862
  27.4 9.9 %collective-permute-start.6 = (f32[4,48,128]{2,1,0:T(8,128)S(1)}, f32[4,48,128]{2,1,0:T(8,128)S(1)}, u32[]{:S(2)}, u32[]{:S(2)}) collective-permute-start(f32[4,48,128]{2,1,0:T(8,128)S(1)} %get-tuple-element.67.refs_3_), channel_id=1, source_target_pairs={{6,8},{8,6},{14,0},{0,14},{7,9},{9,7},{15,1},{1,15},{22,24},{24,22... | collective-permute-start | bytes 294920 | tf_op jit(solution)/shard_map/ppermute | solution.py:858
  31.7 7.1 %collective-permute-start.7 = (f32[4,48,128]{2,1,0:T(8,128)S(1)}, f32[4,48,128]{2,1,0:T(8,128)S(1)}, u32[]{:S(2)}, u32[]{:S(2)}) collective-permute-start(f32[4,48,128]{2,1,0:T(8,128)S(1)} %get-tuple-element.68.refs_4_), channel_id=1, source_target_pairs={{0,2},{2,0},{4,6},{6,4},{8,10},{10,8},{12,14},{14,12},{1,3},{3,1},... | collective-permute-start | bytes 294920 | tf_op jit(solution)/shard_map/ppermute | solution.py:861
  38.9 6.8 %collective-permute-start.10 = (f32[32,8,128]{2,1,0:T(8,128)S(1)}, f32[32,8,128]{2,1,0:T(8,128)S(1)}, u32[]{:S(2)}, u32[]{:S(2)}) collective-permute-start(f32[32,8,128]{2,1,0:T(8,128)S(1)} %get-tuple-element.78.refs_4_), channel_id=1, source_target_pairs={{0,1},{1,0},{2,3},{3,2},{4,5},{5,4},{6,7},{7,6},{8,9},{9,8},{10,11... | collective-permute-start | bytes 393224 | tf_op jit(solution)/shard_map/ppermute | solution.py:862
  39.0 6.7 %collective-permute-start.9 = (f32[4,48,128]{2,1,0:T(8,128)S(1)}, f32[4,48,128]{2,1,0:T(8,128)S(1)}, u32[]{:S(2)}, u32[]{:S(2)}) collective-permute-start(f32[4,48,128]{2,1,0:T(8,128)S(1)} %get-tuple-element.77.refs_3_), channel_id=1, source_target_pairs={{0,2},{2,0},{4,6},{6,4},{8,10},{10,8},{12,14},{14,12},{1,3},{3,1},... | collective-permute-start | bytes 294920 | tf_op jit(solution)/shard_map/ppermute | solution.py:861
  39.1 10.4 %collective-permute-start.11 = (f32[4,48,128]{2,1,0:T(8,128)S(1)}, f32[4,48,128]{2,1,0:T(8,128)S(1)}, u32[]{:S(2)}, u32[]{:S(2)}) collective-permute-start(f32[4,48,128]{2,1,0:T(8,128)S(1)} %get-tuple-element.76.refs_2_), channel_id=1, source_target_pairs={{6,8},{8,6},{14,0},{0,14},{7,9},{9,7},{15,1},{1,15},{22,24},{24,22... | collective-permute-start | bytes 294920 | tf_op jit(solution)/shard_map/ppermute | solution.py:858
  43.3 9.5 %collective-permute-start.12 = (f32[224,128]{1,0:T(8,128)S(1)}, f32[224,128]{1,0:T(8,128)S(1)}, u32[]{:S(2)}, u32[]{:S(2)}) collective-permute-start(f32[224,128]{1,0:T(8,128)S(1)} %get-tuple-element.89), channel_id=1, source_target_pairs={{0,8},{2,10},{4,12},{6,14},{8,0},{10,2},{12,4},{14,6},{1,9},{3,11}... | collective-permute-start | bytes 344072 | tf_op jit(solution)/shard_map/ppermute | solution.py:891
  46.3 9.1 %collective-permute-start.13 = (f32[224,128]{1,0:T(8,128)S(1)}, f32[224,128]{1,0:T(8,128)S(1)}, u32[]{:S(2)}, u32[]{:S(2)}) collective-permute-start(f32[224,128]{1,0:T(8,128)S(1)} %get-tuple-element.93), channel_id=1, source_target_pairs={{0,8},{2,10},{4,12},{6,14},{8,0},{10,2},{12,4},{14,6},{1,9},{3,11}... | collective-permute-start | bytes 344072 | tf_op jit(solution)/shard_map/ppermute | solution.py:898
  49.7 5.8 %collective-permute-start.14 = (f32[48,128]{1,0:T(8,128)S(1)}, f32[48,128]{1,0:T(8,128)S(1)}, u32[]{:S(2)}, u32[]{:S(2)}) collective-permute-start(f32[48,128]{1,0:T(8,128)S(1)} %get-tuple-element.94), channel_id=1, source_target_pairs={{0,8},{2,10},{4,12},{6,14},{8,0},{10,2},{12,4},{14,6},{1,9},{3,11}... | collective-permute-start | bytes 73736 | tf_op jit(solution)/shard_map/ppermute | solution.py:901

commit v7 on v6

--- a/solution.py
+++ b/solution.py
@@ -73,20 +73,17 @@
     count_x, count_y, count_z = field.shape
     top = count_x - WIDTH
 
-    def kernel(field_ref, far_ref, near_ref, side_ref, whole_ref, sems):
+    def kernel(field_ref, far_ref, near_ref, side_ref, sems):
         place = Place()
         far = jnp.where(place.even, 0, top)
         sources = [
             field_ref.at[pl.ds(far, WIDTH)],
             field_ref.at[pl.ds(top - far, WIDTH)],
             field_ref.at[:, pl.ds(place.block(count_y), SIDE)],
-            field_ref,
         ]
         copies = [
             pltpu.make_async_copy(source, target, sems.at[index])
-            for index, (source, target) in enumerate(
-                zip(sources, (far_ref, near_ref, side_ref, whole_ref))
-            )
+            for index, (source, target) in enumerate(zip(sources, (far_ref, near_ref, side_ref)))
         ]
         for copy in copies:
             copy.start()
@@ -95,10 +92,10 @@
 
     return pl.pallas_call(
         kernel,
-        out_shape=(*face_shapes(count_x, count_y, count_z), shape(*field.shape)),
+        out_shape=face_shapes(count_x, count_y, count_z),
         in_specs=[spec(pltpu.HBM)],
-        out_specs=(spec(pltpu.VMEM),) * 4,
-        scratch_shapes=[pltpu.SemaphoreType.DMA((4,))],
+        out_specs=(spec(pltpu.VMEM),) * 3,
+        scratch_shapes=[pltpu.SemaphoreType.DMA((3,))],
         compiler_params=params(8),
         name="first_faces",
     )(field)
@@ -148,7 +145,7 @@
         next_ref, qx_ref, qy_ref = take(3)
         if first:
             kept_ref, cx_ref, cy_ref, points_ref, waves_ref = take(5)
-        elif not last:
+        if not last:
             (whole_ref,) = take(1)
         if snapshot:
             own_out, sent_out, own_matrix, sent_matrix, flag_ref = take(5)
@@ -215,6 +212,27 @@
 
             padded[rows, pl.ds(pl.multiple_of(block + SIDE, SIDE), SIDE)] = side_ref[...]
 
+        gap = jnp.abs(
+            lax.broadcasted_iota(jnp.int32, (count_z, count_z), 0)
+            - lax.broadcasted_iota(jnp.int32, (count_z, count_z), 1)
+        )
+        band = jnp.zeros((count_z, count_z), F32)
+        for offset, weight in enumerate(BAND, 1):
+            band = jnp.where(gap == offset, weight, band)
+        band = band.astype(BF16)
+
+        chunk = 8
+
+        def multiply(index, _):
+            start = pl.multiple_of(index * chunk, chunk)
+            values = padded[pl.ds(start + WIDTH, chunk), columns]
+            zpart[pl.ds(start, chunk)] = exact_dot(
+                values.reshape(chunk * count_y, count_z), band
+            ).reshape(chunk, count_y, count_z)
+            return 0
+
+        lax.fori_loop(0, count_x // chunk, multiply, 0)
+
         if first:
             for copy in copies[:4]:
                 copy.wait()
@@ -250,25 +268,8 @@
             if ahead:
                 spreads.append((ahead_ref, spread_of(STEPS - 1)))
 
-        gap = jnp.abs(
-            lax.broadcasted_iota(jnp.int32, (count_z, count_z), 0)
-            - lax.broadcasted_iota(jnp.int32, (count_z, count_z), 1)
-        )
-        band = jnp.zeros((count_z, count_z), F32)
-        for offset, weight in enumerate(BAND, 1):
-            band = jnp.where(gap == offset, weight, band)
-        band = band.astype(BF16)
-
-        chunk = 8
-
-        def multiply(index, _):
+        def inject(index, _):
             start = pl.multiple_of(index * chunk, chunk)
-            values = padded[pl.ds(start + WIDTH, chunk), columns]
-            zpart[pl.ds(start, chunk)] = exact_dot(
-                values.reshape(chunk * count_y, count_z), band
-            ).reshape(chunk, count_y, count_z)
-            if last:
-                return 0
             here = start * count_y + lax.broadcasted_iota(
                 jnp.int32, (chunk * count_y, count_j), 0
             )
@@ -284,7 +285,8 @@
                 target[pl.ds(start, chunk)] = added.reshape(chunk, count_y, count_z)
             return 0
 
-        lax.fori_loop(0, count_x // chunk, multiply, 0)
+        if not last:
+            lax.fori_loop(0, count_x // chunk, inject, 0)
         if first:
             for copy in copies[4:]:
                 copy.wait()
@@ -299,7 +301,7 @@
                     + padded[x + WIDTH, pl.ds(SIDE - offset, count_y)]
                 )
                 total = total + weight * paired
-            if not first and not last:
+            if not last:
                 whole_ref[x] = middle
             next_ref[x] = (2.0 * middle - before_ref[x] + kept_ref[x] * total) + addpart[x]
             return 0
@@ -344,7 +346,7 @@
     outs = [full, slab, side]
     if first:
         outs += [full, slab, side, shape(8, count_j, dtype=jnp.int32), shape(8, count_j)]
-    elif not last:
+    if not last:
         outs.append(full)
     if snapshot:
         size = GROUP * count_z
@@ -520,23 +522,55 @@
     return [result[:, kind * count_z : (kind + 1) * count_z] for kind in range(4)]
 
 
-def pack_own(even, matrix):
+def lag_shifts(lag, is_source):
+    parity = lag & 1
+    source_shift = -((lag + parity) >> 1)
+    receiver_shift = (lag - parity) >> 1
+    return (
+        parity,
+        jnp.where(is_source, source_shift, receiver_shift),
+        jnp.where(is_source, receiver_shift, source_shift),
+    )
+
+
+def moved(main, edge, shift):
+    count_z = main.shape[1]
+    half = count_z // GROUP
+    lane = lax.broadcasted_iota(jnp.int32, (1, count_z), 1) % half
+    mask = (lane < shift) | (lane >= half + shift)
+    return pltpu.roll(jnp.where(mask, edge, main), (count_z - shift) & (count_z - 1), 1)
+
+
+def pack_own(lags, even, matrix):
     count_b, count_a, count_z = even.shape
     total_rows = count_b // GROUP * count_a
-
-    def kernel(even_ref, matrix_ref, out_ref):
+    (count_h,) = lags.shape
+
+    def kernel(lags_ref, even_ref, matrix_ref, out_ref, windows, lag_of, sem):
+        copy = pltpu.make_async_copy(lags_ref, lag_of, sem)
+        copy.start()
+        place = Place()
         for kind, part in enumerate(packed(even_ref, matrix_ref)):
-            out_ref[kind] = part
+            windows[kind] = part
+        copy.wait()
+        for h in range(count_h):
+            parity, shift, _ = lag_shifts(lag_of[h], place.field == 0)
+            out_ref[h] = moved(windows[parity], windows[2 + parity], shift)
 
     return pl.pallas_call(
         kernel,
-        out_shape=shape(4, total_rows, count_z),
-        in_specs=[spec(pltpu.VMEM)] * 2,
+        out_shape=shape(count_h, total_rows, count_z),
+        in_specs=[spec(pltpu.HBM)] + [spec(pltpu.VMEM)] * 2,
         out_specs=spec(pltpu.VMEM),
+        scratch_shapes=[
+            pltpu.VMEM((4, total_rows, count_z), F32),
+            pltpu.SMEM((count_h,), jnp.int32),
+            pltpu.SemaphoreType.DMA,
+        ],
         compiler_params=params(8),
         cost_estimate=cost(count_b * count_a * count_z, 1024, 4),
         name="pack_own",
-    )(even, matrix)
+    )(lags, even, matrix)
 
 
 def edge_slots(count_a, groups, count_z):
@@ -781,20 +815,13 @@
                 for h in range(k * PER_CODE, min((k + 1) * PER_CODE, count_h)):
                     code = code | ((lag_list[h] + LAGMAX) << (h % PER_CODE * CODE_BITS))
                 codes_ref[k : k + 1, :] = jnp.full((1, count_z), code, jnp.int32)
-        lane = lax.broadcasted_iota(jnp.int32, (1, count_z), 1) % half
-
-        def moved(main, edge, shift):
-            mask = (lane < shift) | (lane >= half + shift)
-            return pltpu.roll(jnp.where(mask, edge, main), (count_z - shift) & (count_z - 1), 1)
-
         for h, lag in enumerate(lag_list):
-            parity = lag & 1
-            source_shift = -((lag + parity) >> 1)
-            receiver_shift = (lag - parity) >> 1
-            own_shift = jnp.where(is_source, source_shift, receiver_shift)
-            other_shift = jnp.where(is_source, receiver_shift, source_shift)
-            product = moved(own_ref[parity], own_ref[2 + parity], own_shift)
-            product = product * moved(mains[parity], edges[parity], other_shift)
+            parity, own_shift, other_shift = lag_shifts(lag, is_source)
+            product = moved(mains[parity], edges[parity], other_shift)
+            if last:
+                product = product * own_ref[h]
+            else:
+                product = product * moved(own_ref[parity], own_ref[2 + parity], own_shift)
             for g in range(groups):
                 part = product[g * count_a : (g + 1) * count_a]
                 lanes = pl.ds(g * count_z, count_z)
@@ -869,16 +896,15 @@
         np.stack([pack_matrix(window, count_z) for window in (0, 1)]), dtype=BF16
     )
     raw = (source_cells, source_wave, receiver_cells, receiver_wave)
-    field_now, field_prev, courant_squared, matrices, snapshot_steps, lag_offsets, *raw = (
+    field_kept, field_prev, courant_squared, matrices, snapshot_steps, lag_offsets, *raw = (
         pltpu.with_memory_space_constraint(array, pltpu.HBM)
         for array in (
             field_now, field_prev, courant_squared, matrices, snapshot_steps, lag_offsets, *raw
         )
     )
-    *faces, whole0 = first_faces(field_now)
-    halos = exchange(faces)
-    next1, qx, qy, courant, cx, cy, points, waves = inner_step(
-        0, raw, None, whole0, None, field_prev, courant_squared
+    halos = exchange(first_faces(field_kept))
+    next1, qx, qy, courant, cx, cy, points, waves, whole0 = inner_step(
+        0, raw, None, field_now, None, field_prev, courant_squared
     )
     faces = halo_step((qx, qy, cx, cy), halos)
     halos = exchange(faces)
@@ -899,7 +925,7 @@
     partial, codes = lag_image(count_x // 2, lag_offsets, own_early, other_early)
     final, late, sent_far = last_far(flag, final, late, cx, far, sent_matrix)
     extra = lax.ppermute(sent_far, "gx", across)
-    own_late = pack_own(late, own_matrix)
+    own_late = pack_own(lag_offsets, late, own_matrix)
     image = lag_image(count_x // 2, codes, own_late, other_late, extra, partial)
     return write_out(final), jnp.transpose(image, (1, 0, 2))
 

time: 57 us -> 57.4 us (level)
  Pallas kernels: 18.7 us -> 20.1 us
  waiting for transfers between devices: 12.8 us -> 11.5 us
    ppermute x4, waiting for transfers between devices: 4.47 us -> 3.34 us  [send_far(): return lax.ppermute(far, 'gx', far_pairs)]
    pallas_call x4, Pallas kernels: 12.4 us -> 13.5 us  [inner_step(): pl.pallas_call(kernel, out_shape=tuple(outs), in_specs=specs, out_specs=(...]
  transfers between devices with their start and end apart: 15 -> 15, of which waited for: 8 -> 8; matrix products, arithmetic and copies ran while one was open for 0% -> 0% of each run, Pallas kernels for 28% -> 31%
where the time goes in v7:
time: 57.4 us; the launch traced here: 56.8 us
  starting transfers between devices  24.4 us (43%)
  Pallas kernels  20.1 us (35%)
  waiting for transfers between devices  11.5 us (20%)
  between operations  0.88 us (2%)
    ppermute x4, starting transfers between devices, send_far(): return lax.ppermute(far, 'gx', far_pairs)  20.2 us
    pallas_call x4, Pallas kernels, inner_step(): pl.pallas_call(kernel, out_shape=tuple(outs), in_specs=specs, out_specs=(...  13.5 us
    ppermute x4, waiting for transfers between devices, send_near(): near = lax.ppermute(near, 'gx', near_pairs)  5.01 us
    ppermute x4, waiting for transfers between devices, send_far(): return lax.ppermute(far, 'gx', far_pairs)  3.34 us
    ppermute x1, waiting for transfers between devices, body(): other_early = lax.ppermute(sent_early, 'gx', across)  3.1 us
    ppermute x1, starting transfers between devices, body(): other_late = lax.ppermute(sent_late, 'gx', across)  2.97 us
    pallas_call x2, Pallas kernels, lag_image(): pl.pallas_call(kernel, out_shape=image if last else (image, shape(8, coun...  2.26 us
  transfers between devices with their start and end apart: 15, of which 8 were waited for; matrix products, arithmetic and copies ran while one was open for 0% of the time, Pallas kernels for 31%

profile of v7, /device:TPU:0, one launch (start us, length us, event | category | flops | bytes accessed | tf_op | source)
XLA Modules:
  0.0 56.8 jit_solution(823539458608924182)
XLA Ops:
  0.6 1.1 %first_faces.1 = (f32[4,48,128]{2,1,0:T(8,128)S(1)}, f32[4,48,128]{2,1,0:T(8,128)S(1)}, f32[32,8,128]{2,1,0:T(8,128)S(1)}) custom-call(f32[32,48,128]{2,1,0:T(8,128)} %field_ref.1), custom_call_target="tpu_custom_call" | custom-call | tf_op jit(solution)/shard_map/first_faces/pallas_call | solution.py:93
  1.8 0.6 collective-permute-start.2
  2.3 7.5 %collective-permute-start = (f32[4,48,128]{2,1,0:T(8,128)S(1)}, f32[4,48,128]{2,1,0:T(8,128)S(1)}, u32[]{:S(2)}, u32[]{:S(2)}) collective-permute-start(f32[4,48,128]{2,1,0:T(8,128)S(1)} %get-tuple-element.56), channel_id=1, source_target_pairs={{6,8},{8,6},{14,0},{0,14},{7,9},{9,7},{15,1},{1,15},{22,24},{24,22... | collective-permute-start | bytes 294920 | tf_op jit(solution)/shard_map/ppermute | solution.py:885
  9.8 0.1 collective-permute-start.1
  9.9 3.3 %shard_map.113 = (f32[32,48,128]{2,1,0:T(8,128)S(1)}, f32[8,48,128]{2,1,0:T(8,128)S(1)}, f32[32,8,128]{2,1,0:T(8,128)S(1)}, f32[32,48,128]{2,1,0:T(8,128)S(1)}, ...) custom-call(s32[3,8]{1,0:T(4,128)} %refs_0_.2, ...), custom_call_target="tpu_custom_call" | custom-call | flops 11796480 | bytes 4718592 | tf_op jit(solution)/shard_map/pallas_call | solution.py:394
  13.3 2.0 %collective-permute-done.1.refs_5_ = f32[4,48,128]{2,1,0:T(8,128)S(1)} collective-permute-done((f32[4,48,128]{2,1,0:T(8,128)S(1)}, f32[4,48,128]{2,1,0:T(8,128)S(1)}, u32[]{:S(2)}, u32[]{:S(2)}) %collective-permute-start.1) | collective-permute-done | bytes 98336 | tf_op jit(solution)/shard_map/ppermute | solution.py:888
  15.3 0.1 halo_step.3
  15.5 0.1 collective-permute-start.5
  15.6 4.2 %collective-permute-start.3 = (f32[4,48,128]{2,1,0:T(8,128)S(1)}, f32[4,48,128]{2,1,0:T(8,128)S(1)}, u32[]{:S(2)}, u32[]{:S(2)}) collective-permute-start(f32[4,48,128]{2,1,0:T(8,128)S(1)} %get-tuple-element.59.refs_3_), channel_id=1, source_target_pairs={{6,8},{8,6},{14,0},{0,14},{7,9},{9,7},{15,1},{1,15},{22,24},{24,22... | collective-permute-start | bytes 294920 | tf_op jit(solution)/shard_map/ppermute | solution.py:885
  19.9 3.9 %shard_map.114 = (f32[32,48,128]{2,1,0:T(8,128)S(1)}, f32[8,48,128]{2,1,0:T(8,128)S(1)}, f32[32,8,128]{2,1,0:T(8,128)S(1)}, f32[32,48,128]{2,1,0:T(8,128)S(1)}, f32[32,48,128]{2,1,0:T(8,128)S(1)}) custom-call(s32[8,256]{1,0:T(8,128)S(1)} %get-tuple-element.49.refs_0_, f32[8,256]{1,0:T(8,128)S(1)} %get-tuple-element.50.refs_1_, ...), custom_call_target="tpu_custom_call" | custom-call | flops 11796480 | bytes 4718592 | tf_op jit(solution)/shard_map/pallas_call | solution.py:394
  23.8 1.6 %collective-permute-done.3.refs_4_ = f32[4,48,128]{2,1,0:T(8,128)S(1)} collective-permute-done((f32[4,48,128]{2,1,0:T(8,128)S(1)}, f32[4,48,128]{2,1,0:T(8,128)S(1)}, u32[]{:S(2)}, u32[]{:S(2)}) %collective-permute-start.3) | collective-permute-done | bytes 98336 | tf_op jit(solution)/shard_map/ppermute | solution.py:885
  25.4 1.4 %collective-permute-done.4.refs_5_ = f32[4,48,128]{2,1,0:T(8,128)S(1)} collective-permute-done((f32[4,48,128]{2,1,0:T(8,128)S(1)}, f32[4,48,128]{2,1,0:T(8,128)S(1)}, u32[]{:S(2)}, u32[]{:S(2)}) %collective-permute-start.4) | collective-permute-done | bytes 98336 | tf_op jit(solution)/shard_map/ppermute | solution.py:888
  26.9 0.1 halo_step.4
  27.1 4.3 %collective-permute-start.6 = (f32[4,48,128]{2,1,0:T(8,128)S(1)}, f32[4,48,128]{2,1,0:T(8,128)S(1)}, u32[]{:S(2)}, u32[]{:S(2)}) collective-permute-start(f32[4,48,128]{2,1,0:T(8,128)S(1)} %get-tuple-element.67.refs_3_), channel_id=1, source_target_pairs={{6,8},{8,6},{14,0},{0,14},{7,9},{9,7},{15,1},{1,15},{22,24},{24,22... | collective-permute-start | bytes 294920 | tf_op jit(solution)/shard_map/ppermute | solution.py:885
  31.4 0.1 collective-permute-start.7
  31.5 4.0 %shard_map.115 = (f32[32,48,128]{2,1,0:T(8,128)S(1)}, f32[8,48,128]{2,1,0:T(8,128)S(1)}, f32[32,8,128]{2,1,0:T(8,128)S(1)}, f32[32,48,128]{2,1,0:T(8,128)S(1)}, ...) custom-call(s32[8,256]{1,0:T(8,128)S(1)} %get-tuple-element.49.refs_, ...), custom_call_target="tpu_custom_call" | custom-call | flops 11796480 | bytes 4718592 | tf_op jit(solution)/shard_map/pallas_call | solution.py:394
  35.5 1.5 %collective-permute-done.6.refs_4_ = f32[4,48,128]{2,1,0:T(8,128)S(1)} collective-permute-done((f32[4,48,128]{2,1,0:T(8,128)S(1)}, f32[4,48,128]{2,1,0:T(8,128)S(1)}, u32[]{:S(2)}, u32[]{:S(2)}) %collective-permute-start.6) | collective-permute-done | bytes 98336 | tf_op jit(solution)/shard_map/ppermute | solution.py:885
  37.0 1.5 %collective-permute-done.7.refs_5_ = f32[4,48,128]{2,1,0:T(8,128)S(1)} collective-permute-done((f32[4,48,128]{2,1,0:T(8,128)S(1)}, f32[4,48,128]{2,1,0:T(8,128)S(1)}, u32[]{:S(2)}, u32[]{:S(2)}) %collective-permute-start.7) | collective-permute-done | bytes 98336 | tf_op jit(solution)/shard_map/ppermute | solution.py:888
  38.5 0.1 halo_step.5
  38.7 0.1 collective-permute-start.10
  38.8 4.2 %collective-permute-start.11 = (f32[4,48,128]{2,1,0:T(8,128)S(1)}, f32[4,48,128]{2,1,0:T(8,128)S(1)}, u32[]{:S(2)}, u32[]{:S(2)}) collective-permute-start(f32[4,48,128]{2,1,0:T(8,128)S(1)} %get-tuple-element.76.refs_2_), channel_id=1, source_target_pairs={{6,8},{8,6},{14,0},{0,14},{7,9},{9,7},{15,1},{1,15},{22,24},{24,22... | collective-permute-start | bytes 294920 | tf_op jit(solution)/shard_map/ppermute | solution.py:885
  43.1 0.1 collective-permute-start.12
  43.2 2.3 %shard_map.116 = (f32[32,48,128]{2,1,0:T(8,128)S(1)}, f32[8,48,128]{2,1,0:T(8,128)S(1)}, f32[32,8,128]{2,1,0:T(8,128)S(1)}, f32[24,16,128]{2,1,0:T(8,128)S(1)}) custom-call(f32[32,48,128]{2,1,0:T(8,128)S(1)} %get-tuple-element.72.refs_0_, f32[32,48,128]{2,1,0:T(8,128)S(1)} %get-tuple-element.73.refs_1_, f32[4,48,128]{2,1,0:T(8,128)S(1)} %get-tuple-element.76.refs_2_, ...), custom_call_target="tpu_custom_call" | custom-call | flops 11796480 | bytes 4718592 | tf_op jit(solution)/shard_map/pallas_call | solution.py:394
  45.4 0.6 %last_step.1 = (f32[32,48,128]{2,1,0:T(8,128)S(1)}, f32[24,16,128]{2,1,0:T(8,128)S(1)}, f32[224,128]{1,0:T(8,128)S(1)}) custom-call(f32[8,128]{1,0:T(8,128)S(1)} %get-tuple-element.71.flag_ref, f32[24,16,128]{2,1,0:T(8,128)S(1)} %get-tuple-element.80.even_ref, f32[32,48,128]{2,1,0:T(8,128)S(1)} %get-tuple-element.81.current_ref, ...), custom_call_target="tpu_custom_call", output_to_operand_aliasing={{0}: (2, {})} | custom-call | flops 1966080 | bytes 2359296 | tf_op jit(solution)/shard_map/last_step/pallas_call | solution.py:641
  46.0 3.0 %collective-permute-start.13 = (f32[224,128]{1,0:T(8,128)S(1)}, f32[224,128]{1,0:T(8,128)S(1)}, u32[]{:S(2)}, u32[]{:S(2)}) collective-permute-start(f32[224,128]{1,0:T(8,128)S(1)} %get-tuple-element.93), channel_id=1, source_target_pairs={{0,8},{2,10},{4,12},{6,14},{8,0},{10,2},{12,4},{14,6},{1,9},{3,11}... | collective-permute-start | bytes 344072 | tf_op jit(solution)/shard_map/ppermute | solution.py:924
  49.0 0.2 collective-permute-done.11.far_ref
  49.2 0.3 last_far.1
  49.5 3.1 %collective-permute-done.12.refs_2_ = f32[224,128]{1,0:T(8,128)S(1)} collective-permute-done((f32[224,128]{1,0:T(8,128)S(1)}, f32[224,128]{1,0:T(8,128)S(1)}, u32[]{:S(2)}, u32[]{:S(2)}) %collective-permute-start.12) | collective-permute-done | bytes 114720 | tf_op jit(solution)/shard_map/ppermute | solution.py:917
  52.6 1.2 %early_image.1 = (f32[17,16,768]{2,1,0:T(8,128)S(1)}, s32[8,128]{1,0:T(8,128)S(1)}) custom-call(s32[17]{0:T(128)} %lags_ref.1, f32[4,96,128]{2,1,0:T(8,128)S(1)} %get-tuple-element.88.refs_1_, f32[224,128]{1,0:T(8,128)S(1)} %collective-permute-done.12.refs_2_), custom_call_target="tpu_custom_call" | custom-call | flops 2088960 | bytes 1671168 | tf_op jit(solution)/shard_map/early_image/pallas_call | solution.py:841
  53.8 0.9 %write_out.1 = f32[32,48,128]{2,1,0:T(8,128)} custom-call(f32[32,48,128]{2,1,0:T(8,128)S(1)} %get-tuple-element.87.level_ref), custom_call_target="tpu_custom_call" | custom-call | bytes 1572864 | tf_op jit(solution)/shard_map/write_out/pallas_call | solution.py:727
  54.7 1.1 %pack_own.1.refs_1_ = f32[17,96,128]{2,1,0:T(8,128)S(1)} custom-call(s32[17]{0:T(128)} %lags_ref.1, f32[24,16,128]{2,1,0:T(8,128)S(1)} %get-tuple-element.91.even_ref, bf16[512,512]{1,0:T(8,128)(2,1)S(1)} %get-tuple-element.92.matrix_ref), custom_call_target="tpu_custom_call" | custom-call | flops 50331648 | bytes 786432 | tf_op jit(solution)/shard_map/pack_own/pallas_call | solution.py:560
  55.8 1.1 %last_image.1 = f32[17,16,768]{2,1,0:T(8,128)} custom-call(s32[8,128]{1,0:T(8,128)S(1)} %get-tuple-element.90.refs_0_, f32[17,96,128]{2,1,0:T(8,128)S(1)} %pack_own.1.refs_1_, f32[224,128]{1,0:T(8,128)S(1)} %collective-permute-done.13.refs_2_, f32[48,128]{1,0:T(8,128)S(1)} %collective-permute-done.14.refs_3_, f32[17,16,768]{2,1,0:T(8,128)S(1)} %get-tuple-element.95.refs_4_), custom_call_target="tpu_custom_call" | custom-call | flops 2088960 | bytes 1671168 | tf_op jit(solution)/shard_map/last_image/pallas_call | solution.py:841
  (14 shorter events, 0.3 us)
Async XLA Ops:
  0.6 9.2 %copy-start = (f32[32,48,128]{2,1,0:T(8,128)S(1)}, f32[32,48,128]{2,1,0:T(8,128)}, u32[]{:S(2)}) copy-start(f32[32,48,128]{2,1,0:T(8,128)} %field_ref.1) | copy-start | bytes 2359300
  1.8 13.6 %collective-permute-start.2 = (f32[32,8,128]{2,1,0:T(8,128)S(1)}, f32[32,8,128]{2,1,0:T(8,128)S(1)}, u32[]{:S(2)}, u32[]{:S(2)}) collective-permute-start(f32[32,8,128]{2,1,0:T(8,128)S(1)} %get-tuple-element.58), channel_id=1, source_target_pairs={{0,1},{1,0},{2,3},{3,2},{4,5},{5,4},{6,7},{7,6},{8,9},{9,8},{10,11... | collective-permute-start | bytes 393224 | tf_op jit(solution)/shard_map/ppermute | solution.py:889
  2.3 11.0 %collective-permute-start = (f32[4,48,128]{2,1,0:T(8,128)S(1)}, f32[4,48,128]{2,1,0:T(8,128)S(1)}, u32[]{:S(2)}, u32[]{:S(2)}) collective-permute-start(f32[4,48,128]{2,1,0:T(8,128)S(1)} %get-tuple-element.56), channel_id=1, source_target_pairs={{6,8},{8,6},{14,0},{0,14},{7,9},{9,7},{15,1},{1,15},{22,24},{24,22... | collective-permute-start | bytes 294920 | tf_op jit(solution)/shard_map/ppermute | solution.py:885
  9.8 5.5 %collective-permute-start.1 = (f32[4,48,128]{2,1,0:T(8,128)S(1)}, f32[4,48,128]{2,1,0:T(8,128)S(1)}, u32[]{:S(2)}, u32[]{:S(2)}) collective-permute-start(f32[4,48,128]{2,1,0:T(8,128)S(1)} %get-tuple-element.57), channel_id=1, source_target_pairs={{0,2},{2,0},{4,6},{6,4},{8,10},{10,8},{12,14},{14,12},{1,3},{3,1},... | collective-permute-start | bytes 294920 | tf_op jit(solution)/shard_map/ppermute | solution.py:888
  15.5 11.4 %collective-permute-start.5 = (f32[32,8,128]{2,1,0:T(8,128)S(1)}, f32[32,8,128]{2,1,0:T(8,128)S(1)}, u32[]{:S(2)}, u32[]{:S(2)}) collective-permute-start(f32[32,8,128]{2,1,0:T(8,128)S(1)} %get-tuple-element.61.refs_5_), channel_id=1, source_target_pairs={{0,1},{1,0},{2,3},{3,2},{4,5},{5,4},{6,7},{7,6},{8,9},{9,8},{10,11... | collective-permute-start | bytes 393224 | tf_op jit(solution)/shard_map/ppermute | solution.py:889
  15.6 9.9 %collective-permute-start.3 = (f32[4,48,128]{2,1,0:T(8,128)S(1)}, f32[4,48,128]{2,1,0:T(8,128)S(1)}, u32[]{:S(2)}, u32[]{:S(2)}) collective-permute-start(f32[4,48,128]{2,1,0:T(8,128)S(1)} %get-tuple-element.59.refs_3_), channel_id=1, source_target_pairs={{6,8},{8,6},{14,0},{0,14},{7,9},{9,7},{15,1},{1,15},{22,24},{24,22... | collective-permute-start | bytes 294920 | tf_op jit(solution)/shard_map/ppermute | solution.py:885
  19.8 7.1 %collective-permute-start.4 = (f32[4,48,128]{2,1,0:T(8,128)S(1)}, f32[4,48,128]{2,1,0:T(8,128)S(1)}, u32[]{:S(2)}, u32[]{:S(2)}) collective-permute-start(f32[4,48,128]{2,1,0:T(8,128)S(1)} %get-tuple-element.60.refs_4_), channel_id=1, source_target_pairs={{0,2},{2,0},{4,6},{6,4},{8,10},{10,8},{12,14},{14,12},{1,3},{3,1},... | collective-permute-start | bytes 294920 | tf_op jit(solution)/shard_map/ppermute | solution.py:888
  27.0 11.5 %collective-permute-start.8 = (f32[32,8,128]{2,1,0:T(8,128)S(1)}, f32[32,8,128]{2,1,0:T(8,128)S(1)}, u32[]{:S(2)}, u32[]{:S(2)}) collective-permute-start(f32[32,8,128]{2,1,0:T(8,128)S(1)} %get-tuple-element.69.refs_5_), channel_id=1, source_target_pairs={{0,1},{1,0},{2,3},{3,2},{4,5},{5,4},{6,7},{7,6},{8,9},{9,8},{10,11... | collective-permute-start | bytes 393224 | tf_op jit(solution)/shard_map/ppermute | solution.py:889
  27.1 9.9 %collective-permute-start.6 = (f32[4,48,128]{2,1,0:T(8,128)S(1)}, f32[4,48,128]{2,1,0:T(8,128)S(1)}, u32[]{:S(2)}, u32[]{:S(2)}) collective-permute-start(f32[4,48,128]{2,1,0:T(8,128)S(1)} %get-tuple-element.67.refs_3_), channel_id=1, source_target_pairs={{6,8},{8,6},{14,0},{0,14},{7,9},{9,7},{15,1},{1,15},{22,24},{24,22... | collective-permute-start | bytes 294920 | tf_op jit(solution)/shard_map/ppermute | solution.py:885
  31.4 7.1 %collective-permute-start.7 = (f32[4,48,128]{2,1,0:T(8,128)S(1)}, f32[4,48,128]{2,1,0:T(8,128)S(1)}, u32[]{:S(2)}, u32[]{:S(2)}) collective-permute-start(f32[4,48,128]{2,1,0:T(8,128)S(1)} %get-tuple-element.68.refs_4_), channel_id=1, source_target_pairs={{0,2},{2,0},{4,6},{6,4},{8,10},{10,8},{12,14},{14,12},{1,3},{3,1},... | collective-permute-start | bytes 294920 | tf_op jit(solution)/shard_map/ppermute | solution.py:888
  38.7 6.8 %collective-permute-start.10 = (f32[32,8,128]{2,1,0:T(8,128)S(1)}, f32[32,8,128]{2,1,0:T(8,128)S(1)}, u32[]{:S(2)}, u32[]{:S(2)}) collective-permute-start(f32[32,8,128]{2,1,0:T(8,128)S(1)} %get-tuple-element.78.refs_4_), channel_id=1, source_target_pairs={{0,1},{1,0},{2,3},{3,2},{4,5},{5,4},{6,7},{7,6},{8,9},{9,8},{10,11... | collective-permute-start | bytes 393224 | tf_op jit(solution)/shard_map/ppermute | solution.py:889
  38.7 6.7 %collective-permute-start.9 = (f32[4,48,128]{2,1,0:T(8,128)S(1)}, f32[4,48,128]{2,1,0:T(8,128)S(1)}, u32[]{:S(2)}, u32[]{:S(2)}) collective-permute-start(f32[4,48,128]{2,1,0:T(8,128)S(1)} %get-tuple-element.77.refs_3_), channel_id=1, source_target_pairs={{0,2},{2,0},{4,6},{6,4},{8,10},{10,8},{12,14},{14,12},{1,3},{3,1},... | collective-permute-start | bytes 294920 | tf_op jit(solution)/shard_map/ppermute | solution.py:888
  38.8 10.4 %collective-permute-start.11 = (f32[4,48,128]{2,1,0:T(8,128)S(1)}, f32[4,48,128]{2,1,0:T(8,128)S(1)}, u32[]{:S(2)}, u32[]{:S(2)}) collective-permute-start(f32[4,48,128]{2,1,0:T(8,128)S(1)} %get-tuple-element.76.refs_2_), channel_id=1, source_target_pairs={{6,8},{8,6},{14,0},{0,14},{7,9},{9,7},{15,1},{1,15},{22,24},{24,22... | collective-permute-start | bytes 294920 | tf_op jit(solution)/shard_map/ppermute | solution.py:885
  43.1 9.5 %collective-permute-start.12 = (f32[224,128]{1,0:T(8,128)S(1)}, f32[224,128]{1,0:T(8,128)S(1)}, u32[]{:S(2)}, u32[]{:S(2)}) collective-permute-start(f32[224,128]{1,0:T(8,128)S(1)} %get-tuple-element.89), channel_id=1, source_target_pairs={{0,8},{2,10},{4,12},{6,14},{8,0},{10,2},{12,4},{14,6},{1,9},{3,11}... | collective-permute-start | bytes 344072 | tf_op jit(solution)/shard_map/ppermute | solution.py:917
  46.0 9.7 %collective-permute-start.13 = (f32[224,128]{1,0:T(8,128)S(1)}, f32[224,128]{1,0:T(8,128)S(1)}, u32[]{:S(2)}, u32[]{:S(2)}) collective-permute-start(f32[224,128]{1,0:T(8,128)S(1)} %get-tuple-element.93), channel_id=1, source_target_pairs={{0,8},{2,10},{4,12},{6,14},{8,0},{10,2},{12,4},{14,6},{1,9},{3,11}... | collective-permute-start | bytes 344072 | tf_op jit(solution)/shard_map/ppermute | solution.py:924
  49.4 6.3 %collective-permute-start.14 = (f32[48,128]{1,0:T(8,128)S(1)}, f32[48,128]{1,0:T(8,128)S(1)}, u32[]{:S(2)}, u32[]{:S(2)}) collective-permute-start(f32[48,128]{1,0:T(8,128)S(1)} %get-tuple-element.94), channel_id=1, source_target_pairs={{0,8},{2,10},{4,12},{6,14},{8,0},{10,2},{12,4},{14,6},{1,9},{3,11}... | collective-permute-start | bytes 73736 | tf_op jit(solution)/shard_map/ppermute | solution.py:927

commit v8 on v7

--- a/solution.py
+++ b/solution.py
@@ -231,7 +231,11 @@
             ).reshape(chunk, count_y, count_z)
             return 0
 
-        lax.fori_loop(0, count_x // chunk, multiply, 0)
+        chunks = count_x // chunk
+        if last:
+            lax.fori_loop(0, chunks, multiply, 0)
+        else:
+            multiply(0, 0)
 
         if first:
             for copy in copies[:4]:
@@ -268,7 +272,7 @@
             if ahead:
                 spreads.append((ahead_ref, spread_of(STEPS - 1)))
 
-        def inject(index, _):
+        def inject(index):
             start = pl.multiple_of(index * chunk, chunk)
             here = start * count_y + lax.broadcasted_iota(
                 jnp.int32, (chunk * count_y, count_j), 0
@@ -285,8 +289,13 @@
                 target[pl.ds(start, chunk)] = added.reshape(chunk, count_y, count_z)
             return 0
 
+        def both(index, _):
+            inject(index)
+            return multiply(index + 1, 0)
+
         if not last:
-            lax.fori_loop(0, count_x // chunk, inject, 0)
+            lax.fori_loop(0, chunks - 1, both, 0)
+            inject(chunks - 1)
         if first:
             for copy in copies[4:]:
                 copy.wait()
@@ -421,6 +430,7 @@
 def add_halo(place, parts, halos, outs):
     qx_ref, qy_ref, cx_ref, cy_ref = parts
     far_in, near_in, side_in = halos
+    near_even, near_odd = near_in if isinstance(near_in, tuple) else (near_in, near_in)
     far_out, near_out, side_out = outs
     count_y, count_x = qx_ref.shape[1], qy_ref.shape[0]
     block = place.block(count_y)
@@ -441,11 +451,11 @@
 
     @pl.when(place.even)
     def _():
-        along_x(far_in, near_in, far_out, near_out)
+        along_x(far_in, near_even, far_out, near_out)
 
     @pl.when(jnp.logical_not(place.even))
     def _():
-        along_x(near_in, far_in, near_out, far_out)
+        along_x(near_odd, far_in, near_out, far_out)
 
     def along_y(shifts, masks):
         halo = side_in[...]
@@ -481,19 +491,25 @@
 
 def halo_step(parts, halos):
     count_y, (count_x, _, count_z) = parts[0].shape[1], parts[1].shape
+    far, near, side = halos
+    nears = near if isinstance(near, tuple) else (near,)
 
     def kernel(*refs):
-        add_halo(Place(), refs[:4], refs[4:7], refs[7:])
+        refs = list(refs)
+        take = lambda count: [refs.pop(0) for _ in range(count)]
+        parts_in, (far_in,), nears_in, (side_in,) = take(4), take(1), take(len(nears)), take(1)
+        near_in = tuple(nears_in) if len(nears) == 2 else nears_in[0]
+        add_halo(Place(), parts_in, (far_in, near_in, side_in), refs)
 
     return pl.pallas_call(
         kernel,
         out_shape=face_shapes(count_x, count_y, count_z),
-        in_specs=[spec(pltpu.VMEM)] * 7,
+        in_specs=[spec(pltpu.VMEM)] * (6 + len(nears)),
         out_specs=(spec(pltpu.VMEM),) * 3,
         compiler_params=params(8),
         cost_estimate=cost(16 * count_y * count_z, 10, 6),
         name="halo_step",
-    )(*parts, *halos)
+    )(*parts, far, *nears, side)
 
 
 def pack_matrix(window, count_z):
@@ -892,6 +908,14 @@
         far, near, side = faces
         return (send_far(far), *send_near(near, side))
 
+    def first_exchange(faces):
+        far, near, side = faces
+        near_even = lax.ppermute(near, "gx", [pair for pair in near_pairs if slabs[pair[0]] % 2])
+        far = send_far(far)
+        near_odd = lax.ppermute(near, "gx", [pair for pair in near_pairs if not slabs[pair[0]] % 2])
+        side = lax.ppermute(side, "gy", [(0, 1), (1, 0)])
+        return far, (near_even, near_odd), side
+
     matrices = jnp.asarray(
         np.stack([pack_matrix(window, count_z) for window in (0, 1)]), dtype=BF16
     )
@@ -902,7 +926,7 @@
             field_now, field_prev, courant_squared, matrices, snapshot_steps, lag_offsets, *raw
         )
     )
-    halos = exchange(first_faces(field_kept))
+    halos = first_exchange(first_faces(field_kept))
     next1, qx, qy, courant, cx, cy, points, waves, whole0 = inner_step(
         0, raw, None, field_now, None, field_prev, courant_squared
     )

time: 57.4 us -> 60.5 us (1.054)
  starting transfers between devices: 24.4 us -> 29.3 us
  waiting for transfers between devices: 11.5 us -> 9.99 us
  Pallas kernels: 20.1 us -> 19.4 us
    ppermute x0 -> x3, starting transfers between devices: none -> 6.39 us  [the longest x1 4.55 us: first_exchange(): lax.ppermute(near, 'gx', [pair for pair in near_pairs if not slabs[pair[0...]
    ppermute x4 -> x3, waiting for transfers between devices: 5.01 us -> 2.96 us  [send_near(): near = lax.ppermute(near, 'gx', near_pairs)]
    ppermute x4, starting transfers between devices: 20.2 us -> 19.3 us  [send_far(): return lax.ppermute(far, 'gx', far_pairs)]
    pallas_call x4, Pallas kernels: 13.5 us -> 12.8 us  [inner_step(): pl.pallas_call(kernel, out_shape=tuple(outs), in_specs=specs, out_specs=(...]
  transfers between devices with their start and end apart: 15 -> 16, of which waited for: 8 -> 6; matrix products, arithmetic and copies ran while one was open for 0% -> 0% of each run, Pallas kernels for 31% -> 28%
where the time goes in v8:
time: 60.5 us; the launch traced here: 59.6 us
  starting transfers between devices  29.3 us (48%)
  Pallas kernels  19.4 us (32%)
  waiting for transfers between devices  9.99 us (17%)
  between operations  0.89 us (1%)
    ppermute x4, starting transfers between devices, send_far(): return lax.ppermute(far, 'gx', far_pairs)  19.3 us
    pallas_call x4, Pallas kernels, inner_step(): pl.pallas_call(kernel, out_shape=tuple(outs), in_specs=specs, out_specs=(...  12.8 us
    ppermute x1, starting transfers between devices, first_exchange(): lax.ppermute(near, 'gx', [pair for pair in near_pairs if not slabs[pair[0...  4.55 us
    ppermute x4, waiting for transfers between devices, send_far(): return lax.ppermute(far, 'gx', far_pairs)  3.84 us
    ppermute x1, waiting for transfers between devices, body(): other_early = lax.ppermute(sent_early, 'gx', across)  3.17 us
    ppermute x1, starting transfers between devices, body(): other_late = lax.ppermute(sent_late, 'gx', across)  2.97 us
    ppermute x3, waiting for transfers between devices, send_near(): near = lax.ppermute(near, 'gx', near_pairs)  2.96 us
    pallas_call x2, Pallas kernels, lag_image(): pl.pallas_call(kernel, out_shape=image if last else (image, shape(8, coun...  2.26 us
  transfers between devices with their start and end apart: 16, of which 6 were waited for; matrix products, arithmetic and copies ran while one was open for 0% of the time, Pallas kernels for 28%

profile of v8, /device:TPU:0, one launch (start us, length us, event | category | flops | bytes accessed | tf_op | source)
XLA Modules:
  0.0 59.6 jit_solution(13973527485172117533)
XLA Ops:
  0.6 1.1 %first_faces.1 = (f32[4,48,128]{2,1,0:T(8,128)S(1)}, f32[4,48,128]{2,1,0:T(8,128)S(1)}, f32[32,8,128]{2,1,0:T(8,128)S(1)}) custom-call(f32[32,48,128]{2,1,0:T(8,128)} %field_ref.1), custom_call_target="tpu_custom_call" | custom-call | tf_op jit(solution)/shard_map/first_faces/pallas_call | solution.py:93
  1.8 0.6 collective-permute-start.3
  2.3 1.3 %collective-permute-start.1 = (f32[4,48,128]{2,1,0:T(8,128)S(1)}, f32[4,48,128]{2,1,0:T(8,128)S(1)}, u32[]{:S(2)}, u32[]{:S(2)}) collective-permute-start(f32[4,48,128]{2,1,0:T(8,128)S(1)} %get-tuple-element.57), channel_id=1, source_target_pairs={{2,0},{6,4},{10,8},{14,12},{3,1},{7,5},{11,9},{15,13},{18,16},{22,... | collective-permute-start | bytes 294920 | tf_op jit(solution)/shard_map/ppermute | solution.py:913
  3.6 4.6 %collective-permute-start.2 = (f32[4,48,128]{2,1,0:T(8,128)S(1)}, f32[4,48,128]{2,1,0:T(8,128)S(1)}, u32[]{:S(2)}, u32[]{:S(2)}) collective-permute-start(f32[4,48,128]{2,1,0:T(8,128)S(1)} %get-tuple-element.57), channel_id=1, source_target_pairs={{0,2},{4,6},{8,10},{12,14},{1,3},{5,7},{9,11},{13,15},{16,18},{20,... | collective-permute-start | bytes 294920 | tf_op jit(solution)/shard_map/ppermute | solution.py:915
  8.2 5.3 %collective-permute-start = (f32[4,48,128]{2,1,0:T(8,128)S(1)}, f32[4,48,128]{2,1,0:T(8,128)S(1)}, u32[]{:S(2)}, u32[]{:S(2)}) collective-permute-start(f32[4,48,128]{2,1,0:T(8,128)S(1)} %get-tuple-element.56), channel_id=1, source_target_pairs={{6,8},{8,6},{14,0},{0,14},{7,9},{9,7},{15,1},{1,15},{22,24},{24,22... | collective-permute-start | bytes 294920 | tf_op jit(solution)/shard_map/ppermute | solution.py:901
  13.5 3.3 %shard_map.113 = (f32[32,48,128]{2,1,0:T(8,128)S(1)}, f32[8,48,128]{2,1,0:T(8,128)S(1)}, f32[32,8,128]{2,1,0:T(8,128)S(1)}, f32[32,48,128]{2,1,0:T(8,128)S(1)}, ...) custom-call(s32[3,8]{1,0:T(4,128)} %refs_0_.2, ...), custom_call_target="tpu_custom_call" | custom-call | flops 11796480 | bytes 4718592 | tf_op jit(solution)/shard_map/pallas_call | solution.py:403
  16.9 0.7 %collective-permute-done.refs_4_ = f32[4,48,128]{2,1,0:T(8,128)S(1)} collective-permute-done((f32[4,48,128]{2,1,0:T(8,128)S(1)}, f32[4,48,128]{2,1,0:T(8,128)S(1)}, u32[]{:S(2)}, u32[]{:S(2)}) %collective-permute-start) | collective-permute-done | bytes 98336 | tf_op jit(solution)/shard_map/ppermute | solution.py:901
  17.6 0.1 halo_step.3
  17.7 0.1 collective-permute-start.6
  17.8 5.5 %collective-permute-start.4 = (f32[4,48,128]{2,1,0:T(8,128)S(1)}, f32[4,48,128]{2,1,0:T(8,128)S(1)}, u32[]{:S(2)}, u32[]{:S(2)}) collective-permute-start(f32[4,48,128]{2,1,0:T(8,128)S(1)} %get-tuple-element.59.refs_3_), channel_id=1, source_target_pairs={{6,8},{8,6},{14,0},{0,14},{7,9},{9,7},{15,1},{1,15},{22,24},{24,22... | collective-permute-start | bytes 294920 | tf_op jit(solution)/shard_map/ppermute | solution.py:901
  23.2 0.1 collective-permute-start.5
  23.3 3.4 %shard_map.114 = (f32[32,48,128]{2,1,0:T(8,128)S(1)}, f32[8,48,128]{2,1,0:T(8,128)S(1)}, f32[32,8,128]{2,1,0:T(8,128)S(1)}, f32[32,48,128]{2,1,0:T(8,128)S(1)}, f32[32,48,128]{2,1,0:T(8,128)S(1)}) custom-call(s32[8,256]{1,0:T(8,128)S(1)} %get-tuple-element.49.refs_0_, f32[8,256]{1,0:T(8,128)S(1)} %get-tuple-element.50.refs_1_, ...), custom_call_target="tpu_custom_call" | custom-call | flops 11796480 | bytes 4718592 | tf_op jit(solution)/shard_map/pallas_call | solution.py:403
  26.8 0.9 %collective-permute-done.4.refs_4_ = f32[4,48,128]{2,1,0:T(8,128)S(1)} collective-permute-done((f32[4,48,128]{2,1,0:T(8,128)S(1)}, f32[4,48,128]{2,1,0:T(8,128)S(1)}, u32[]{:S(2)}, u32[]{:S(2)}) %collective-permute-start.4) | collective-permute-done | bytes 98336 | tf_op jit(solution)/shard_map/ppermute | solution.py:901
  27.7 2.0 %collective-permute-done.5.refs_5_ = f32[4,48,128]{2,1,0:T(8,128)S(1)} collective-permute-done((f32[4,48,128]{2,1,0:T(8,128)S(1)}, f32[4,48,128]{2,1,0:T(8,128)S(1)}, u32[]{:S(2)}, u32[]{:S(2)}) %collective-permute-start.5) | collective-permute-done | bytes 98336 | tf_op jit(solution)/shard_map/ppermute | solution.py:904
  29.7 0.1 halo_step.4
  29.8 0.1 collective-permute-start.9
  29.9 3.7 %collective-permute-start.7 = (f32[4,48,128]{2,1,0:T(8,128)S(1)}, f32[4,48,128]{2,1,0:T(8,128)S(1)}, u32[]{:S(2)}, u32[]{:S(2)}) collective-permute-start(f32[4,48,128]{2,1,0:T(8,128)S(1)} %get-tuple-element.67.refs_3_), channel_id=1, source_target_pairs={{6,8},{8,6},{14,0},{0,14},{7,9},{9,7},{15,1},{1,15},{22,24},{24,22... | collective-permute-start | bytes 294920 | tf_op jit(solution)/shard_map/ppermute | solution.py:901
  33.7 3.8 %shard_map.115 = (f32[32,48,128]{2,1,0:T(8,128)S(1)}, f32[8,48,128]{2,1,0:T(8,128)S(1)}, f32[32,8,128]{2,1,0:T(8,128)S(1)}, f32[32,48,128]{2,1,0:T(8,128)S(1)}, ...) custom-call(s32[8,256]{1,0:T(8,128)S(1)} %get-tuple-element.49.refs_, ...), custom_call_target="tpu_custom_call" | custom-call | flops 11796480 | bytes 4718592 | tf_op jit(solution)/shard_map/pallas_call | solution.py:403
  37.5 2.3 %collective-permute-done.7.refs_4_ = f32[4,48,128]{2,1,0:T(8,128)S(1)} collective-permute-done((f32[4,48,128]{2,1,0:T(8,128)S(1)}, f32[4,48,128]{2,1,0:T(8,128)S(1)}, u32[]{:S(2)}, u32[]{:S(2)}) %collective-permute-start.7) | collective-permute-done | bytes 98336 | tf_op jit(solution)/shard_map/ppermute | solution.py:901
  39.8 1.0 %collective-permute-done.8.refs_5_ = f32[4,48,128]{2,1,0:T(8,128)S(1)} collective-permute-done((f32[4,48,128]{2,1,0:T(8,128)S(1)}, f32[4,48,128]{2,1,0:T(8,128)S(1)}, u32[]{:S(2)}, u32[]{:S(2)}) %collective-permute-start.8) | collective-permute-done | bytes 98336 | tf_op jit(solution)/shard_map/ppermute | solution.py:904
  40.7 0.1 halo_step.5
  41.1 4.8 %collective-permute-start.12 = (f32[4,48,128]{2,1,0:T(8,128)S(1)}, f32[4,48,128]{2,1,0:T(8,128)S(1)}, u32[]{:S(2)}, u32[]{:S(2)}) collective-permute-start(f32[4,48,128]{2,1,0:T(8,128)S(1)} %get-tuple-element.76.refs_2_), channel_id=1, source_target_pairs={{6,8},{8,6},{14,0},{0,14},{7,9},{9,7},{15,1},{1,15},{22,24},{24,22... | collective-permute-start | bytes 294920 | tf_op jit(solution)/shard_map/ppermute | solution.py:901
  45.9 2.3 %shard_map.116 = (f32[32,48,128]{2,1,0:T(8,128)S(1)}, f32[8,48,128]{2,1,0:T(8,128)S(1)}, f32[32,8,128]{2,1,0:T(8,128)S(1)}, f32[24,16,128]{2,1,0:T(8,128)S(1)}) custom-call(f32[32,48,128]{2,1,0:T(8,128)S(1)} %get-tuple-element.72.refs_0_, f32[32,48,128]{2,1,0:T(8,128)S(1)} %get-tuple-element.73.refs_1_, f32[4,48,128]{2,1,0:T(8,128)S(1)} %get-tuple-element.76.refs_2_, ...), custom_call_target="tpu_custom_call" | custom-call | flops 11796480 | bytes 4718592 | tf_op jit(solution)/shard_map/pallas_call | solution.py:403
  48.2 0.6 last_step.1
  48.8 3.0 %collective-permute-start.14 = (f32[224,128]{1,0:T(8,128)S(1)}, f32[224,128]{1,0:T(8,128)S(1)}, u32[]{:S(2)}, u32[]{:S(2)}) collective-permute-start(f32[224,128]{1,0:T(8,128)S(1)} %get-tuple-element.93), channel_id=1, source_target_pairs={{0,8},{2,10},{4,12},{6,14},{8,0},{10,2},{12,4},{14,6},{1,9},{3,11}... | collective-permute-start | bytes 344072 | tf_op jit(solution)/shard_map/ppermute | solution.py:948
  51.8 0.2 last_far.1
  52.1 0.1 collective-permute-start.15
  52.2 3.2 %collective-permute-done.13.refs_2_ = f32[224,128]{1,0:T(8,128)S(1)} collective-permute-done((f32[224,128]{1,0:T(8,128)S(1)}, f32[224,128]{1,0:T(8,128)S(1)}, u32[]{:S(2)}, u32[]{:S(2)}) %collective-permute-start.13) | collective-permute-done | bytes 114720 | tf_op jit(solution)/shard_map/ppermute | solution.py:941
  55.3 1.2 %early_image.1 = (f32[17,16,768]{2,1,0:T(8,128)S(1)}, s32[8,128]{1,0:T(8,128)S(1)}) custom-call(s32[17]{0:T(128)} %lags_ref.1, f32[4,96,128]{2,1,0:T(8,128)S(1)} %get-tuple-element.88.refs_1_, f32[224,128]{1,0:T(8,128)S(1)} %collective-permute-done.13.refs_2_), custom_call_target="tpu_custom_call" | custom-call | flops 2088960 | bytes 1671168 | tf_op jit(solution)/shard_map/early_image/pallas_call | solution.py:857
  56.6 0.9 %write_out.1 = f32[32,48,128]{2,1,0:T(8,128)} custom-call(f32[32,48,128]{2,1,0:T(8,128)S(1)} %get-tuple-element.87.level_ref), custom_call_target="tpu_custom_call" | custom-call | bytes 1572864 | tf_op jit(solution)/shard_map/write_out/pallas_call | solution.py:743
  57.4 1.1 %pack_own.1.refs_1_ = f32[17,96,128]{2,1,0:T(8,128)S(1)} custom-call(s32[17]{0:T(128)} %lags_ref.1, f32[24,16,128]{2,1,0:T(8,128)S(1)} %get-tuple-element.91.even_ref, bf16[512,512]{1,0:T(8,128)(2,1)S(1)} %get-tuple-element.92.matrix_ref), custom_call_target="tpu_custom_call" | custom-call | flops 50331648 | bytes 786432 | tf_op jit(solution)/shard_map/pack_own/pallas_call | solution.py:576
  58.6 1.1 %last_image.1 = f32[17,16,768]{2,1,0:T(8,128)} custom-call(s32[8,128]{1,0:T(8,128)S(1)} %get-tuple-element.90.refs_0_, f32[17,96,128]{2,1,0:T(8,128)S(1)} %pack_own.1.refs_1_, f32[224,128]{1,0:T(8,128)S(1)} %collective-permute-done.14.refs_2_, f32[48,128]{1,0:T(8,128)S(1)} %collective-permute-done.15.refs_3_, f32[17,16,768]{2,1,0:T(8,128)S(1)} %get-tuple-element.95.refs_4_), custom_call_target="tpu_custom_call" | custom-call | flops 2088960 | bytes 1671168 | tf_op jit(solution)/shard_map/last_image/pallas_call | solution.py:857
  (16 shorter events, 0.3 us)
Async XLA Ops:
  0.6 12.9 %copy-start = (f32[32,48,128]{2,1,0:T(8,128)S(1)}, f32[32,48,128]{2,1,0:T(8,128)}, u32[]{:S(2)}) copy-start(f32[32,48,128]{2,1,0:T(8,128)} %field_ref.1) | copy-start | bytes 2359300
  1.8 15.8 %collective-permute-start.3 = (f32[32,8,128]{2,1,0:T(8,128)S(1)}, f32[32,8,128]{2,1,0:T(8,128)S(1)}, u32[]{:S(2)}, u32[]{:S(2)}) collective-permute-start(f32[32,8,128]{2,1,0:T(8,128)S(1)} %get-tuple-element.58), channel_id=1, source_target_pairs={{0,1},{1,0},{2,3},{3,2},{4,5},{5,4},{6,7},{7,6},{8,9},{9,8},{10,11... | collective-permute-start | bytes 393224 | tf_op jit(solution)/shard_map/ppermute | solution.py:916
  2.3 14.6 %collective-permute-start.1 = (f32[4,48,128]{2,1,0:T(8,128)S(1)}, f32[4,48,128]{2,1,0:T(8,128)S(1)}, u32[]{:S(2)}, u32[]{:S(2)}) collective-permute-start(f32[4,48,128]{2,1,0:T(8,128)S(1)} %get-tuple-element.57), channel_id=1, source_target_pairs={{2,0},{6,4},{10,8},{14,12},{3,1},{7,5},{11,9},{15,13},{18,16},{22,... | collective-permute-start | bytes 294920 | tf_op jit(solution)/shard_map/ppermute | solution.py:913
  3.6 13.3 %collective-permute-start.2 = (f32[4,48,128]{2,1,0:T(8,128)S(1)}, f32[4,48,128]{2,1,0:T(8,128)S(1)}, u32[]{:S(2)}, u32[]{:S(2)}) collective-permute-start(f32[4,48,128]{2,1,0:T(8,128)S(1)} %get-tuple-element.57), channel_id=1, source_target_pairs={{0,2},{4,6},{8,10},{12,14},{1,3},{5,7},{9,11},{13,15},{16,18},{20,... | collective-permute-start | bytes 294920 | tf_op jit(solution)/shard_map/ppermute | solution.py:915
  8.2 9.4 %collective-permute-start = (f32[4,48,128]{2,1,0:T(8,128)S(1)}, f32[4,48,128]{2,1,0:T(8,128)S(1)}, u32[]{:S(2)}, u32[]{:S(2)}) collective-permute-start(f32[4,48,128]{2,1,0:T(8,128)S(1)} %get-tuple-element.56), channel_id=1, source_target_pairs={{6,8},{8,6},{14,0},{0,14},{7,9},{9,7},{15,1},{1,15},{22,24},{24,22... | collective-permute-start | bytes 294920 | tf_op jit(solution)/shard_map/ppermute | solution.py:901
  17.7 12.0 %collective-permute-start.6 = (f32[32,8,128]{2,1,0:T(8,128)S(1)}, f32[32,8,128]{2,1,0:T(8,128)S(1)}, u32[]{:S(2)}, u32[]{:S(2)}) collective-permute-start(f32[32,8,128]{2,1,0:T(8,128)S(1)} %get-tuple-element.61.refs_5_), channel_id=1, source_target_pairs={{0,1},{1,0},{2,3},{3,2},{4,5},{5,4},{6,7},{7,6},{8,9},{9,8},{10,11... | collective-permute-start | bytes 393224 | tf_op jit(solution)/shard_map/ppermute | solution.py:905
  17.8 9.9 %collective-permute-start.4 = (f32[4,48,128]{2,1,0:T(8,128)S(1)}, f32[4,48,128]{2,1,0:T(8,128)S(1)}, u32[]{:S(2)}, u32[]{:S(2)}) collective-permute-start(f32[4,48,128]{2,1,0:T(8,128)S(1)} %get-tuple-element.59.refs_3_), channel_id=1, source_target_pairs={{6,8},{8,6},{14,0},{0,14},{7,9},{9,7},{15,1},{1,15},{22,24},{24,22... | collective-permute-start | bytes 294920 | tf_op jit(solution)/shard_map/ppermute | solution.py:901
  23.2 6.4 %collective-permute-start.5 = (f32[4,48,128]{2,1,0:T(8,128)S(1)}, f32[4,48,128]{2,1,0:T(8,128)S(1)}, u32[]{:S(2)}, u32[]{:S(2)}) collective-permute-start(f32[4,48,128]{2,1,0:T(8,128)S(1)} %get-tuple-element.60.refs_4_), channel_id=1, source_target_pairs={{0,2},{2,0},{4,6},{6,4},{8,10},{10,8},{12,14},{14,12},{1,3},{3,1},... | collective-permute-start | bytes 294920 | tf_op jit(solution)/shard_map/ppermute | solution.py:904
  29.8 10.9 %collective-permute-start.9 = (f32[32,8,128]{2,1,0:T(8,128)S(1)}, f32[32,8,128]{2,1,0:T(8,128)S(1)}, u32[]{:S(2)}, u32[]{:S(2)}) collective-permute-start(f32[32,8,128]{2,1,0:T(8,128)S(1)} %get-tuple-element.69.refs_5_), channel_id=1, source_target_pairs={{0,1},{1,0},{2,3},{3,2},{4,5},{5,4},{6,7},{7,6},{8,9},{9,8},{10,11... | collective-permute-start | bytes 393224 | tf_op jit(solution)/shard_map/ppermute | solution.py:905
  29.9 9.8 %collective-permute-start.7 = (f32[4,48,128]{2,1,0:T(8,128)S(1)}, f32[4,48,128]{2,1,0:T(8,128)S(1)}, u32[]{:S(2)}, u32[]{:S(2)}) collective-permute-start(f32[4,48,128]{2,1,0:T(8,128)S(1)} %get-tuple-element.67.refs_3_), channel_id=1, source_target_pairs={{6,8},{8,6},{14,0},{0,14},{7,9},{9,7},{15,1},{1,15},{22,24},{24,22... | collective-permute-start | bytes 294920 | tf_op jit(solution)/shard_map/ppermute | solution.py:901
  33.7 7.1 %collective-permute-start.8 = (f32[4,48,128]{2,1,0:T(8,128)S(1)}, f32[4,48,128]{2,1,0:T(8,128)S(1)}, u32[]{:S(2)}, u32[]{:S(2)}) collective-permute-start(f32[4,48,128]{2,1,0:T(8,128)S(1)} %get-tuple-element.68.refs_4_), channel_id=1, source_target_pairs={{0,2},{2,0},{4,6},{6,4},{8,10},{10,8},{12,14},{14,12},{1,3},{3,1},... | collective-permute-start | bytes 294920 | tf_op jit(solution)/shard_map/ppermute | solution.py:904
  40.9 7.3 %collective-permute-start.11 = (f32[32,8,128]{2,1,0:T(8,128)S(1)}, f32[32,8,128]{2,1,0:T(8,128)S(1)}, u32[]{:S(2)}, u32[]{:S(2)}) collective-permute-start(f32[32,8,128]{2,1,0:T(8,128)S(1)} %get-tuple-element.78.refs_4_), channel_id=1, source_target_pairs={{0,1},{1,0},{2,3},{3,2},{4,5},{5,4},{6,7},{7,6},{8,9},{9,8},{10,11... | collective-permute-start | bytes 393224 | tf_op jit(solution)/shard_map/ppermute | solution.py:905
  41.0 7.2 %collective-permute-start.10 = (f32[4,48,128]{2,1,0:T(8,128)S(1)}, f32[4,48,128]{2,1,0:T(8,128)S(1)}, u32[]{:S(2)}, u32[]{:S(2)}) collective-permute-start(f32[4,48,128]{2,1,0:T(8,128)S(1)} %get-tuple-element.77.refs_3_), channel_id=1, source_target_pairs={{0,2},{2,0},{4,6},{6,4},{8,10},{10,8},{12,14},{14,12},{1,3},{3,1},... | collective-permute-start | bytes 294920 | tf_op jit(solution)/shard_map/ppermute | solution.py:904
  41.1 10.8 %collective-permute-start.12 = (f32[4,48,128]{2,1,0:T(8,128)S(1)}, f32[4,48,128]{2,1,0:T(8,128)S(1)}, u32[]{:S(2)}, u32[]{:S(2)}) collective-permute-start(f32[4,48,128]{2,1,0:T(8,128)S(1)} %get-tuple-element.76.refs_2_), channel_id=1, source_target_pairs={{6,8},{8,6},{14,0},{0,14},{7,9},{9,7},{15,1},{1,15},{22,24},{24,22... | collective-permute-start | bytes 294920 | tf_op jit(solution)/shard_map/ppermute | solution.py:901
  45.9 9.5 %collective-permute-start.13 = (f32[224,128]{1,0:T(8,128)S(1)}, f32[224,128]{1,0:T(8,128)S(1)}, u32[]{:S(2)}, u32[]{:S(2)}) collective-permute-start(f32[224,128]{1,0:T(8,128)S(1)} %get-tuple-element.89), channel_id=1, source_target_pairs={{0,8},{2,10},{4,12},{6,14},{8,0},{10,2},{12,4},{14,6},{1,9},{3,11}... | collective-permute-start | bytes 344072 | tf_op jit(solution)/shard_map/ppermute | solution.py:941
  48.8 9.7 %collective-permute-start.14 = (f32[224,128]{1,0:T(8,128)S(1)}, f32[224,128]{1,0:T(8,128)S(1)}, u32[]{:S(2)}, u32[]{:S(2)}) collective-permute-start(f32[224,128]{1,0:T(8,128)S(1)} %get-tuple-element.93), channel_id=1, source_target_pairs={{0,8},{2,10},{4,12},{6,14},{8,0},{10,2},{12,4},{14,6},{1,9},{3,11}... | collective-permute-start | bytes 344072 | tf_op jit(solution)/shard_map/ppermute | solution.py:948
  52.1 6.5 %collective-permute-start.15 = (f32[48,128]{1,0:T(8,128)S(1)}, f32[48,128]{1,0:T(8,128)S(1)}, u32[]{:S(2)}, u32[]{:S(2)}) collective-permute-start(f32[48,128]{1,0:T(8,128)S(1)} %get-tuple-element.94), channel_id=1, source_target_pairs={{0,8},{2,10},{4,12},{6,14},{8,0},{10,2},{12,4},{14,6},{1,9},{3,11}... | collective-permute-start | bytes 73736 | tf_op jit(solution)/shard_map/ppermute | solution.py:951

commit v9 on v7

--- a/solution.py
+++ b/solution.py
@@ -219,19 +219,22 @@
         band = jnp.zeros((count_z, count_z), F32)
         for offset, weight in enumerate(BAND, 1):
             band = jnp.where(gap == offset, weight, band)
-        band = band.astype(BF16)
+        band = jnp.concatenate([band.astype(BF16)] * 3, axis=0)
 
         chunk = 8
 
         def multiply(index, _):
             start = pl.multiple_of(index * chunk, chunk)
             values = padded[pl.ds(start + WIDTH, chunk), columns]
-            zpart[pl.ds(start, chunk)] = exact_dot(
-                values.reshape(chunk * count_y, count_z), band
+            terms = jnp.concatenate(split3(values.reshape(chunk * count_y, count_z)), axis=1)
+            zpart[pl.ds(start, chunk)] = jnp.dot(
+                terms, band, preferred_element_type=F32
             ).reshape(chunk, count_y, count_z)
             return 0
 
-        lax.fori_loop(0, count_x // chunk, multiply, 0)
+        chunks = count_x // chunk
+        if first or last:
+            lax.fori_loop(0, chunks, multiply, 0)
 
         if first:
             for copy in copies[:4]:
@@ -262,7 +265,8 @@
             )
 
             def spread_of(step):
-                return split3(jnp.where(at_z, waves_ref[step : step + 1, :], 0.0))
+                terms = split3(jnp.where(at_z, waves_ref[step : step + 1, :], 0.0))
+                return jnp.concatenate(terms, axis=1)
 
             spreads = [(addpart, spread_of(number))]
             if ahead:
@@ -274,19 +278,20 @@
                 jnp.int32, (chunk * count_y, count_j), 0
             )
             hit = jnp.where(here == home, 1.0, 0.0).astype(BF16)
+            hit = jnp.concatenate([hit] * 3, axis=1)
             for target, spread in spreads:
-                added = [
-                    lax.dot_general(
-                        hit, part, (((1,), (1,)), ((), ())), preferred_element_type=F32
-                    )
-                    for part in spread
-                ]
-                added = (added[2] + added[1]) + added[0]
+                added = lax.dot_general(
+                    hit, spread, (((1,), (1,)), ((), ())), preferred_element_type=F32
+                )
                 target[pl.ds(start, chunk)] = added.reshape(chunk, count_y, count_z)
             return 0
 
+        def both(index, _):
+            multiply(index, 0)
+            return inject(index, 0)
+
         if not last:
-            lax.fori_loop(0, count_x // chunk, inject, 0)
+            lax.fori_loop(0, chunks, inject if first else both, 0)
         if first:
             for copy in copies[4:]:
                 copy.wait()

time: 57.4 us -> 57.3 us (level)
  Pallas kernels: 20.1 us -> 19 us
  waiting for transfers between devices: 11.5 us -> 12.6 us
    ppermute x4, waiting for transfers between devices: 3.34 us -> 4.52 us  [send_far(): return lax.ppermute(far, 'gx', far_pairs)]
    pallas_call x4, Pallas kernels: 13.5 us -> 12.3 us  [inner_step(): pl.pallas_call(kernel, out_shape=tuple(outs), in_specs=specs, out_specs=(...]
  transfers between devices with their start and end apart: 15 -> 15, of which waited for: 8 -> 7; matrix products, arithmetic and copies ran while one was open for 0% -> 0% of each run, Pallas kernels for 31% -> 29%
where the time goes in v9:
time: 57.3 us; the launch traced here: 56.8 us
  starting transfers between devices  24.4 us (43%)
  Pallas kernels  19 us (33%)
  waiting for transfers between devices  12.6 us (22%)
  between operations  0.88 us (2%)
    ppermute x4, starting transfers between devices, send_far(): return lax.ppermute(far, 'gx', far_pairs)  20.2 us
    pallas_call x4, Pallas kernels, inner_step(): pl.pallas_call(kernel, out_shape=tuple(outs), in_specs=specs, out_specs=(...  12.3 us
    ppermute x4, waiting for transfers between devices, send_near(): near = lax.ppermute(near, 'gx', near_pairs)  4.99 us
    ppermute x4, waiting for transfers between devices, send_far(): return lax.ppermute(far, 'gx', far_pairs)  4.52 us
    ppermute x1, waiting for transfers between devices, body(): other_early = lax.ppermute(sent_early, 'gx', across)  3.04 us
    ppermute x1, starting transfers between devices, body(): other_late = lax.ppermute(sent_late, 'gx', across)  2.97 us
    pallas_call x2, Pallas kernels, lag_image(): pl.pallas_call(kernel, out_shape=image if last else (image, shape(8, coun...  2.26 us
  transfers between devices with their start and end apart: 15, of which 7 were waited for; matrix products, arithmetic and copies ran while one was open for 0% of the time, Pallas kernels for 29%

profile of v9, /device:TPU:0, one launch (start us, length us, event | category | flops | bytes accessed | tf_op | source)
XLA Modules:
  0.0 56.8 jit_solution(10528145129557717659)
XLA Ops:
  0.6 1.1 %first_faces.1 = (f32[4,48,128]{2,1,0:T(8,128)S(1)}, f32[4,48,128]{2,1,0:T(8,128)S(1)}, f32[32,8,128]{2,1,0:T(8,128)S(1)}) custom-call(f32[32,48,128]{2,1,0:T(8,128)} %field_ref.1), custom_call_target="tpu_custom_call" | custom-call | tf_op jit(solution)/shard_map/first_faces/pallas_call | solution.py:93
  1.8 0.6 collective-permute-start.2
  2.3 7.5 %collective-permute-start = (f32[4,48,128]{2,1,0:T(8,128)S(1)}, f32[4,48,128]{2,1,0:T(8,128)S(1)}, u32[]{:S(2)}, u32[]{:S(2)}) collective-permute-start(f32[4,48,128]{2,1,0:T(8,128)S(1)} %get-tuple-element.56), channel_id=1, source_target_pairs={{6,8},{8,6},{14,0},{0,14},{7,9},{9,7},{15,1},{1,15},{22,24},{24,22... | collective-permute-start | bytes 294920 | tf_op jit(solution)/shard_map/ppermute | solution.py:890
  9.8 0.1 collective-permute-start.1
  9.9 3.4 %shard_map.113 = (f32[32,48,128]{2,1,0:T(8,128)S(1)}, f32[8,48,128]{2,1,0:T(8,128)S(1)}, f32[32,8,128]{2,1,0:T(8,128)S(1)}, f32[32,48,128]{2,1,0:T(8,128)S(1)}, ...) custom-call(s32[3,8]{1,0:T(4,128)} %refs_0_.2, ...), custom_call_target="tpu_custom_call" | custom-call | flops 11796480 | bytes 4718592 | tf_op jit(solution)/shard_map/pallas_call | solution.py:399
  13.3 2.0 %collective-permute-done.1.refs_5_ = f32[4,48,128]{2,1,0:T(8,128)S(1)} collective-permute-done((f32[4,48,128]{2,1,0:T(8,128)S(1)}, f32[4,48,128]{2,1,0:T(8,128)S(1)}, u32[]{:S(2)}, u32[]{:S(2)}) %collective-permute-start.1) | collective-permute-done | bytes 98336 | tf_op jit(solution)/shard_map/ppermute | solution.py:893
  15.3 0.1 halo_step.3
  15.5 0.1 collective-permute-start.5
  15.6 4.2 %collective-permute-start.3 = (f32[4,48,128]{2,1,0:T(8,128)S(1)}, f32[4,48,128]{2,1,0:T(8,128)S(1)}, u32[]{:S(2)}, u32[]{:S(2)}) collective-permute-start(f32[4,48,128]{2,1,0:T(8,128)S(1)} %get-tuple-element.59.refs_3_), channel_id=1, source_target_pairs={{6,8},{8,6},{14,0},{0,14},{7,9},{9,7},{15,1},{1,15},{22,24},{24,22... | collective-permute-start | bytes 294920 | tf_op jit(solution)/shard_map/ppermute | solution.py:890
  19.9 3.3 %shard_map.114 = (f32[32,48,128]{2,1,0:T(8,128)S(1)}, f32[8,48,128]{2,1,0:T(8,128)S(1)}, f32[32,8,128]{2,1,0:T(8,128)S(1)}, f32[32,48,128]{2,1,0:T(8,128)S(1)}, f32[32,48,128]{2,1,0:T(8,128)S(1)}) custom-call(s32[8,256]{1,0:T(8,128)S(1)} %get-tuple-element.49.refs_0_, f32[8,256]{1,0:T(8,128)S(1)} %get-tuple-element.50.refs_1_, ...), custom_call_target="tpu_custom_call" | custom-call | flops 11796480 | bytes 4718592 | tf_op jit(solution)/shard_map/pallas_call | solution.py:399
  23.2 2.3 %collective-permute-done.3.refs_4_ = f32[4,48,128]{2,1,0:T(8,128)S(1)} collective-permute-done((f32[4,48,128]{2,1,0:T(8,128)S(1)}, f32[4,48,128]{2,1,0:T(8,128)S(1)}, u32[]{:S(2)}, u32[]{:S(2)}) %collective-permute-start.3) | collective-permute-done | bytes 98336 | tf_op jit(solution)/shard_map/ppermute | solution.py:890
  25.4 1.4 %collective-permute-done.4.refs_5_ = f32[4,48,128]{2,1,0:T(8,128)S(1)} collective-permute-done((f32[4,48,128]{2,1,0:T(8,128)S(1)}, f32[4,48,128]{2,1,0:T(8,128)S(1)}, u32[]{:S(2)}, u32[]{:S(2)}) %collective-permute-start.4) | collective-permute-done | bytes 98336 | tf_op jit(solution)/shard_map/ppermute | solution.py:893
  26.9 0.1 halo_step.4
  27.1 4.3 %collective-permute-start.6 = (f32[4,48,128]{2,1,0:T(8,128)S(1)}, f32[4,48,128]{2,1,0:T(8,128)S(1)}, u32[]{:S(2)}, u32[]{:S(2)}) collective-permute-start(f32[4,48,128]{2,1,0:T(8,128)S(1)} %get-tuple-element.67.refs_3_), channel_id=1, source_target_pairs={{6,8},{8,6},{14,0},{0,14},{7,9},{9,7},{15,1},{1,15},{22,24},{24,22... | collective-permute-start | bytes 294920 | tf_op jit(solution)/shard_map/ppermute | solution.py:890
  31.4 0.1 collective-permute-start.7
  31.5 3.3 %shard_map.115 = (f32[32,48,128]{2,1,0:T(8,128)S(1)}, f32[8,48,128]{2,1,0:T(8,128)S(1)}, f32[32,8,128]{2,1,0:T(8,128)S(1)}, f32[32,48,128]{2,1,0:T(8,128)S(1)}, ...) custom-call(s32[8,256]{1,0:T(8,128)S(1)} %get-tuple-element.49.refs_, ...), custom_call_target="tpu_custom_call" | custom-call | flops 11796480 | bytes 4718592 | tf_op jit(solution)/shard_map/pallas_call | solution.py:399
  34.9 2.1 %collective-permute-done.6.refs_4_ = f32[4,48,128]{2,1,0:T(8,128)S(1)} collective-permute-done((f32[4,48,128]{2,1,0:T(8,128)S(1)}, f32[4,48,128]{2,1,0:T(8,128)S(1)}, u32[]{:S(2)}, u32[]{:S(2)}) %collective-permute-start.6) | collective-permute-done | bytes 98336 | tf_op jit(solution)/shard_map/ppermute | solution.py:890
  37.0 1.5 %collective-permute-done.7.refs_5_ = f32[4,48,128]{2,1,0:T(8,128)S(1)} collective-permute-done((f32[4,48,128]{2,1,0:T(8,128)S(1)}, f32[4,48,128]{2,1,0:T(8,128)S(1)}, u32[]{:S(2)}, u32[]{:S(2)}) %collective-permute-start.7) | collective-permute-done | bytes 98336 | tf_op jit(solution)/shard_map/ppermute | solution.py:893
  38.5 0.1 halo_step.5
  38.7 0.1 collective-permute-start.10
  38.8 4.2 %collective-permute-start.11 = (f32[4,48,128]{2,1,0:T(8,128)S(1)}, f32[4,48,128]{2,1,0:T(8,128)S(1)}, u32[]{:S(2)}, u32[]{:S(2)}) collective-permute-start(f32[4,48,128]{2,1,0:T(8,128)S(1)} %get-tuple-element.76.refs_2_), channel_id=1, source_target_pairs={{6,8},{8,6},{14,0},{0,14},{7,9},{9,7},{15,1},{1,15},{22,24},{24,22... | collective-permute-start | bytes 294920 | tf_op jit(solution)/shard_map/ppermute | solution.py:890
  43.1 0.1 collective-permute-start.12
  43.2 2.3 %shard_map.116 = (f32[32,48,128]{2,1,0:T(8,128)S(1)}, f32[8,48,128]{2,1,0:T(8,128)S(1)}, f32[32,8,128]{2,1,0:T(8,128)S(1)}, f32[24,16,128]{2,1,0:T(8,128)S(1)}) custom-call(f32[32,48,128]{2,1,0:T(8,128)S(1)} %get-tuple-element.72.refs_0_, f32[32,48,128]{2,1,0:T(8,128)S(1)} %get-tuple-element.73.refs_1_, f32[4,48,128]{2,1,0:T(8,128)S(1)} %get-tuple-element.76.refs_2_, ...), custom_call_target="tpu_custom_call" | custom-call | flops 11796480 | bytes 4718592 | tf_op jit(solution)/shard_map/pallas_call | solution.py:399
  45.5 0.6 %last_step.1 = (f32[32,48,128]{2,1,0:T(8,128)S(1)}, f32[24,16,128]{2,1,0:T(8,128)S(1)}, f32[224,128]{1,0:T(8,128)S(1)}) custom-call(f32[8,128]{1,0:T(8,128)S(1)} %get-tuple-element.71.flag_ref, f32[24,16,128]{2,1,0:T(8,128)S(1)} %get-tuple-element.80.even_ref, f32[32,48,128]{2,1,0:T(8,128)S(1)} %get-tuple-element.81.current_ref, ...), custom_call_target="tpu_custom_call", output_to_operand_aliasing={{0}: (2, {})} | custom-call | flops 1966080 | bytes 2359296 | tf_op jit(solution)/shard_map/last_step/pallas_call | solution.py:646
  46.1 3.0 %collective-permute-start.13 = (f32[224,128]{1,0:T(8,128)S(1)}, f32[224,128]{1,0:T(8,128)S(1)}, u32[]{:S(2)}, u32[]{:S(2)}) collective-permute-start(f32[224,128]{1,0:T(8,128)S(1)} %get-tuple-element.93), channel_id=1, source_target_pairs={{0,8},{2,10},{4,12},{6,14},{8,0},{10,2},{12,4},{14,6},{1,9},{3,11}... | collective-permute-start | bytes 344072 | tf_op jit(solution)/shard_map/ppermute | solution.py:929
  49.1 0.1 collective-permute-done.11.far_ref
  49.2 0.3 last_far.1
  49.5 3.0 %collective-permute-done.12.refs_2_ = f32[224,128]{1,0:T(8,128)S(1)} collective-permute-done((f32[224,128]{1,0:T(8,128)S(1)}, f32[224,128]{1,0:T(8,128)S(1)}, u32[]{:S(2)}, u32[]{:S(2)}) %collective-permute-start.12) | collective-permute-done | bytes 114720 | tf_op jit(solution)/shard_map/ppermute | solution.py:922
  52.5 1.2 %early_image.1 = (f32[17,16,768]{2,1,0:T(8,128)S(1)}, s32[8,128]{1,0:T(8,128)S(1)}) custom-call(s32[17]{0:T(128)} %lags_ref.1, f32[4,96,128]{2,1,0:T(8,128)S(1)} %get-tuple-element.88.refs_1_, f32[224,128]{1,0:T(8,128)S(1)} %collective-permute-done.12.refs_2_), custom_call_target="tpu_custom_call" | custom-call | flops 2088960 | bytes 1671168 | tf_op jit(solution)/shard_map/early_image/pallas_call | solution.py:846
  53.7 0.9 %write_out.1 = f32[32,48,128]{2,1,0:T(8,128)} custom-call(f32[32,48,128]{2,1,0:T(8,128)S(1)} %get-tuple-element.87.level_ref), custom_call_target="tpu_custom_call" | custom-call | bytes 1572864 | tf_op jit(solution)/shard_map/write_out/pallas_call | solution.py:732
  54.6 1.1 %pack_own.1.refs_1_ = f32[17,96,128]{2,1,0:T(8,128)S(1)} custom-call(s32[17]{0:T(128)} %lags_ref.1, f32[24,16,128]{2,1,0:T(8,128)S(1)} %get-tuple-element.91.even_ref, bf16[512,512]{1,0:T(8,128)(2,1)S(1)} %get-tuple-element.92.matrix_ref), custom_call_target="tpu_custom_call" | custom-call | flops 50331648 | bytes 786432 | tf_op jit(solution)/shard_map/pack_own/pallas_call | solution.py:565
  55.7 1.1 %last_image.1 = f32[17,16,768]{2,1,0:T(8,128)} custom-call(s32[8,128]{1,0:T(8,128)S(1)} %get-tuple-element.90.refs_0_, f32[17,96,128]{2,1,0:T(8,128)S(1)} %pack_own.1.refs_1_, f32[224,128]{1,0:T(8,128)S(1)} %collective-permute-done.13.refs_2_, f32[48,128]{1,0:T(8,128)S(1)} %collective-permute-done.14.refs_3_, f32[17,16,768]{2,1,0:T(8,128)S(1)} %get-tuple-element.95.refs_4_), custom_call_target="tpu_custom_call" | custom-call | flops 2088960 | bytes 1671168 | tf_op jit(solution)/shard_map/last_image/pallas_call | solution.py:846
  (14 shorter events, 0.3 us)
Async XLA Ops:
  0.6 9.2 %copy-start = (f32[32,48,128]{2,1,0:T(8,128)S(1)}, f32[32,48,128]{2,1,0:T(8,128)}, u32[]{:S(2)}) copy-start(f32[32,48,128]{2,1,0:T(8,128)} %field_ref.1) | copy-start | bytes 2359300
  1.8 13.6 %collective-permute-start.2 = (f32[32,8,128]{2,1,0:T(8,128)S(1)}, f32[32,8,128]{2,1,0:T(8,128)S(1)}, u32[]{:S(2)}, u32[]{:S(2)}) collective-permute-start(f32[32,8,128]{2,1,0:T(8,128)S(1)} %get-tuple-element.58), channel_id=1, source_target_pairs={{0,1},{1,0},{2,3},{3,2},{4,5},{5,4},{6,7},{7,6},{8,9},{9,8},{10,11... | collective-permute-start | bytes 393224 | tf_op jit(solution)/shard_map/ppermute | solution.py:894
  2.3 11.0 %collective-permute-start = (f32[4,48,128]{2,1,0:T(8,128)S(1)}, f32[4,48,128]{2,1,0:T(8,128)S(1)}, u32[]{:S(2)}, u32[]{:S(2)}) collective-permute-start(f32[4,48,128]{2,1,0:T(8,128)S(1)} %get-tuple-element.56), channel_id=1, source_target_pairs={{6,8},{8,6},{14,0},{0,14},{7,9},{9,7},{15,1},{1,15},{22,24},{24,22... | collective-permute-start | bytes 294920 | tf_op jit(solution)/shard_map/ppermute | solution.py:890
  9.8 5.5 %collective-permute-start.1 = (f32[4,48,128]{2,1,0:T(8,128)S(1)}, f32[4,48,128]{2,1,0:T(8,128)S(1)}, u32[]{:S(2)}, u32[]{:S(2)}) collective-permute-start(f32[4,48,128]{2,1,0:T(8,128)S(1)} %get-tuple-element.57), channel_id=1, source_target_pairs={{0,2},{2,0},{4,6},{6,4},{8,10},{10,8},{12,14},{14,12},{1,3},{3,1},... | collective-permute-start | bytes 294920 | tf_op jit(solution)/shard_map/ppermute | solution.py:893
  15.5 11.4 %collective-permute-start.5 = (f32[32,8,128]{2,1,0:T(8,128)S(1)}, f32[32,8,128]{2,1,0:T(8,128)S(1)}, u32[]{:S(2)}, u32[]{:S(2)}) collective-permute-start(f32[32,8,128]{2,1,0:T(8,128)S(1)} %get-tuple-element.61.refs_5_), channel_id=1, source_target_pairs={{0,1},{1,0},{2,3},{3,2},{4,5},{5,4},{6,7},{7,6},{8,9},{9,8},{10,11... | collective-permute-start | bytes 393224 | tf_op jit(solution)/shard_map/ppermute | solution.py:894
  15.6 9.9 %collective-permute-start.3 = (f32[4,48,128]{2,1,0:T(8,128)S(1)}, f32[4,48,128]{2,1,0:T(8,128)S(1)}, u32[]{:S(2)}, u32[]{:S(2)}) collective-permute-start(f32[4,48,128]{2,1,0:T(8,128)S(1)} %get-tuple-element.59.refs_3_), channel_id=1, source_target_pairs={{6,8},{8,6},{14,0},{0,14},{7,9},{9,7},{15,1},{1,15},{22,24},{24,22... | collective-permute-start | bytes 294920 | tf_op jit(solution)/shard_map/ppermute | solution.py:890
  19.8 7.1 %collective-permute-start.4 = (f32[4,48,128]{2,1,0:T(8,128)S(1)}, f32[4,48,128]{2,1,0:T(8,128)S(1)}, u32[]{:S(2)}, u32[]{:S(2)}) collective-permute-start(f32[4,48,128]{2,1,0:T(8,128)S(1)} %get-tuple-element.60.refs_4_), channel_id=1, source_target_pairs={{0,2},{2,0},{4,6},{6,4},{8,10},{10,8},{12,14},{14,12},{1,3},{3,1},... | collective-permute-start | bytes 294920 | tf_op jit(solution)/shard_map/ppermute | solution.py:893
  27.0 11.5 %collective-permute-start.8 = (f32[32,8,128]{2,1,0:T(8,128)S(1)}, f32[32,8,128]{2,1,0:T(8,128)S(1)}, u32[]{:S(2)}, u32[]{:S(2)}) collective-permute-start(f32[32,8,128]{2,1,0:T(8,128)S(1)} %get-tuple-element.69.refs_5_), channel_id=1, source_target_pairs={{0,1},{1,0},{2,3},{3,2},{4,5},{5,4},{6,7},{7,6},{8,9},{9,8},{10,11... | collective-permute-start | bytes 393224 | tf_op jit(solution)/shard_map/ppermute | solution.py:894
  27.1 9.9 %collective-permute-start.6 = (f32[4,48,128]{2,1,0:T(8,128)S(1)}, f32[4,48,128]{2,1,0:T(8,128)S(1)}, u32[]{:S(2)}, u32[]{:S(2)}) collective-permute-start(f32[4,48,128]{2,1,0:T(8,128)S(1)} %get-tuple-element.67.refs_3_), channel_id=1, source_target_pairs={{6,8},{8,6},{14,0},{0,14},{7,9},{9,7},{15,1},{1,15},{22,24},{24,22... | collective-permute-start | bytes 294920 | tf_op jit(solution)/shard_map/ppermute | solution.py:890
  31.4 7.1 %collective-permute-start.7 = (f32[4,48,128]{2,1,0:T(8,128)S(1)}, f32[4,48,128]{2,1,0:T(8,128)S(1)}, u32[]{:S(2)}, u32[]{:S(2)}) collective-permute-start(f32[4,48,128]{2,1,0:T(8,128)S(1)} %get-tuple-element.68.refs_4_), channel_id=1, source_target_pairs={{0,2},{2,0},{4,6},{6,4},{8,10},{10,8},{12,14},{14,12},{1,3},{3,1},... | collective-permute-start | bytes 294920 | tf_op jit(solution)/shard_map/ppermute | solution.py:893
  38.7 6.8 %collective-permute-start.10 = (f32[32,8,128]{2,1,0:T(8,128)S(1)}, f32[32,8,128]{2,1,0:T(8,128)S(1)}, u32[]{:S(2)}, u32[]{:S(2)}) collective-permute-start(f32[32,8,128]{2,1,0:T(8,128)S(1)} %get-tuple-element.78.refs_4_), channel_id=1, source_target_pairs={{0,1},{1,0},{2,3},{3,2},{4,5},{5,4},{6,7},{7,6},{8,9},{9,8},{10,11... | collective-permute-start | bytes 393224 | tf_op jit(solution)/shard_map/ppermute | solution.py:894
  38.7 6.7 %collective-permute-start.9 = (f32[4,48,128]{2,1,0:T(8,128)S(1)}, f32[4,48,128]{2,1,0:T(8,128)S(1)}, u32[]{:S(2)}, u32[]{:S(2)}) collective-permute-start(f32[4,48,128]{2,1,0:T(8,128)S(1)} %get-tuple-element.77.refs_3_), channel_id=1, source_target_pairs={{0,2},{2,0},{4,6},{6,4},{8,10},{10,8},{12,14},{14,12},{1,3},{3,1},... | collective-permute-start | bytes 294920 | tf_op jit(solution)/shard_map/ppermute | solution.py:893
  38.8 10.4 %collective-permute-start.11 = (f32[4,48,128]{2,1,0:T(8,128)S(1)}, f32[4,48,128]{2,1,0:T(8,128)S(1)}, u32[]{:S(2)}, u32[]{:S(2)}) collective-permute-start(f32[4,48,128]{2,1,0:T(8,128)S(1)} %get-tuple-element.76.refs_2_), channel_id=1, source_target_pairs={{6,8},{8,6},{14,0},{0,14},{7,9},{9,7},{15,1},{1,15},{22,24},{24,22... | collective-permute-start | bytes 294920 | tf_op jit(solution)/shard_map/ppermute | solution.py:890
  43.1 9.4 %collective-permute-start.12 = (f32[224,128]{1,0:T(8,128)S(1)}, f32[224,128]{1,0:T(8,128)S(1)}, u32[]{:S(2)}, u32[]{:S(2)}) collective-permute-start(f32[224,128]{1,0:T(8,128)S(1)} %get-tuple-element.89), channel_id=1, source_target_pairs={{0,8},{2,10},{4,12},{6,14},{8,0},{10,2},{12,4},{14,6},{1,9},{3,11}... | collective-permute-start | bytes 344072 | tf_op jit(solution)/shard_map/ppermute | solution.py:922
  46.1 9.6 %collective-permute-start.13 = (f32[224,128]{1,0:T(8,128)S(1)}, f32[224,128]{1,0:T(8,128)S(1)}, u32[]{:S(2)}, u32[]{:S(2)}) collective-permute-start(f32[224,128]{1,0:T(8,128)S(1)} %get-tuple-element.93), channel_id=1, source_target_pairs={{0,8},{2,10},{4,12},{6,14},{8,0},{10,2},{12,4},{14,6},{1,9},{3,11}... | collective-permute-start | bytes 344072 | tf_op jit(solution)/shard_map/ppermute | solution.py:929
  49.4 6.2 %collective-permute-start.14 = (f32[48,128]{1,0:T(8,128)S(1)}, f32[48,128]{1,0:T(8,128)S(1)}, u32[]{:S(2)}, u32[]{:S(2)}) collective-permute-start(f32[48,128]{1,0:T(8,128)S(1)} %get-tuple-element.94), channel_id=1, source_target_pairs={{0,8},{2,10},{4,12},{6,14},{8,0},{10,2},{12,4},{14,6},{1,9},{3,11}... | collective-permute-start | bytes 73736 | tf_op jit(solution)/shard_map/ppermute | solution.py:932

commit v10 on v9

--- a/solution.py
+++ b/solution.py
@@ -114,7 +114,7 @@
 
 
 def inner_step(number, points, waves, current, faces, previous, courant, snapshots=None, matrices=None):
-    count_x, count_y, count_z = current.shape
+    count_x, count_y, count_z = courant.shape
     count_a, count_b = count_x // 2, count_y // 2
     first = faces is None
     last = number == STEPS - 1
@@ -142,18 +142,16 @@
         previous_ref, courant_ref = take(2)
         if snapshot:
             steps_ref, matrices_ref = take(2)
-        next_ref, qx_ref, qy_ref = take(3)
+        padded, next_ref, qx_ref, qy_ref = take(4)
         if first:
             kept_ref, cx_ref, cy_ref, points_ref, waves_ref = take(5)
-        if not last:
-            (whole_ref,) = take(1)
         if snapshot:
             own_out, sent_out, own_matrix, sent_matrix, flag_ref = take(5)
         if ahead:
             (ahead_ref,) = take(1)
         if last:
             (even_ref,) = take(1)
-        padded, zpart, addpart = take(3)
+        zpart, addpart = take(2)
         if last:
             addpart = added_ref
         if first:
@@ -189,14 +187,21 @@
             for copy in copies:
                 copy.start()
 
-        zero_x = jnp.zeros((WIDTH, count_y + 2 * SIDE, count_z), F32)
-        padded[pl.ds(0, WIDTH)] = zero_x
-        padded[pl.ds(count_x + WIDTH, WIDTH)] = zero_x
-        zero_y = jnp.zeros((count_x, SIDE, count_z), F32)
-        padded[rows, pl.ds(0, SIDE)] = zero_y
-        padded[rows, pl.ds(count_y + SIDE, SIDE)] = zero_y
-
-        padded[rows, columns] = current_ref[...]
+        def clear_border(level_ref):
+            zero_x = jnp.zeros((WIDTH, count_y + 2 * SIDE, count_z), F32)
+            level_ref[pl.ds(0, WIDTH)] = zero_x
+            level_ref[pl.ds(count_x + WIDTH, WIDTH)] = zero_x
+            zero_y = jnp.zeros((count_x, SIDE, count_z), F32)
+            level_ref[rows, pl.ds(0, SIDE)] = zero_y
+            level_ref[rows, pl.ds(count_y + SIDE, SIDE)] = zero_y
+
+        if first:
+            clear_border(padded)
+            padded[rows, columns] = current_ref[...]
+        if not last:
+            clear_border(next_ref)
+        next_x, next_y = (0, 0) if last else (WIDTH, SIDE)
+        before_x, before_y = (0, 0) if first else (WIDTH, SIDE)
         if not first:
             low, high = pl.ds(WIDTH, WIDTH), pl.ds(count_x, WIDTH)
 
@@ -296,26 +301,40 @@
             for copy in copies[4:]:
                 copy.wait()
 
-        def row(x, _):
-            middle = padded[x + WIDTH, columns]
-            total = CENTRE * middle + (1.0 / SCALE) * zpart[x]
-            for offset, weight in enumerate(WEIGHTS, 1):
-                paired = padded[x + WIDTH + offset, columns] + padded[x + WIDTH - offset, columns]
-                paired = paired + (
-                    padded[x + WIDTH, pl.ds(SIDE + offset, count_y)]
-                    + padded[x + WIDTH, pl.ds(SIDE - offset, count_y)]
-                )
-                total = total + weight * paired
-            if not last:
-                whole_ref[x] = middle
-            next_ref[x] = (2.0 * middle - before_ref[x] + kept_ref[x] * total) + addpart[x]
+        depth = 4
+
+        def row_group(index, _):
+            x = index * depth
+            for y in range(0, count_y, SIDE):
+                here, inner = pl.ds(y + SIDE, SIDE), pl.ds(y, SIDE)
+                lines = [padded[x + i, here] for i in range(depth + 2 * WIDTH)]
+                for j in range(depth):
+                    middle = lines[WIDTH + j]
+                    total = CENTRE * middle + (1.0 / SCALE) * zpart[x + j, inner]
+                    for offset, weight in enumerate(WEIGHTS, 1):
+                        paired = lines[WIDTH + j + offset] + lines[WIDTH + j - offset]
+                        paired = paired + (
+                            padded[x + WIDTH + j, pl.ds(y + SIDE + offset, SIDE)]
+                            + padded[x + WIDTH + j, pl.ds(y + SIDE - offset, SIDE)]
+                        )
+                        total = total + weight * paired
+                    old = before_ref[x + j + before_x, pl.ds(y + before_y, SIDE)]
+                    value = 2.0 * middle - old + kept_ref[x + j, inner] * total
+                    next_ref[x + j + next_x, pl.ds(y + next_y, SIDE)] = (
+                        value + addpart[x + j, inner]
+                    )
             return 0
 
-        lax.fori_loop(0, count_x, row, 0, unroll=4)
-
-        qx_ref[pl.ds(0, WIDTH)] = next_ref[pl.ds(0, WIDTH)]
-        qx_ref[pl.ds(WIDTH, WIDTH)] = next_ref[pl.ds(count_x - WIDTH, WIDTH)]
-        qy_ref[...] = next_ref[:, pl.ds(block, SIDE)]
+        lax.fori_loop(0, count_x // depth, row_group, 0)
+
+        next_columns = pl.ds(next_y, count_y)
+        qx_ref[pl.ds(0, WIDTH)] = next_ref[pl.ds(next_x, WIDTH), next_columns]
+        qx_ref[pl.ds(WIDTH, WIDTH)] = next_ref[
+            pl.ds(next_x + count_x - WIDTH, WIDTH), next_columns
+        ]
+        qy_ref[...] = next_ref[
+            pl.ds(next_x, count_x), pl.ds(pl.multiple_of(block + next_y, SIDE), SIDE)
+        ]
         if first:
             cx_ref[pl.ds(0, WIDTH)] = kept_ref[pl.ds(0, WIDTH)]
             cx_ref[pl.ds(WIDTH, WIDTH)] = kept_ref[pl.ds(count_x - WIDTH, WIDTH)]
@@ -334,7 +353,7 @@
             @pl.when(earlier)
             def _():
                 for b in range(count_b):
-                    even_ref[b] = even_rows(previous_ref, 0, 0, count_a, b)
+                    even_ref[b] = even_rows(previous_ref, WIDTH, SIDE, count_a, b)
 
             @pl.when(jnp.logical_not(earlier))
             def _():
@@ -348,11 +367,10 @@
     full = shape(count_x, count_y, count_z)
     slab, side = shape(2 * WIDTH, count_y, count_z), shape(count_x, SIDE, count_z)
     even = shape(count_b, count_a, count_z)
-    outs = [full, slab, side]
+    bordered = shape(count_x + 2 * WIDTH, count_y + 2 * SIDE, count_z)
+    outs = [bordered, full if last else bordered, slab, side]
     if first:
         outs += [full, slab, side, shape(8, count_j, dtype=jnp.int32), shape(8, count_j)]
-    if not last:
-        outs.append(full)
     if snapshot:
         size = GROUP * count_z
         outs += [
@@ -373,17 +391,14 @@
         operands = [points, current]
     else:
         operands = [points, waves, current]
+    aliases = {} if first else {len(operands) - 1: 0}
     specs = [place_of] * (len(operands) - 1) + [spec(pltpu.VMEM)]
     if not first:
         operands += list(faces)
         specs += [spec(pltpu.VMEM)] * 3
     operands += [previous, courant]
     specs += [place_of] * 2
-    scratch = [
-        pltpu.VMEM((count_x + 2 * WIDTH, count_y + 2 * SIDE, count_z), F32),
-        pltpu.VMEM(full.shape, F32),
-        pltpu.VMEM(full.shape, F32),
-    ]
+    scratch = [pltpu.VMEM(full.shape, F32)] * 2
     if first:
         scratch.append(pltpu.VMEM(full.shape, F32))
         scratch += [pltpu.VMEM(array.shape, array.dtype) for array in points]
@@ -402,6 +417,7 @@
         in_specs=specs,
         out_specs=(spec(pltpu.VMEM),) * len(outs),
         scratch_shapes=scratch,
+        input_output_aliases=aliases,
         compiler_params=params(20),
         cost_estimate=cost(count_x * count_y * count_z, 60, 6),
     )(*operands)
@@ -908,21 +924,21 @@
         )
     )
     halos = exchange(first_faces(field_kept))
-    next1, qx, qy, courant, cx, cy, points, waves, whole0 = inner_step(
+    whole0, next1, qx, qy, courant, cx, cy, points, waves = inner_step(
         0, raw, None, field_now, None, field_prev, courant_squared
     )
     faces = halo_step((qx, qy, cx, cy), halos)
     halos = exchange(faces)
-    next2, qx, qy, whole1, added = inner_step(1, points, waves, next1, faces, whole0, courant)
+    whole1, next2, qx, qy, added = inner_step(1, points, waves, next1, faces, whole0, courant)
     faces = halo_step((qx, qy, cx, cy), halos)
     halos = exchange(faces)
-    next3, qx, qy, whole2, own_early, sent_early, own_matrix, sent_matrix, flag = inner_step(
+    whole2, next3, qx, qy, own_early, sent_early, own_matrix, sent_matrix, flag = inner_step(
         2, points, waves, next2, faces, whole1, courant, snapshot_steps, matrices
     )
     other_early = lax.ppermute(sent_early, "gx", across)
     faces = halo_step((qx, qy, cx, cy), halos)
     far, near, side = exchange(faces)
-    next4, qx, qy, even3 = inner_step(3, added, None, next3, faces, whole2, courant)
+    _, next4, qx, qy, even3 = inner_step(3, added, None, next3, faces, whole2, courant)
     final, late, sent_late = last_step(
         flag, even3, next4, (qx, qy, cx, cy), near, side, sent_matrix
     )

time: 57.3 us -> 57.4 us (level)
  no operation moved by 1% of the time
where the time goes in v10:
time: 57.4 us; the launch traced here: 56.9 us
  starting transfers between devices  24.3 us (42%)
  Pallas kernels  19.3 us (34%)
  waiting for transfers between devices  12.3 us (21%)
  between operations  0.89 us (2%)
    ppermute x4, starting transfers between devices, send_far(): return lax.ppermute(far, 'gx', far_pairs)  20.2 us
    pallas_call x4, Pallas kernels, inner_step(): pl.pallas_call(kernel, out_shape=tuple(outs), in_specs=specs, out_specs=(...  12.7 us
    ppermute x4, waiting for transfers between devices, send_near(): near = lax.ppermute(near, 'gx', near_pairs)  4.83 us
    ppermute x4, waiting for transfers between devices, send_far(): return lax.ppermute(far, 'gx', far_pairs)  4.33 us
    ppermute x1, waiting for transfers between devices, body(): other_early = lax.ppermute(sent_early, 'gx', across)  3.12 us
    ppermute x1, starting transfers between devices, body(): other_late = lax.ppermute(sent_late, 'gx', across)  2.95 us
    pallas_call x2, Pallas kernels, lag_image(): pl.pallas_call(kernel, out_shape=image if last else (image, shape(8, coun...  2.26 us
  transfers between devices with their start and end apart: 15, of which 7 were waited for; matrix products, arithmetic and copies ran while one was open for 0% of the time, Pallas kernels for 29%

profile of v10, /device:TPU:0, one launch (start us, length us, event | category | flops | bytes accessed | tf_op | source)
XLA Modules:
  0.0 56.9 jit_solution(4780542641151599907)
XLA Ops:
  0.6 1.1 %first_faces.1 = (f32[4,48,128]{2,1,0:T(8,128)S(1)}, f32[4,48,128]{2,1,0:T(8,128)S(1)}, f32[32,8,128]{2,1,0:T(8,128)S(1)}) custom-call(f32[32,48,128]{2,1,0:T(8,128)} %field_ref.1), custom_call_target="tpu_custom_call" | custom-call | tf_op jit(solution)/shard_map/first_faces/pallas_call | solution.py:93
  1.8 0.6 collective-permute-start.2
  2.3 7.5 %collective-permute-start = (f32[4,48,128]{2,1,0:T(8,128)S(1)}, f32[4,48,128]{2,1,0:T(8,128)S(1)}, u32[]{:S(2)}, u32[]{:S(2)}) collective-permute-start(f32[4,48,128]{2,1,0:T(8,128)S(1)} %get-tuple-element.56), channel_id=1, source_target_pairs={{6,8},{8,6},{14,0},{0,14},{7,9},{9,7},{15,1},{1,15},{22,24},{24,22... | collective-permute-start | bytes 294920 | tf_op jit(solution)/shard_map/ppermute | solution.py:906
  9.8 0.1 collective-permute-start.1
  9.9 3.6 %shard_map.113 = (f32[40,64,128]{2,1,0:T(8,128)S(1)}, f32[40,64,128]{2,1,0:T(8,128)S(1)}, f32[8,48,128]{2,1,0:T(8,128)S(1)}, f32[32,8,128]{2,1,0:T(8,128)S(1)}, ...) custom-call(s32[3,8]{1,0:T(4,128)} %refs_0_.2, ...), custom_call_target="tpu_custom_call" | custom-call | flops 11796480 | bytes 4718592 | tf_op jit(solution)/shard_map/pallas_call | solution.py:414
  13.5 1.9 %collective-permute-done.1.refs_5_ = f32[4,48,128]{2,1,0:T(8,128)S(1)} collective-permute-done((f32[4,48,128]{2,1,0:T(8,128)S(1)}, f32[4,48,128]{2,1,0:T(8,128)S(1)}, u32[]{:S(2)}, u32[]{:S(2)}) %collective-permute-start.1) | collective-permute-done | bytes 98336 | tf_op jit(solution)/shard_map/ppermute | solution.py:909
  15.3 0.1 halo_step.3
  15.5 0.1 collective-permute-start.5
  15.6 4.2 %collective-permute-start.3 = (f32[4,48,128]{2,1,0:T(8,128)S(1)}, f32[4,48,128]{2,1,0:T(8,128)S(1)}, u32[]{:S(2)}, u32[]{:S(2)}) collective-permute-start(f32[4,48,128]{2,1,0:T(8,128)S(1)} %get-tuple-element.59.refs_3_), channel_id=1, source_target_pairs={{6,8},{8,6},{14,0},{0,14},{7,9},{9,7},{15,1},{1,15},{22,24},{24,22... | collective-permute-start | bytes 294920 | tf_op jit(solution)/shard_map/ppermute | solution.py:906
  19.9 3.4 %shard_map.114 = (f32[40,64,128]{2,1,0:T(8,128)S(1)}, f32[40,64,128]{2,1,0:T(8,128)S(1)}, f32[8,48,128]{2,1,0:T(8,128)S(1)}, f32[32,8,128]{2,1,0:T(8,128)S(1)}, f32[32,48,128]{2,1,0:T(8,128)S(1)}) custom-call(s32[8,256]{1,0:T(8,128)S(1)} %get-tuple-element.49.refs_0_, f32[8,256]{1,0:T(8,128)S(1)} %get-tuple-element.50.refs_1_, ...), custom_call_target="tpu_custom_call", output_to_operand_aliasing={{0}: (2, {})} | custom-call | flops 11796480 | bytes 4718592 | tf_op jit(solution)/shard_map/pallas_call | solution.py:414
  23.3 2.1 %collective-permute-done.3.refs_4_ = f32[4,48,128]{2,1,0:T(8,128)S(1)} collective-permute-done((f32[4,48,128]{2,1,0:T(8,128)S(1)}, f32[4,48,128]{2,1,0:T(8,128)S(1)}, u32[]{:S(2)}, u32[]{:S(2)}) %collective-permute-start.3) | collective-permute-done | bytes 98336 | tf_op jit(solution)/shard_map/ppermute | solution.py:906
  25.4 1.4 %collective-permute-done.4.refs_5_ = f32[4,48,128]{2,1,0:T(8,128)S(1)} collective-permute-done((f32[4,48,128]{2,1,0:T(8,128)S(1)}, f32[4,48,128]{2,1,0:T(8,128)S(1)}, u32[]{:S(2)}, u32[]{:S(2)}) %collective-permute-start.4) | collective-permute-done | bytes 98336 | tf_op jit(solution)/shard_map/ppermute | solution.py:909
  26.9 0.1 halo_step.4
  27.1 4.3 %collective-permute-start.6 = (f32[4,48,128]{2,1,0:T(8,128)S(1)}, f32[4,48,128]{2,1,0:T(8,128)S(1)}, u32[]{:S(2)}, u32[]{:S(2)}) collective-permute-start(f32[4,48,128]{2,1,0:T(8,128)S(1)} %get-tuple-element.67.refs_3_), channel_id=1, source_target_pairs={{6,8},{8,6},{14,0},{0,14},{7,9},{9,7},{15,1},{1,15},{22,24},{24,22... | collective-permute-start | bytes 294920 | tf_op jit(solution)/shard_map/ppermute | solution.py:906
  31.4 0.1 collective-permute-start.7
  31.5 3.5 %shard_map.115 = (f32[40,64,128]{2,1,0:T(8,128)S(1)}, f32[40,64,128]{2,1,0:T(8,128)S(1)}, f32[8,48,128]{2,1,0:T(8,128)S(1)}, f32[32,8,128]{2,1,0:T(8,128)S(1)}, ...) custom-call(s32[8,256]{1,0:T(8,128)S(1)} %get-tuple-element.49.refs_, ...), custom_call_target="tpu_custom_call", output_to_operand_aliasing={{0}: (2, {})} | custom-call | flops 11796480 | bytes 4718592 | tf_op jit(solution)/shard_map/pallas_call | solution.py:414
  35.0 2.0 %collective-permute-done.6.refs_4_ = f32[4,48,128]{2,1,0:T(8,128)S(1)} collective-permute-done((f32[4,48,128]{2,1,0:T(8,128)S(1)}, f32[4,48,128]{2,1,0:T(8,128)S(1)}, u32[]{:S(2)}, u32[]{:S(2)}) %collective-permute-start.6) | collective-permute-done | bytes 98336 | tf_op jit(solution)/shard_map/ppermute | solution.py:906
  37.0 1.5 %collective-permute-done.7.refs_5_ = f32[4,48,128]{2,1,0:T(8,128)S(1)} collective-permute-done((f32[4,48,128]{2,1,0:T(8,128)S(1)}, f32[4,48,128]{2,1,0:T(8,128)S(1)}, u32[]{:S(2)}, u32[]{:S(2)}) %collective-permute-start.7) | collective-permute-done | bytes 98336 | tf_op jit(solution)/shard_map/ppermute | solution.py:909
  38.5 0.1 halo_step.5
  38.7 0.1 collective-permute-start.10
  38.8 4.2 %collective-permute-start.11 = (f32[4,48,128]{2,1,0:T(8,128)S(1)}, f32[4,48,128]{2,1,0:T(8,128)S(1)}, u32[]{:S(2)}, u32[]{:S(2)}) collective-permute-start(f32[4,48,128]{2,1,0:T(8,128)S(1)} %get-tuple-element.76.refs_2_), channel_id=1, source_target_pairs={{6,8},{8,6},{14,0},{0,14},{7,9},{9,7},{15,1},{1,15},{22,24},{24,22... | collective-permute-start | bytes 294920 | tf_op jit(solution)/shard_map/ppermute | solution.py:906
  43.1 0.1 collective-permute-start.12
  43.2 2.3 %shard_map.116 = (f32[40,64,128]{2,1,0:T(8,128)S(1)}, f32[32,48,128]{2,1,0:T(8,128)S(1)}, f32[8,48,128]{2,1,0:T(8,128)S(1)}, f32[32,8,128]{2,1,0:T(8,128)S(1)}, f32[24,16,128]{2,1,0:T(8,128)S(1)}) custom-call(f32[32,48,128]{2,1,0:T(8,128)S(1)} %get-tuple-element.72.refs_0_, ...), custom_call_target="tpu_custom_call", output_to_operand_aliasing={{0}: (1, {})} | custom-call | flops 11796480 | bytes 4718592 | tf_op jit(solution)/shard_map/pallas_call | solution.py:414
  45.4 0.6 %last_step.1 = (f32[32,48,128]{2,1,0:T(8,128)S(1)}, f32[24,16,128]{2,1,0:T(8,128)S(1)}, f32[224,128]{1,0:T(8,128)S(1)}) custom-call(f32[8,128]{1,0:T(8,128)S(1)} %get-tuple-element.71.flag_ref, f32[24,16,128]{2,1,0:T(8,128)S(1)} %get-tuple-element.80.even_ref, f32[32,48,128]{2,1,0:T(8,128)S(1)} %get-tuple-element.81.current_ref, ...), custom_call_target="tpu_custom_call", output_to_operand_aliasing={{0}: (2, {})} | custom-call | flops 1966080 | bytes 2359296 | tf_op jit(solution)/shard_map/last_step/pallas_call | solution.py:662
  46.0 3.0 %collective-permute-start.13 = (f32[224,128]{1,0:T(8,128)S(1)}, f32[224,128]{1,0:T(8,128)S(1)}, u32[]{:S(2)}, u32[]{:S(2)}) collective-permute-start(f32[224,128]{1,0:T(8,128)S(1)} %get-tuple-element.93), channel_id=1, source_target_pairs={{0,8},{2,10},{4,12},{6,14},{8,0},{10,2},{12,4},{14,6},{1,9},{3,11}... | collective-permute-start | bytes 344072 | tf_op jit(solution)/shard_map/ppermute | solution.py:945
  49.0 0.2 collective-permute-done.11.far_ref
  49.2 0.3 last_far.1
  49.5 3.1 %collective-permute-done.12.refs_2_ = f32[224,128]{1,0:T(8,128)S(1)} collective-permute-done((f32[224,128]{1,0:T(8,128)S(1)}, f32[224,128]{1,0:T(8,128)S(1)}, u32[]{:S(2)}, u32[]{:S(2)}) %collective-permute-start.12) | collective-permute-done | bytes 114720 | tf_op jit(solution)/shard_map/ppermute | solution.py:938
  52.6 1.2 %early_image.1 = (f32[17,16,768]{2,1,0:T(8,128)S(1)}, s32[8,128]{1,0:T(8,128)S(1)}) custom-call(s32[17]{0:T(128)} %lags_ref.1, f32[4,96,128]{2,1,0:T(8,128)S(1)} %get-tuple-element.88.refs_1_, f32[224,128]{1,0:T(8,128)S(1)} %collective-permute-done.12.refs_2_), custom_call_target="tpu_custom_call" | custom-call | flops 2088960 | bytes 1671168 | tf_op jit(solution)/shard_map/early_image/pallas_call | solution.py:862
  53.8 0.9 %write_out.1 = f32[32,48,128]{2,1,0:T(8,128)} custom-call(f32[32,48,128]{2,1,0:T(8,128)S(1)} %get-tuple-element.87.level_ref), custom_call_target="tpu_custom_call" | custom-call | bytes 1572864 | tf_op jit(solution)/shard_map/write_out/pallas_call | solution.py:748
  54.7 1.1 %pack_own.1.refs_1_ = f32[17,96,128]{2,1,0:T(8,128)S(1)} custom-call(s32[17]{0:T(128)} %lags_ref.1, f32[24,16,128]{2,1,0:T(8,128)S(1)} %get-tuple-element.91.even_ref, bf16[512,512]{1,0:T(8,128)(2,1)S(1)} %get-tuple-element.92.matrix_ref), custom_call_target="tpu_custom_call" | custom-call | flops 50331648 | bytes 786432 | tf_op jit(solution)/shard_map/pack_own/pallas_call | solution.py:581
  55.8 1.1 %last_image.1 = f32[17,16,768]{2,1,0:T(8,128)} custom-call(s32[8,128]{1,0:T(8,128)S(1)} %get-tuple-element.90.refs_0_, f32[17,96,128]{2,1,0:T(8,128)S(1)} %pack_own.1.refs_1_, f32[224,128]{1,0:T(8,128)S(1)} %collective-permute-done.13.refs_2_, f32[48,128]{1,0:T(8,128)S(1)} %collective-permute-done.14.refs_3_, f32[17,16,768]{2,1,0:T(8,128)S(1)} %get-tuple-element.95.refs_4_), custom_call_target="tpu_custom_call" | custom-call | flops 2088960 | bytes 1671168 | tf_op jit(solution)/shard_map/last_image/pallas_call | solution.py:862
  (14 shorter events, 0.3 us)
Async XLA Ops:
  0.6 9.2 %copy-start = (f32[32,48,128]{2,1,0:T(8,128)S(1)}, f32[32,48,128]{2,1,0:T(8,128)}, u32[]{:S(2)}) copy-start(f32[32,48,128]{2,1,0:T(8,128)} %field_ref.1) | copy-start | bytes 2359300
  1.8 13.6 %collective-permute-start.2 = (f32[32,8,128]{2,1,0:T(8,128)S(1)}, f32[32,8,128]{2,1,0:T(8,128)S(1)}, u32[]{:S(2)}, u32[]{:S(2)}) collective-permute-start(f32[32,8,128]{2,1,0:T(8,128)S(1)} %get-tuple-element.58), channel_id=1, source_target_pairs={{0,1},{1,0},{2,3},{3,2},{4,5},{5,4},{6,7},{7,6},{8,9},{9,8},{10,11... | collective-permute-start | bytes 393224 | tf_op jit(solution)/shard_map/ppermute | solution.py:910
  2.3 11.1 %collective-permute-start = (f32[4,48,128]{2,1,0:T(8,128)S(1)}, f32[4,48,128]{2,1,0:T(8,128)S(1)}, u32[]{:S(2)}, u32[]{:S(2)}) collective-permute-start(f32[4,48,128]{2,1,0:T(8,128)S(1)} %get-tuple-element.56), channel_id=1, source_target_pairs={{6,8},{8,6},{14,0},{0,14},{7,9},{9,7},{15,1},{1,15},{22,24},{24,22... | collective-permute-start | bytes 294920 | tf_op jit(solution)/shard_map/ppermute | solution.py:906
  9.8 5.5 %collective-permute-start.1 = (f32[4,48,128]{2,1,0:T(8,128)S(1)}, f32[4,48,128]{2,1,0:T(8,128)S(1)}, u32[]{:S(2)}, u32[]{:S(2)}) collective-permute-start(f32[4,48,128]{2,1,0:T(8,128)S(1)} %get-tuple-element.57), channel_id=1, source_target_pairs={{0,2},{2,0},{4,6},{6,4},{8,10},{10,8},{12,14},{14,12},{1,3},{3,1},... | collective-permute-start | bytes 294920 | tf_op jit(solution)/shard_map/ppermute | solution.py:909
  15.5 11.4 %collective-permute-start.5 = (f32[32,8,128]{2,1,0:T(8,128)S(1)}, f32[32,8,128]{2,1,0:T(8,128)S(1)}, u32[]{:S(2)}, u32[]{:S(2)}) collective-permute-start(f32[32,8,128]{2,1,0:T(8,128)S(1)} %get-tuple-element.61.refs_5_), channel_id=1, source_target_pairs={{0,1},{1,0},{2,3},{3,2},{4,5},{5,4},{6,7},{7,6},{8,9},{9,8},{10,11... | collective-permute-start | bytes 393224 | tf_op jit(solution)/shard_map/ppermute | solution.py:910
  15.6 9.9 %collective-permute-start.3 = (f32[4,48,128]{2,1,0:T(8,128)S(1)}, f32[4,48,128]{2,1,0:T(8,128)S(1)}, u32[]{:S(2)}, u32[]{:S(2)}) collective-permute-start(f32[4,48,128]{2,1,0:T(8,128)S(1)} %get-tuple-element.59.refs_3_), channel_id=1, source_target_pairs={{6,8},{8,6},{14,0},{0,14},{7,9},{9,7},{15,1},{1,15},{22,24},{24,22... | collective-permute-start | bytes 294920 | tf_op jit(solution)/shard_map/ppermute | solution.py:906
  19.8 7.1 %collective-permute-start.4 = (f32[4,48,128]{2,1,0:T(8,128)S(1)}, f32[4,48,128]{2,1,0:T(8,128)S(1)}, u32[]{:S(2)}, u32[]{:S(2)}) collective-permute-start(f32[4,48,128]{2,1,0:T(8,128)S(1)} %get-tuple-element.60.refs_4_), channel_id=1, source_target_pairs={{0,2},{2,0},{4,6},{6,4},{8,10},{10,8},{12,14},{14,12},{1,3},{3,1},... | collective-permute-start | bytes 294920 | tf_op jit(solution)/shard_map/ppermute | solution.py:909
  27.0 11.5 %collective-permute-start.8 = (f32[32,8,128]{2,1,0:T(8,128)S(1)}, f32[32,8,128]{2,1,0:T(8,128)S(1)}, u32[]{:S(2)}, u32[]{:S(2)}) collective-permute-start(f32[32,8,128]{2,1,0:T(8,128)S(1)} %get-tuple-element.69.refs_5_), channel_id=1, source_target_pairs={{0,1},{1,0},{2,3},{3,2},{4,5},{5,4},{6,7},{7,6},{8,9},{9,8},{10,11... | collective-permute-start | bytes 393224 | tf_op jit(solution)/shard_map/ppermute | solution.py:910
  27.1 9.9 %collective-permute-start.6 = (f32[4,48,128]{2,1,0:T(8,128)S(1)}, f32[4,48,128]{2,1,0:T(8,128)S(1)}, u32[]{:S(2)}, u32[]{:S(2)}) collective-permute-start(f32[4,48,128]{2,1,0:T(8,128)S(1)} %get-tuple-element.67.refs_3_), channel_id=1, source_target_pairs={{6,8},{8,6},{14,0},{0,14},{7,9},{9,7},{15,1},{1,15},{22,24},{24,22... | collective-permute-start | bytes 294920 | tf_op jit(solution)/shard_map/ppermute | solution.py:906
  31.4 7.1 %collective-permute-start.7 = (f32[4,48,128]{2,1,0:T(8,128)S(1)}, f32[4,48,128]{2,1,0:T(8,128)S(1)}, u32[]{:S(2)}, u32[]{:S(2)}) collective-permute-start(f32[4,48,128]{2,1,0:T(8,128)S(1)} %get-tuple-element.68.refs_4_), channel_id=1, source_target_pairs={{0,2},{2,0},{4,6},{6,4},{8,10},{10,8},{12,14},{14,12},{1,3},{3,1},... | collective-permute-start | bytes 294920 | tf_op jit(solution)/shard_map/ppermute | solution.py:909
  38.7 6.8 %collective-permute-start.10 = (f32[32,8,128]{2,1,0:T(8,128)S(1)}, f32[32,8,128]{2,1,0:T(8,128)S(1)}, u32[]{:S(2)}, u32[]{:S(2)}) collective-permute-start(f32[32,8,128]{2,1,0:T(8,128)S(1)} %get-tuple-element.78.refs_4_), channel_id=1, source_target_pairs={{0,1},{1,0},{2,3},{3,2},{4,5},{5,4},{6,7},{7,6},{8,9},{9,8},{10,11... | collective-permute-start | bytes 393224 | tf_op jit(solution)/shard_map/ppermute | solution.py:910
  38.7 6.7 %collective-permute-start.9 = (f32[4,48,128]{2,1,0:T(8,128)S(1)}, f32[4,48,128]{2,1,0:T(8,128)S(1)}, u32[]{:S(2)}, u32[]{:S(2)}) collective-permute-start(f32[4,48,128]{2,1,0:T(8,128)S(1)} %get-tuple-element.77.refs_3_), channel_id=1, source_target_pairs={{0,2},{2,0},{4,6},{6,4},{8,10},{10,8},{12,14},{14,12},{1,3},{3,1},... | collective-permute-start | bytes 294920 | tf_op jit(solution)/shard_map/ppermute | solution.py:909
  38.8 10.4 %collective-permute-start.11 = (f32[4,48,128]{2,1,0:T(8,128)S(1)}, f32[4,48,128]{2,1,0:T(8,128)S(1)}, u32[]{:S(2)}, u32[]{:S(2)}) collective-permute-start(f32[4,48,128]{2,1,0:T(8,128)S(1)} %get-tuple-element.76.refs_2_), channel_id=1, source_target_pairs={{6,8},{8,6},{14,0},{0,14},{7,9},{9,7},{15,1},{1,15},{22,24},{24,22... | collective-permute-start | bytes 294920 | tf_op jit(solution)/shard_map/ppermute | solution.py:906
  43.1 9.5 %collective-permute-start.12 = (f32[224,128]{1,0:T(8,128)S(1)}, f32[224,128]{1,0:T(8,128)S(1)}, u32[]{:S(2)}, u32[]{:S(2)}) collective-permute-start(f32[224,128]{1,0:T(8,128)S(1)} %get-tuple-element.89), channel_id=1, source_target_pairs={{0,8},{2,10},{4,12},{6,14},{8,0},{10,2},{12,4},{14,6},{1,9},{3,11}... | collective-permute-start | bytes 344072 | tf_op jit(solution)/shard_map/ppermute | solution.py:938
  46.0 9.8 %collective-permute-start.13 = (f32[224,128]{1,0:T(8,128)S(1)}, f32[224,128]{1,0:T(8,128)S(1)}, u32[]{:S(2)}, u32[]{:S(2)}) collective-permute-start(f32[224,128]{1,0:T(8,128)S(1)} %get-tuple-element.93), channel_id=1, source_target_pairs={{0,8},{2,10},{4,12},{6,14},{8,0},{10,2},{12,4},{14,6},{1,9},{3,11}... | collective-permute-start | bytes 344072 | tf_op jit(solution)/shard_map/ppermute | solution.py:945
  49.4 6.3 %collective-permute-start.14 = (f32[48,128]{1,0:T(8,128)S(1)}, f32[48,128]{1,0:T(8,128)S(1)}, u32[]{:S(2)}, u32[]{:S(2)}) collective-permute-start(f32[48,128]{1,0:T(8,128)S(1)} %get-tuple-element.94), channel_id=1, source_target_pairs={{0,8},{2,10},{4,12},{6,14},{8,0},{10,2},{12,4},{14,6},{1,9},{3,11}... | collective-permute-start | bytes 73736 | tf_op jit(solution)/shard_map/ppermute | solution.py:948

commit v11 on v10

--- a/solution.py
+++ b/solution.py
@@ -602,6 +602,16 @@
     return slots, -(-2 * groups // fits) * count_a
 
 
+def edge_sums(parts, count_a, groups, count_z):
+    slots, extra = edge_slots(count_a, groups, count_z)
+    sums = {}
+    for parity, g, row, shift in slots:
+        part = parts[2 + parity][g * count_a : (g + 1) * count_a]
+        part = pltpu.roll(part, shift, 1) if shift else part
+        sums[row] = sums[row] + part if row in sums else part
+    return sums, extra
+
+
 def send_into(even_ref, matrix_ref, out_ref):
     count_b, count_a, count_z = even_ref.shape
     groups = count_b // GROUP
@@ -609,13 +619,7 @@
     parts = packed(even_ref, matrix_ref)
     out_ref[pl.ds(0, total_rows), :] = parts[0]
     out_ref[pl.ds(total_rows, total_rows), :] = parts[1]
-    slots, _ = edge_slots(count_a, groups, count_z)
-    sums = {}
-    for parity, g, row, shift in slots:
-        part = parts[2 + parity][g * count_a : (g + 1) * count_a]
-        part = pltpu.roll(part, shift, 1) if shift else part
-        sums[row] = sums[row] + part if row in sums else part
-    for row, part in sums.items():
+    for row, part in edge_sums(parts, count_a, groups, count_z)[0].items():
         out_ref[pl.ds(2 * total_rows + row, count_a), :] = part
 
 
@@ -623,6 +627,81 @@
     groups = count_b // GROUP
     _, extra = edge_slots(count_a, groups, count_z)
     return shape(2 * groups * count_a + extra, count_z)
+
+
+KEPT = SIDE - WIDTH // 2
+FREE = SIDE - KEPT
+BATCH = KEPT // FREE + 1
+
+
+def give_rows(groups):
+    tiles = 2 * groups
+    return SIDE * tiles, SIDE * (tiles // BATCH * (BATCH - 1))
+
+
+def give_into(place, even_ref, matrix_ref, out_ref):
+    count_b, count_a, count_z = even_ref.shape
+    groups = count_b // GROUP
+    assert count_a == 2 * SIDE and 2 * groups % BATCH == 0
+    parts = packed(even_ref, matrix_ref)
+    whole_rows, part_rows = give_rows(groups)
+    line = lax.broadcasted_iota(jnp.int32, (SIDE, count_z), 0)
+
+    def store(far_tile, shift):
+        fars = []
+        for index in range(2 * groups):
+            start = index % groups * count_a
+            both = [
+                parts[index // groups][start + SIDE * tile : start + SIDE * (tile + 1)]
+                for tile in range(2)
+            ]
+            out_ref[pl.ds(SIDE * index, SIDE), :] = both[1 - far_tile]
+            fars.append(pltpu.roll(both[far_tile], shift, 0) if shift else both[far_tile])
+        row = whole_rows
+        for first in range(0, 2 * groups, BATCH):
+            *hosts, guest = fars[first : first + BATCH]
+            for i, host in enumerate(hosts):
+                moved_guest = pltpu.roll(guest, KEPT - FREE * i, 0)
+                out_ref[pl.ds(row, SIDE), :] = jnp.where(line < KEPT, host, moved_guest)
+                row += SIDE
+
+    pl.when(place.even)(lambda: store(0, KEPT))
+    pl.when(jnp.logical_not(place.even))(lambda: store(1, 0))
+    for row, part in edge_sums(parts, count_a, groups, count_z)[0].items():
+        out_ref[pl.ds(whole_rows + part_rows + row, count_a), :] = part
+
+
+def take_windows(place, other_ref, mains, groups, count_a):
+    count_z = other_ref.shape[1]
+    whole_rows, _ = give_rows(groups)
+    line = lax.broadcasted_iota(jnp.int32, (SIDE, count_z), 0)
+
+    def load(far_tile, shift):
+        fars = []
+        row = whole_rows
+        for _ in range(0, 2 * groups, BATCH):
+            hosts = [other_ref[pl.ds(row + SIDE * i, SIDE), :] for i in range(BATCH - 1)]
+            row += SIDE * (BATCH - 1)
+            guest = None
+            for i, host in enumerate(hosts):
+                piece = pltpu.roll(host, (FREE * (i + 1)) % SIDE, 0)
+                guest = piece if guest is None else jnp.where(line < FREE * i, guest, piece)
+            fars += [*hosts, guest]
+        for index, far in enumerate(fars):
+            start = index % groups * count_a
+            far = pltpu.roll(far, shift, 0) if shift else far
+            mains[index // groups, pl.ds(start + SIDE * far_tile, SIDE), :] = far
+            mains[index // groups, pl.ds(start + SIDE * (1 - far_tile), SIDE), :] = other_ref[
+                pl.ds(SIDE * index, SIDE), :
+            ]
+
+    pl.when(place.even)(lambda: load(0, FREE))
+    pl.when(jnp.logical_not(place.even))(lambda: load(1, 0))
+
+
+def given_shape(count_a, count_b, count_z):
+    groups = count_b // GROUP
+    return shape(sum(give_rows(groups)) + edge_slots(count_a, groups, count_z)[1], count_z)
 
 
 def last_step(flag, even_before, current, parts, near, side, matrix):
@@ -656,7 +735,7 @@
             late_ref[b] = jnp.where(
                 wants_last, even_rows(final_ref, 0, 0, count_a, b), even_ref[b]
             )
-        send_into(late_ref, matrix_ref, sent_ref)
+        give_into(place, late_ref, matrix_ref, sent_ref)
 
     slab, _, side_shape = face_shapes(count_x, count_y, count_z)
     return pl.pallas_call(
@@ -664,7 +743,7 @@
         out_shape=(
             shape(*current.shape),
             shape(count_b, count_a, count_z),
-            sent_shape(count_a, count_b, count_z),
+            given_shape(count_a, count_b, count_z),
         ),
         in_specs=[spec(pltpu.VMEM)] * 10,
         out_specs=(spec(pltpu.VMEM),) * 3,
@@ -803,10 +882,15 @@
             return jnp.where(is_source, lane, half - 1 - lane) < REACH
 
         slots, _ = edge_slots(count_a, groups, count_z)
-        for parity in range(2):
-            mains[parity] = other_ref[pl.ds(parity * total_rows, total_rows), :]
+        if last:
+            take_windows(place, other_ref, mains, groups, count_a)
+            edge_row = sum(give_rows(groups))
+        else:
+            for parity in range(2):
+                mains[parity] = other_ref[pl.ds(parity * total_rows, total_rows), :]
+            edge_row = 2 * total_rows
         for parity, g, row, shift in slots:
-            part = other_ref[pl.ds(2 * total_rows + row, count_a), :]
+            part = other_ref[pl.ds(edge_row + row, count_a), :]
             part = pltpu.roll(part, count_z - shift, 1) if shift else part
             edges[parity, pl.ds(g * count_a, count_a), :] = jnp.where(useful(count_a), part, 0.0)
         if last:

time: 57.4 us -> 57.1 us (level)
  transfers between devices with their start and end apart: 15 -> 15, of which waited for: 7 -> 7; matrix products, arithmetic and copies ran while one was open for 0% -> 0% of each run, Pallas kernels for 29% -> 30%
where the time goes in v11:
time: 57.1 us; the launch traced here: 56.6 us
  starting transfers between devices  24.3 us (43%)
  Pallas kernels  19.4 us (34%)
  waiting for transfers between devices  12 us (21%)
  between operations  0.89 us (2%)
    ppermute x4, starting transfers between devices, send_far(): return lax.ppermute(far, 'gx', far_pairs)  20.2 us
    pallas_call x4, Pallas kernels, inner_step(): pl.pallas_call(kernel, out_shape=tuple(outs), in_specs=specs, out_specs=(...  12.7 us
    ppermute x4, waiting for transfers between devices, send_near(): near = lax.ppermute(near, 'gx', near_pairs)  4.83 us
    ppermute x4, waiting for transfers between devices, send_far(): return lax.ppermute(far, 'gx', far_pairs)  4.33 us
    ppermute x1, starting transfers between devices, body(): other_late = lax.ppermute(sent_late, 'gx', across)  2.95 us
    ppermute x1, waiting for transfers between devices, body(): other_early = lax.ppermute(sent_early, 'gx', across)  2.86 us
    pallas_call x2, Pallas kernels, lag_image(): pl.pallas_call(kernel, out_shape=image if last else (image, shape(8, coun...  2.31 us
  transfers between devices with their start and end apart: 15, of which 7 were waited for; matrix products, arithmetic and copies ran while one was open for 0% of the time, Pallas kernels for 30%

profile of v11, /device:TPU:0, one launch (start us, length us, event | category | flops | bytes accessed | tf_op | source)
XLA Modules:
  0.0 56.6 jit_solution(12266605106528564563)
XLA Ops:
  0.6 1.1 %first_faces.1 = (f32[4,48,128]{2,1,0:T(8,128)S(1)}, f32[4,48,128]{2,1,0:T(8,128)S(1)}, f32[32,8,128]{2,1,0:T(8,128)S(1)}) custom-call(f32[32,48,128]{2,1,0:T(8,128)} %field_ref.1), custom_call_target="tpu_custom_call" | custom-call | tf_op jit(solution)/shard_map/first_faces/pallas_call | solution.py:93
  1.8 0.6 collective-permute-start.2
  2.3 7.5 %collective-permute-start = (f32[4,48,128]{2,1,0:T(8,128)S(1)}, f32[4,48,128]{2,1,0:T(8,128)S(1)}, u32[]{:S(2)}, u32[]{:S(2)}) collective-permute-start(f32[4,48,128]{2,1,0:T(8,128)S(1)} %get-tuple-element.56), channel_id=1, source_target_pairs={{6,8},{8,6},{14,0},{0,14},{7,9},{9,7},{15,1},{1,15},{22,24},{24,22... | collective-permute-start | bytes 294920 | tf_op jit(solution)/shard_map/ppermute | solution.py:990
  9.8 0.1 collective-permute-start.1
  9.9 3.6 %shard_map.113 = (f32[40,64,128]{2,1,0:T(8,128)S(1)}, f32[40,64,128]{2,1,0:T(8,128)S(1)}, f32[8,48,128]{2,1,0:T(8,128)S(1)}, f32[32,8,128]{2,1,0:T(8,128)S(1)}, ...) custom-call(s32[3,8]{1,0:T(4,128)} %refs_0_.2, ...), custom_call_target="tpu_custom_call" | custom-call | flops 11796480 | bytes 4718592 | tf_op jit(solution)/shard_map/pallas_call | solution.py:414
  13.5 1.9 %collective-permute-done.1.refs_5_ = f32[4,48,128]{2,1,0:T(8,128)S(1)} collective-permute-done((f32[4,48,128]{2,1,0:T(8,128)S(1)}, f32[4,48,128]{2,1,0:T(8,128)S(1)}, u32[]{:S(2)}, u32[]{:S(2)}) %collective-permute-start.1) | collective-permute-done | bytes 98336 | tf_op jit(solution)/shard_map/ppermute | solution.py:993
  15.3 0.1 halo_step.3
  15.5 0.1 collective-permute-start.5
  15.6 4.2 %collective-permute-start.3 = (f32[4,48,128]{2,1,0:T(8,128)S(1)}, f32[4,48,128]{2,1,0:T(8,128)S(1)}, u32[]{:S(2)}, u32[]{:S(2)}) collective-permute-start(f32[4,48,128]{2,1,0:T(8,128)S(1)} %get-tuple-element.59.refs_3_), channel_id=1, source_target_pairs={{6,8},{8,6},{14,0},{0,14},{7,9},{9,7},{15,1},{1,15},{22,24},{24,22... | collective-permute-start | bytes 294920 | tf_op jit(solution)/shard_map/ppermute | solution.py:990
  19.9 3.4 %shard_map.114 = (f32[40,64,128]{2,1,0:T(8,128)S(1)}, f32[40,64,128]{2,1,0:T(8,128)S(1)}, f32[8,48,128]{2,1,0:T(8,128)S(1)}, f32[32,8,128]{2,1,0:T(8,128)S(1)}, f32[32,48,128]{2,1,0:T(8,128)S(1)}) custom-call(s32[8,256]{1,0:T(8,128)S(1)} %get-tuple-element.49.refs_0_, f32[8,256]{1,0:T(8,128)S(1)} %get-tuple-element.50.refs_1_, ...), custom_call_target="tpu_custom_call", output_to_operand_aliasing={{0}: (2, {})} | custom-call | flops 11796480 | bytes 4718592 | tf_op jit(solution)/shard_map/pallas_call | solution.py:414
  23.3 2.1 %collective-permute-done.3.refs_4_ = f32[4,48,128]{2,1,0:T(8,128)S(1)} collective-permute-done((f32[4,48,128]{2,1,0:T(8,128)S(1)}, f32[4,48,128]{2,1,0:T(8,128)S(1)}, u32[]{:S(2)}, u32[]{:S(2)}) %collective-permute-start.3) | collective-permute-done | bytes 98336 | tf_op jit(solution)/shard_map/ppermute | solution.py:990
  25.4 1.4 %collective-permute-done.4.refs_5_ = f32[4,48,128]{2,1,0:T(8,128)S(1)} collective-permute-done((f32[4,48,128]{2,1,0:T(8,128)S(1)}, f32[4,48,128]{2,1,0:T(8,128)S(1)}, u32[]{:S(2)}, u32[]{:S(2)}) %collective-permute-start.4) | collective-permute-done | bytes 98336 | tf_op jit(solution)/shard_map/ppermute | solution.py:993
  26.9 0.1 halo_step.4
  27.1 4.3 %collective-permute-start.6 = (f32[4,48,128]{2,1,0:T(8,128)S(1)}, f32[4,48,128]{2,1,0:T(8,128)S(1)}, u32[]{:S(2)}, u32[]{:S(2)}) collective-permute-start(f32[4,48,128]{2,1,0:T(8,128)S(1)} %get-tuple-element.67.refs_3_), channel_id=1, source_target_pairs={{6,8},{8,6},{14,0},{0,14},{7,9},{9,7},{15,1},{1,15},{22,24},{24,22... | collective-permute-start | bytes 294920 | tf_op jit(solution)/shard_map/ppermute | solution.py:990
  31.4 0.1 collective-permute-start.7
  31.5 3.5 %shard_map.115 = (f32[40,64,128]{2,1,0:T(8,128)S(1)}, f32[40,64,128]{2,1,0:T(8,128)S(1)}, f32[8,48,128]{2,1,0:T(8,128)S(1)}, f32[32,8,128]{2,1,0:T(8,128)S(1)}, ...) custom-call(s32[8,256]{1,0:T(8,128)S(1)} %get-tuple-element.49.refs_, ...), custom_call_target="tpu_custom_call", output_to_operand_aliasing={{0}: (2, {})} | custom-call | flops 11796480 | bytes 4718592 | tf_op jit(solution)/shard_map/pallas_call | solution.py:414
  35.0 2.0 %collective-permute-done.6.refs_4_ = f32[4,48,128]{2,1,0:T(8,128)S(1)} collective-permute-done((f32[4,48,128]{2,1,0:T(8,128)S(1)}, f32[4,48,128]{2,1,0:T(8,128)S(1)}, u32[]{:S(2)}, u32[]{:S(2)}) %collective-permute-start.6) | collective-permute-done | bytes 98336 | tf_op jit(solution)/shard_map/ppermute | solution.py:990
  37.0 1.5 %collective-permute-done.7.refs_5_ = f32[4,48,128]{2,1,0:T(8,128)S(1)} collective-permute-done((f32[4,48,128]{2,1,0:T(8,128)S(1)}, f32[4,48,128]{2,1,0:T(8,128)S(1)}, u32[]{:S(2)}, u32[]{:S(2)}) %collective-permute-start.7) | collective-permute-done | bytes 98336 | tf_op jit(solution)/shard_map/ppermute | solution.py:993
  38.5 0.1 halo_step.5
  38.7 0.1 collective-permute-start.10
  38.8 4.2 %collective-permute-start.11 = (f32[4,48,128]{2,1,0:T(8,128)S(1)}, f32[4,48,128]{2,1,0:T(8,128)S(1)}, u32[]{:S(2)}, u32[]{:S(2)}) collective-permute-start(f32[4,48,128]{2,1,0:T(8,128)S(1)} %get-tuple-element.76.refs_2_), channel_id=1, source_target_pairs={{6,8},{8,6},{14,0},{0,14},{7,9},{9,7},{15,1},{1,15},{22,24},{24,22... | collective-permute-start | bytes 294920 | tf_op jit(solution)/shard_map/ppermute | solution.py:990
  43.1 0.1 collective-permute-start.12
  43.2 2.3 %shard_map.116 = (f32[40,64,128]{2,1,0:T(8,128)S(1)}, f32[32,48,128]{2,1,0:T(8,128)S(1)}, f32[8,48,128]{2,1,0:T(8,128)S(1)}, f32[32,8,128]{2,1,0:T(8,128)S(1)}, f32[24,16,128]{2,1,0:T(8,128)S(1)}) custom-call(f32[32,48,128]{2,1,0:T(8,128)S(1)} %get-tuple-element.72.refs_0_, ...), custom_call_target="tpu_custom_call", output_to_operand_aliasing={{0}: (1, {})} | custom-call | flops 11796480 | bytes 4718592 | tf_op jit(solution)/shard_map/pallas_call | solution.py:414
  45.4 0.6 %last_step.1 = (f32[32,48,128]{2,1,0:T(8,128)S(1)}, f32[24,16,128]{2,1,0:T(8,128)S(1)}, f32[200,128]{1,0:T(8,128)S(1)}) custom-call(f32[8,128]{1,0:T(8,128)S(1)} %get-tuple-element.71.flag_ref, f32[24,16,128]{2,1,0:T(8,128)S(1)} %get-tuple-element.80.even_ref, f32[32,48,128]{2,1,0:T(8,128)S(1)} %get-tuple-element.81.current_ref, ...), custom_call_target="tpu_custom_call", output_to_operand_aliasing={{0}: (2, {})} | custom-call | flops 1966080 | bytes 2359296 | tf_op jit(solution)/shard_map/last_step/pallas_call | solution.py:741
  46.0 3.0 %collective-permute-start.13 = (f32[200,128]{1,0:T(8,128)S(1)}, f32[200,128]{1,0:T(8,128)S(1)}, u32[]{:S(2)}, u32[]{:S(2)}) collective-permute-start(f32[200,128]{1,0:T(8,128)S(1)} %get-tuple-element.93), channel_id=1, source_target_pairs={{0,8},{2,10},{4,12},{6,14},{8,0},{10,2},{12,4},{14,6},{1,9},{3,11}... | collective-permute-start | bytes 307208 | tf_op jit(solution)/shard_map/ppermute | solution.py:1029
  49.0 0.2 collective-permute-done.11.far_ref
  49.2 0.3 last_far.1
  49.5 2.9 %collective-permute-done.12.refs_2_ = f32[224,128]{1,0:T(8,128)S(1)} collective-permute-done((f32[224,128]{1,0:T(8,128)S(1)}, f32[224,128]{1,0:T(8,128)S(1)}, u32[]{:S(2)}, u32[]{:S(2)}) %collective-permute-start.12) | collective-permute-done | bytes 114720 | tf_op jit(solution)/shard_map/ppermute | solution.py:1022
  52.3 1.2 %early_image.1 = (f32[17,16,768]{2,1,0:T(8,128)S(1)}, s32[8,128]{1,0:T(8,128)S(1)}) custom-call(s32[17]{0:T(128)} %lags_ref.1, f32[4,96,128]{2,1,0:T(8,128)S(1)} %get-tuple-element.88.refs_1_, f32[224,128]{1,0:T(8,128)S(1)} %collective-permute-done.12.refs_2_), custom_call_target="tpu_custom_call" | custom-call | flops 2088960 | bytes 1671168 | tf_op jit(solution)/shard_map/early_image/pallas_call | solution.py:946
  53.5 0.9 %write_out.1 = f32[32,48,128]{2,1,0:T(8,128)} custom-call(f32[32,48,128]{2,1,0:T(8,128)S(1)} %get-tuple-element.87.level_ref), custom_call_target="tpu_custom_call" | custom-call | bytes 1572864 | tf_op jit(solution)/shard_map/write_out/pallas_call | solution.py:827
  54.4 1.1 %pack_own.1.refs_1_ = f32[17,96,128]{2,1,0:T(8,128)S(1)} custom-call(s32[17]{0:T(128)} %lags_ref.1, f32[24,16,128]{2,1,0:T(8,128)S(1)} %get-tuple-element.91.even_ref, bf16[512,512]{1,0:T(8,128)(2,1)S(1)} %get-tuple-element.92.matrix_ref), custom_call_target="tpu_custom_call" | custom-call | flops 50331648 | bytes 786432 | tf_op jit(solution)/shard_map/pack_own/pallas_call | solution.py:581
  55.5 1.1 %last_image.1 = f32[17,16,768]{2,1,0:T(8,128)} custom-call(s32[8,128]{1,0:T(8,128)S(1)} %get-tuple-element.90.refs_0_, f32[17,96,128]{2,1,0:T(8,128)S(1)} %pack_own.1.refs_1_, f32[200,128]{1,0:T(8,128)S(1)} %collective-permute-done.13.refs_2_, f32[48,128]{1,0:T(8,128)S(1)} %collective-permute-done.14.refs_3_, f32[17,16,768]{2,1,0:T(8,128)S(1)} %get-tuple-element.95.refs_4_), custom_call_target="tpu_custom_call" | custom-call | flops 2088960 | bytes 1671168 | tf_op jit(solution)/shard_map/last_image/pallas_call | solution.py:946
  (14 shorter events, 0.3 us)
Async XLA Ops:
  0.6 9.2 %copy-start = (f32[32,48,128]{2,1,0:T(8,128)S(1)}, f32[32,48,128]{2,1,0:T(8,128)}, u32[]{:S(2)}) copy-start(f32[32,48,128]{2,1,0:T(8,128)} %field_ref.1) | copy-start | bytes 2359300
  1.8 13.6 %collective-permute-start.2 = (f32[32,8,128]{2,1,0:T(8,128)S(1)}, f32[32,8,128]{2,1,0:T(8,128)S(1)}, u32[]{:S(2)}, u32[]{:S(2)}) collective-permute-start(f32[32,8,128]{2,1,0:T(8,128)S(1)} %get-tuple-element.58), channel_id=1, source_target_pairs={{0,1},{1,0},{2,3},{3,2},{4,5},{5,4},{6,7},{7,6},{8,9},{9,8},{10,11... | collective-permute-start | bytes 393224 | tf_op jit(solution)/shard_map/ppermute | solution.py:994
  2.3 11.1 %collective-permute-start = (f32[4,48,128]{2,1,0:T(8,128)S(1)}, f32[4,48,128]{2,1,0:T(8,128)S(1)}, u32[]{:S(2)}, u32[]{:S(2)}) collective-permute-start(f32[4,48,128]{2,1,0:T(8,128)S(1)} %get-tuple-element.56), channel_id=1, source_target_pairs={{6,8},{8,6},{14,0},{0,14},{7,9},{9,7},{15,1},{1,15},{22,24},{24,22... | collective-permute-start | bytes 294920 | tf_op jit(solution)/shard_map/ppermute | solution.py:990
  9.8 5.5 %collective-permute-start.1 = (f32[4,48,128]{2,1,0:T(8,128)S(1)}, f32[4,48,128]{2,1,0:T(8,128)S(1)}, u32[]{:S(2)}, u32[]{:S(2)}) collective-permute-start(f32[4,48,128]{2,1,0:T(8,128)S(1)} %get-tuple-element.57), channel_id=1, source_target_pairs={{0,2},{2,0},{4,6},{6,4},{8,10},{10,8},{12,14},{14,12},{1,3},{3,1},... | collective-permute-start | bytes 294920 | tf_op jit(solution)/shard_map/ppermute | solution.py:993
  15.5 11.4 %collective-permute-start.5 = (f32[32,8,128]{2,1,0:T(8,128)S(1)}, f32[32,8,128]{2,1,0:T(8,128)S(1)}, u32[]{:S(2)}, u32[]{:S(2)}) collective-permute-start(f32[32,8,128]{2,1,0:T(8,128)S(1)} %get-tuple-element.61.refs_5_), channel_id=1, source_target_pairs={{0,1},{1,0},{2,3},{3,2},{4,5},{5,4},{6,7},{7,6},{8,9},{9,8},{10,11... | collective-permute-start | bytes 393224 | tf_op jit(solution)/shard_map/ppermute | solution.py:994
  15.6 9.9 %collective-permute-start.3 = (f32[4,48,128]{2,1,0:T(8,128)S(1)}, f32[4,48,128]{2,1,0:T(8,128)S(1)}, u32[]{:S(2)}, u32[]{:S(2)}) collective-permute-start(f32[4,48,128]{2,1,0:T(8,128)S(1)} %get-tuple-element.59.refs_3_), channel_id=1, source_target_pairs={{6,8},{8,6},{14,0},{0,14},{7,9},{9,7},{15,1},{1,15},{22,24},{24,22... | collective-permute-start | bytes 294920 | tf_op jit(solution)/shard_map/ppermute | solution.py:990
  19.8 7.1 %collective-permute-start.4 = (f32[4,48,128]{2,1,0:T(8,128)S(1)}, f32[4,48,128]{2,1,0:T(8,128)S(1)}, u32[]{:S(2)}, u32[]{:S(2)}) collective-permute-start(f32[4,48,128]{2,1,0:T(8,128)S(1)} %get-tuple-element.60.refs_4_), channel_id=1, source_target_pairs={{0,2},{2,0},{4,6},{6,4},{8,10},{10,8},{12,14},{14,12},{1,3},{3,1},... | collective-permute-start | bytes 294920 | tf_op jit(solution)/shard_map/ppermute | solution.py:993
  27.0 11.5 %collective-permute-start.8 = (f32[32,8,128]{2,1,0:T(8,128)S(1)}, f32[32,8,128]{2,1,0:T(8,128)S(1)}, u32[]{:S(2)}, u32[]{:S(2)}) collective-permute-start(f32[32,8,128]{2,1,0:T(8,128)S(1)} %get-tuple-element.69.refs_5_), channel_id=1, source_target_pairs={{0,1},{1,0},{2,3},{3,2},{4,5},{5,4},{6,7},{7,6},{8,9},{9,8},{10,11... | collective-permute-start | bytes 393224 | tf_op jit(solution)/shard_map/ppermute | solution.py:994
  27.1 9.9 %collective-permute-start.6 = (f32[4,48,128]{2,1,0:T(8,128)S(1)}, f32[4,48,128]{2,1,0:T(8,128)S(1)}, u32[]{:S(2)}, u32[]{:S(2)}) collective-permute-start(f32[4,48,128]{2,1,0:T(8,128)S(1)} %get-tuple-element.67.refs_3_), channel_id=1, source_target_pairs={{6,8},{8,6},{14,0},{0,14},{7,9},{9,7},{15,1},{1,15},{22,24},{24,22... | collective-permute-start | bytes 294920 | tf_op jit(solution)/shard_map/ppermute | solution.py:990
  31.4 7.1 %collective-permute-start.7 = (f32[4,48,128]{2,1,0:T(8,128)S(1)}, f32[4,48,128]{2,1,0:T(8,128)S(1)}, u32[]{:S(2)}, u32[]{:S(2)}) collective-permute-start(f32[4,48,128]{2,1,0:T(8,128)S(1)} %get-tuple-element.68.refs_4_), channel_id=1, source_target_pairs={{0,2},{2,0},{4,6},{6,4},{8,10},{10,8},{12,14},{14,12},{1,3},{3,1},... | collective-permute-start | bytes 294920 | tf_op jit(solution)/shard_map/ppermute | solution.py:993
  38.7 6.8 %collective-permute-start.10 = (f32[32,8,128]{2,1,0:T(8,128)S(1)}, f32[32,8,128]{2,1,0:T(8,128)S(1)}, u32[]{:S(2)}, u32[]{:S(2)}) collective-permute-start(f32[32,8,128]{2,1,0:T(8,128)S(1)} %get-tuple-element.78.refs_4_), channel_id=1, source_target_pairs={{0,1},{1,0},{2,3},{3,2},{4,5},{5,4},{6,7},{7,6},{8,9},{9,8},{10,11... | collective-permute-start | bytes 393224 | tf_op jit(solution)/shard_map/ppermute | solution.py:994
  38.7 6.7 %collective-permute-start.9 = (f32[4,48,128]{2,1,0:T(8,128)S(1)}, f32[4,48,128]{2,1,0:T(8,128)S(1)}, u32[]{:S(2)}, u32[]{:S(2)}) collective-permute-start(f32[4,48,128]{2,1,0:T(8,128)S(1)} %get-tuple-element.77.refs_3_), channel_id=1, source_target_pairs={{0,2},{2,0},{4,6},{6,4},{8,10},{10,8},{12,14},{14,12},{1,3},{3,1},... | collective-permute-start | bytes 294920 | tf_op jit(solution)/shard_map/ppermute | solution.py:993
  38.8 10.4 %collective-permute-start.11 = (f32[4,48,128]{2,1,0:T(8,128)S(1)}, f32[4,48,128]{2,1,0:T(8,128)S(1)}, u32[]{:S(2)}, u32[]{:S(2)}) collective-permute-start(f32[4,48,128]{2,1,0:T(8,128)S(1)} %get-tuple-element.76.refs_2_), channel_id=1, source_target_pairs={{6,8},{8,6},{14,0},{0,14},{7,9},{9,7},{15,1},{1,15},{22,24},{24,22... | collective-permute-start | bytes 294920 | tf_op jit(solution)/shard_map/ppermute | solution.py:990
  43.1 9.3 %collective-permute-start.12 = (f32[224,128]{1,0:T(8,128)S(1)}, f32[224,128]{1,0:T(8,128)S(1)}, u32[]{:S(2)}, u32[]{:S(2)}) collective-permute-start(f32[224,128]{1,0:T(8,128)S(1)} %get-tuple-element.89), channel_id=1, source_target_pairs={{0,8},{2,10},{4,12},{6,14},{8,0},{10,2},{12,4},{14,6},{1,9},{3,11}... | collective-permute-start | bytes 344072 | tf_op jit(solution)/shard_map/ppermute | solution.py:1022
  46.0 9.5 %collective-permute-start.13 = (f32[200,128]{1,0:T(8,128)S(1)}, f32[200,128]{1,0:T(8,128)S(1)}, u32[]{:S(2)}, u32[]{:S(2)}) collective-permute-start(f32[200,128]{1,0:T(8,128)S(1)} %get-tuple-element.93), channel_id=1, source_target_pairs={{0,8},{2,10},{4,12},{6,14},{8,0},{10,2},{12,4},{14,6},{1,9},{3,11}... | collective-permute-start | bytes 307208 | tf_op jit(solution)/shard_map/ppermute | solution.py:1029
  49.4 6.1 %collective-permute-start.14 = (f32[48,128]{1,0:T(8,128)S(1)}, f32[48,128]{1,0:T(8,128)S(1)}, u32[]{:S(2)}, u32[]{:S(2)}) collective-permute-start(f32[48,128]{1,0:T(8,128)S(1)} %get-tuple-element.94), channel_id=1, source_target_pairs={{0,8},{2,10},{4,12},{6,14},{8,0},{10,2},{12,4},{14,6},{1,9},{3,11}... | collective-permute-start | bytes 73736 | tf_op jit(solution)/shard_map/ppermute | solution.py:1032

commit v12 on v11

--- a/solution.py
+++ b/solution.py
@@ -113,7 +113,9 @@
     return flat[pl.ds(start, count_a, stride=2 * stride), :]
 
 
-def inner_step(number, points, waves, current, faces, previous, courant, snapshots=None, matrices=None):
+def inner_step(number, points, waves, current, faces, previous, courant, snapshots=None, matrices=None,
+    halos=None,
+):
     count_x, count_y, count_z = courant.shape
     count_a, count_b = count_x // 2, count_y // 2
     first = faces is None
@@ -142,15 +144,19 @@
         previous_ref, courant_ref = take(2)
         if snapshot:
             steps_ref, matrices_ref = take(2)
-        padded, next_ref, qx_ref, qy_ref = take(4)
+        if last:
+            near_in, side_in, steps_ref, matrix_ref = take(4)
+        padded, next_ref = take(2)
+        if last:
+            late_ref, sent_ref = take(2)
+        else:
+            qx_ref, qy_ref = take(2)
         if first:
             kept_ref, cx_ref, cy_ref, points_ref, waves_ref = take(5)
         if snapshot:
             own_out, sent_out, own_matrix, sent_matrix, flag_ref = take(5)
         if ahead:
             (ahead_ref,) = take(1)
-        if last:
-            (even_ref,) = take(1)
         zpart, addpart = take(2)
         if last:
             addpart = added_ref
@@ -160,6 +166,10 @@
             (sems,) = take(1)
         if snapshot:
             even_ref, wanted, sems = take(3)
+        if last:
+            wanted, sem = take(2)
+            last_copy = pltpu.make_async_copy(steps_ref, wanted, sem)
+            last_copy.start()
 
         place = Place()
         block = place.block(count_y)
@@ -216,6 +226,17 @@
                 padded[high, columns] = far_ref[...]
 
             padded[rows, pl.ds(pl.multiple_of(block + SIDE, SIDE), SIDE)] = side_ref[...]
+        if last:
+            beside = pl.multiple_of((1 - place.y) * (count_y + SIDE), SIDE)
+            padded[rows, pl.ds(beside, SIDE)] = side_in[...]
+
+            @pl.when(place.even)
+            def _():
+                padded[pl.ds(count_x + WIDTH, WIDTH), columns] = near_in[...]
+
+            @pl.when(jnp.logical_not(place.even))
+            def _():
+                padded[pl.ds(0, WIDTH), columns] = near_in[...]
 
         gap = jnp.abs(
             lax.broadcasted_iota(jnp.int32, (count_z, count_z), 0)
@@ -327,21 +348,34 @@
 
         lax.fori_loop(0, count_x // depth, row_group, 0)
 
-        next_columns = pl.ds(next_y, count_y)
-        qx_ref[pl.ds(0, WIDTH)] = next_ref[pl.ds(next_x, WIDTH), next_columns]
-        qx_ref[pl.ds(WIDTH, WIDTH)] = next_ref[
-            pl.ds(next_x + count_x - WIDTH, WIDTH), next_columns
-        ]
-        qy_ref[...] = next_ref[
-            pl.ds(next_x, count_x), pl.ds(pl.multiple_of(block + next_y, SIDE), SIDE)
-        ]
+        if not last:
+            next_columns = pl.ds(next_y, count_y)
+            qx_ref[pl.ds(0, WIDTH)] = next_ref[pl.ds(next_x, WIDTH), next_columns]
+            qx_ref[pl.ds(WIDTH, WIDTH)] = next_ref[
+                pl.ds(next_x + count_x - WIDTH, WIDTH), next_columns
+            ]
+            qy_ref[...] = next_ref[
+                pl.ds(next_x, count_x), pl.ds(pl.multiple_of(block + next_y, SIDE), SIDE)
+            ]
         if first:
             cx_ref[pl.ds(0, WIDTH)] = kept_ref[pl.ds(0, WIDTH)]
             cx_ref[pl.ds(WIDTH, WIDTH)] = kept_ref[pl.ds(count_x - WIDTH, WIDTH)]
             cy_ref[...] = kept_ref[:, pl.ds(block, SIDE)]
         if last:
-            for b in range(count_b):
-                even_ref[b] = even_rows(padded, WIDTH, SIDE, count_a, b)
+            last_copy.wait()
+            wants_last = wanted[place.field, 1] == STEPS
+
+            @pl.when(wants_last)
+            def _():
+                for b in range(count_b):
+                    late_ref[b] = even_rows(next_ref, 0, 0, count_a, b)
+
+            @pl.when(jnp.logical_not(wants_last))
+            def _():
+                for b in range(count_b):
+                    late_ref[b] = even_rows(padded, WIDTH, SIDE, count_a, b)
+
+            give_into(place, late_ref, matrix_ref, sent_ref)
         if snapshot:
             for copy in copies:
                 copy.wait()
@@ -368,7 +402,10 @@
     slab, side = shape(2 * WIDTH, count_y, count_z), shape(count_x, SIDE, count_z)
     even = shape(count_b, count_a, count_z)
     bordered = shape(count_x + 2 * WIDTH, count_y + 2 * SIDE, count_z)
-    outs = [bordered, full if last else bordered, slab, side]
+    if last:
+        outs = [bordered, full, even, given_shape(count_a, count_b, count_z)]
+    else:
+        outs = [bordered, bordered, slab, side]
     if first:
         outs += [full, slab, side, shape(8, count_j, dtype=jnp.int32), shape(8, count_j)]
     if snapshot:
@@ -382,8 +419,6 @@
         ]
     if ahead:
         outs.append(full)
-    if last:
-        outs.append(even)
     place_of = spec(pltpu.HBM) if first else spec(pltpu.VMEM)
     if first:
         operands = [*points, current]
@@ -403,6 +438,10 @@
         scratch.append(pltpu.VMEM(full.shape, F32))
         scratch += [pltpu.VMEM(array.shape, array.dtype) for array in points]
         scratch.append(pltpu.SemaphoreType.DMA((6,)))
+    if last:
+        operands += [*halos, snapshots, matrices]
+        specs += [spec(pltpu.VMEM)] * 2 + [spec(pltpu.HBM), spec(pltpu.VMEM)]
+        scratch += [pltpu.SMEM(snapshots.shape, jnp.int32), pltpu.SemaphoreType.DMA]
     if snapshot:
         operands += [snapshots, matrices]
         specs += [spec(pltpu.HBM)] * 2
@@ -702,61 +741,6 @@
 def given_shape(count_a, count_b, count_z):
     groups = count_b // GROUP
     return shape(sum(give_rows(groups)) + edge_slots(count_a, groups, count_z)[1], count_z)
-
-
-def last_step(flag, even_before, current, parts, near, side, matrix):
-    count_x, count_y, count_z = current.shape
-    count_a, count_b = count_x // 2, count_y // 2
-
-    def kernel(
-        flag_ref, even_ref, current_ref, qx_ref, qy_ref, cx_ref, cy_ref, near_ref, side_ref,
-        matrix_ref, final_ref, late_ref, sent_ref, far_out, near_out, side_out,
-    ):
-        place = Place()
-        add_halo(
-            place, (qx_ref, qy_ref, cx_ref, cy_ref), (None, near_ref, side_ref),
-            (far_out, near_out, side_out),
-        )
-        low, high = pl.ds(0, WIDTH), pl.ds(count_x - WIDTH, WIDTH)
-
-        @pl.when(place.even)
-        def _():
-            final_ref[high] = near_out[...]
-            final_ref[low] = far_out[...]
-
-        @pl.when(jnp.logical_not(place.even))
-        def _():
-            final_ref[low] = near_out[...]
-            final_ref[high] = far_out[...]
-
-        final_ref[:, pl.ds(place.block(count_y), SIDE)] = side_out[...]
-        wants_last = jnp.broadcast_to(flag_ref[0:1, :], (count_a, count_z)) > 0.5
-        for b in range(count_b):
-            late_ref[b] = jnp.where(
-                wants_last, even_rows(final_ref, 0, 0, count_a, b), even_ref[b]
-            )
-        give_into(place, late_ref, matrix_ref, sent_ref)
-
-    slab, _, side_shape = face_shapes(count_x, count_y, count_z)
-    return pl.pallas_call(
-        kernel,
-        out_shape=(
-            shape(*current.shape),
-            shape(count_b, count_a, count_z),
-            given_shape(count_a, count_b, count_z),
-        ),
-        in_specs=[spec(pltpu.VMEM)] * 10,
-        out_specs=(spec(pltpu.VMEM),) * 3,
-        scratch_shapes=[
-            pltpu.VMEM(slab.shape, F32),
-            pltpu.VMEM(slab.shape, F32),
-            pltpu.VMEM(side_shape.shape, F32),
-        ],
-        input_output_aliases={2: 0},
-        compiler_params=params(12),
-        cost_estimate=cost(count_x * count_y * count_z, 10, 3),
-        name="last_step",
-    )(flag, even_before, current, *parts, near, side, matrix)
 
 
 def far_rows(count_b):
@@ -1021,10 +1005,9 @@
     )
     other_early = lax.ppermute(sent_early, "gx", across)
     faces = halo_step((qx, qy, cx, cy), halos)
-    far, near, side = exchange(faces)
-    _, next4, qx, qy, even3 = inner_step(3, added, None, next3, faces, whole2, courant)
-    final, late, sent_late = last_step(
-        flag, even3, next4, (qx, qy, cx, cy), near, side, sent_matrix
+    far, *halos = exchange(faces)
+    _, final, late, sent_late = inner_step(
+        3, added, None, next3, faces, whole2, courant, snapshot_steps, sent_matrix, halos
     )
     other_late = lax.ppermute(sent_late, "gx", across)
     partial, codes = lag_image(count_x // 2, lag_offsets, own_early, other_early)

time: 57.1 us -> 57.1 us (level)
    ppermute x4, waiting for transfers between devices: 4.83 us -> 5.61 us  [send_near(): near = lax.ppermute(near, 'gx', near_pairs)]
    ppermute x1, starting transfers between devices: 2.95 us -> 2.19 us  [body(): other_late = lax.ppermute(sent_late, 'gx', across)]
    pallas_call x1 -> x0, Pallas kernels: 0.59 us -> none  [last_step(): pl.pallas_call(kernel, out_shape=(shape(*current.shape), shape(count_b, c...]
    ppermute x1, waiting for transfers between devices: 2.86 us -> 2.27 us  [body(): other_early = lax.ppermute(sent_early, 'gx', across)]
  transfers between devices with their start and end apart: 15 -> 15, of which waited for: 7 -> 8; matrix products, arithmetic and copies ran while one was open for 0% -> 0% of each run, Pallas kernels for 30% -> 29%
where the time goes in v12:
time: 57.1 us; the launch traced here: 56.6 us
  starting transfers between devices  24.1 us (42%)
  Pallas kernels  19.2 us (34%)
  waiting for transfers between devices  12.4 us (22%)
  between operations  0.86 us (2%)
    ppermute x4, starting transfers between devices, send_far(): return lax.ppermute(far, 'gx', far_pairs)  20.2 us
    pallas_call x4, Pallas kernels, inner_step(): pl.pallas_call(kernel, out_shape=tuple(outs), in_specs=specs, out_specs=(...  13.1 us
    ppermute x4, waiting for transfers between devices, send_near(): near = lax.ppermute(near, 'gx', near_pairs)  5.61 us
    ppermute x4, waiting for transfers between devices, send_far(): return lax.ppermute(far, 'gx', far_pairs)  4.5 us
    pallas_call x2, Pallas kernels, lag_image(): pl.pallas_call(kernel, out_shape=image if last else (image, shape(8, coun...  2.31 us
    ppermute x1, waiting for transfers between devices, body(): other_early = lax.ppermute(sent_early, 'gx', across)  2.27 us
    ppermute x1, starting transfers between devices, body(): other_late = lax.ppermute(sent_late, 'gx', across)  2.19 us
  transfers between devices with their start and end apart: 15, of which 8 were waited for; matrix products, arithmetic and copies ran while one was open for 0% of the time, Pallas kernels for 29%

profile of v12, /device:TPU:0, one launch (start us, length us, event | category | flops | bytes accessed | tf_op | source)
XLA Modules:
  0.0 56.6 jit_solution(840899795321676055)
XLA Ops:
  0.6 1.1 %first_faces.1 = (f32[4,48,128]{2,1,0:T(8,128)S(1)}, f32[4,48,128]{2,1,0:T(8,128)S(1)}, f32[32,8,128]{2,1,0:T(8,128)S(1)}) custom-call(f32[32,48,128]{2,1,0:T(8,128)} %field_ref.1), custom_call_target="tpu_custom_call" | custom-call | tf_op jit(solution)/shard_map/first_faces/pallas_call | solution.py:93
  1.8 0.6 collective-permute-start.2
  2.3 7.5 %collective-permute-start = (f32[4,48,128]{2,1,0:T(8,128)S(1)}, f32[4,48,128]{2,1,0:T(8,128)S(1)}, u32[]{:S(2)}, u32[]{:S(2)}) collective-permute-start(f32[4,48,128]{2,1,0:T(8,128)S(1)} %get-tuple-element.52), channel_id=1, source_target_pairs={{6,8},{8,6},{14,0},{0,14},{7,9},{9,7},{15,1},{1,15},{22,24},{24,22... | collective-permute-start | bytes 294920 | tf_op jit(solution)/shard_map/ppermute | solution.py:974
  9.9 3.6 %shard_map.113 = (f32[40,64,128]{2,1,0:T(8,128)S(1)}, f32[40,64,128]{2,1,0:T(8,128)S(1)}, f32[8,48,128]{2,1,0:T(8,128)S(1)}, f32[32,8,128]{2,1,0:T(8,128)S(1)}, ...) custom-call(s32[3,8]{1,0:T(4,128)} %refs_0_.2, ...), custom_call_target="tpu_custom_call" | custom-call | flops 11796480 | bytes 4718592 | tf_op jit(solution)/shard_map/pallas_call | solution.py:453
  13.5 1.9 %collective-permute-done.1.refs_5_ = f32[4,48,128]{2,1,0:T(8,128)S(1)} collective-permute-done((f32[4,48,128]{2,1,0:T(8,128)S(1)}, f32[4,48,128]{2,1,0:T(8,128)S(1)}, u32[]{:S(2)}, u32[]{:S(2)}) %collective-permute-start.1) | collective-permute-done | bytes 98336 | tf_op jit(solution)/shard_map/ppermute | solution.py:977
  15.3 0.1 halo_step.3
  15.5 0.1 collective-permute-start.5
  15.6 4.2 %collective-permute-start.3 = (f32[4,48,128]{2,1,0:T(8,128)S(1)}, f32[4,48,128]{2,1,0:T(8,128)S(1)}, u32[]{:S(2)}, u32[]{:S(2)}) collective-permute-start(f32[4,48,128]{2,1,0:T(8,128)S(1)} %get-tuple-element.55.refs_3_), channel_id=1, source_target_pairs={{6,8},{8,6},{14,0},{0,14},{7,9},{9,7},{15,1},{1,15},{22,24},{24,22... | collective-permute-start | bytes 294920 | tf_op jit(solution)/shard_map/ppermute | solution.py:974
  19.9 3.4 %shard_map.114 = (f32[40,64,128]{2,1,0:T(8,128)S(1)}, f32[40,64,128]{2,1,0:T(8,128)S(1)}, f32[8,48,128]{2,1,0:T(8,128)S(1)}, f32[32,8,128]{2,1,0:T(8,128)S(1)}, f32[32,48,128]{2,1,0:T(8,128)S(1)}) custom-call(s32[8,256]{1,0:T(8,128)S(1)} %get-tuple-element.45.refs_0_, f32[8,256]{1,0:T(8,128)S(1)} %get-tuple-element.46.refs_1_, ...), custom_call_target="tpu_custom_call", output_to_operand_aliasing={{0}: (2, {})} | custom-call | flops 11796480 | bytes 4718592 | tf_op jit(solution)/shard_map/pallas_call | solution.py:453
  23.3 2.1 %collective-permute-done.3.refs_4_ = f32[4,48,128]{2,1,0:T(8,128)S(1)} collective-permute-done((f32[4,48,128]{2,1,0:T(8,128)S(1)}, f32[4,48,128]{2,1,0:T(8,128)S(1)}, u32[]{:S(2)}, u32[]{:S(2)}) %collective-permute-start.3) | collective-permute-done | bytes 98336 | tf_op jit(solution)/shard_map/ppermute | solution.py:974
  25.4 1.4 %collective-permute-done.4.refs_5_ = f32[4,48,128]{2,1,0:T(8,128)S(1)} collective-permute-done((f32[4,48,128]{2,1,0:T(8,128)S(1)}, f32[4,48,128]{2,1,0:T(8,128)S(1)}, u32[]{:S(2)}, u32[]{:S(2)}) %collective-permute-start.4) | collective-permute-done | bytes 98336 | tf_op jit(solution)/shard_map/ppermute | solution.py:977
  26.9 0.1 halo_step.4
  27.0 0.1 collective-permute-start.8
  27.1 4.3 %collective-permute-start.6 = (f32[4,48,128]{2,1,0:T(8,128)S(1)}, f32[4,48,128]{2,1,0:T(8,128)S(1)}, u32[]{:S(2)}, u32[]{:S(2)}) collective-permute-start(f32[4,48,128]{2,1,0:T(8,128)S(1)} %get-tuple-element.63.refs_3_), channel_id=1, source_target_pairs={{6,8},{8,6},{14,0},{0,14},{7,9},{9,7},{15,1},{1,15},{22,24},{24,22... | collective-permute-start | bytes 294920 | tf_op jit(solution)/shard_map/ppermute | solution.py:974
  31.4 0.1 collective-permute-start.7
  31.5 3.5 %shard_map.115 = (f32[40,64,128]{2,1,0:T(8,128)S(1)}, f32[40,64,128]{2,1,0:T(8,128)S(1)}, f32[8,48,128]{2,1,0:T(8,128)S(1)}, f32[32,8,128]{2,1,0:T(8,128)S(1)}, ...) custom-call(s32[8,256]{1,0:T(8,128)S(1)} %get-tuple-element.45.refs_, ...), custom_call_target="tpu_custom_call", output_to_operand_aliasing={{0}: (2, {})} | custom-call | flops 11796480 | bytes 4718592 | tf_op jit(solution)/shard_map/pallas_call | solution.py:453
  35.0 2.0 %collective-permute-done.6.refs_4_ = f32[4,48,128]{2,1,0:T(8,128)S(1)} collective-permute-done((f32[4,48,128]{2,1,0:T(8,128)S(1)}, f32[4,48,128]{2,1,0:T(8,128)S(1)}, u32[]{:S(2)}, u32[]{:S(2)}) %collective-permute-start.6) | collective-permute-done | bytes 98336 | tf_op jit(solution)/shard_map/ppermute | solution.py:974
  37.0 1.5 %collective-permute-done.7.refs_5_ = f32[4,48,128]{2,1,0:T(8,128)S(1)} collective-permute-done((f32[4,48,128]{2,1,0:T(8,128)S(1)}, f32[4,48,128]{2,1,0:T(8,128)S(1)}, u32[]{:S(2)}, u32[]{:S(2)}) %collective-permute-start.7) | collective-permute-done | bytes 98336 | tf_op jit(solution)/shard_map/ppermute | solution.py:977
  38.5 0.1 halo_step.5
  38.7 0.1 collective-permute-start.10
  38.8 4.2 %collective-permute-start.11 = (f32[4,48,128]{2,1,0:T(8,128)S(1)}, f32[4,48,128]{2,1,0:T(8,128)S(1)}, u32[]{:S(2)}, u32[]{:S(2)}) collective-permute-start(f32[4,48,128]{2,1,0:T(8,128)S(1)} %get-tuple-element.72.refs_2_), channel_id=1, source_target_pairs={{6,8},{8,6},{14,0},{0,14},{7,9},{9,7},{15,1},{1,15},{22,24},{24,22... | collective-permute-start | bytes 294920 | tf_op jit(solution)/shard_map/ppermute | solution.py:974
  43.2 0.8 %collective-permute-done.9.refs_7_ = f32[4,48,128]{2,1,0:T(8,128)S(1)} collective-permute-done((f32[4,48,128]{2,1,0:T(8,128)S(1)}, f32[4,48,128]{2,1,0:T(8,128)S(1)}, u32[]{:S(2)}, u32[]{:S(2)}) %collective-permute-start.9) | collective-permute-done | bytes 98336 | tf_op jit(solution)/shard_map/ppermute | solution.py:977
  43.9 2.7 %shard_map.116 = (f32[40,64,128]{2,1,0:T(8,128)S(1)}, f32[32,48,128]{2,1,0:T(8,128)S(1)}, f32[24,16,128]{2,1,0:T(8,128)S(1)}, f32[200,128]{1,0:T(8,128)S(1)}) custom-call(f32[32,48,128]{2,1,0:T(8,128)S(1)} %get-tuple-element.68.refs_0_, f32[40,64,128]{2,1,0:T(8,128)S(1)} %get-tuple-element.69.refs_1_, ...), custom_call_target="tpu_custom_call", output_to_operand_aliasing={{0}: (1, {})} | custom-call | flops 11796480 | bytes 4718592 | tf_op jit(solution)/shard_map/pallas_call | solution.py:453
  46.6 2.2 %collective-permute-start.13 = (f32[200,128]{1,0:T(8,128)S(1)}, f32[200,128]{1,0:T(8,128)S(1)}, u32[]{:S(2)}, u32[]{:S(2)}) collective-permute-start(f32[200,128]{1,0:T(8,128)S(1)} %get-tuple-element.85), channel_id=1, source_target_pairs={{0,8},{2,10},{4,12},{6,14},{8,0},{10,2},{12,4},{14,6},{1,9},{3,11}... | collective-permute-start | bytes 307208 | tf_op jit(solution)/shard_map/ppermute | solution.py:1012
  48.8 0.4 collective-permute-done.11.far_ref
  49.2 0.3 last_far.1
  49.4 0.5 collective-permute-start.14
  50.0 2.3 %collective-permute-done.12.refs_2_ = f32[224,128]{1,0:T(8,128)S(1)} collective-permute-done((f32[224,128]{1,0:T(8,128)S(1)}, f32[224,128]{1,0:T(8,128)S(1)}, u32[]{:S(2)}, u32[]{:S(2)}) %collective-permute-start.12) | collective-permute-done | bytes 114720 | tf_op jit(solution)/shard_map/ppermute | solution.py:1006
  52.2 1.2 %early_image.1 = (f32[17,16,768]{2,1,0:T(8,128)S(1)}, s32[8,128]{1,0:T(8,128)S(1)}) custom-call(s32[17]{0:T(128)} %lags_ref.1, f32[4,96,128]{2,1,0:T(8,128)S(1)} %get-tuple-element.80.refs_1_, f32[224,128]{1,0:T(8,128)S(1)} %collective-permute-done.12.refs_2_), custom_call_target="tpu_custom_call" | custom-call | flops 2088960 | bytes 1671168 | tf_op jit(solution)/shard_map/early_image/pallas_call | solution.py:930
  53.4 0.9 %write_out.1 = f32[32,48,128]{2,1,0:T(8,128)} custom-call(f32[32,48,128]{2,1,0:T(8,128)S(1)} %get-tuple-element.79.level_ref), custom_call_target="tpu_custom_call" | custom-call | bytes 1572864 | tf_op jit(solution)/shard_map/write_out/pallas_call | solution.py:811
  54.3 1.1 %pack_own.1.refs_1_ = f32[17,96,128]{2,1,0:T(8,128)S(1)} custom-call(s32[17]{0:T(128)} %lags_ref.1, f32[24,16,128]{2,1,0:T(8,128)S(1)} %get-tuple-element.83.even_ref, bf16[512,512]{1,0:T(8,128)(2,1)S(1)} %get-tuple-element.84.matrix_ref), custom_call_target="tpu_custom_call" | custom-call | flops 50331648 | bytes 786432 | tf_op jit(solution)/shard_map/pack_own/pallas_call | solution.py:620
  55.4 1.1 %last_image.1 = f32[17,16,768]{2,1,0:T(8,128)} custom-call(s32[8,128]{1,0:T(8,128)S(1)} %get-tuple-element.82.refs_0_, f32[17,96,128]{2,1,0:T(8,128)S(1)} %pack_own.1.refs_1_, f32[200,128]{1,0:T(8,128)S(1)} %collective-permute-done.13.refs_2_, f32[48,128]{1,0:T(8,128)S(1)} %collective-permute-done.14.refs_3_, f32[17,16,768]{2,1,0:T(8,128)S(1)} %get-tuple-element.87.refs_4_), custom_call_target="tpu_custom_call" | custom-call | flops 2088960 | bytes 1671168 | tf_op jit(solution)/shard_map/last_image/pallas_call | solution.py:930
  (13 shorter events, 0.3 us)
Async XLA Ops:
  0.6 9.2 %copy-start = (f32[32,48,128]{2,1,0:T(8,128)S(1)}, f32[32,48,128]{2,1,0:T(8,128)}, u32[]{:S(2)}) copy-start(f32[32,48,128]{2,1,0:T(8,128)} %field_ref.1) | copy-start | bytes 2359300
  1.8 13.6 %collective-permute-start.2 = (f32[32,8,128]{2,1,0:T(8,128)S(1)}, f32[32,8,128]{2,1,0:T(8,128)S(1)}, u32[]{:S(2)}, u32[]{:S(2)}) collective-permute-start(f32[32,8,128]{2,1,0:T(8,128)S(1)} %get-tuple-element.54), channel_id=1, source_target_pairs={{0,1},{1,0},{2,3},{3,2},{4,5},{5,4},{6,7},{7,6},{8,9},{9,8},{10,11... | collective-permute-start | bytes 393224 | tf_op jit(solution)/shard_map/ppermute | solution.py:978
  2.3 11.1 %collective-permute-start = (f32[4,48,128]{2,1,0:T(8,128)S(1)}, f32[4,48,128]{2,1,0:T(8,128)S(1)}, u32[]{:S(2)}, u32[]{:S(2)}) collective-permute-start(f32[4,48,128]{2,1,0:T(8,128)S(1)} %get-tuple-element.52), channel_id=1, source_target_pairs={{6,8},{8,6},{14,0},{0,14},{7,9},{9,7},{15,1},{1,15},{22,24},{24,22... | collective-permute-start | bytes 294920 | tf_op jit(solution)/shard_map/ppermute | solution.py:974
  9.8 5.5 %collective-permute-start.1 = (f32[4,48,128]{2,1,0:T(8,128)S(1)}, f32[4,48,128]{2,1,0:T(8,128)S(1)}, u32[]{:S(2)}, u32[]{:S(2)}) collective-permute-start(f32[4,48,128]{2,1,0:T(8,128)S(1)} %get-tuple-element.53), channel_id=1, source_target_pairs={{0,2},{2,0},{4,6},{6,4},{8,10},{10,8},{12,14},{14,12},{1,3},{3,1},... | collective-permute-start | bytes 294920 | tf_op jit(solution)/shard_map/ppermute | solution.py:977
  15.5 11.4 %collective-permute-start.5 = (f32[32,8,128]{2,1,0:T(8,128)S(1)}, f32[32,8,128]{2,1,0:T(8,128)S(1)}, u32[]{:S(2)}, u32[]{:S(2)}) collective-permute-start(f32[32,8,128]{2,1,0:T(8,128)S(1)} %get-tuple-element.57.refs_5_), channel_id=1, source_target_pairs={{0,1},{1,0},{2,3},{3,2},{4,5},{5,4},{6,7},{7,6},{8,9},{9,8},{10,11... | collective-permute-start | bytes 393224 | tf_op jit(solution)/shard_map/ppermute | solution.py:978
  15.6 9.9 %collective-permute-start.3 = (f32[4,48,128]{2,1,0:T(8,128)S(1)}, f32[4,48,128]{2,1,0:T(8,128)S(1)}, u32[]{:S(2)}, u32[]{:S(2)}) collective-permute-start(f32[4,48,128]{2,1,0:T(8,128)S(1)} %get-tuple-element.55.refs_3_), channel_id=1, source_target_pairs={{6,8},{8,6},{14,0},{0,14},{7,9},{9,7},{15,1},{1,15},{22,24},{24,22... | collective-permute-start | bytes 294920 | tf_op jit(solution)/shard_map/ppermute | solution.py:974
  19.8 7.1 %collective-permute-start.4 = (f32[4,48,128]{2,1,0:T(8,128)S(1)}, f32[4,48,128]{2,1,0:T(8,128)S(1)}, u32[]{:S(2)}, u32[]{:S(2)}) collective-permute-start(f32[4,48,128]{2,1,0:T(8,128)S(1)} %get-tuple-element.56.refs_4_), channel_id=1, source_target_pairs={{0,2},{2,0},{4,6},{6,4},{8,10},{10,8},{12,14},{14,12},{1,3},{3,1},... | collective-permute-start | bytes 294920 | tf_op jit(solution)/shard_map/ppermute | solution.py:977
  27.0 11.5 %collective-permute-start.8 = (f32[32,8,128]{2,1,0:T(8,128)S(1)}, f32[32,8,128]{2,1,0:T(8,128)S(1)}, u32[]{:S(2)}, u32[]{:S(2)}) collective-permute-start(f32[32,8,128]{2,1,0:T(8,128)S(1)} %get-tuple-element.65.refs_5_), channel_id=1, source_target_pairs={{0,1},{1,0},{2,3},{3,2},{4,5},{5,4},{6,7},{7,6},{8,9},{9,8},{10,11... | collective-permute-start | bytes 393224 | tf_op jit(solution)/shard_map/ppermute | solution.py:978
  27.1 9.9 %collective-permute-start.6 = (f32[4,48,128]{2,1,0:T(8,128)S(1)}, f32[4,48,128]{2,1,0:T(8,128)S(1)}, u32[]{:S(2)}, u32[]{:S(2)}) collective-permute-start(f32[4,48,128]{2,1,0:T(8,128)S(1)} %get-tuple-element.63.refs_3_), channel_id=1, source_target_pairs={{6,8},{8,6},{14,0},{0,14},{7,9},{9,7},{15,1},{1,15},{22,24},{24,22... | collective-permute-start | bytes 294920 | tf_op jit(solution)/shard_map/ppermute | solution.py:974
  31.4 7.1 %collective-permute-start.7 = (f32[4,48,128]{2,1,0:T(8,128)S(1)}, f32[4,48,128]{2,1,0:T(8,128)S(1)}, u32[]{:S(2)}, u32[]{:S(2)}) collective-permute-start(f32[4,48,128]{2,1,0:T(8,128)S(1)} %get-tuple-element.64.refs_4_), channel_id=1, source_target_pairs={{0,2},{2,0},{4,6},{6,4},{8,10},{10,8},{12,14},{14,12},{1,3},{3,1},... | collective-permute-start | bytes 294920 | tf_op jit(solution)/shard_map/ppermute | solution.py:977
  38.7 5.3 %collective-permute-start.10 = (f32[32,8,128]{2,1,0:T(8,128)S(1)}, f32[32,8,128]{2,1,0:T(8,128)S(1)}, u32[]{:S(2)}, u32[]{:S(2)}) collective-permute-start(f32[32,8,128]{2,1,0:T(8,128)S(1)} %get-tuple-element.74.refs_4_), channel_id=1, source_target_pairs={{0,1},{1,0},{2,3},{3,2},{4,5},{5,4},{6,7},{7,6},{8,9},{9,8},{10,11... | collective-permute-start | bytes 393224 | tf_op jit(solution)/shard_map/ppermute | solution.py:978
  38.7 5.2 %collective-permute-start.9 = (f32[4,48,128]{2,1,0:T(8,128)S(1)}, f32[4,48,128]{2,1,0:T(8,128)S(1)}, u32[]{:S(2)}, u32[]{:S(2)}) collective-permute-start(f32[4,48,128]{2,1,0:T(8,128)S(1)} %get-tuple-element.73.refs_3_), channel_id=1, source_target_pairs={{0,2},{2,0},{4,6},{6,4},{8,10},{10,8},{12,14},{14,12},{1,3},{3,1},... | collective-permute-start | bytes 294920 | tf_op jit(solution)/shard_map/ppermute | solution.py:977
  38.8 10.4 %collective-permute-start.11 = (f32[4,48,128]{2,1,0:T(8,128)S(1)}, f32[4,48,128]{2,1,0:T(8,128)S(1)}, u32[]{:S(2)}, u32[]{:S(2)}) collective-permute-start(f32[4,48,128]{2,1,0:T(8,128)S(1)} %get-tuple-element.72.refs_2_), channel_id=1, source_target_pairs={{6,8},{8,6},{14,0},{0,14},{7,9},{9,7},{15,1},{1,15},{22,24},{24,22... | collective-permute-start | bytes 294920 | tf_op jit(solution)/shard_map/ppermute | solution.py:974
  43.1 9.2 %collective-permute-start.12 = (f32[224,128]{1,0:T(8,128)S(1)}, f32[224,128]{1,0:T(8,128)S(1)}, u32[]{:S(2)}, u32[]{:S(2)}) collective-permute-start(f32[224,128]{1,0:T(8,128)S(1)} %get-tuple-element.81), channel_id=1, source_target_pairs={{0,8},{2,10},{4,12},{6,14},{8,0},{10,2},{12,4},{14,6},{1,9},{3,11}... | collective-permute-start | bytes 344072 | tf_op jit(solution)/shard_map/ppermute | solution.py:1006
  46.6 8.8 %collective-permute-start.13 = (f32[200,128]{1,0:T(8,128)S(1)}, f32[200,128]{1,0:T(8,128)S(1)}, u32[]{:S(2)}, u32[]{:S(2)}) collective-permute-start(f32[200,128]{1,0:T(8,128)S(1)} %get-tuple-element.85), channel_id=1, source_target_pairs={{0,8},{2,10},{4,12},{6,14},{8,0},{10,2},{12,4},{14,6},{1,9},{3,11}... | collective-permute-start | bytes 307208 | tf_op jit(solution)/shard_map/ppermute | solution.py:1012
  49.4 6.0 %collective-permute-start.14 = (f32[48,128]{1,0:T(8,128)S(1)}, f32[48,128]{1,0:T(8,128)S(1)}, u32[]{:S(2)}, u32[]{:S(2)}) collective-permute-start(f32[48,128]{1,0:T(8,128)S(1)} %get-tuple-element.86), channel_id=1, source_target_pairs={{0,8},{2,10},{4,12},{6,14},{8,0},{10,2},{12,4},{14,6},{1,9},{3,11}... | collective-permute-start | bytes 73736 | tf_op jit(solution)/shard_map/ppermute | solution.py:1015

commit v13 on v11

--- a/solution.py
+++ b/solution.py
@@ -470,7 +470,7 @@
 
     def along_y(shifts, masks):
         halo = side_in[...]
-        lanes = halo.shape[2]
+        depth, lanes = halo.shape[0], halo.shape[2]
         line = lax.broadcasted_iota(jnp.int32, (1, SIDE, lanes), 1)
         total = None
         for k in range(1, WIDTH + 1):
@@ -766,7 +766,7 @@
 def last_far(flag, final, late, cx, far, matrix):
     count_x, count_y, count_z = final.shape
     count_b, count_a, _ = late.shape
-    rows, pair = far_rows(count_b), WIDTH // 2
+    groups, rows, pair = count_b // GROUP, far_rows(count_b), WIDTH // 2
 
     def kernel(
         flag_ref, final_in, late_in, cx_ref, far_ref, matrix_ref, final_ref, late_ref, sent_ref, lhs,
@@ -836,6 +836,15 @@
     )(level)
 
 
+class Either:
+    def __init__(self, first, second):
+        self.both = first, second
+        self.shape = first.shape
+
+    def __getitem__(self, index):
+        return self.both[0][index] + self.both[1][index]
+
+
 CODE_BITS = 5
 PER_CODE = 6
 
@@ -852,7 +861,8 @@
     def kernel(*refs):
         refs = list(refs)
         take = lambda count: [refs.pop(0) for _ in range(count)]
-        lags_ref, own_ref, other_ref = take(3)
+        lags_ref, own_ref = take(2)
+        other_ref = Either(*take(2)) if last else take(1)[0]
         if last:
             extra_ref, before_ref = take(2)
         (out_ref,) = take(1)
@@ -939,7 +949,7 @@
             pltpu.make_async_copy(store, out_ref, sem).wait()
 
     image = shape(count_h, count_a, groups * count_z)
-    operands = [lags, own, other] + ([extra, before] if last else [])
+    operands = [lags, own] + ([*other, extra, before] if last else [other])
     scratch = [pltpu.VMEM((2, total_rows, count_z), F32)] * 2
     scratch.append(pltpu.VMEM(image.shape, F32) if last else pltpu.SMEM((count_h,), jnp.int32))
     scratch.append(pltpu.SemaphoreType.DMA)
@@ -973,6 +983,7 @@
     turn = loop_size // 4
     assert lax.axis_size("gy") == 2 and half_size % 2 == 0
 
+    field = ((lax.axis_index("gx") - turn + loop_size) % loop_size) // half_size
     slabs = [(i - turn) % loop_size % half_size for i in range(loop_size)]
 
     def pairs(odd):
@@ -985,6 +996,7 @@
 
     near_pairs, far_pairs = pairs(0), pairs(1)
     across = [(i, (i + half_size) % loop_size) for i in range(loop_size)]
+    outer = [pair for pair in across if min(pair) < turn]
 
     def send_far(far):
         return lax.ppermute(far, "gx", far_pairs)
@@ -1026,12 +1038,13 @@
     final, late, sent_late = last_step(
         flag, even3, next4, (qx, qy, cx, cy), near, side, sent_matrix
     )
-    other_late = lax.ppermute(sent_late, "gx", across)
+    first_late = lax.ppermute(sent_late, "gx", outer)
     partial, codes = lag_image(count_x // 2, lag_offsets, own_early, other_early)
+    second_late = lax.ppermute(sent_late, "gx", [p for p in across if p not in outer])
     final, late, sent_far = last_far(flag, final, late, cx, far, sent_matrix)
     extra = lax.ppermute(sent_far, "gx", across)
     own_late = pack_own(lag_offsets, late, own_matrix)
-    image = lag_image(count_x // 2, codes, own_late, other_late, extra, partial)
+    image = lag_image(count_x // 2, codes, own_late, (first_late, second_late), extra, partial)
     return write_out(final), jnp.transpose(image, (1, 0, 2))
 
 

time: 57.1 us -> 58.1 us (1.018)
  starting transfers between devices: 24.3 us -> 27 us
  waiting for transfers between devices: 12 us -> 10.5 us
    ppermute x1, waiting for transfers between devices: 2.86 us -> 0.01 us  [body(): other_early = lax.ppermute(sent_early, 'gx', across)]
    ppermute x1 -> x2, starting transfers between devices: 2.95 us -> 5.46 us  [the longest x1 4.79 us: body(): first_late = lax.ppermute(sent_late, 'gx', outer)]
    ppermute x1, waiting for transfers between devices: 0.01 us -> 1.56 us  [body(): extra = lax.ppermute(sent_far, 'gx', across)]
  transfers between devices with their start and end apart: 15 -> 16, of which waited for: 7 -> 6; matrix products, arithmetic and copies ran while one was open for 0% -> 0% of each run, Pallas kernels for 30% -> 29%
where the time goes in v13:
time: 58.1 us; the launch traced here: 57.8 us
  starting transfers between devices  27 us (46%)
  Pallas kernels  19.4 us (33%)
  waiting for transfers between devices  10.5 us (18%)
  between operations  0.89 us (2%)
    ppermute x4, starting transfers between devices, send_far(): return lax.ppermute(far, 'gx', far_pairs)  20.2 us
    pallas_call x4, Pallas kernels, inner_step(): pl.pallas_call(kernel, out_shape=tuple(outs), in_specs=specs, out_specs=(...  12.7 us
    ppermute x4, waiting for transfers between devices, send_near(): near = lax.ppermute(near, 'gx', near_pairs)  4.83 us
    ppermute x1, starting transfers between devices, body(): first_late = lax.ppermute(sent_late, 'gx', outer)  4.79 us
    ppermute x4, waiting for transfers between devices, send_far(): return lax.ppermute(far, 'gx', far_pairs)  4.14 us
    pallas_call x2, Pallas kernels, lag_image(): pl.pallas_call(kernel, out_shape=image if last else (image, shape(8, coun...  2.31 us
    ppermute x1, waiting for transfers between devices, body(): extra = lax.ppermute(sent_far, 'gx', across)  1.56 us
  transfers between devices with their start and end apart: 16, of which 6 were waited for; matrix products, arithmetic and copies ran while one was open for 0% of the time, Pallas kernels for 29%

profile of v13, /device:TPU:0, one launch (start us, length us, event | category | flops | bytes accessed | tf_op | source)
XLA Modules:
  0.0 57.8 jit_solution(17310322957156689230)
XLA Ops:
  0.6 1.1 %first_faces.1 = (f32[4,48,128]{2,1,0:T(8,128)S(1)}, f32[4,48,128]{2,1,0:T(8,128)S(1)}, f32[32,8,128]{2,1,0:T(8,128)S(1)}) custom-call(f32[32,48,128]{2,1,0:T(8,128)} %field_ref.1), custom_call_target="tpu_custom_call" | custom-call | tf_op jit(solution)/shard_map/first_faces/pallas_call | solution.py:93
  1.8 0.6 collective-permute-start.2
  2.3 7.5 %collective-permute-start = (f32[4,48,128]{2,1,0:T(8,128)S(1)}, f32[4,48,128]{2,1,0:T(8,128)S(1)}, u32[]{:S(2)}, u32[]{:S(2)}) collective-permute-start(f32[4,48,128]{2,1,0:T(8,128)S(1)} %get-tuple-element.56), channel_id=1, source_target_pairs={{6,8},{8,6},{14,0},{0,14},{7,9},{9,7},{15,1},{1,15},{22,24},{24,22... | collective-permute-start | bytes 294920 | tf_op jit(solution)/shard_map/ppermute | solution.py:1002
  9.9 3.6 %shard_map.113 = (f32[40,64,128]{2,1,0:T(8,128)S(1)}, f32[40,64,128]{2,1,0:T(8,128)S(1)}, f32[8,48,128]{2,1,0:T(8,128)S(1)}, f32[32,8,128]{2,1,0:T(8,128)S(1)}, ...) custom-call(s32[3,8]{1,0:T(4,128)} %refs_0_.2, ...), custom_call_target="tpu_custom_call" | custom-call | flops 11796480 | bytes 4718592 | tf_op jit(solution)/shard_map/pallas_call | solution.py:414
  13.5 1.9 %collective-permute-done.1.refs_5_ = f32[4,48,128]{2,1,0:T(8,128)S(1)} collective-permute-done((f32[4,48,128]{2,1,0:T(8,128)S(1)}, f32[4,48,128]{2,1,0:T(8,128)S(1)}, u32[]{:S(2)}, u32[]{:S(2)}) %collective-permute-start.1) | collective-permute-done | bytes 98336 | tf_op jit(solution)/shard_map/ppermute | solution.py:1005
  15.3 0.1 halo_step.3
  15.5 0.1 collective-permute-start.5
  15.6 4.2 %collective-permute-start.3 = (f32[4,48,128]{2,1,0:T(8,128)S(1)}, f32[4,48,128]{2,1,0:T(8,128)S(1)}, u32[]{:S(2)}, u32[]{:S(2)}) collective-permute-start(f32[4,48,128]{2,1,0:T(8,128)S(1)} %get-tuple-element.59.refs_3_), channel_id=1, source_target_pairs={{6,8},{8,6},{14,0},{0,14},{7,9},{9,7},{15,1},{1,15},{22,24},{24,22... | collective-permute-start | bytes 294920 | tf_op jit(solution)/shard_map/ppermute | solution.py:1002
  19.9 3.4 %shard_map.114 = (f32[40,64,128]{2,1,0:T(8,128)S(1)}, f32[40,64,128]{2,1,0:T(8,128)S(1)}, f32[8,48,128]{2,1,0:T(8,128)S(1)}, f32[32,8,128]{2,1,0:T(8,128)S(1)}, f32[32,48,128]{2,1,0:T(8,128)S(1)}) custom-call(s32[8,256]{1,0:T(8,128)S(1)} %get-tuple-element.49.refs_0_, f32[8,256]{1,0:T(8,128)S(1)} %get-tuple-element.50.refs_1_, ...), custom_call_target="tpu_custom_call", output_to_operand_aliasing={{0}: (2, {})} | custom-call | flops 11796480 | bytes 4718592 | tf_op jit(solution)/shard_map/pallas_call | solution.py:414
  23.3 2.1 %collective-permute-done.3.refs_4_ = f32[4,48,128]{2,1,0:T(8,128)S(1)} collective-permute-done((f32[4,48,128]{2,1,0:T(8,128)S(1)}, f32[4,48,128]{2,1,0:T(8,128)S(1)}, u32[]{:S(2)}, u32[]{:S(2)}) %collective-permute-start.3) | collective-permute-done | bytes 98336 | tf_op jit(solution)/shard_map/ppermute | solution.py:1002
  25.4 1.4 %collective-permute-done.4.refs_5_ = f32[4,48,128]{2,1,0:T(8,128)S(1)} collective-permute-done((f32[4,48,128]{2,1,0:T(8,128)S(1)}, f32[4,48,128]{2,1,0:T(8,128)S(1)}, u32[]{:S(2)}, u32[]{:S(2)}) %collective-permute-start.4) | collective-permute-done | bytes 98336 | tf_op jit(solution)/shard_map/ppermute | solution.py:1005
  26.9 0.1 halo_step.4
  27.1 4.3 %collective-permute-start.6 = (f32[4,48,128]{2,1,0:T(8,128)S(1)}, f32[4,48,128]{2,1,0:T(8,128)S(1)}, u32[]{:S(2)}, u32[]{:S(2)}) collective-permute-start(f32[4,48,128]{2,1,0:T(8,128)S(1)} %get-tuple-element.67.refs_3_), channel_id=1, source_target_pairs={{6,8},{8,6},{14,0},{0,14},{7,9},{9,7},{15,1},{1,15},{22,24},{24,22... | collective-permute-start | bytes 294920 | tf_op jit(solution)/shard_map/ppermute | solution.py:1002
  31.4 0.1 collective-permute-start.7
  31.5 3.5 %shard_map.115 = (f32[40,64,128]{2,1,0:T(8,128)S(1)}, f32[40,64,128]{2,1,0:T(8,128)S(1)}, f32[8,48,128]{2,1,0:T(8,128)S(1)}, f32[32,8,128]{2,1,0:T(8,128)S(1)}, ...) custom-call(s32[8,256]{1,0:T(8,128)S(1)} %get-tuple-element.49.refs_, ...), custom_call_target="tpu_custom_call", output_to_operand_aliasing={{0}: (2, {})} | custom-call | flops 11796480 | bytes 4718592 | tf_op jit(solution)/shard_map/pallas_call | solution.py:414
  35.0 2.0 %collective-permute-done.6.refs_4_ = f32[4,48,128]{2,1,0:T(8,128)S(1)} collective-permute-done((f32[4,48,128]{2,1,0:T(8,128)S(1)}, f32[4,48,128]{2,1,0:T(8,128)S(1)}, u32[]{:S(2)}, u32[]{:S(2)}) %collective-permute-start.6) | collective-permute-done | bytes 98336 | tf_op jit(solution)/shard_map/ppermute | solution.py:1002
  37.0 1.5 %collective-permute-done.7.refs_5_ = f32[4,48,128]{2,1,0:T(8,128)S(1)} collective-permute-done((f32[4,48,128]{2,1,0:T(8,128)S(1)}, f32[4,48,128]{2,1,0:T(8,128)S(1)}, u32[]{:S(2)}, u32[]{:S(2)}) %collective-permute-start.7) | collective-permute-done | bytes 98336 | tf_op jit(solution)/shard_map/ppermute | solution.py:1005
  38.5 0.1 halo_step.5
  38.7 0.1 collective-permute-start.10
  38.8 4.2 %collective-permute-start.11 = (f32[4,48,128]{2,1,0:T(8,128)S(1)}, f32[4,48,128]{2,1,0:T(8,128)S(1)}, u32[]{:S(2)}, u32[]{:S(2)}) collective-permute-start(f32[4,48,128]{2,1,0:T(8,128)S(1)} %get-tuple-element.76.refs_2_), channel_id=1, source_target_pairs={{6,8},{8,6},{14,0},{0,14},{7,9},{9,7},{15,1},{1,15},{22,24},{24,22... | collective-permute-start | bytes 294920 | tf_op jit(solution)/shard_map/ppermute | solution.py:1002
  43.1 0.1 collective-permute-start.12
  43.2 2.3 %shard_map.116 = (f32[40,64,128]{2,1,0:T(8,128)S(1)}, f32[32,48,128]{2,1,0:T(8,128)S(1)}, f32[8,48,128]{2,1,0:T(8,128)S(1)}, f32[32,8,128]{2,1,0:T(8,128)S(1)}, f32[24,16,128]{2,1,0:T(8,128)S(1)}) custom-call(f32[32,48,128]{2,1,0:T(8,128)S(1)} %get-tuple-element.72.refs_0_, ...), custom_call_target="tpu_custom_call", output_to_operand_aliasing={{0}: (1, {})} | custom-call | flops 11796480 | bytes 4718592 | tf_op jit(solution)/shard_map/pallas_call | solution.py:414
  45.4 0.6 %last_step.1 = (f32[32,48,128]{2,1,0:T(8,128)S(1)}, f32[24,16,128]{2,1,0:T(8,128)S(1)}, f32[200,128]{1,0:T(8,128)S(1)}) custom-call(f32[8,128]{1,0:T(8,128)S(1)} %get-tuple-element.71.flag_ref, f32[24,16,128]{2,1,0:T(8,128)S(1)} %get-tuple-element.80.even_ref, f32[32,48,128]{2,1,0:T(8,128)S(1)} %get-tuple-element.81.current_ref, ...), custom_call_target="tpu_custom_call", output_to_operand_aliasing={{0}: (2, {})} | custom-call | flops 1966080 | bytes 2359296 | tf_op jit(solution)/shard_map/last_step/pallas_call | solution.py:741
  46.0 4.8 %collective-permute-start.13 = (f32[200,128]{1,0:T(8,128)S(1)}, f32[200,128]{1,0:T(8,128)S(1)}, u32[]{:S(2)}, u32[]{:S(2)}) collective-permute-start(f32[200,128]{1,0:T(8,128)S(1)} %get-tuple-element.93), channel_id=1, source_target_pairs={{0,8},{2,10},{8,0},{10,2},{1,9},{3,11},{9,1},{11,3},{16,24},{18,26... | collective-permute-start | bytes 307208 | tf_op jit(solution)/shard_map/ppermute | solution.py:1041
  50.8 0.7 %collective-permute-start.14 = (f32[200,128]{1,0:T(8,128)S(1)}, f32[200,128]{1,0:T(8,128)S(1)}, u32[]{:S(2)}, u32[]{:S(2)}) collective-permute-start(f32[200,128]{1,0:T(8,128)S(1)} %get-tuple-element.93), channel_id=1, source_target_pairs={{4,12},{6,14},{12,4},{14,6},{5,13},{7,15},{13,5},{15,7},{20,28},{2... | collective-permute-start | bytes 307208 | tf_op jit(solution)/shard_map/ppermute | solution.py:1043
  51.5 0.3 last_far.1
  51.8 0.1 collective-permute-start.15
  51.9 1.2 %early_image.1 = (f32[17,16,768]{2,1,0:T(8,128)S(1)}, s32[8,128]{1,0:T(8,128)S(1)}) custom-call(s32[17]{0:T(128)} %lags_ref.1, f32[4,96,128]{2,1,0:T(8,128)S(1)} %get-tuple-element.88.refs_1_, f32[224,128]{1,0:T(8,128)S(1)} %collective-permute-done.12.refs_2_), custom_call_target="tpu_custom_call" | custom-call | flops 2088960 | bytes 1671168 | tf_op jit(solution)/shard_map/early_image/pallas_call | solution.py:956
  53.1 0.9 %write_out.1 = f32[32,48,128]{2,1,0:T(8,128)} custom-call(f32[32,48,128]{2,1,0:T(8,128)S(1)} %get-tuple-element.87.level_ref), custom_call_target="tpu_custom_call" | custom-call | bytes 1572864 | tf_op jit(solution)/shard_map/write_out/pallas_call | solution.py:827
  54.0 1.1 %pack_own.1.refs_1_ = f32[17,96,128]{2,1,0:T(8,128)S(1)} custom-call(s32[17]{0:T(128)} %lags_ref.1, f32[24,16,128]{2,1,0:T(8,128)S(1)} %get-tuple-element.91.even_ref, bf16[512,512]{1,0:T(8,128)(2,1)S(1)} %get-tuple-element.92.matrix_ref), custom_call_target="tpu_custom_call" | custom-call | flops 50331648 | bytes 786432 | tf_op jit(solution)/shard_map/pack_own/pallas_call | solution.py:581
  55.1 1.6 %collective-permute-done.15.refs_4_ = f32[48,128]{1,0:T(8,128)S(1)} collective-permute-done((f32[48,128]{1,0:T(8,128)S(1)}, f32[48,128]{1,0:T(8,128)S(1)}, u32[]{:S(2)}, u32[]{:S(2)}) %collective-permute-start.15) | collective-permute-done | bytes 24608 | tf_op jit(solution)/shard_map/ppermute | solution.py:1045
  56.7 1.1 %last_image.1 = f32[17,16,768]{2,1,0:T(8,128)} custom-call(s32[8,128]{1,0:T(8,128)S(1)} %get-tuple-element.90.refs_0_, f32[17,96,128]{2,1,0:T(8,128)S(1)} %pack_own.1.refs_1_, f32[200,128]{1,0:T(8,128)S(1)} %collective-permute-done.13.refs_2_, f32[200,128]{1,0:T(8,128)S(1)} %collective-permute-done.14.refs_3_, ...), custom_call_target="tpu_custom_call" | custom-call | flops 2088960 | bytes 1671168 | tf_op jit(solution)/shard_map/last_image/pallas_call | solution.py:956
  (16 shorter events, 0.3 us)
Async XLA Ops:
  0.6 9.2 %copy-start = (f32[32,48,128]{2,1,0:T(8,128)S(1)}, f32[32,48,128]{2,1,0:T(8,128)}, u32[]{:S(2)}) copy-start(f32[32,48,128]{2,1,0:T(8,128)} %field_ref.1) | copy-start | bytes 2359300
  1.8 13.6 %collective-permute-start.2 = (f32[32,8,128]{2,1,0:T(8,128)S(1)}, f32[32,8,128]{2,1,0:T(8,128)S(1)}, u32[]{:S(2)}, u32[]{:S(2)}) collective-permute-start(f32[32,8,128]{2,1,0:T(8,128)S(1)} %get-tuple-element.58), channel_id=1, source_target_pairs={{0,1},{1,0},{2,3},{3,2},{4,5},{5,4},{6,7},{7,6},{8,9},{9,8},{10,11... | collective-permute-start | bytes 393224 | tf_op jit(solution)/shard_map/ppermute | solution.py:1006
  2.3 11.1 %collective-permute-start = (f32[4,48,128]{2,1,0:T(8,128)S(1)}, f32[4,48,128]{2,1,0:T(8,128)S(1)}, u32[]{:S(2)}, u32[]{:S(2)}) collective-permute-start(f32[4,48,128]{2,1,0:T(8,128)S(1)} %get-tuple-element.56), channel_id=1, source_target_pairs={{6,8},{8,6},{14,0},{0,14},{7,9},{9,7},{15,1},{1,15},{22,24},{24,22... | collective-permute-start | bytes 294920 | tf_op jit(solution)/shard_map/ppermute | solution.py:1002
  9.8 5.5 %collective-permute-start.1 = (f32[4,48,128]{2,1,0:T(8,128)S(1)}, f32[4,48,128]{2,1,0:T(8,128)S(1)}, u32[]{:S(2)}, u32[]{:S(2)}) collective-permute-start(f32[4,48,128]{2,1,0:T(8,128)S(1)} %get-tuple-element.57), channel_id=1, source_target_pairs={{0,2},{2,0},{4,6},{6,4},{8,10},{10,8},{12,14},{14,12},{1,3},{3,1},... | collective-permute-start | bytes 294920 | tf_op jit(solution)/shard_map/ppermute | solution.py:1005
  15.5 11.4 %collective-permute-start.5 = (f32[32,8,128]{2,1,0:T(8,128)S(1)}, f32[32,8,128]{2,1,0:T(8,128)S(1)}, u32[]{:S(2)}, u32[]{:S(2)}) collective-permute-start(f32[32,8,128]{2,1,0:T(8,128)S(1)} %get-tuple-element.61.refs_5_), channel_id=1, source_target_pairs={{0,1},{1,0},{2,3},{3,2},{4,5},{5,4},{6,7},{7,6},{8,9},{9,8},{10,11... | collective-permute-start | bytes 393224 | tf_op jit(solution)/shard_map/ppermute | solution.py:1006
  15.6 9.9 %collective-permute-start.3 = (f32[4,48,128]{2,1,0:T(8,128)S(1)}, f32[4,48,128]{2,1,0:T(8,128)S(1)}, u32[]{:S(2)}, u32[]{:S(2)}) collective-permute-start(f32[4,48,128]{2,1,0:T(8,128)S(1)} %get-tuple-element.59.refs_3_), channel_id=1, source_target_pairs={{6,8},{8,6},{14,0},{0,14},{7,9},{9,7},{15,1},{1,15},{22,24},{24,22... | collective-permute-start | bytes 294920 | tf_op jit(solution)/shard_map/ppermute | solution.py:1002
  19.8 7.1 %collective-permute-start.4 = (f32[4,48,128]{2,1,0:T(8,128)S(1)}, f32[4,48,128]{2,1,0:T(8,128)S(1)}, u32[]{:S(2)}, u32[]{:S(2)}) collective-permute-start(f32[4,48,128]{2,1,0:T(8,128)S(1)} %get-tuple-element.60.refs_4_), channel_id=1, source_target_pairs={{0,2},{2,0},{4,6},{6,4},{8,10},{10,8},{12,14},{14,12},{1,3},{3,1},... | collective-permute-start | bytes 294920 | tf_op jit(solution)/shard_map/ppermute | solution.py:1005
  27.0 11.5 %collective-permute-start.8 = (f32[32,8,128]{2,1,0:T(8,128)S(1)}, f32[32,8,128]{2,1,0:T(8,128)S(1)}, u32[]{:S(2)}, u32[]{:S(2)}) collective-permute-start(f32[32,8,128]{2,1,0:T(8,128)S(1)} %get-tuple-element.69.refs_5_), channel_id=1, source_target_pairs={{0,1},{1,0},{2,3},{3,2},{4,5},{5,4},{6,7},{7,6},{8,9},{9,8},{10,11... | collective-permute-start | bytes 393224 | tf_op jit(solution)/shard_map/ppermute | solution.py:1006
  27.1 9.9 %collective-permute-start.6 = (f32[4,48,128]{2,1,0:T(8,128)S(1)}, f32[4,48,128]{2,1,0:T(8,128)S(1)}, u32[]{:S(2)}, u32[]{:S(2)}) collective-permute-start(f32[4,48,128]{2,1,0:T(8,128)S(1)} %get-tuple-element.67.refs_3_), channel_id=1, source_target_pairs={{6,8},{8,6},{14,0},{0,14},{7,9},{9,7},{15,1},{1,15},{22,24},{24,22... | collective-permute-start | bytes 294920 | tf_op jit(solution)/shard_map/ppermute | solution.py:1002
  31.4 7.1 %collective-permute-start.7 = (f32[4,48,128]{2,1,0:T(8,128)S(1)}, f32[4,48,128]{2,1,0:T(8,128)S(1)}, u32[]{:S(2)}, u32[]{:S(2)}) collective-permute-start(f32[4,48,128]{2,1,0:T(8,128)S(1)} %get-tuple-element.68.refs_4_), channel_id=1, source_target_pairs={{0,2},{2,0},{4,6},{6,4},{8,10},{10,8},{12,14},{14,12},{1,3},{3,1},... | collective-permute-start | bytes 294920 | tf_op jit(solution)/shard_map/ppermute | solution.py:1005
  38.7 6.8 %collective-permute-start.10 = (f32[32,8,128]{2,1,0:T(8,128)S(1)}, f32[32,8,128]{2,1,0:T(8,128)S(1)}, u32[]{:S(2)}, u32[]{:S(2)}) collective-permute-start(f32[32,8,128]{2,1,0:T(8,128)S(1)} %get-tuple-element.78.refs_4_), channel_id=1, source_target_pairs={{0,1},{1,0},{2,3},{3,2},{4,5},{5,4},{6,7},{7,6},{8,9},{9,8},{10,11... | collective-permute-start | bytes 393224 | tf_op jit(solution)/shard_map/ppermute | solution.py:1006
  38.7 6.7 %collective-permute-start.9 = (f32[4,48,128]{2,1,0:T(8,128)S(1)}, f32[4,48,128]{2,1,0:T(8,128)S(1)}, u32[]{:S(2)}, u32[]{:S(2)}) collective-permute-start(f32[4,48,128]{2,1,0:T(8,128)S(1)} %get-tuple-element.77.refs_3_), channel_id=1, source_target_pairs={{0,2},{2,0},{4,6},{6,4},{8,10},{10,8},{12,14},{14,12},{1,3},{3,1},... | collective-permute-start | bytes 294920 | tf_op jit(solution)/shard_map/ppermute | solution.py:1005
  38.8 12.7 %collective-permute-start.11 = (f32[4,48,128]{2,1,0:T(8,128)S(1)}, f32[4,48,128]{2,1,0:T(8,128)S(1)}, u32[]{:S(2)}, u32[]{:S(2)}) collective-permute-start(f32[4,48,128]{2,1,0:T(8,128)S(1)} %get-tuple-element.76.refs_2_), channel_id=1, source_target_pairs={{6,8},{8,6},{14,0},{0,14},{7,9},{9,7},{15,1},{1,15},{22,24},{24,22... | collective-permute-start | bytes 294920 | tf_op jit(solution)/shard_map/ppermute | solution.py:1002
  43.1 8.9 %collective-permute-start.12 = (f32[224,128]{1,0:T(8,128)S(1)}, f32[224,128]{1,0:T(8,128)S(1)}, u32[]{:S(2)}, u32[]{:S(2)}) collective-permute-start(f32[224,128]{1,0:T(8,128)S(1)} %get-tuple-element.89), channel_id=1, source_target_pairs={{0,8},{2,10},{4,12},{6,14},{8,0},{10,2},{12,4},{14,6},{1,9},{3,11}... | collective-permute-start | bytes 344072 | tf_op jit(solution)/shard_map/ppermute | solution.py:1034
  46.0 10.6 %collective-permute-start.13 = (f32[200,128]{1,0:T(8,128)S(1)}, f32[200,128]{1,0:T(8,128)S(1)}, u32[]{:S(2)}, u32[]{:S(2)}) collective-permute-start(f32[200,128]{1,0:T(8,128)S(1)} %get-tuple-element.93), channel_id=1, source_target_pairs={{0,8},{2,10},{8,0},{10,2},{1,9},{3,11},{9,1},{11,3},{16,24},{18,26... | collective-permute-start | bytes 307208 | tf_op jit(solution)/shard_map/ppermute | solution.py:1041
  50.8 5.8 %collective-permute-start.14 = (f32[200,128]{1,0:T(8,128)S(1)}, f32[200,128]{1,0:T(8,128)S(1)}, u32[]{:S(2)}, u32[]{:S(2)}) collective-permute-start(f32[200,128]{1,0:T(8,128)S(1)} %get-tuple-element.93), channel_id=1, source_target_pairs={{4,12},{6,14},{12,4},{14,6},{5,13},{7,15},{13,5},{15,7},{20,28},{2... | collective-permute-start | bytes 307208 | tf_op jit(solution)/shard_map/ppermute | solution.py:1043
  51.8 4.9 %collective-permute-start.15 = (f32[48,128]{1,0:T(8,128)S(1)}, f32[48,128]{1,0:T(8,128)S(1)}, u32[]{:S(2)}, u32[]{:S(2)}) collective-permute-start(f32[48,128]{1,0:T(8,128)S(1)} %get-tuple-element.94), channel_id=1, source_target_pairs={{0,8},{2,10},{4,12},{6,14},{8,0},{10,2},{12,4},{14,6},{1,9},{3,11}... | collective-permute-start | bytes 73736 | tf_op jit(solution)/shard_map/ppermute | solution.py:1045

commit v14 on v11

--- a/solution.py
+++ b/solution.py
@@ -149,8 +149,6 @@
             own_out, sent_out, own_matrix, sent_matrix, flag_ref = take(5)
         if ahead:
             (ahead_ref,) = take(1)
-        if last:
-            (even_ref,) = take(1)
         zpart, addpart = take(2)
         if last:
             addpart = added_ref
@@ -339,9 +337,6 @@
             cx_ref[pl.ds(0, WIDTH)] = kept_ref[pl.ds(0, WIDTH)]
             cx_ref[pl.ds(WIDTH, WIDTH)] = kept_ref[pl.ds(count_x - WIDTH, WIDTH)]
             cy_ref[...] = kept_ref[:, pl.ds(block, SIDE)]
-        if last:
-            for b in range(count_b):
-                even_ref[b] = even_rows(padded, WIDTH, SIDE, count_a, b)
         if snapshot:
             for copy in copies:
                 copy.wait()
@@ -382,8 +377,6 @@
         ]
     if ahead:
         outs.append(full)
-    if last:
-        outs.append(even)
     place_of = spec(pltpu.HBM) if first else spec(pltpu.VMEM)
     if first:
         operands = [*points, current]
@@ -704,12 +697,12 @@
     return shape(sum(give_rows(groups)) + edge_slots(count_a, groups, count_z)[1], count_z)
 
 
-def last_step(flag, even_before, current, parts, near, side, matrix):
+def last_step(flag, before, current, parts, near, side, matrix):
     count_x, count_y, count_z = current.shape
     count_a, count_b = count_x // 2, count_y // 2
 
     def kernel(
-        flag_ref, even_ref, current_ref, qx_ref, qy_ref, cx_ref, cy_ref, near_ref, side_ref,
+        flag_ref, before_ref, current_ref, qx_ref, qy_ref, cx_ref, cy_ref, near_ref, side_ref,
         matrix_ref, final_ref, late_ref, sent_ref, far_out, near_out, side_out,
     ):
         place = Place()
@@ -730,11 +723,18 @@
             final_ref[high] = far_out[...]
 
         final_ref[:, pl.ds(place.block(count_y), SIDE)] = side_out[...]
-        wants_last = jnp.broadcast_to(flag_ref[0:1, :], (count_a, count_z)) > 0.5
-        for b in range(count_b):
-            late_ref[b] = jnp.where(
-                wants_last, even_rows(final_ref, 0, 0, count_a, b), even_ref[b]
-            )
+        wants_last = flag_ref[0:1, :][0, 0] > 0.5
+
+        @pl.when(wants_last)
+        def _():
+            for b in range(count_b):
+                late_ref[b] = even_rows(final_ref, 0, 0, count_a, b)
+
+        @pl.when(jnp.logical_not(wants_last))
+        def _():
+            for b in range(count_b):
+                late_ref[b] = even_rows(before_ref, WIDTH, SIDE, count_a, b)
+
         give_into(place, late_ref, matrix_ref, sent_ref)
 
     slab, _, side_shape = face_shapes(count_x, count_y, count_z)
@@ -756,7 +756,7 @@
         compiler_params=params(12),
         cost_estimate=cost(count_x * count_y * count_z, 10, 3),
         name="last_step",
-    )(flag, even_before, current, *parts, near, side, matrix)
+    )(flag, before, current, *parts, near, side, matrix)
 
 
 def far_rows(count_b):
@@ -1022,9 +1022,9 @@
     other_early = lax.ppermute(sent_early, "gx", across)
     faces = halo_step((qx, qy, cx, cy), halos)
     far, near, side = exchange(faces)
-    _, next4, qx, qy, even3 = inner_step(3, added, None, next3, faces, whole2, courant)
+    whole3, next4, qx, qy = inner_step(3, added, None, next3, faces, whole2, courant)
     final, late, sent_late = last_step(
-        flag, even3, next4, (qx, qy, cx, cy), near, side, sent_matrix
+        flag, whole3, next4, (qx, qy, cx, cy), near, side, sent_matrix
     )
     other_late = lax.ppermute(sent_late, "gx", across)
     partial, codes = lag_image(count_x // 2, lag_offsets, own_early, other_early)

time: 57.1 us -> 57.1 us (level)
  no operation moved by 1% of the time
where the time goes in v14:
time: 57.1 us; the launch traced here: 56.7 us
  starting transfers between devices  24.3 us (43%)
  Pallas kernels  19.4 us (34%)
  waiting for transfers between devices  12 us (21%)
  between operations  0.89 us (2%)
    ppermute x4, starting transfers between devices, send_far(): return lax.ppermute(far, 'gx', far_pairs)  20.2 us
    pallas_call x4, Pallas kernels, inner_step(): pl.pallas_call(kernel, out_shape=tuple(outs), in_specs=specs, out_specs=(...  12.6 us
    ppermute x4, waiting for transfers between devices, send_near(): near = lax.ppermute(near, 'gx', near_pairs)  4.77 us
    ppermute x4, waiting for transfers between devices, send_far(): return lax.ppermute(far, 'gx', far_pairs)  4.34 us
    ppermute x1, starting transfers between devices, body(): other_late = lax.ppermute(sent_late, 'gx', across)  2.95 us
    ppermute x1, waiting for transfers between devices, body(): other_early = lax.ppermute(sent_early, 'gx', across)  2.88 us
    pallas_call x2, Pallas kernels, lag_image(): pl.pallas_call(kernel, out_shape=image if last else (image, shape(8, coun...  2.31 us
  transfers between devices with their start and end apart: 15, of which 7 were waited for; matrix products, arithmetic and copies ran while one was open for 0% of the time, Pallas kernels for 30%

profile of v14, /device:TPU:0, one launch (start us, length us, event | category | flops | bytes accessed | tf_op | source)
XLA Modules:
  0.0 56.7 jit_solution(3045492194737148736)
XLA Ops:
  0.6 1.1 %first_faces.1 = (f32[4,48,128]{2,1,0:T(8,128)S(1)}, f32[4,48,128]{2,1,0:T(8,128)S(1)}, f32[32,8,128]{2,1,0:T(8,128)S(1)}) custom-call(f32[32,48,128]{2,1,0:T(8,128)} %field_ref.1), custom_call_target="tpu_custom_call" | custom-call | tf_op jit(solution)/shard_map/first_faces/pallas_call | solution.py:93
  1.8 0.6 collective-permute-start.2
  2.3 7.5 %collective-permute-start = (f32[4,48,128]{2,1,0:T(8,128)S(1)}, f32[4,48,128]{2,1,0:T(8,128)S(1)}, u32[]{:S(2)}, u32[]{:S(2)}) collective-permute-start(f32[4,48,128]{2,1,0:T(8,128)S(1)} %get-tuple-element.56), channel_id=1, source_target_pairs={{6,8},{8,6},{14,0},{0,14},{7,9},{9,7},{15,1},{1,15},{22,24},{24,22... | collective-permute-start | bytes 294920 | tf_op jit(solution)/shard_map/ppermute | solution.py:990
  9.9 3.6 %shard_map.113 = (f32[40,64,128]{2,1,0:T(8,128)S(1)}, f32[40,64,128]{2,1,0:T(8,128)S(1)}, f32[8,48,128]{2,1,0:T(8,128)S(1)}, f32[32,8,128]{2,1,0:T(8,128)S(1)}, ...) custom-call(s32[3,8]{1,0:T(4,128)} %refs_0_.2, ...), custom_call_target="tpu_custom_call" | custom-call | flops 11796480 | bytes 4718592 | tf_op jit(solution)/shard_map/pallas_call | solution.py:407
  13.5 1.8 %collective-permute-done.1.refs_5_ = f32[4,48,128]{2,1,0:T(8,128)S(1)} collective-permute-done((f32[4,48,128]{2,1,0:T(8,128)S(1)}, f32[4,48,128]{2,1,0:T(8,128)S(1)}, u32[]{:S(2)}, u32[]{:S(2)}) %collective-permute-start.1) | collective-permute-done | bytes 98336 | tf_op jit(solution)/shard_map/ppermute | solution.py:993
  15.3 0.1 halo_step.3
  15.5 0.1 collective-permute-start.5
  15.6 4.2 %collective-permute-start.3 = (f32[4,48,128]{2,1,0:T(8,128)S(1)}, f32[4,48,128]{2,1,0:T(8,128)S(1)}, u32[]{:S(2)}, u32[]{:S(2)}) collective-permute-start(f32[4,48,128]{2,1,0:T(8,128)S(1)} %get-tuple-element.59.refs_3_), channel_id=1, source_target_pairs={{6,8},{8,6},{14,0},{0,14},{7,9},{9,7},{15,1},{1,15},{22,24},{24,22... | collective-permute-start | bytes 294920 | tf_op jit(solution)/shard_map/ppermute | solution.py:990
  19.8 0.1 collective-permute-start.4
  19.9 3.4 %shard_map.114 = (f32[40,64,128]{2,1,0:T(8,128)S(1)}, f32[40,64,128]{2,1,0:T(8,128)S(1)}, f32[8,48,128]{2,1,0:T(8,128)S(1)}, f32[32,8,128]{2,1,0:T(8,128)S(1)}, f32[32,48,128]{2,1,0:T(8,128)S(1)}) custom-call(s32[8,256]{1,0:T(8,128)S(1)} %get-tuple-element.49.refs_0_, f32[8,256]{1,0:T(8,128)S(1)} %get-tuple-element.50.refs_1_, ...), custom_call_target="tpu_custom_call", output_to_operand_aliasing={{0}: (2, {})} | custom-call | flops 11796480 | bytes 4718592 | tf_op jit(solution)/shard_map/pallas_call | solution.py:407
  23.3 2.1 %collective-permute-done.3.refs_4_ = f32[4,48,128]{2,1,0:T(8,128)S(1)} collective-permute-done((f32[4,48,128]{2,1,0:T(8,128)S(1)}, f32[4,48,128]{2,1,0:T(8,128)S(1)}, u32[]{:S(2)}, u32[]{:S(2)}) %collective-permute-start.3) | collective-permute-done | bytes 98336 | tf_op jit(solution)/shard_map/ppermute | solution.py:990
  25.4 1.4 %collective-permute-done.4.refs_5_ = f32[4,48,128]{2,1,0:T(8,128)S(1)} collective-permute-done((f32[4,48,128]{2,1,0:T(8,128)S(1)}, f32[4,48,128]{2,1,0:T(8,128)S(1)}, u32[]{:S(2)}, u32[]{:S(2)}) %collective-permute-start.4) | collective-permute-done | bytes 98336 | tf_op jit(solution)/shard_map/ppermute | solution.py:993
  26.9 0.1 halo_step.4
  27.0 0.1 collective-permute-start.8
  27.1 4.3 %collective-permute-start.6 = (f32[4,48,128]{2,1,0:T(8,128)S(1)}, f32[4,48,128]{2,1,0:T(8,128)S(1)}, u32[]{:S(2)}, u32[]{:S(2)}) collective-permute-start(f32[4,48,128]{2,1,0:T(8,128)S(1)} %get-tuple-element.67.refs_3_), channel_id=1, source_target_pairs={{6,8},{8,6},{14,0},{0,14},{7,9},{9,7},{15,1},{1,15},{22,24},{24,22... | collective-permute-start | bytes 294920 | tf_op jit(solution)/shard_map/ppermute | solution.py:990
  31.5 3.5 %shard_map.115 = (f32[40,64,128]{2,1,0:T(8,128)S(1)}, f32[40,64,128]{2,1,0:T(8,128)S(1)}, f32[8,48,128]{2,1,0:T(8,128)S(1)}, f32[32,8,128]{2,1,0:T(8,128)S(1)}, ...) custom-call(s32[8,256]{1,0:T(8,128)S(1)} %get-tuple-element.49.refs_, ...), custom_call_target="tpu_custom_call", output_to_operand_aliasing={{0}: (2, {})} | custom-call | flops 11796480 | bytes 4718592 | tf_op jit(solution)/shard_map/pallas_call | solution.py:407
  35.0 2.0 %collective-permute-done.6.refs_4_ = f32[4,48,128]{2,1,0:T(8,128)S(1)} collective-permute-done((f32[4,48,128]{2,1,0:T(8,128)S(1)}, f32[4,48,128]{2,1,0:T(8,128)S(1)}, u32[]{:S(2)}, u32[]{:S(2)}) %collective-permute-start.6) | collective-permute-done | bytes 98336 | tf_op jit(solution)/shard_map/ppermute | solution.py:990
  37.0 1.5 %collective-permute-done.7.refs_5_ = f32[4,48,128]{2,1,0:T(8,128)S(1)} collective-permute-done((f32[4,48,128]{2,1,0:T(8,128)S(1)}, f32[4,48,128]{2,1,0:T(8,128)S(1)}, u32[]{:S(2)}, u32[]{:S(2)}) %collective-permute-start.7) | collective-permute-done | bytes 98336 | tf_op jit(solution)/shard_map/ppermute | solution.py:993
  38.5 0.1 halo_step.5
  38.7 0.1 collective-permute-start.10
  38.7 0.1 collective-permute-start.9
  38.8 4.2 %collective-permute-start.11 = (f32[4,48,128]{2,1,0:T(8,128)S(1)}, f32[4,48,128]{2,1,0:T(8,128)S(1)}, u32[]{:S(2)}, u32[]{:S(2)}) collective-permute-start(f32[4,48,128]{2,1,0:T(8,128)S(1)} %get-tuple-element.76.refs_2_), channel_id=1, source_target_pairs={{6,8},{8,6},{14,0},{0,14},{7,9},{9,7},{15,1},{1,15},{22,24},{24,22... | collective-permute-start | bytes 294920 | tf_op jit(solution)/shard_map/ppermute | solution.py:990
  43.1 2.1 %shard_map.116 = (f32[40,64,128]{2,1,0:T(8,128)S(1)}, f32[32,48,128]{2,1,0:T(8,128)S(1)}, f32[8,48,128]{2,1,0:T(8,128)S(1)}, f32[32,8,128]{2,1,0:T(8,128)S(1)}) custom-call(f32[32,48,128]{2,1,0:T(8,128)S(1)} %get-tuple-element.72.refs_0_, f32[40,64,128]{2,1,0:T(8,128)S(1)} %get-tuple-element.73.refs_1_, ...), custom_call_target="tpu_custom_call", output_to_operand_aliasing={{0}: (1, {})} | custom-call | flops 11796480 | bytes 4718592 | tf_op jit(solution)/shard_map/pallas_call | solution.py:407
  45.3 0.7 %last_step.1 = (f32[32,48,128]{2,1,0:T(8,128)S(1)}, f32[24,16,128]{2,1,0:T(8,128)S(1)}, f32[200,128]{1,0:T(8,128)S(1)}) custom-call(f32[8,128]{1,0:T(8,128)S(1)} %get-tuple-element.71.flag_ref, f32[40,64,128]{2,1,0:T(8,128)S(1)} %get-tuple-element.80.before_ref, f32[32,48,128]{2,1,0:T(8,128)S(1)} %get-tuple-element.81.current_ref, ...), custom_call_target="tpu_custom_call", output_to_operand_aliasing={{0}: (2, {})} | custom-call | flops 1966080 | bytes 2359296 | tf_op jit(solution)/shard_map/last_step/pallas_call | solution.py:741
  46.0 3.0 %collective-permute-start.13 = (f32[200,128]{1,0:T(8,128)S(1)}, f32[200,128]{1,0:T(8,128)S(1)}, u32[]{:S(2)}, u32[]{:S(2)}) collective-permute-start(f32[200,128]{1,0:T(8,128)S(1)} %get-tuple-element.93), channel_id=1, source_target_pairs={{0,8},{2,10},{4,12},{6,14},{8,0},{10,2},{12,4},{14,6},{1,9},{3,11}... | collective-permute-start | bytes 307208 | tf_op jit(solution)/shard_map/ppermute | solution.py:1029
  49.0 0.2 collective-permute-done.11.far_ref
  49.2 0.2 last_far.1
  49.5 2.9 %collective-permute-done.12.refs_2_ = f32[224,128]{1,0:T(8,128)S(1)} collective-permute-done((f32[224,128]{1,0:T(8,128)S(1)}, f32[224,128]{1,0:T(8,128)S(1)}, u32[]{:S(2)}, u32[]{:S(2)}) %collective-permute-start.12) | collective-permute-done | bytes 114720 | tf_op jit(solution)/shard_map/ppermute | solution.py:1022
  52.3 1.2 %early_image.1 = (f32[17,16,768]{2,1,0:T(8,128)S(1)}, s32[8,128]{1,0:T(8,128)S(1)}) custom-call(s32[17]{0:T(128)} %lags_ref.1, f32[4,96,128]{2,1,0:T(8,128)S(1)} %get-tuple-element.88.refs_1_, f32[224,128]{1,0:T(8,128)S(1)} %collective-permute-done.12.refs_2_), custom_call_target="tpu_custom_call" | custom-call | flops 2088960 | bytes 1671168 | tf_op jit(solution)/shard_map/early_image/pallas_call | solution.py:946
  53.5 0.9 %write_out.1 = f32[32,48,128]{2,1,0:T(8,128)} custom-call(f32[32,48,128]{2,1,0:T(8,128)S(1)} %get-tuple-element.87.level_ref), custom_call_target="tpu_custom_call" | custom-call | bytes 1572864 | tf_op jit(solution)/shard_map/write_out/pallas_call | solution.py:827
  54.4 1.1 %pack_own.1.refs_1_ = f32[17,96,128]{2,1,0:T(8,128)S(1)} custom-call(s32[17]{0:T(128)} %lags_ref.1, f32[24,16,128]{2,1,0:T(8,128)S(1)} %get-tuple-element.91.even_ref, bf16[512,512]{1,0:T(8,128)(2,1)S(1)} %get-tuple-element.92.matrix_ref), custom_call_target="tpu_custom_call" | custom-call | flops 50331648 | bytes 786432 | tf_op jit(solution)/shard_map/pack_own/pallas_call | solution.py:574
  55.5 1.1 %last_image.1 = f32[17,16,768]{2,1,0:T(8,128)} custom-call(s32[8,128]{1,0:T(8,128)S(1)} %get-tuple-element.90.refs_0_, f32[17,96,128]{2,1,0:T(8,128)S(1)} %pack_own.1.refs_1_, f32[200,128]{1,0:T(8,128)S(1)} %collective-permute-done.13.refs_2_, f32[48,128]{1,0:T(8,128)S(1)} %collective-permute-done.14.refs_3_, f32[17,16,768]{2,1,0:T(8,128)S(1)} %get-tuple-element.95.refs_4_), custom_call_target="tpu_custom_call" | custom-call | flops 2088960 | bytes 1671168 | tf_op jit(solution)/shard_map/last_image/pallas_call | solution.py:946
  (14 shorter events, 0.3 us)
Async XLA Ops:
  0.6 9.2 %copy-start = (f32[32,48,128]{2,1,0:T(8,128)S(1)}, f32[32,48,128]{2,1,0:T(8,128)}, u32[]{:S(2)}) copy-start(f32[32,48,128]{2,1,0:T(8,128)} %field_ref.1) | copy-start | bytes 2359300
  1.8 13.6 %collective-permute-start.2 = (f32[32,8,128]{2,1,0:T(8,128)S(1)}, f32[32,8,128]{2,1,0:T(8,128)S(1)}, u32[]{:S(2)}, u32[]{:S(2)}) collective-permute-start(f32[32,8,128]{2,1,0:T(8,128)S(1)} %get-tuple-element.58), channel_id=1, source_target_pairs={{0,1},{1,0},{2,3},{3,2},{4,5},{5,4},{6,7},{7,6},{8,9},{9,8},{10,11... | collective-permute-start | bytes 393224 | tf_op jit(solution)/shard_map/ppermute | solution.py:994
  2.3 11.2 %collective-permute-start = (f32[4,48,128]{2,1,0:T(8,128)S(1)}, f32[4,48,128]{2,1,0:T(8,128)S(1)}, u32[]{:S(2)}, u32[]{:S(2)}) collective-permute-start(f32[4,48,128]{2,1,0:T(8,128)S(1)} %get-tuple-element.56), channel_id=1, source_target_pairs={{6,8},{8,6},{14,0},{0,14},{7,9},{9,7},{15,1},{1,15},{22,24},{24,22... | collective-permute-start | bytes 294920 | tf_op jit(solution)/shard_map/ppermute | solution.py:990
  9.8 5.5 %collective-permute-start.1 = (f32[4,48,128]{2,1,0:T(8,128)S(1)}, f32[4,48,128]{2,1,0:T(8,128)S(1)}, u32[]{:S(2)}, u32[]{:S(2)}) collective-permute-start(f32[4,48,128]{2,1,0:T(8,128)S(1)} %get-tuple-element.57), channel_id=1, source_target_pairs={{0,2},{2,0},{4,6},{6,4},{8,10},{10,8},{12,14},{14,12},{1,3},{3,1},... | collective-permute-start | bytes 294920 | tf_op jit(solution)/shard_map/ppermute | solution.py:993
  15.5 11.4 %collective-permute-start.5 = (f32[32,8,128]{2,1,0:T(8,128)S(1)}, f32[32,8,128]{2,1,0:T(8,128)S(1)}, u32[]{:S(2)}, u32[]{:S(2)}) collective-permute-start(f32[32,8,128]{2,1,0:T(8,128)S(1)} %get-tuple-element.61.refs_5_), channel_id=1, source_target_pairs={{0,1},{1,0},{2,3},{3,2},{4,5},{5,4},{6,7},{7,6},{8,9},{9,8},{10,11... | collective-permute-start | bytes 393224 | tf_op jit(solution)/shard_map/ppermute | solution.py:994
  15.6 9.9 %collective-permute-start.3 = (f32[4,48,128]{2,1,0:T(8,128)S(1)}, f32[4,48,128]{2,1,0:T(8,128)S(1)}, u32[]{:S(2)}, u32[]{:S(2)}) collective-permute-start(f32[4,48,128]{2,1,0:T(8,128)S(1)} %get-tuple-element.59.refs_3_), channel_id=1, source_target_pairs={{6,8},{8,6},{14,0},{0,14},{7,9},{9,7},{15,1},{1,15},{22,24},{24,22... | collective-permute-start | bytes 294920 | tf_op jit(solution)/shard_map/ppermute | solution.py:990
  19.8 7.1 %collective-permute-start.4 = (f32[4,48,128]{2,1,0:T(8,128)S(1)}, f32[4,48,128]{2,1,0:T(8,128)S(1)}, u32[]{:S(2)}, u32[]{:S(2)}) collective-permute-start(f32[4,48,128]{2,1,0:T(8,128)S(1)} %get-tuple-element.60.refs_4_), channel_id=1, source_target_pairs={{0,2},{2,0},{4,6},{6,4},{8,10},{10,8},{12,14},{14,12},{1,3},{3,1},... | collective-permute-start | bytes 294920 | tf_op jit(solution)/shard_map/ppermute | solution.py:993
  27.0 11.5 %collective-permute-start.8 = (f32[32,8,128]{2,1,0:T(8,128)S(1)}, f32[32,8,128]{2,1,0:T(8,128)S(1)}, u32[]{:S(2)}, u32[]{:S(2)}) collective-permute-start(f32[32,8,128]{2,1,0:T(8,128)S(1)} %get-tuple-element.69.refs_5_), channel_id=1, source_target_pairs={{0,1},{1,0},{2,3},{3,2},{4,5},{5,4},{6,7},{7,6},{8,9},{9,8},{10,11... | collective-permute-start | bytes 393224 | tf_op jit(solution)/shard_map/ppermute | solution.py:994
  27.1 9.9 %collective-permute-start.6 = (f32[4,48,128]{2,1,0:T(8,128)S(1)}, f32[4,48,128]{2,1,0:T(8,128)S(1)}, u32[]{:S(2)}, u32[]{:S(2)}) collective-permute-start(f32[4,48,128]{2,1,0:T(8,128)S(1)} %get-tuple-element.67.refs_3_), channel_id=1, source_target_pairs={{6,8},{8,6},{14,0},{0,14},{7,9},{9,7},{15,1},{1,15},{22,24},{24,22... | collective-permute-start | bytes 294920 | tf_op jit(solution)/shard_map/ppermute | solution.py:990
  31.4 7.1 %collective-permute-start.7 = (f32[4,48,128]{2,1,0:T(8,128)S(1)}, f32[4,48,128]{2,1,0:T(8,128)S(1)}, u32[]{:S(2)}, u32[]{:S(2)}) collective-permute-start(f32[4,48,128]{2,1,0:T(8,128)S(1)} %get-tuple-element.68.refs_4_), channel_id=1, source_target_pairs={{0,2},{2,0},{4,6},{6,4},{8,10},{10,8},{12,14},{14,12},{1,3},{3,1},... | collective-permute-start | bytes 294920 | tf_op jit(solution)/shard_map/ppermute | solution.py:993
  38.7 6.6 %collective-permute-start.10 = (f32[32,8,128]{2,1,0:T(8,128)S(1)}, f32[32,8,128]{2,1,0:T(8,128)S(1)}, u32[]{:S(2)}, u32[]{:S(2)}) collective-permute-start(f32[32,8,128]{2,1,0:T(8,128)S(1)} %get-tuple-element.78.refs_4_), channel_id=1, source_target_pairs={{0,1},{1,0},{2,3},{3,2},{4,5},{5,4},{6,7},{7,6},{8,9},{9,8},{10,11... | collective-permute-start | bytes 393224 | tf_op jit(solution)/shard_map/ppermute | solution.py:994
  38.7 6.5 %collective-permute-start.9 = (f32[4,48,128]{2,1,0:T(8,128)S(1)}, f32[4,48,128]{2,1,0:T(8,128)S(1)}, u32[]{:S(2)}, u32[]{:S(2)}) collective-permute-start(f32[4,48,128]{2,1,0:T(8,128)S(1)} %get-tuple-element.77.refs_3_), channel_id=1, source_target_pairs={{0,2},{2,0},{4,6},{6,4},{8,10},{10,8},{12,14},{14,12},{1,3},{3,1},... | collective-permute-start | bytes 294920 | tf_op jit(solution)/shard_map/ppermute | solution.py:993
  38.8 10.4 %collective-permute-start.11 = (f32[4,48,128]{2,1,0:T(8,128)S(1)}, f32[4,48,128]{2,1,0:T(8,128)S(1)}, u32[]{:S(2)}, u32[]{:S(2)}) collective-permute-start(f32[4,48,128]{2,1,0:T(8,128)S(1)} %get-tuple-element.76.refs_2_), channel_id=1, source_target_pairs={{6,8},{8,6},{14,0},{0,14},{7,9},{9,7},{15,1},{1,15},{22,24},{24,22... | collective-permute-start | bytes 294920 | tf_op jit(solution)/shard_map/ppermute | solution.py:990
  43.1 9.3 %collective-permute-start.12 = (f32[224,128]{1,0:T(8,128)S(1)}, f32[224,128]{1,0:T(8,128)S(1)}, u32[]{:S(2)}, u32[]{:S(2)}) collective-permute-start(f32[224,128]{1,0:T(8,128)S(1)} %get-tuple-element.89), channel_id=1, source_target_pairs={{0,8},{2,10},{4,12},{6,14},{8,0},{10,2},{12,4},{14,6},{1,9},{3,11}... | collective-permute-start | bytes 344072 | tf_op jit(solution)/shard_map/ppermute | solution.py:1022
  46.0 9.5 %collective-permute-start.13 = (f32[200,128]{1,0:T(8,128)S(1)}, f32[200,128]{1,0:T(8,128)S(1)}, u32[]{:S(2)}, u32[]{:S(2)}) collective-permute-start(f32[200,128]{1,0:T(8,128)S(1)} %get-tuple-element.93), channel_id=1, source_target_pairs={{0,8},{2,10},{4,12},{6,14},{8,0},{10,2},{12,4},{14,6},{1,9},{3,11}... | collective-permute-start | bytes 307208 | tf_op jit(solution)/shard_map/ppermute | solution.py:1029
  49.4 6.1 %collective-permute-start.14 = (f32[48,128]{1,0:T(8,128)S(1)}, f32[48,128]{1,0:T(8,128)S(1)}, u32[]{:S(2)}, u32[]{:S(2)}) collective-permute-start(f32[48,128]{1,0:T(8,128)S(1)} %get-tuple-element.94), channel_id=1, source_target_pairs={{0,8},{2,10},{4,12},{6,14},{8,0},{10,2},{12,4},{14,6},{1,9},{3,11}... | collective-permute-start | bytes 73736 | tf_op jit(solution)/shard_map/ppermute | solution.py:1032
